TPU v7x, 256 devices: a whole 4x4x8 slice. The times are simulated.
256 devices in a mesh: layer: 32 (over y_lo, z, core), col: 4 (over x), row: 2 (over y_hi).
Axes of the slice: x: 4, y: 4 (y_hi: 2, y_lo: 2; y = y_hi * 2 + y_lo), z: 8, core: 2. Of those that a mesh axis runs over, the one named last changes fastest.
Arguments:
- front_copies: bfloat16 [32, 3072, 3072], P('layer', 'row', 'col'), may hold values from -6 to 6
- lower_panels: bfloat16 [32, 2, 3072, 512], P('layer', None, 'row', 'col'), may hold values from -0.25 to 0.25
- upper_panels: bfloat16 [32, 2, 512, 3072], P('layer', None, 'row', 'col'), may hold values from -6 to 6
- diag_blocks: float32 [32, 2, 512, 512], P('layer'), may hold values from -2 to 4, as said below
- block_fill: int32 [32, 2, 24], P('layer'), may hold values 0 or 1
- widths: int32 [32, 2], P('layer'), may hold values from 256 to 512, as said below
Outputs:
- summed_strips: float32 [32, 384, 3072], P('layer', 'row', 'col')
Inputs may be any that keep to these rules, and one draw needn't show every extreme that they name: `widths`: each supernode uses between half and all of its 512 columns; some supernode uses all. `diag_blocks`: diagonal entries lie between 1 and 4.
All inputs are finite; a program needn't handle non-finite values. No bound on the sum of `block_fill` on one device may be relied on, other than what follows from the above.
Results may differ from a plain program's by a relative error of at most 0.0014.
Values may be sent and summed in bfloat16 or wider, within the bound.
No kernel may reach another device: no remote copies, remote signals or barrier semaphores. Data moves between devices by JAX's collectives and lax.ppermute only.
A program may use at most 320 MiB of HBM per device.

v0:
```python
import jax
import jax.numpy as jnp
from jax import lax
from jax.sharding import PartitionSpec as P

BLOCK = 128
NS_ITERS = 3


def partner(block, axis, stride):
    count = lax.axis_size(axis)
    route = []
    for low in range(count):
        high = low | 1 << stride
        if high != low and high < count:
            route += [(low, high), (high, low)]
    return lax.ppermute(block, axis, route)


def masked_system(system_in, width_vec):
    order = system_in.shape[-1]
    indices = jnp.arange(order, dtype=jnp.int32)
    inside = indices[None, :] < width_vec[:, None]
    square = inside[:, :, None] & inside[:, None, :]
    identity = jnp.eye(order, dtype=system_in.dtype)
    return (jnp.where(square, system_in, identity[None]), square)


def on_device(front_copies, lower_panels, upper_panels, diag_blocks, block_fill, widths):
    front = front_copies[0]
    lower = lower_panels[0]
    upper = upper_panels[0]
    system_in = diag_blocks[0]
    fill = block_fill[0]
    width_vec = widths[0]
    row_count = front.shape[0]
    col_count = front.shape[1]
    members = upper.shape[0]
    fill_all = jnp.repeat(fill, BLOCK, axis=1).astype(jnp.float32)
    row_begin = lax.axis_index("row") * row_count
    col_begin = lax.axis_index("col") * col_count
    rows_mask = lax.dynamic_slice_in_dim(fill_all, row_begin, row_count, 1)
    cols_mask = lax.dynamic_slice_in_dim(fill_all, col_begin, col_count, 1)
    system, square = masked_system(system_in, width_vec)
    diagonal = jnp.diagonal(system, axis1=1, axis2=2)
    order = system.shape[-1]
    start_inverse = jnp.eye(order, dtype=jnp.float32)[None] / diagonal[:, None, :]
    inverse = start_inverse
    for sweep_no in range(NS_ITERS):
        product = jnp.einsum("sij,sjk->sik", system, inverse, precision=lax.Precision.HIGHEST)
        inverse = 2.0 * inverse - jnp.einsum(
            "sij,sjk->sik", inverse, product, precision=lax.Precision.HIGHEST
        )
    kept_inverse = jnp.where(square, inverse, 0.0)
    piece = lax.all_gather(upper, "row", axis=1, tiled=True)
    columns = lax.slice_in_dim(kept_inverse, 0, piece.shape[1], axis=2)
    scaled = jnp.zeros((members, order, col_count), jnp.float32) + jnp.einsum(
        "sij,sjk->sik", columns, piece.astype(jnp.float32), precision=lax.Precision.HIGHEST
    )
    scaled_upper = (scaled * cols_mask[:, None, :]).astype(jnp.bfloat16)
    masked_lower = lower * rows_mask[:, :, None].astype(jnp.bfloat16)
    total = jnp.zeros((row_count, col_count), jnp.float32)
    piece = lax.all_gather(masked_lower, "col", axis=2, tiled=True)
    band = lax.slice_in_dim(scaled_upper, 0, piece.shape[2], axis=1)
    for member in range(members):
        total = total + jnp.dot(piece[member], band[member], preferred_element_type=jnp.float32)
    own_copy = front.astype(jnp.float32) - total
    group = min(8, lax.axis_size("layer"))
    levels = group.bit_length() - 1
    strip = row_count // group
    blocks = own_copy.reshape((2,) * levels + (strip, col_count))
    bit_order = list(range(levels))
    axis_bits = list(range(levels - 1, -1, -1))
    layer_index = lax.axis_index("layer")
    for bit_pos in bit_order:
        axis_pos = axis_bits.index(bit_pos)
        upper_side = layer_index >> bit_pos & 1 == 1
        low_half = lax.index_in_dim(blocks, 0, axis_pos, keepdims=False)
        high_half = lax.index_in_dim(blocks, 1, axis_pos, keepdims=False)
        keep_half = jnp.where(upper_side, high_half, low_half)
        send_half = jnp.where(upper_side, low_half, high_half)
        blocks = keep_half + partner(send_half, "layer", bit_pos)
        axis_bits.pop(axis_pos)
    return blocks.reshape(1, strip, col_count)


def solution(mesh):
    placed = (
        P("layer", "row", "col"),
        P("layer", None, "row", "col"),
        P("layer", None, "row", "col"),
        P("layer", None, None, None),
        P("layer", None, None),
        P("layer", None),
    )
    return jax.shard_map(
        on_device, mesh=mesh, in_specs=placed, out_specs=P("layer", "row", "col"), check_vma=False
    )
```

profile of v0, /device:TPU:1, one launch (start us, length us, event | category | flops | bytes accessed | tf_op | source)
XLA Modules:
  0.0 190.7 jit_solution(5535278846581699069)
XLA Ops:
  6.5 0.0 copy-start.6
  6.5 0.0 all-gather.6.cloned.1.call-start
  6.5 0.7 all-gather.6.cloned.1.call-update
  7.3 0.0 all-gather.4.cloned.1.call-start
  7.3 0.7 convert_bitcast_fusion
  8.0 0.1 broadcast_bitcast_fusion
  8.1 2.5 %bitcast_multiply_fusion = bf16[2,1536,128]{2,1,0:T(8,128)(2,1)} fusion(bf16[1,2,1536,128]{3,2,1,0:T(8,128)(2,1)} %param.7, bf16[2,1536]{1,0:T(2,128)(2,1)S(1)} %dynamic-slice_convert_fusion), kind=kLoop, calls=%fused_computation.34 | loop fusion | flops 393216 | bytes 1579008 | tf_op jit(solution)/shard_map/mul | solution.py:61
  10.6 0.0 all-gather.4.cloned.1.call-update
  10.7 0.1 fusion.17
  10.8 0.0 copy-done.6
  10.8 0.1 iota_compare_fusion.1
  10.9 1.9 and_select_fusion.1
  12.8 60.2 %copy.11 = f32[2,512,512]{0,2,1:T(8,128)} copy(f32[2,512,512]{2,1,0:T(8,128)S(1)} %and_select_fusion.1) | data formatting | bytes 4194304 | tf_op jit(solution)/shard_map/jit(_where)/select_n | solution.py:26
  73.0 5.6 %gather_fusion = f32[512,2]{1,0:T(8,128)S(1)} fusion(f32[2,512,512]{0,2,1:T(8,128)} %copy.11, s32[512]{0:T(512)S(1)} %bitcast.59), kind=kCustom, calls=%fused_computation | custom fusion | bytes 12288 | tf_op jit(solution)/shard_map/jit(diagonal)/gather | solution.py:45
  78.6 0.1 copy.12
  78.7 3.6 %fusion.5 = f32[2,512,512]{2,1,0:T(8,128)S(1)} fusion(f32[2,512,512]{2,1,0:T(8,128)S(1)} %and_select_fusion.1, f32[2,512]{1,0:T(2,128)S(1)} %copy.12, f32[512,512]{1,0:T(8,128)S(1)} %fusion.17), kind=kOutput, calls=%fused_computation.14 | convolution fusion | flops 3221749760 | bytes 5246976 | tf_op jit(solution)/shard_map/sij,sjk->sik/dot_general | solution.py:50
  82.3 3.7 %multiply_subtract_fusion.1 = f32[2,512,512]{2,1,0:T(8,128)S(1)} fusion(f32[2,512,512]{2,1,0:T(8,128)S(1)} %fusion.5, f32[2,512]{1,0:T(2,128)S(1)} %copy.12, f32[512,512]{1,0:T(8,128)S(1)} %fusion.17), kind=kOutput, calls=%fused_computation.11 | convolution fusion | flops 3223322624 | bytes 5246976 | tf_op jit(solution)/shard_map/sij,sjk->sik/dot_general | solution.py:51
  86.0 3.6 %fusion.24 = f32[2,512,512]{2,1,0:T(8,128)S(1)} fusion(f32[2,512,512]{2,1,0:T(8,128)S(1)} %and_select_fusion.1, f32[2,512,512]{2,1,0:T(8,128)S(1)} %multiply_subtract_fusion.1), kind=kOutput, calls=%fused_computation.48 | convolution fusion | flops 3221225472 | bytes 6291456 | tf_op jit(solution)/shard_map/sij,sjk->sik/dot_general | solution.py:50
  89.6 3.8 %multiply_subtract_fusion = f32[2,512,512]{2,1,0:T(8,128)S(1)} fusion(f32[2,512,512]{2,1,0:T(8,128)S(1)} %multiply_subtract_fusion.1, f32[2,512,512]{2,1,0:T(8,128)S(1)} %fusion.24), kind=kOutput, calls=%fused_computation.10 | convolution fusion | flops 3222274048 | bytes 6291456 | tf_op jit(solution)/shard_map/sij,sjk->sik/dot_general | solution.py:51
  93.4 0.0 copy-start
  93.4 3.5 %fusion.25 = f32[2,512,512]{2,1,0:T(8,128)S(1)} fusion(f32[2,512,512]{2,1,0:T(8,128)S(1)} %and_select_fusion.1, f32[2,512,512]{2,1,0:T(8,128)S(1)} %multiply_subtract_fusion), kind=kOutput, calls=%fused_computation.49 | convolution fusion | flops 3221225472 | bytes 6291456 | tf_op jit(solution)/shard_map/sij,sjk->sik/dot_general | solution.py:50
  97.0 0.0 copy-done
  97.0 3.5 %fusion.26 = f32[2,512,512]{2,1,0:T(8,128)S(1)} fusion(f32[2,512,512]{2,1,0:T(8,128)S(1)} %multiply_subtract_fusion, f32[2,512,512]{2,1,0:T(8,128)S(1)} %fusion.25), kind=kOutput, calls=%fused_computation.50 | convolution fusion | flops 3221225472 | bytes 6291456 | tf_op jit(solution)/shard_map/sij,sjk->sik/dot_general | solution.py:51
  100.5 0.0 all-gather.6.cloned.1.call-done
  100.6 6.1 %multiply_convert_fusion = bf16[2,512,768]{2,1,0:T(8,128)(2,1)} fusion(f32[2,512,512]{2,1,0:T(8,128)S(1)} %fusion.26, f32[2,512,512]{2,1,0:T(8,128)} %copy-done, bf16[1,2,512,768]{3,2,1,0:T(8,128)(2,1)} %all-gather.6.cloned.1.call-done, f32[2,768]{1,0:T(2,128)S(1)} %constant_dynamic-slice_fusion, pred[2,512]{1,0:T(4,128)(4,1)S(1)} %iota_compare_fusion.1), kind=kOutput, calls=%fused_computation.2 | convolution fusion | flops 4835508224 | bytes 7347200 | tf_op jit(solution)/shard_map/sij,sjk->sik/dot_general | solution.py:57
  106.6 0.0 copy-start.3
  106.7 3.1 %fusion.7 = f32[1536,768]{1,0:T(8,128)S(1)} fusion(bf16[2,1536,512]{2,1,0:T(8,128)(2,1)} %all-gather.4.cloned.1.call-done, bf16[2,512,768]{2,1,0:T(8,128)(2,1)} %multiply_convert_fusion), kind=kOutput, calls=%fused_computation.18 | convolution fusion | flops 1207959552 | bytes 7077888 | tf_op jit(solution)/shard_map/dot_general | solution.py:66
  109.8 0.0 copy-done.3
  109.8 0.0 copy-done.4
  109.8 0.6 copy-done.5
  110.5 1.4 convert_subtract_fusion
  111.9 0.5 fusion.23
  112.4 0.0 copy-start.1
  112.4 0.0 copy-start.2
  112.4 0.3 select_bitcast_fusion
  112.7 1.1 copy-done.1
  113.8 0.7 copy-done.2
  114.5 3.2 %collective-permute-start = (f32[2,2,192,768]{3,2,0,1:T(8,128)S(1)}, f32[2,2,192,768]{3,2,0,1:T(8,128)}, u32[]{:S(2)}, u32[]{:S(2)}) collective-permute-start(f32[2,2,192,768]{3,2,0,1:T(8,128)S(1)} %select_bitcast_fusion), channel_id=1, source_target_pairs={{0,8},{8,0},{16,24},{24,16},{32,40},{40,32},{48,56},{56,48},{64,72... | collective-permute-start | bytes 7077896 | tf_op jit(solution)/shard_map/ppermute | solution.py:17
  117.7 4.3 %collective-permute-done = f32[2,2,192,768]{3,2,0,1:T(8,128)} collective-permute-done((f32[2,2,192,768]{3,2,0,1:T(8,128)S(1)}, f32[2,2,192,768]{3,2,0,1:T(8,128)}, u32[]{:S(2)}, u32[]{:S(2)}) %collective-permute-start) | collective-permute-done | bytes 2359328 | tf_op jit(solution)/shard_map/ppermute | solution.py:17
  122.0 3.5 %bitcast_add_fusion = f32[2,2,192,768]{3,2,0,1:T(8,128)S(1)} fusion(f32[2,2,192,768]{3,2,0,1:T(8,128)} %collective-permute-done, f32[2,2,1,192,768]{4,3,2,1,0:T(8,128)} %copy-done.2, f32[2,2,1,192,768]{4,3,2,1,0:T(8,128)} %copy-done.1, pred[]{:T(512)S(6)} %eq.21), kind=kLoop, calls=%fused_computation.5 | loop fusion | flops 1179648 | bytes 9437185 | tf_op jit(solution)/shard_map/add | solution.py:82
  125.5 1.2 select_bitcast_fusion.1
  126.7 0.0 collective-permute-start.1
  126.7 27.4 %collective-permute-done.1 = f32[2,192,768]{2,1,0:T(8,128)S(1)} collective-permute-done((f32[2,192,768]{2,1,0:T(8,128)}, f32[2,192,768]{2,1,0:T(8,128)S(1)}, u32[]{:S(2)}, u32[]{:S(2)}) %collective-permute-start.1) | collective-permute-done | bytes 1179680 | tf_op jit(solution)/shard_map/ppermute | solution.py:17
  154.1 0.2 bitcast_add_fusion.1
  154.3 0.1 select_bitcast_fusion.2
  154.4 1.8 collective-permute-start.2
  156.1 26.8 %collective-permute-done.2 = f32[192,768]{1,0:T(8,128)S(1)} collective-permute-done((f32[192,768]{1,0:T(8,128)S(1)}, f32[192,768]{1,0:T(8,128)S(1)}, u32[]{:S(2)}, u32[]{:S(2)}) %collective-permute-start.2) | collective-permute-done | bytes 589856 | tf_op jit(solution)/shard_map/ppermute | solution.py:17
  182.9 0.9 fusion.20
  (7 shorter events, 0.0 us)
Async XLA Ops:
  6.5 4.2 %copy-start.6 = (s32[1,2]{1,0:T(1,128)S(1)}, s32[1,2]{1,0:T(1,128)}, u32[]{:S(2)}) copy-start(s32[1,2]{1,0:T(1,128)} %param.11) | copy-start | bytes 28
  6.5 94.0 %all-gather.6.cloned.1.call-start = ((), (), s32[]{:S(2)}) async-start(), calls=%async_computation.1 | async-start | bytes 2359296 | tf_op jit(solution)/shard_map/all_gather | solution.py:55
  7.3 99.4 %all-gather.4.cloned.1.call-start = ((), (), s32[]{:S(2)}) async-start(), calls=%async_computation | async-start | bytes 3932160 | tf_op jit(solution)/shard_map/all_gather | solution.py:63
  93.4 3.6 %copy-start = (f32[2,512,512]{2,1,0:T(8,128)}, f32[2,512,512]{2,1,0:T(8,128)S(1)}, u32[]{:S(2)}) copy-start(f32[2,512,512]{2,1,0:T(8,128)S(1)} %multiply_subtract_fusion) | copy-start | bytes 6291460
  106.6 3.2 %copy-start.3 = (bf16[2,512,768]{2,1,0:T(8,128)(2,1)S(1)}, bf16[2,512,768]{2,1,0:T(8,128)(2,1)}, u32[]{:S(2)}) copy-start(bf16[2,512,768]{2,1,0:T(8,128)(2,1)} %multiply_convert_fusion) | copy-start | bytes 4718596
  106.6 3.2 %copy-start.4 = (bf16[2,1536,512]{2,1,0:T(8,128)(2,1)S(1)}, bf16[2,1536,512]{2,1,0:T(8,128)(2,1)}, u32[]{:S(2)}) copy-start(bf16[2,1536,512]{2,1,0:T(8,128)(2,1)} %all-gather.4.cloned.1.call-done) | copy-start | bytes 9437188
  106.6 3.8 %copy-start.5 = (bf16[1,1536,768]{2,1,0:T(8,128)(2,1)S(1)}, bf16[1,1536,768]{2,1,0:T(8,128)(2,1)}, u32[]{:S(2)}) copy-start(bf16[1,1536,768]{2,1,0:T(8,128)(2,1)} %param.6) | copy-start | bytes 7077892
  112.4 1.4 copy-start.1
  112.4 2.1 %copy-start.2 = (f32[2,2,1,192,768]{4,3,2,1,0:T(8,128)}, f32[2,2,1,192,768]{4,3,2,1,0:T(8,128)S(1)}, u32[]{:S(2)}) copy-start(f32[2,2,1,192,768]{4,3,2,1,0:T(8,128)S(1)} %get-tuple-element.6) | copy-start | bytes 7077892
  114.5 7.5 %collective-permute-start = (f32[2,2,192,768]{3,2,0,1:T(8,128)S(1)}, f32[2,2,192,768]{3,2,0,1:T(8,128)}, u32[]{:S(2)}, u32[]{:S(2)}) collective-permute-start(f32[2,2,192,768]{3,2,0,1:T(8,128)S(1)} %select_bitcast_fusion), channel_id=1, source_target_pairs={{0,8},{8,0},{16,24},{24,16},{32,40},{40,32},{48,56},{56,48},{64,72... | collective-permute-start | bytes 7077896 | tf_op jit(solution)/shard_map/ppermute | solution.py:17
  126.7 27.4 %collective-permute-start.1 = (f32[2,192,768]{2,1,0:T(8,128)}, f32[2,192,768]{2,1,0:T(8,128)S(1)}, u32[]{:S(2)}, u32[]{:S(2)}) collective-permute-start(f32[2,192,768]{2,1,0:T(8,128)} %select_bitcast_fusion.1), channel_id=1, source_target_pairs={{0,16},{16,0},{8,24},{24,8},{32,48},{48,32},{40,56},{56,40},{64,80... | collective-permute-start | bytes 3538952 | tf_op jit(solution)/shard_map/ppermute | solution.py:17
  154.4 28.6 %collective-permute-start.2 = (f32[192,768]{1,0:T(8,128)S(1)}, f32[192,768]{1,0:T(8,128)S(1)}, u32[]{:S(2)}, u32[]{:S(2)}) collective-permute-start(f32[192,768]{1,0:T(8,128)S(1)} %select_bitcast_fusion.2), channel_id=1, source_target_pairs={{0,32},{32,0},{8,40},{40,8},{16,48},{48,16},{24,56},{56,24},{64,96... | collective-permute-start | bytes 1769480 | tf_op jit(solution)/shard_map/ppermute | solution.py:17
Sparse Core Ops, SparseCore 0:
  9.1 37.4 all-gather.5
  48.4 43.3 all-gather.3
where the time goes:
time: 191 us
  local copies, waits for them, and re-layouts  69 us (36%)
  waiting for transfers between devices  59.2 us (31%)
  matrix products  32.4 us (17%)
  between operations  13.6 us (7%)
  other arithmetic  11.5 us (6%)
  starting transfers between devices  4.99 us (3%)
    select_n x1, local copies, waits for them, and re-layouts, masked_system(): return (jnp.where(square, system_in, identity[None]), square)  60.2 us
    ppermute x3, waiting for transfers between devices, partner(): return lax.ppermute(block, axis, route)  58.5 us
    dot_general x3, matrix products, on_device(): jnp.einsum('sij,sjk->sik', inverse, product, precision=lax.Precision.HIGH...  11 us
    dot_general x3, matrix products, on_device(): jnp.einsum('sij,sjk->sik', system, inverse, precision=lax.Precision.HIGHEST)  10.7 us
    dot_general x1, matrix products, on_device(): jnp.einsum('sij,sjk->sik', columns, piece.astype(jnp.float32), precision=...  6.06 us
    gather x2, local copies, waits for them, and re-layouts, on_device(): diagonal = jnp.diagonal(system, axis1=1, axis2=2)  5.73 us
    ppermute x3, starting transfers between devices, partner(): return lax.ppermute(block, axis, route)  4.94 us
    dot_general x2, matrix products, on_device(): jnp.dot(piece[member], band[member], preferred_element_type=jnp.float32)  4.53 us
  transfers between devices with their start and end apart: 5, of which 3 were waited for; matrix products, arithmetic and copies ran while one was open for 52% of the time, Pallas kernels for 0%

commit v1 on v0

v1 whole, which is shorter than its diff:
```python
import jax
import jax.numpy as jnp
from jax import lax
from jax.experimental import pallas as pl
from jax.experimental.pallas import tpu as pltpu
from jax.sharding import PartitionSpec as P


BLOCK = 128
SUB = 32
F32 = jnp.float32
BF16 = jnp.bfloat16


def split(x):
    high = x.astype(BF16)
    return high, (x - high.astype(F32)).astype(BF16)


def dot(a, b):
    return jnp.dot(a, b, preferred_element_type=F32)


def dot3(a, b):
    return dot(a[0], b[0]) + (dot(a[0], b[1]) + dot(a[1], b[0]))


def grant(mebibytes):
    return pltpu.CompilerParams(vmem_limit_bytes=mebibytes * 1024 * 1024)


def cost(flops, moved):
    return pl.CostEstimate(flops=flops, bytes_accessed=moved, transcendentals=0)


def first_kernel(width_ref, system_ref, high_ref, low_ref, inverse_ref):
    width = width_ref[pl.program_id(0)]
    order = system_ref.shape[1]
    rows = lax.broadcasted_iota(jnp.int32, (order, order), 0)
    cols = lax.broadcasted_iota(jnp.int32, (order, order), 1)
    on_diag = rows == cols
    inside = (rows < width) & (cols < width)
    system = jnp.where(inside, system_ref[0], jnp.where(on_diag, 1.0, 0.0))
    picked = jnp.where(on_diag, system, 0.0)
    start = jnp.where(on_diag, 1.0 / jnp.where(on_diag, system, 1.0), 0.0)
    down = 1.0 / jnp.sum(picked, axis=1, keepdims=True)
    across = 1.0 / jnp.sum(picked, axis=0, keepdims=True)
    inverse = 2.0 * start - down * (system * across)
    high, low = split(system)
    high_ref[0] = high
    low_ref[0] = low
    both = split(inverse)
    product = split(dot3((high, low), both))
    inverse_ref[0] = 2.0 * inverse - dot3(both, product)


def first_call(widths, systems):
    members, order, _ = systems.shape
    block = pl.BlockSpec((1, order, order), lambda s, w: (s, 0, 0))
    return pl.pallas_call(
        first_kernel,
        grid_spec=pltpu.PrefetchScalarGridSpec(
            num_scalar_prefetch=1,
            grid=(members,),
            in_specs=[block],
            out_specs=[block] * 3,
        ),
        out_shape=[
            jax.ShapeDtypeStruct(systems.shape, BF16),
            jax.ShapeDtypeStruct(systems.shape, BF16),
            jax.ShapeDtypeStruct(systems.shape, F32),
        ],
        cost_estimate=cost(12 * members * order**3, 12 * members * order**2),
        name="first_inverse",
        compiler_params=grant(20),
    )(widths, systems)


def second_kernel(width_ref, pos_ref, high_ref, low_ref, inverse_ref, upper_ref, xh_ref, xl_ref, part_ref):
    width = width_ref[pl.program_id(0)]
    order = high_ref.shape[1]
    half = upper_ref.shape[1]
    inverse = inverse_ref[0]
    both = split(inverse)
    product = split(dot3((high_ref[0], low_ref[0]), both))
    inverse = 2.0 * inverse - dot3(both, product)
    rows = lax.broadcasted_iota(jnp.int32, (order, order), 0)
    cols = lax.broadcasted_iota(jnp.int32, (order, order), 1)
    inverse = jnp.where((rows < width) & (cols < width), inverse, 0.0)
    swap = pos_ref[2] == 1
    mine = jnp.where(swap, inverse[:, half:], inverse[:, :half])
    other = jnp.where(swap, inverse[:, :half], inverse[:, half:])
    high, low = split(mine)
    upper = upper_ref[0]
    part_ref[0] = dot(high, upper) + dot(low, upper)
    high, low = split(other)
    xh_ref[0] = high
    xl_ref[0] = low


def second_call(widths, pos, high, low, inverse, upper):
    members, order, _ = high.shape
    half, cols = upper.shape[1:]
    square = pl.BlockSpec((1, order, order), lambda s, w, p: (s, 0, 0))
    tall = pl.BlockSpec((1, order, half), lambda s, w, p: (s, 0, 0))
    return pl.pallas_call(
        second_kernel,
        grid_spec=pltpu.PrefetchScalarGridSpec(
            num_scalar_prefetch=2,
            grid=(members,),
            in_specs=[square] * 3 + [pl.BlockSpec((1, half, cols), lambda s, w, p: (s, 0, 0))],
            out_specs=[tall, tall, pl.BlockSpec((1, order, cols), lambda s, w, p: (s, 0, 0))],
        ),
        out_shape=[
            jax.ShapeDtypeStruct((members, order, half), BF16),
            jax.ShapeDtypeStruct((members, order, half), BF16),
            jax.ShapeDtypeStruct((members, order, cols), F32),
        ],
        cost_estimate=cost(14 * members * order**3, 14 * members * order**2),
        name="second_inverse",
        compiler_params=grant(24),
    )(widths, pos, high, low, inverse, upper)


def scale_kernel(pos_ref, fill_ref, xh_ref, xl_ref, part_ref, upper_ref, out_ref):
    s = pl.program_id(0)
    order, cols = part_ref.shape[1:]
    pieces = order // BLOCK
    upper = upper_ref[0]
    scaled = part_ref[0] + (dot(xh_ref[0], upper) + dot(xl_ref[0], upper))
    col = pos_ref[1]
    blocks = cols // BLOCK
    parts = []
    for j in range(blocks):
        used = fill_ref[s, col * blocks + j] != 0
        tile = scaled[:, j * BLOCK : (j + 1) * BLOCK]
        parts.append(jnp.where(used, tile, jnp.zeros_like(tile)).astype(BF16))
    scaled = jnp.concatenate(parts, axis=1)
    for k in range(pieces):
        spot = lax.rem(k - col + pieces, pieces)
        out_ref[0, spot] = scaled[k * BLOCK : (k + 1) * BLOCK]


def scale_call(pos, fill, xh, xl, part, upper):
    members, order, half = xh.shape
    cols = upper.shape[2]
    pieces = order // BLOCK
    tall = pl.BlockSpec((1, order, half), lambda s, p, f: (s, 0, 0))
    return pl.pallas_call(
        scale_kernel,
        grid_spec=pltpu.PrefetchScalarGridSpec(
            num_scalar_prefetch=2,
            grid=(members,),
            in_specs=[
                tall,
                tall,
                pl.BlockSpec((1, order, cols), lambda s, p, f: (s, 0, 0)),
                pl.BlockSpec((1, half, cols), lambda s, p, f: (s, 0, 0)),
            ],
            out_specs=pl.BlockSpec((1, pieces, BLOCK, cols), lambda s, p, f: (s, 0, 0, 0)),
        ),
        out_shape=jax.ShapeDtypeStruct((members, pieces, BLOCK, cols), BF16),
        cost_estimate=cost(4 * members * order * half * cols, 8 * members * order * cols),
        name="scale_upper",
        compiler_params=grant(20),
    )(pos, fill, xh, xl, part, upper)


def update_kernel(flip, chunk, pos_ref, fill_ref, front_ref, own_ref, next_ref, far_ref, last_ref, scaled_ref, after_ref, out_ref, wide):
    members, spots, rows = own_ref.shape[0], own_ref.shape[1], own_ref.shape[3]
    side = pos_ref[0] if not flip else 1 - pos_ref[0]
    strip = 2 * rows
    base = pos_ref[2] * (spots * 2 * strip) + side * strip + chunk * rows
    pieces = (own_ref, next_ref, far_ref, last_ref)
    order = len(pieces) * BLOCK
    for s in range(members):
        for d in range(spots):
            for j in range(rows // SUB):
                spot = lax.div(base + d * 2 * strip + j * SUB, BLOCK)
                used = fill_ref[s, spot] != 0
                for k, ref in enumerate(pieces):
                    tile = ref[s, d, 0, j * SUB : (j + 1) * SUB, :]
                    begin = s * order + k * BLOCK
                    top = d * rows + j * SUB
                    wide[top : top + SUB, begin : begin + BLOCK] = jnp.where(used, tile, jnp.zeros_like(tile))
    scaled = scaled_ref[...].reshape(members * order, scaled_ref.shape[-1])
    update = dot(wide[...], scaled).reshape(spots, rows, scaled.shape[1])
    out_ref[...] = front_ref[:, 0, 0].astype(F32) - update


def update_call(flip, chunk, pos, fill, front, lowers, scaled, after):
    spots, _, _, rows, cols = front.shape
    members = scaled.shape[0]
    order = scaled.shape[1] * scaled.shape[2]

    def side(p):
        return 1 - p[0] if flip else p[0]

    piece = pl.BlockSpec((members, spots, 1, rows, BLOCK), lambda i, p, f: (0, 0, side(p), 0, 0))

    def body(*refs):
        update_kernel(flip, chunk, *refs)

    return pl.pallas_call(
        body,
        grid_spec=pltpu.PrefetchScalarGridSpec(
            num_scalar_prefetch=2,
            grid=(1,),
            in_specs=[pl.BlockSpec((spots, 1, 1, rows, cols), lambda i, p, f: (0, side(p), chunk, 0, 0))]
            + [piece] * 4
            + [pl.BlockSpec(scaled.shape, lambda i, p, f: (0, 0, 0, 0)), pl.BlockSpec(memory_space=pl.ANY)],
            out_specs=pl.BlockSpec((spots, rows, cols), lambda i, p, f: (0, 0, 0)),
            scratch_shapes=[pltpu.VMEM((spots * rows, members * order), BF16)],
        ),
        out_shape=jax.ShapeDtypeStruct((spots, rows, cols), F32),
        cost_estimate=cost(2 * spots * rows * members * order * cols, 4000000),
        compiler_params=grant(16),
    )(pos, fill, front, *lowers, scaled, after)


def round_kernel(pos_ref, kept_ref, got_ref, own_ref, *out_refs):
    place = pos_ref[3]
    own_ref[...] = kept_ref[place] + got_ref[place]
    for k, out_ref in enumerate(out_refs):
        spot = lax.bitwise_xor(place, k + 1)
        out_ref[...] = (kept_ref[spot] + got_ref[spot]).astype(out_ref.dtype)


def round_call(pos, kept, got):
    spots, rows, cols = kept.shape
    whole = pl.BlockSpec((spots, rows, cols), lambda i, p: (0, 0, 0))
    tile = pl.BlockSpec((rows, cols), lambda i, p: (0, 0))
    return pl.pallas_call(
        round_kernel,
        grid_spec=pltpu.PrefetchScalarGridSpec(
            num_scalar_prefetch=1, grid=(1,), in_specs=[whole, whole], out_specs=[tile] * spots
        ),
        out_shape=[jax.ShapeDtypeStruct((rows, cols), F32)]
        + [jax.ShapeDtypeStruct((rows, cols), F32)]
        + [jax.ShapeDtypeStruct((rows, cols), BF16)] * (spots - 2),
        cost_estimate=cost(spots * rows * cols, 10 * spots * rows * cols),
        name="round_sums",
        compiler_params=grant(12),
    )(pos, kept, got)


def final_kernel(*refs):
    out_ref = refs[-1]
    per = (len(refs) - 1) // 2
    rows = refs[0].shape[0]
    for chunk in range(2):
        group = refs[chunk * per : (chunk + 1) * per]
        total = group[0][...]
        for ref in group[1:]:
            total = total + ref[...].astype(F32)
        out_ref[0, chunk * rows : (chunk + 1) * rows] = total


def final_call(parts):
    rows, cols = parts[0].shape
    return pl.pallas_call(
        final_kernel,
        out_shape=jax.ShapeDtypeStruct((1, 2 * rows, cols), F32),
        cost_estimate=cost(len(parts) * rows * cols, 3 * len(parts) * rows * cols),
        name="final_sums",
        compiler_params=grant(8),
    )(*parts)


def on_device(front_copies, lower_panels, upper_panels, diag_blocks, block_fill, widths):
    layers, col_devices = lax.axis_size("layer"), lax.axis_size("col")
    layer = lax.axis_index("layer")
    row_index, col_index = lax.axis_index("row"), lax.axis_index("col")
    which = jnp.arange(4, dtype=jnp.int32)
    pos = jnp.where(
        which == 0,
        layer & 1,
        jnp.where(which == 1, col_index, jnp.where(which == 2, row_index, layer >> 1 & 3)),
    ).astype(jnp.int32)
    upper, fill, width_vec = upper_panels[0], block_fill[0], widths[0]
    row_count, cols = front_copies.shape[1:]
    members = upper.shape[0]
    spots = 4
    rows = row_count // (spots * 4)
    front = front_copies.reshape(spots, 2, 2, rows, cols)
    lower = lower_panels.reshape(members, spots, 2, 2, rows, BLOCK)

    def shift(block, step):
        return lax.ppermute(block, "col", [(i, (i + step) % col_devices) for i in range(col_devices)])

    def across(block, flip):
        return lax.ppermute(block, "layer", [(i, i ^ flip) for i in range(layers)])

    other_upper = lax.ppermute(upper, "row", [(0, 1), (1, 0)])
    lowers = []
    for chunk in range(2):
        own = lower[:, :, :, chunk]
        last = shift(own, 1)
        following = shift(own, -1)
        far = shift(own, 2)
        lowers.append((own, following, far, last))
    high, low, inverse = first_call(width_vec, diag_blocks[0])
    xh, xl, part = second_call(width_vec, pos, high, low, inverse, upper)
    scaled = scale_call(pos, fill, xh, xl, part, other_upper)
    finals = []
    after = scaled
    for chunk in range(2):
        sent = update_call(True, chunk, pos, fill, front, lowers[chunk], scaled, after)
        got = across(sent, 1)
        kept = update_call(False, chunk, pos, fill, front, lowers[chunk], scaled, after)
        own, one, two, three = round_call(pos, kept, got)
        after = one
        finals += [own, across(two, 4), across(three, 6), across(one, 2)]
    return final_call(finals)


def solution(mesh):
    placed = (
        P("layer", "row", "col"),
        P("layer", None, "row", "col"),
        P("layer", None, "row", "col"),
        P("layer", None, None, None),
        P("layer", None, None),
        P("layer", None),
    )

    return jax.shard_map(
        on_device, mesh=mesh, in_specs=placed, out_specs=P("layer", "row", "col"), check_vma=False
    )
```

time: 191 us -> 85 us (0.45)
  local copies, waits for them, and re-layouts: 69 us -> 2.77 us
  matrix products: 32.4 us -> 0 us
  Pallas kernels: 0 us -> 21.1 us
  waiting for transfers between devices: 59.2 us -> 38.7 us
  starting transfers between devices: 4.99 us -> 21.9 us
  between operations: 13.6 us -> 0.18 us
  other arithmetic: 11.5 us -> 0.01 us
    select_n x1 -> x0, local copies, waits for them, and re-layouts: 60.2 us -> none  [masked_system(): return (jnp.where(square, system_in, identity[None]), square)]
    dot_general x9 -> x0, matrix products: 32.4 us -> none  [the longest x3 11 us: on_device(): jnp.einsum('sij,sjk->sik', inverse, product, precision=lax.Precision.HIGH...]
    pallas_call x0 -> x10, Pallas kernels: none -> 21.1 us  [the longest x1 6 us: second_call(): pl.pallas_call(second_kernel, grid_spec=pltpu.PrefetchScalarGridSpec(num_...]
    ppermute x3 -> x15, waiting for transfers between devices: 58.5 us -> 38.7 us  [the longest x6 20.6 us: shift(): lax.ppermute(block, 'col', [(i, (i + step) % col_devices) for i in range(...]
    ppermute x3 -> x15, starting transfers between devices: 4.94 us -> 21.9 us  [the longest x8 11.8 us: across(): return lax.ppermute(block, 'layer', [(i, i ^ flip) for i in range(layers)])]
    gather x2 -> x0, local copies, waits for them, and re-layouts: 5.73 us -> none  [on_device(): diagonal = jnp.diagonal(system, axis1=1, axis2=2)]
    add x2 -> x0, other arithmetic: 3.74 us -> none  [on_device(): blocks = keep_half + partner(send_half, 'layer', bit_pos)]
    select_n x4 -> x1, other arithmetic: 3.43 us -> 0.01 us  [on_device(): jnp.where(which == 0, layer & 1, jnp.where(which == 1, col_index, jnp.whe...]
  transfers between devices with their start and end apart: 5 -> 15, of which waited for: 3 -> 5; matrix products, arithmetic and copies ran while one was open for 52% -> 1% of each run, Pallas kernels for 0% -> 20%
where the time goes in v1:
time: 85 us; the launch traced here: 84.8 us
  waiting for transfers between devices  38.7 us (46%)
  starting transfers between devices  21.9 us (26%)
  Pallas kernels  21.1 us (25%)
  local copies, waits for them, and re-layouts  2.77 us (3%)
    ppermute x6, waiting for transfers between devices, shift(): lax.ppermute(block, 'col', [(i, (i + step) % col_devices) for i in range(...  20.6 us
    ppermute x8, waiting for transfers between devices, across(): return lax.ppermute(block, 'layer', [(i, i ^ flip) for i in range(layers)])  18.2 us
    ppermute x8, starting transfers between devices, across(): return lax.ppermute(block, 'layer', [(i, i ^ flip) for i in range(layers)])  11.8 us
    ppermute x6, starting transfers between devices, shift(): lax.ppermute(block, 'col', [(i, (i + step) % col_devices) for i in range(...  6.36 us
    pallas_call x1, Pallas kernels, second_call(): pl.pallas_call(second_kernel, grid_spec=pltpu.PrefetchScalarGridSpec(num_...  6 us
    pallas_call x4, Pallas kernels, update_call(): pl.pallas_call(body, grid_spec=pltpu.PrefetchScalarGridSpec(num_scalar_pr...  5.91 us
    pallas_call x1, Pallas kernels, first_call(): pl.pallas_call(first_kernel, grid_spec=pltpu.PrefetchScalarGridSpec(num_s...  5.19 us
    ppermute x1, starting transfers between devices, on_device(): other_upper = lax.ppermute(upper, 'row', [(0, 1), (1, 0)])  3.73 us
  transfers between devices with their start and end apart: 15, of which 5 were waited for; matrix products, arithmetic and copies ran while one was open for 1% of the time, Pallas kernels for 20%

profile of v1, /device:TPU:1, one launch (start us, length us, event | category | flops | bytes accessed | tf_op | source)
XLA Modules:
  0.0 84.8 jit_solution(15534642545867595288)
XLA Ops:
  0.0 3.7 %collective-permute-start.3 = (bf16[2,256,768]{2,1,0:T(8,128)(2,1)}, bf16[2,256,768]{2,1,0:T(8,128)(2,1)S(1)}, u32[]{:S(2)}, u32[]{:S(2)}) collective-permute-start(bf16[2,256,768]{2,1,0:T(8,128)(2,1)} %bitcast.24), channel_id=1, source_target_pairs={{0,1},{1,0},{2,3},{3,2},{4,5},{5,4},{6,7},{7,6},{8,9},{9,8},{10,11... | collective-permute-start | bytes 2359304 | tf_op jit(solution)/shard_map/ppermute | solution.py:294
  3.7 1.2 %slice_bitcast_fusion = (bf16[2,4,2,96,128]{4,3,2,1,0:T(8,128)(2,1)S(1)}, bf16[2,4,2,96,128]{4,3,2,1,0:T(8,128)(2,1)S(1)}) fusion(bf16[2,4,2,2,96,128]{5,4,3,2,1,0:T(8,128)(2,1)} %bitcast.28), kind=kLoop, calls=%fused_computation | loop fusion | bytes 1572864 | tf_op jit(solution)/shard_map/squeeze | solution.py:297
  4.9 2.6 %collective-permute-start = (bf16[2,4,2,96,128]{4,3,2,1,0:T(8,128)(2,1)S(1)}, bf16[2,4,2,96,128]{4,3,2,1,0:T(8,128)(2,1)S(1)}, u32[]{:S(2)}, u32[]{:S(2)}) collective-permute-start(bf16[2,4,2,96,128]{4,3,2,1,0:T(8,128)(2,1)S(1)} %get-tuple-element.34.refs_3_), channel_id=1, source_target_pairs={{0,6},{2,0},{4,2},{6,4},{1,7},{3,1},{5,3},{7,5},{8,14},{10,8},{12,... | collective-permute-start | bytes 1179656 | tf_op jit(solution)/shard_map/ppermute | solution.py:289
  7.5 0.5 collective-permute-start.1
  8.0 0.6 collective-permute-start.2
  8.6 0.0 copy-done.4
  8.6 1.6 %copy-done.2 = f32[1,2,512,512]{3,2,1,0:T(8,128)S(1)} copy-done((f32[1,2,512,512]{3,2,1,0:T(8,128)S(1)}, f32[1,2,512,512]{3,2,1,0:T(8,128)}, u32[]{:S(2)}) %copy-start.2) | copy-done | bytes 2097176
  10.2 5.2 %first_inverse.1 = (bf16[2,512,512]{2,1,0:T(8,128)(2,1)S(1)}, bf16[2,512,512]{2,1,0:T(8,128)(2,1)S(1)}, f32[2,512,512]{2,1,0:T(8,128)S(1)}) custom-call(s32[2]{0:T(128)S(1)} %bitcast.26, f32[2,512,512]{2,1,0:T(8,128)S(1)} %bitcast.23), custom_call_target="tpu_custom_call" | custom-call | flops 3221225472 | bytes 6291456 | tf_op jit(solution)/shard_map/first_inverse/pallas_call | solution.py:60
  15.4 0.0 copy-done.3
  15.4 0.0 copy-start.1
  15.4 6.0 %second_inverse.1 = (bf16[2,512,256]{2,1,0:T(8,128)(2,1)S(1)}, bf16[2,512,256]{2,1,0:T(8,128)(2,1)S(1)}, f32[2,512,768]{2,1,0:T(8,128)S(1)}) custom-call(s32[2]{0:T(128)S(1)} %bitcast.27, s32[4]{0:T(128)S(1)} %compare_select_fusion.2.pos_ref.refs_0_, bf16[2,512,512]{2,1,0:T(8,128)(2,1)S(1)} %get-tuple-element.19.high_ref, ...), custom_call_target="tpu_custom_call" | custom-call | flops 3758096384 | bytes 7340032 | tf_op jit(solution)/shard_map/second_inverse/pallas_call | solution.py:106
  21.4 0.0 collective-permute-done.3.upper_ref
  21.4 0.0 copy-done.1
  21.4 0.0 copy-start
  21.5 1.8 %scale_upper.1.refs_7_.refs_8_ = bf16[2,4,128,768]{3,2,1,0:T(8,128)(2,1)S(1)} custom-call(s32[4]{0:T(128)S(1)} %compare_select_fusion.2.pos_ref.refs_0_, s32[2,24]{1,0:T(2,128)S(1)} %bitcast.18, bf16[2,512,256]{2,1,0:T(8,128)(2,1)S(1)} %get-tuple-element.22.xh_ref, bf16[2,512,256]{2,1,0:T(8,128)(2,1)S(1)} %get-tuple-element.23.xl_ref, ...), custom_call_target="tpu_custom_call" | custom-call | flops 805306368 | bytes 6291456 | tf_op jit(solution)/shard_map/scale_upper/pallas_call | solution.py:149
  23.2 0.0 collective-permute-done.refs_4_
  23.2 0.0 collective-permute-done.1.refs_5_
  23.3 5.2 %collective-permute-done.2.refs_6_ = bf16[2,4,2,96,128]{4,3,2,1,0:T(8,128)(2,1)S(1)} collective-permute-done((bf16[2,4,2,96,128]{4,3,2,1,0:T(8,128)(2,1)S(1)}, bf16[2,4,2,96,128]{4,3,2,1,0:T(8,128)(2,1)S(1)}, u32[]{:S(2)}, u32[]{:S(2)}) %collective-permute-start.2) | collective-permute-done | bytes 393248 | tf_op jit(solution)/shard_map/ppermute | solution.py:289
  28.4 0.0 copy-done
  28.4 1.5 %shard_map.65 = f32[4,96,768]{2,1,0:T(8,128)S(1)} custom-call(s32[4]{0:T(128)S(1)} %compare_select_fusion.2.pos_ref.refs_0_, s32[2,24]{1,0:T(2,128)S(1)} %bitcast.19, bf16[4,2,2,96,768]{4,3,2,1,0:T(8,128)(2,1)S(1)} %bitcast.14, bf16[2,4,2,96,128]{4,3,2,1,0:T(8,128)(2,1)S(1)} %get-tuple-element.34.refs_3_, ...), custom_call_target="tpu_custom_call" | custom-call | flops 603979776 | bytes 4000000 | tf_op jit(solution)/shard_map/pallas_call | solution.py:204
  29.9 0.6 collective-permute-start.4
  30.5 0.0 collective-permute-start.10
  30.5 2.7 %collective-permute-start.8 = (bf16[2,4,2,96,128]{4,3,2,1,0:T(8,128)(2,1)S(1)}, bf16[2,4,2,96,128]{4,3,2,1,0:T(8,128)(2,1)S(1)}, u32[]{:S(2)}, u32[]{:S(2)}) collective-permute-start(bf16[2,4,2,96,128]{4,3,2,1,0:T(8,128)(2,1)S(1)} %get-tuple-element.33.refs_3_), channel_id=1, source_target_pairs={{0,6},{2,0},{4,2},{6,4},{1,7},{3,1},{5,3},{7,5},{8,14},{10,8},{12,... | collective-permute-start | bytes 1179656 | tf_op jit(solution)/shard_map/ppermute | solution.py:289
  33.2 0.0 collective-permute-start.9
  33.2 1.5 %shard_map.64.kept_ref = f32[4,96,768]{2,1,0:T(8,128)S(1)} custom-call(s32[4]{0:T(128)S(1)} %compare_select_fusion.2.pos_ref.refs_0_, s32[2,24]{1,0:T(2,128)S(1)} %bitcast.20, bf16[4,2,2,96,768]{4,3,2,1,0:T(8,128)(2,1)S(1)} %bitcast.15, bf16[2,4,2,96,128]{4,3,2,1,0:T(8,128)(2,1)S(1)} %get-tuple-element.34.refs_3_, ...), custom_call_target="tpu_custom_call" | custom-call | flops 603979776 | bytes 4000000 | tf_op jit(solution)/shard_map/pallas_call | solution.py:204
  34.7 0.0 collective-permute-done.4.got_ref
  34.7 0.7 round_sums.2
  35.4 15.4 %collective-permute-done.10.refs_6_ = bf16[2,4,2,96,128]{4,3,2,1,0:T(8,128)(2,1)S(1)} collective-permute-done((bf16[2,4,2,96,128]{4,3,2,1,0:T(8,128)(2,1)S(1)}, bf16[2,4,2,96,128]{4,3,2,1,0:T(8,128)(2,1)S(1)}, u32[]{:S(2)}, u32[]{:S(2)}) %collective-permute-start.10) | collective-permute-done | bytes 393248 | tf_op jit(solution)/shard_map/ppermute | solution.py:289
  50.7 0.0 collective-permute-done.8.refs_4_
  50.7 0.0 collective-permute-done.9.refs_5_
  50.7 1.5 %shard_map.67 = f32[4,96,768]{2,1,0:T(8,128)S(1)} custom-call(s32[4]{0:T(128)S(1)} %compare_select_fusion.2.pos_ref.refs_0_, s32[2,24]{1,0:T(2,128)S(1)} %bitcast.21, bf16[4,2,2,96,768]{4,3,2,1,0:T(8,128)(2,1)S(1)} %bitcast.16, bf16[2,4,2,96,128]{4,3,2,1,0:T(8,128)(2,1)S(1)} %get-tuple-element.33.refs_3_, ...), custom_call_target="tpu_custom_call" | custom-call | flops 603979776 | bytes 4000000 | tf_op jit(solution)/shard_map/pallas_call | solution.py:204
  52.2 1.0 %collective-permute-start.11 = (f32[4,96,768]{2,1,0:T(8,128)S(1)}, f32[4,96,768]{2,1,0:T(8,128)S(1)}, u32[]{:S(2)}, u32[]{:S(2)}) collective-permute-start(f32[4,96,768]{2,1,0:T(8,128)S(1)} %shard_map.67), channel_id=1, source_target_pairs={{0,8},{8,0},{16,24},{24,16},{32,40},{40,32},{48,56},{56,48},{64,72... | collective-permute-start | bytes 3538952 | tf_op jit(solution)/shard_map/ppermute | solution.py:292
  53.2 1.6 %collective-permute-start.7 = (f32[96,768]{1,0:T(8,128)S(1)}, f32[96,768]{1,0:T(8,128)S(1)}, u32[]{:S(2)}, u32[]{:S(2)}) collective-permute-start(f32[96,768]{1,0:T(8,128)S(1)} %get-tuple-element.28.refs_8_), channel_id=1, source_target_pairs={{0,16},{8,24},{16,0},{24,8},{32,48},{40,56},{48,32},{56,40},{64,80... | collective-permute-start | bytes 884744 | tf_op jit(solution)/shard_map/ppermute | solution.py:292
  54.9 3.0 %collective-permute-start.5 = (bf16[96,768]{1,0:T(8,128)(2,1)S(1)}, bf16[96,768]{1,0:T(8,128)(2,1)S(1)}, u32[]{:S(2)}, u32[]{:S(2)}) collective-permute-start(bf16[96,768]{1,0:T(8,128)(2,1)S(1)} %get-tuple-element.26), channel_id=1, source_target_pairs={{0,32},{8,40},{16,48},{24,56},{32,0},{40,8},{48,16},{56,24},{64,96... | collective-permute-start | bytes 442376 | tf_op jit(solution)/shard_map/ppermute | solution.py:292
  57.9 1.5 %shard_map.66.kept_ref = f32[4,96,768]{2,1,0:T(8,128)S(1)} custom-call(s32[4]{0:T(128)S(1)} %compare_select_fusion.2.pos_ref.refs_0_, s32[2,24]{1,0:T(2,128)S(1)} %bitcast.22, bf16[4,2,2,96,768]{4,3,2,1,0:T(8,128)(2,1)S(1)} %bitcast.17, bf16[2,4,2,96,128]{4,3,2,1,0:T(8,128)(2,1)S(1)} %get-tuple-element.33.refs_3_, ...), custom_call_target="tpu_custom_call" | custom-call | flops 603979776 | bytes 4000000 | tf_op jit(solution)/shard_map/pallas_call | solution.py:204
  59.4 0.0 collective-permute-done.11.got_ref
  59.4 0.7 round_sums.3
  60.0 0.1 collective-permute-start.14
  60.1 1.2 %collective-permute-start.6 = (bf16[96,768]{1,0:T(8,128)(2,1)S(1)}, bf16[96,768]{1,0:T(8,128)(2,1)S(1)}, u32[]{:S(2)}, u32[]{:S(2)}) collective-permute-start(bf16[96,768]{1,0:T(8,128)(2,1)S(1)} %get-tuple-element.27), channel_id=1, source_target_pairs={{0,48},{8,56},{16,32},{24,40},{32,16},{40,24},{48,0},{56,8},{64,11... | collective-permute-start | bytes 442376 | tf_op jit(solution)/shard_map/ppermute | solution.py:292
  61.3 1.5 %collective-permute-start.12 = (bf16[96,768]{1,0:T(8,128)(2,1)S(1)}, bf16[96,768]{1,0:T(8,128)(2,1)S(1)}, u32[]{:S(2)}, u32[]{:S(2)}) collective-permute-start(bf16[96,768]{1,0:T(8,128)(2,1)S(1)} %get-tuple-element.30), channel_id=1, source_target_pairs={{0,32},{8,40},{16,48},{24,56},{32,0},{40,8},{48,16},{56,24},{64,96... | collective-permute-start | bytes 442376 | tf_op jit(solution)/shard_map/ppermute | solution.py:292
  62.8 1.6 %collective-permute-done.5.refs_1_ = bf16[96,768]{1,0:T(8,128)(2,1)S(1)} collective-permute-done((bf16[96,768]{1,0:T(8,128)(2,1)S(1)}, bf16[96,768]{1,0:T(8,128)(2,1)S(1)}, u32[]{:S(2)}, u32[]{:S(2)}) %collective-permute-start.5) | collective-permute-done | bytes 147488 | tf_op jit(solution)/shard_map/ppermute | solution.py:292
  64.3 2.9 %collective-permute-start.13 = (bf16[96,768]{1,0:T(8,128)(2,1)S(1)}, bf16[96,768]{1,0:T(8,128)(2,1)S(1)}, u32[]{:S(2)}, u32[]{:S(2)}) collective-permute-start(bf16[96,768]{1,0:T(8,128)(2,1)S(1)} %get-tuple-element.31), channel_id=1, source_target_pairs={{0,48},{8,56},{16,32},{24,40},{32,16},{40,24},{48,0},{56,8},{64,11... | collective-permute-start | bytes 442376 | tf_op jit(solution)/shard_map/ppermute | solution.py:292
  67.2 10.3 %collective-permute-done.6.refs_2_ = bf16[96,768]{1,0:T(8,128)(2,1)S(1)} collective-permute-done((bf16[96,768]{1,0:T(8,128)(2,1)S(1)}, bf16[96,768]{1,0:T(8,128)(2,1)S(1)}, u32[]{:S(2)}, u32[]{:S(2)}) %collective-permute-start.6) | collective-permute-done | bytes 147488 | tf_op jit(solution)/shard_map/ppermute | solution.py:292
  77.5 0.0 collective-permute-done.7.refs_3_
  77.5 0.0 collective-permute-done.12.refs_5_
  77.5 6.3 %collective-permute-done.13.refs_6_ = bf16[96,768]{1,0:T(8,128)(2,1)S(1)} collective-permute-done((bf16[96,768]{1,0:T(8,128)(2,1)S(1)}, bf16[96,768]{1,0:T(8,128)(2,1)S(1)}, u32[]{:S(2)}, u32[]{:S(2)}) %collective-permute-start.13) | collective-permute-done | bytes 147488 | tf_op jit(solution)/shard_map/ppermute | solution.py:292
  83.8 0.0 collective-permute-done.14.refs_7_
  83.8 0.9 %final_sums.1 = f32[1,192,768]{2,1,0:T(8,128)} custom-call(f32[96,768]{1,0:T(8,128)S(1)} %get-tuple-element.25.refs_0_, bf16[96,768]{1,0:T(8,128)(2,1)S(1)} %collective-permute-done.5.refs_1_, bf16[96,768]{1,0:T(8,128)(2,1)S(1)} %collective-permute-done.6.refs_2_, f32[96,768]{1,0:T(8,128)S(1)} %collective-permute-done.7.refs_3_, ...), custom_call_target="tpu_custom_call" | custom-call | flops 589824 | bytes 1769472 | tf_op jit(solution)/shard_map/final_sums/pallas_call | solution.py:261
  (4 shorter events, 0.0 us)
Async XLA Ops:
  0.0 8.6 %copy-start.4 = (s32[1,2]{1,0:T(1,128)S(1)}, s32[1,2]{1,0:T(1,128)}, u32[]{:S(2)}) copy-start(s32[1,2]{1,0:T(1,128)} %param.11) | copy-start | bytes 28
  0.0 21.4 %collective-permute-start.3 = (bf16[2,256,768]{2,1,0:T(8,128)(2,1)}, bf16[2,256,768]{2,1,0:T(8,128)(2,1)S(1)}, u32[]{:S(2)}, u32[]{:S(2)}) collective-permute-start(bf16[2,256,768]{2,1,0:T(8,128)(2,1)} %bitcast.24), channel_id=1, source_target_pairs={{0,1},{1,0},{2,3},{3,2},{4,5},{5,4},{6,7},{7,6},{8,9},{9,8},{10,11... | collective-permute-start | bytes 2359304 | tf_op jit(solution)/shard_map/ppermute | solution.py:294
  4.9 18.3 %collective-permute-start = (bf16[2,4,2,96,128]{4,3,2,1,0:T(8,128)(2,1)S(1)}, bf16[2,4,2,96,128]{4,3,2,1,0:T(8,128)(2,1)S(1)}, u32[]{:S(2)}, u32[]{:S(2)}) collective-permute-start(bf16[2,4,2,96,128]{4,3,2,1,0:T(8,128)(2,1)S(1)} %get-tuple-element.34.refs_3_), channel_id=1, source_target_pairs={{0,6},{2,0},{4,2},{6,4},{1,7},{3,1},{5,3},{7,5},{8,14},{10,8},{12,... | collective-permute-start | bytes 1179656 | tf_op jit(solution)/shard_map/ppermute | solution.py:289
  7.5 15.8 %collective-permute-start.1 = (bf16[2,4,2,96,128]{4,3,2,1,0:T(8,128)(2,1)S(1)}, bf16[2,4,2,96,128]{4,3,2,1,0:T(8,128)(2,1)S(1)}, u32[]{:S(2)}, u32[]{:S(2)}) collective-permute-start(bf16[2,4,2,96,128]{4,3,2,1,0:T(8,128)(2,1)S(1)} %get-tuple-element.34.refs_3_), channel_id=1, source_target_pairs={{0,4},{2,6},{4,0},{6,2},{1,5},{3,7},{5,1},{7,3},{8,12},{10,14},{12... | collective-permute-start | bytes 1179656 | tf_op jit(solution)/shard_map/ppermute | solution.py:289
  8.0 20.4 %collective-permute-start.2 = (bf16[2,4,2,96,128]{4,3,2,1,0:T(8,128)(2,1)S(1)}, bf16[2,4,2,96,128]{4,3,2,1,0:T(8,128)(2,1)S(1)}, u32[]{:S(2)}, u32[]{:S(2)}) collective-permute-start(bf16[2,4,2,96,128]{4,3,2,1,0:T(8,128)(2,1)S(1)} %get-tuple-element.34.refs_3_), channel_id=1, source_target_pairs={{0,2},{2,4},{4,6},{6,0},{1,3},{3,5},{5,7},{7,1},{8,10},{10,12},{12... | collective-permute-start | bytes 1179656 | tf_op jit(solution)/shard_map/ppermute | solution.py:289
  8.6 1.6 %copy-start.2 = (f32[1,2,512,512]{3,2,1,0:T(8,128)S(1)}, f32[1,2,512,512]{3,2,1,0:T(8,128)}, u32[]{:S(2)}) copy-start(f32[1,2,512,512]{3,2,1,0:T(8,128)} %param.9) | copy-start | bytes 6291460
  10.2 5.2 %copy-start.3 = (bf16[1,2,256,768]{3,2,1,0:T(8,128)(2,1)S(1)}, bf16[1,2,256,768]{3,2,1,0:T(8,128)(2,1)}, u32[]{:S(2)}) copy-start(bf16[1,2,256,768]{3,2,1,0:T(8,128)(2,1)} %param.8) | copy-start | bytes 2359300
  15.4 6.0 %copy-start.1 = (s32[1,2,24]{2,1,0:T(2,128)S(1)}, s32[1,2,24]{2,1,0:T(2,128)}, u32[]{:S(2)}) copy-start(s32[1,2,24]{2,1,0:T(2,128)} %param.10) | copy-start | bytes 580
  21.4 7.0 %copy-start = (bf16[1,1536,768]{2,1,0:T(8,128)(2,1)S(1)}, bf16[1,1536,768]{2,1,0:T(8,128)(2,1)}, u32[]{:S(2)}) copy-start(bf16[1,1536,768]{2,1,0:T(8,128)(2,1)} %param.6) | copy-start | bytes 7077892
  29.9 4.8 %collective-permute-start.4 = (f32[4,96,768]{2,1,0:T(8,128)S(1)}, f32[4,96,768]{2,1,0:T(8,128)S(1)}, u32[]{:S(2)}, u32[]{:S(2)}) collective-permute-start(f32[4,96,768]{2,1,0:T(8,128)S(1)} %shard_map.65), channel_id=1, source_target_pairs={{0,8},{8,0},{16,24},{24,16},{32,40},{40,32},{48,56},{56,48},{64,72... | collective-permute-start | bytes 3538952 | tf_op jit(solution)/shard_map/ppermute | solution.py:292
  30.5 20.2 %collective-permute-start.10 = (bf16[2,4,2,96,128]{4,3,2,1,0:T(8,128)(2,1)S(1)}, bf16[2,4,2,96,128]{4,3,2,1,0:T(8,128)(2,1)S(1)}, u32[]{:S(2)}, u32[]{:S(2)}) collective-permute-start(bf16[2,4,2,96,128]{4,3,2,1,0:T(8,128)(2,1)S(1)} %get-tuple-element.33.refs_3_), channel_id=1, source_target_pairs={{0,2},{2,4},{4,6},{6,0},{1,3},{3,5},{5,7},{7,1},{8,10},{10,12},{12... | collective-permute-start | bytes 1179656 | tf_op jit(solution)/shard_map/ppermute | solution.py:289
  30.5 20.2 %collective-permute-start.8 = (bf16[2,4,2,96,128]{4,3,2,1,0:T(8,128)(2,1)S(1)}, bf16[2,4,2,96,128]{4,3,2,1,0:T(8,128)(2,1)S(1)}, u32[]{:S(2)}, u32[]{:S(2)}) collective-permute-start(bf16[2,4,2,96,128]{4,3,2,1,0:T(8,128)(2,1)S(1)} %get-tuple-element.33.refs_3_), channel_id=1, source_target_pairs={{0,6},{2,0},{4,2},{6,4},{1,7},{3,1},{5,3},{7,5},{8,14},{10,8},{12,... | collective-permute-start | bytes 1179656 | tf_op jit(solution)/shard_map/ppermute | solution.py:289
  33.2 17.5 %collective-permute-start.9 = (bf16[2,4,2,96,128]{4,3,2,1,0:T(8,128)(2,1)S(1)}, bf16[2,4,2,96,128]{4,3,2,1,0:T(8,128)(2,1)S(1)}, u32[]{:S(2)}, u32[]{:S(2)}) collective-permute-start(bf16[2,4,2,96,128]{4,3,2,1,0:T(8,128)(2,1)S(1)} %get-tuple-element.33.refs_3_), channel_id=1, source_target_pairs={{0,4},{2,6},{4,0},{6,2},{1,5},{3,7},{5,1},{7,3},{8,12},{10,14},{12... | collective-permute-start | bytes 1179656 | tf_op jit(solution)/shard_map/ppermute | solution.py:289
  52.2 7.1 %collective-permute-start.11 = (f32[4,96,768]{2,1,0:T(8,128)S(1)}, f32[4,96,768]{2,1,0:T(8,128)S(1)}, u32[]{:S(2)}, u32[]{:S(2)}) collective-permute-start(f32[4,96,768]{2,1,0:T(8,128)S(1)} %shard_map.67), channel_id=1, source_target_pairs={{0,8},{8,0},{16,24},{24,16},{32,40},{40,32},{48,56},{56,48},{64,72... | collective-permute-start | bytes 3538952 | tf_op jit(solution)/shard_map/ppermute | solution.py:292
  53.2 24.3 %collective-permute-start.7 = (f32[96,768]{1,0:T(8,128)S(1)}, f32[96,768]{1,0:T(8,128)S(1)}, u32[]{:S(2)}, u32[]{:S(2)}) collective-permute-start(f32[96,768]{1,0:T(8,128)S(1)} %get-tuple-element.28.refs_8_), channel_id=1, source_target_pairs={{0,16},{8,24},{16,0},{24,8},{32,48},{40,56},{48,32},{56,40},{64,80... | collective-permute-start | bytes 884744 | tf_op jit(solution)/shard_map/ppermute | solution.py:292
  54.9 9.5 %collective-permute-start.5 = (bf16[96,768]{1,0:T(8,128)(2,1)S(1)}, bf16[96,768]{1,0:T(8,128)(2,1)S(1)}, u32[]{:S(2)}, u32[]{:S(2)}) collective-permute-start(bf16[96,768]{1,0:T(8,128)(2,1)S(1)} %get-tuple-element.26), channel_id=1, source_target_pairs={{0,32},{8,40},{16,48},{24,56},{32,0},{40,8},{48,16},{56,24},{64,96... | collective-permute-start | bytes 442376 | tf_op jit(solution)/shard_map/ppermute | solution.py:292
  60.0 23.8 %collective-permute-start.14 = (f32[96,768]{1,0:T(8,128)S(1)}, f32[96,768]{1,0:T(8,128)S(1)}, u32[]{:S(2)}, u32[]{:S(2)}) collective-permute-start(f32[96,768]{1,0:T(8,128)S(1)} %get-tuple-element.32), channel_id=1, source_target_pairs={{0,16},{8,24},{16,0},{24,8},{32,48},{40,56},{48,32},{56,40},{64,80... | collective-permute-start | bytes 884744 | tf_op jit(solution)/shard_map/ppermute | solution.py:292
  60.1 17.4 %collective-permute-start.6 = (bf16[96,768]{1,0:T(8,128)(2,1)S(1)}, bf16[96,768]{1,0:T(8,128)(2,1)S(1)}, u32[]{:S(2)}, u32[]{:S(2)}) collective-permute-start(bf16[96,768]{1,0:T(8,128)(2,1)S(1)} %get-tuple-element.27), channel_id=1, source_target_pairs={{0,48},{8,56},{16,32},{24,40},{32,16},{40,24},{48,0},{56,8},{64,11... | collective-permute-start | bytes 442376 | tf_op jit(solution)/shard_map/ppermute | solution.py:292
  61.3 16.2 %collective-permute-start.12 = (bf16[96,768]{1,0:T(8,128)(2,1)S(1)}, bf16[96,768]{1,0:T(8,128)(2,1)S(1)}, u32[]{:S(2)}, u32[]{:S(2)}) collective-permute-start(bf16[96,768]{1,0:T(8,128)(2,1)S(1)} %get-tuple-element.30), channel_id=1, source_target_pairs={{0,32},{8,40},{16,48},{24,56},{32,0},{40,8},{48,16},{56,24},{64,96... | collective-permute-start | bytes 442376 | tf_op jit(solution)/shard_map/ppermute | solution.py:292
  64.3 19.5 %collective-permute-start.13 = (bf16[96,768]{1,0:T(8,128)(2,1)S(1)}, bf16[96,768]{1,0:T(8,128)(2,1)S(1)}, u32[]{:S(2)}, u32[]{:S(2)}) collective-permute-start(bf16[96,768]{1,0:T(8,128)(2,1)S(1)} %get-tuple-element.31), channel_id=1, source_target_pairs={{0,48},{8,56},{16,32},{24,40},{32,16},{40,24},{48,0},{56,8},{64,11... | collective-permute-start | bytes 442376 | tf_op jit(solution)/shard_map/ppermute | solution.py:292

commit v2 on v1

v2 whole, which is shorter than its diff:
```python
import jax
import jax.numpy as jnp
from jax import lax
from jax.experimental import pallas as pl
from jax.experimental.pallas import tpu as pltpu
from jax.sharding import PartitionSpec as P


BLOCK = 128
SUB = 32
KNEE = 32.0
STEEP = 1024.0
F32 = jnp.float32
BF16 = jnp.bfloat16
VMEM = pl.BlockSpec(memory_space=pltpu.VMEM)
SMEM = pl.BlockSpec(memory_space=pltpu.SMEM)
ANY = pl.BlockSpec(memory_space=pl.ANY)


def split(x):
    high = x.astype(BF16)
    return high, (x - high.astype(F32)).astype(BF16)


def dot(a, b):
    return jnp.dot(a, b, preferred_element_type=F32)


def dot3(a, b):
    return dot(a[0], b[0]) + (dot(a[0], b[1]) + dot(a[1], b[0]))


def code(v):
    return (v * jnp.clip(jnp.abs(v) * (1.0 / KNEE), 1.0 / STEEP, 1.0)).astype(BF16)


def decode(y):
    y = y.astype(F32)
    return y * jnp.clip(lax.rsqrt(jnp.abs(y) * (1.0 / KNEE)), 1.0, STEEP)


def grant(mebibytes):
    return pltpu.CompilerParams(vmem_limit_bytes=mebibytes * 1024 * 1024)


def cost(flops, moved):
    return pl.CostEstimate(flops=flops, bytes_accessed=moved, transcendentals=0)


def square_masks(order, width):
    rows = lax.broadcasted_iota(jnp.int32, (order, order), 0)
    cols = lax.broadcasted_iota(jnp.int32, (order, order), 1)
    return rows == cols, (rows < width) & (cols < width)


def inverse_kernel(width_ref, pos_ref, system_ref, upper_ref, xh_ref, xl_ref, part_ref):
    members, order, _ = system_ref.shape
    half = upper_ref.shape[1]
    swap = pos_ref[2] == 1
    for s in range(members):
        on_diag, inside = square_masks(order, width_ref[s])
        identity = jnp.where(on_diag, 1.0, 0.0)
        system = jnp.where(inside, system_ref[s], identity)
        picked = jnp.where(on_diag, system, 0.0)
        down = 1.0 / jnp.sum(picked, axis=1, keepdims=True)
        across = 1.0 / jnp.sum(picked, axis=0, keepdims=True)
        start = jnp.where(on_diag, down, 0.0)
        inverse = (2.0 * start - down * (system * across)).astype(BF16)
        high, low = split(system)
        residual = identity - (dot(high, inverse) + dot(low, inverse))
        inverse = inverse.astype(F32) + dot(inverse, residual.astype(BF16))
        both = split(inverse)
        residual = identity - dot3((high, low), both)
        inverse = inverse + dot3(both, split(residual))
        inverse = jnp.where(inside, inverse, 0.0)
        mine = jnp.where(swap, inverse[:, half:], inverse[:, :half])
        other = jnp.where(swap, inverse[:, :half], inverse[:, half:])
        high, low = split(mine)
        upper = upper_ref[s]
        part_ref[s] = dot(high, upper) + dot(low, upper)
        high, low = split(other)
        xh_ref[s] = high
        xl_ref[s] = low


def inverse_call(widths, pos, systems, upper):
    members, order, _ = systems.shape
    half, cols = upper.shape[1:]
    return pl.pallas_call(
        inverse_kernel,
        in_specs=[SMEM, SMEM, VMEM, VMEM],
        out_specs=[VMEM] * 3,
        out_shape=[
            jax.ShapeDtypeStruct((members, order, half), BF16),
            jax.ShapeDtypeStruct((members, order, half), BF16),
            jax.ShapeDtypeStruct((members, order, cols), F32),
        ],
        cost_estimate=cost(14 * members * order**3, 8000000),
        name="inverse",
        compiler_params=grant(20),
    )(widths, pos, systems, upper)


def scale_kernel(pos_ref, fill_ref, xh_ref, xl_ref, part_ref, upper_ref, out_ref):
    members, order, cols = part_ref.shape
    pieces = order // BLOCK
    blocks = cols // BLOCK
    col = pos_ref[1]
    for s in range(members):
        upper = upper_ref[s]
        scaled = part_ref[s] + (dot(xh_ref[s], upper) + dot(xl_ref[s], upper))
        for j in range(blocks):
            used = fill_ref[s, col * blocks + j] != 0
            lanes = slice(j * BLOCK, (j + 1) * BLOCK)
            tile = scaled[:, lanes]
            tile = jnp.where(used, tile, jnp.zeros_like(tile)).astype(BF16)
            for k in range(pieces):
                spot = lax.rem(k - col + pieces, pieces)
                out_ref[s, spot, :, lanes] = tile[k * BLOCK : (k + 1) * BLOCK]


def scale_call(pos, fill, xh, xl, part, upper):
    members, order, half = xh.shape
    cols = upper.shape[2]
    return pl.pallas_call(
        scale_kernel,
        in_specs=[SMEM, SMEM] + [VMEM] * 4,
        out_specs=VMEM,
        out_shape=jax.ShapeDtypeStruct((members, order // BLOCK, BLOCK, cols), BF16),
        cost_estimate=cost(4 * members * order * half * cols, 8 * members * order * cols),
        name="scale_upper",
        compiler_params=grant(16),
    )(pos, fill, xh, xl, part, upper)


def update_call(flip, chunk, pos, fill, front, lowers, scaled, after):
    spots, _, _, rows, cols = front.shape
    members = scaled.shape[0]
    order = scaled.shape[1] * scaled.shape[2]

    def update_kernel(pos_ref, fill_ref, front_ref, *refs):
        *piece_refs, scaled_ref, after_ref, out_ref, wide = refs
        side = 1 - pos_ref[0] if flip else pos_ref[0]
        strip = 2 * rows
        base = pos_ref[2] * (spots * 2 * strip) + side * strip + chunk * rows
        for s in range(members):
            for d in range(spots):
                for j in range(rows // SUB):
                    spot = lax.div(base + d * 2 * strip + j * SUB, BLOCK)
                    used = fill_ref[s, spot] != 0
                    for k, ref in enumerate(piece_refs):
                        tile = ref[s, d, side, j * SUB : (j + 1) * SUB, :]
                        begin = s * order + k * BLOCK
                        top = d * rows + j * SUB
                        wide[top : top + SUB, begin : begin + BLOCK] = jnp.where(used, tile, jnp.zeros_like(tile))
        flat = scaled_ref[...].reshape(members * order, cols)
        update = dot(wide[...], flat).reshape(spots, rows, cols)
        for d in range(spots):
            out_ref[d] = front_ref[d, side, chunk].astype(F32) - update[d]

    return pl.pallas_call(
        update_kernel,
        in_specs=[SMEM, SMEM] + [VMEM] * 6 + [ANY],
        out_specs=VMEM,
        scratch_shapes=[pltpu.VMEM((spots * rows, members * order), BF16)],
        out_shape=jax.ShapeDtypeStruct((spots, rows, cols), F32),
        cost_estimate=cost(2 * spots * rows * members * order * cols, 4000000),
        compiler_params=grant(12),
    )(pos, fill, front, *lowers, scaled, after)


def round_kernel(pos_ref, kept_ref, got_ref, own_ref, *out_refs):
    place = pos_ref[3]
    for k, out_ref in enumerate(out_refs):
        spot = lax.bitwise_xor(place, k + 1)
        out_ref[...] = code(kept_ref[spot] + got_ref[spot])
    own_ref[...] = kept_ref[place] + got_ref[place]


def round_call(pos, kept, got):
    spots, rows, cols = kept.shape
    return pl.pallas_call(
        round_kernel,
        in_specs=[SMEM, VMEM, VMEM],
        out_specs=[VMEM] * spots,
        out_shape=[jax.ShapeDtypeStruct((rows, cols), F32)]
        + [jax.ShapeDtypeStruct((rows, cols), BF16)] * (spots - 1),
        cost_estimate=cost(spots * rows * cols, 10 * spots * rows * cols),
        name="round_sums",
        compiler_params=grant(8),
    )(pos, kept, got)


def final_kernel(*refs):
    out_ref = refs[-1]
    per = (len(refs) - 1) // 2
    rows = refs[0].shape[0]
    for chunk in range(2):
        group = refs[chunk * per : (chunk + 1) * per]
        total = group[0][...]
        for ref in group[1:]:
            total = total + decode(ref[...])
        out_ref[0, chunk * rows : (chunk + 1) * rows] = total


def final_call(parts):
    rows, cols = parts[0].shape
    return pl.pallas_call(
        final_kernel,
        in_specs=[VMEM] * len(parts),
        out_specs=VMEM,
        out_shape=jax.ShapeDtypeStruct((1, 2 * rows, cols), F32),
        cost_estimate=cost(len(parts) * rows * cols, 3 * len(parts) * rows * cols),
        name="final_sums",
        compiler_params=grant(8),
    )(*parts)


def on_device(front_copies, lower_panels, upper_panels, diag_blocks, block_fill, widths):
    layers, col_devices = lax.axis_size("layer"), lax.axis_size("col")
    layer = lax.axis_index("layer")
    row_index, col_index = lax.axis_index("row"), lax.axis_index("col")
    which = jnp.arange(4, dtype=jnp.int32)
    pos = jnp.where(
        which == 0,
        layer & 1,
        jnp.where(which == 1, col_index, jnp.where(which == 2, row_index, layer >> 1 & 3)),
    ).astype(jnp.int32)
    upper, fill, width_vec = upper_panels[0], block_fill[0], widths[0]
    row_count, cols = front_copies.shape[1:]
    members = upper.shape[0]
    spots = 4
    rows = row_count // (spots * 4)
    front = front_copies.reshape(spots, 2, 2, rows, cols)
    lower = lower_panels.reshape(members, spots, 2, 2, rows, BLOCK)

    def shift(block, step):
        return lax.ppermute(block, "col", [(i, (i + step) % col_devices) for i in range(col_devices)])

    def across(block, flip):
        return lax.ppermute(block, "layer", [(i, i ^ flip) for i in range(layers)])

    other_upper = lax.ppermute(upper, "row", [(0, 1), (1, 0)])
    lowers = []
    for chunk in range(2):
        own = lower[:, :, :, chunk]
        last = shift(own, 1)
        following = shift(own, -1)
        far = shift(own, 2)
        lowers.append((own, following, far, last))
    xh, xl, part = inverse_call(width_vec, pos, diag_blocks[0], upper)
    scaled = scale_call(pos, fill, xh, xl, part, other_upper)
    finals = []
    after = scaled
    for chunk in range(2):
        sent = update_call(True, chunk, pos, fill, front, lowers[chunk], scaled, after)
        got = across(sent, 1)
        kept = update_call(False, chunk, pos, fill, front, lowers[chunk], scaled, after)
        own, one, two, three = round_call(pos, kept, got)
        after = one
        finals += [own, across(two, 4), across(three, 6), across(one, 2)]
    return final_call(finals)


def solution(mesh):
    placed = (
        P("layer", "row", "col"),
        P("layer", None, "row", "col"),
        P("layer", None, "row", "col"),
        P("layer", None, None, None),
        P("layer", None, None),
        P("layer", None),
    )

    return jax.shard_map(
        on_device, mesh=mesh, in_specs=placed, out_specs=P("layer", "row", "col"), check_vma=False
    )
```

time: 85 us -> 82.7 us (0.973)
  the two profiles are of different devices: /device:TPU:1 before, /device:TPU:71 now
where the time goes in v2:
time: 82.7 us; the launch traced here: 82.6 us
  waiting for transfers between devices  39.9 us (48%)
  starting transfers between devices  22 us (27%)
  Pallas kernels  17.7 us (21%)
  local copies, waits for them, and re-layouts  2.77 us (3%)
    ppermute x6, waiting for transfers between devices, shift(): lax.ppermute(block, 'col', [(i, (i + step) % col_devices) for i in range(...  19.2 us
    ppermute x8, waiting for transfers between devices, across(): return lax.ppermute(block, 'layer', [(i, i ^ flip) for i in range(layers)])  17.3 us
    ppermute x8, starting transfers between devices, across(): return lax.ppermute(block, 'layer', [(i, i ^ flip) for i in range(layers)])  12.3 us
    pallas_call x1, Pallas kernels, inverse_call(): pl.pallas_call(inverse_kernel, in_specs=[SMEM, SMEM, VMEM, VMEM], out_spe...  7.8 us
    ppermute x6, starting transfers between devices, shift(): lax.ppermute(block, 'col', [(i, (i + step) % col_devices) for i in range(...  6.81 us
    pallas_call x4, Pallas kernels, update_call(): pl.pallas_call(update_kernel, in_specs=[SMEM, SMEM] + [VMEM] * 6 + [ANY],...  5.67 us
    ppermute x1, waiting for transfers between devices, on_device(): other_upper = lax.ppermute(upper, 'row', [(0, 1), (1, 0)])  3.39 us
    ppermute x1, starting transfers between devices, on_device(): other_upper = lax.ppermute(upper, 'row', [(0, 1), (1, 0)])  2.91 us
  transfers between devices with their start and end apart: 15, of which 7 were waited for; matrix products, arithmetic and copies ran while one was open for 1% of the time, Pallas kernels for 17%

profile of v2, /device:TPU:71, one launch (start us, length us, event | category | flops | bytes accessed | tf_op | source)
XLA Modules:
  0.0 82.6 jit_solution(5431781194836889983)
XLA Ops:
  0.0 0.0 copy-start.3
  0.0 0.0 copy-start.4
  0.0 2.9 %collective-permute-start.3 = (bf16[2,256,768]{2,1,0:T(8,128)(2,1)}, bf16[2,256,768]{2,1,0:T(8,128)(2,1)S(1)}, u32[]{:S(2)}, u32[]{:S(2)}) collective-permute-start(bf16[2,256,768]{2,1,0:T(8,128)(2,1)} %bitcast.24), channel_id=1, source_target_pairs={{0,1},{1,0},{2,3},{3,2},{4,5},{5,4},{6,7},{7,6},{8,9},{9,8},{10,11... | collective-permute-start | bytes 2359304 | tf_op jit(solution)/shard_map/ppermute | solution.py:243
  2.9 1.2 %slice_bitcast_fusion = (bf16[2,4,2,96,128]{4,3,2,1,0:T(8,128)(2,1)S(1)}, bf16[2,4,2,96,128]{4,3,2,1,0:T(8,128)(2,1)S(1)}) fusion(bf16[2,4,2,2,96,128]{5,4,3,2,1,0:T(8,128)(2,1)} %bitcast.27), kind=kLoop, calls=%fused_computation | loop fusion | bytes 1572864 | tf_op jit(solution)/shard_map/squeeze | solution.py:246
  4.1 0.6 collective-permute-start
  4.7 0.8 %collective-permute-start.1 = (bf16[2,4,2,96,128]{4,3,2,1,0:T(8,128)(2,1)S(1)}, bf16[2,4,2,96,128]{4,3,2,1,0:T(8,128)(2,1)S(1)}, u32[]{:S(2)}, u32[]{:S(2)}) collective-permute-start(bf16[2,4,2,96,128]{4,3,2,1,0:T(8,128)(2,1)S(1)} %get-tuple-element.28.refs_0_), channel_id=1, source_target_pairs={{0,4},{2,6},{4,0},{6,2},{1,5},{3,7},{5,1},{7,3},{8,12},{10,14},{12... | collective-permute-start | bytes 1179656 | tf_op jit(solution)/shard_map/ppermute | solution.py:238
  5.6 1.8 %collective-permute-start.2 = (bf16[2,4,2,96,128]{4,3,2,1,0:T(8,128)(2,1)S(1)}, bf16[2,4,2,96,128]{4,3,2,1,0:T(8,128)(2,1)S(1)}, u32[]{:S(2)}, u32[]{:S(2)}) collective-permute-start(bf16[2,4,2,96,128]{4,3,2,1,0:T(8,128)(2,1)S(1)} %get-tuple-element.28.refs_0_), channel_id=1, source_target_pairs={{0,2},{2,4},{4,6},{6,0},{1,3},{3,5},{5,7},{7,1},{8,10},{10,12},{12... | collective-permute-start | bytes 1179656 | tf_op jit(solution)/shard_map/ppermute | solution.py:238
  7.4 0.0 copy-done.3
  7.4 0.0 copy-done.4
  7.4 0.0 copy-start.2
  7.4 1.6 %copy-done.2 = f32[1,2,512,512]{3,2,1,0:T(8,128)S(1)} copy-done((f32[1,2,512,512]{3,2,1,0:T(8,128)S(1)}, f32[1,2,512,512]{3,2,1,0:T(8,128)}, u32[]{:S(2)}) %copy-start.2) | copy-done | bytes 2097176
  9.0 7.8 %inverse.1 = (bf16[2,512,256]{2,1,0:T(8,128)(2,1)S(1)}, bf16[2,512,256]{2,1,0:T(8,128)(2,1)S(1)}, f32[2,512,768]{2,1,0:T(8,128)S(1)}) custom-call(s32[2]{0:T(128)S(1)} %bitcast.26, s32[4]{0:T(128)S(1)} %compare_select_fusion.2.pos_ref, f32[2,512,512]{2,1,0:T(8,128)S(1)} %bitcast.23, bf16[2,256,768]{2,1,0:T(8,128)(2,1)S(1)} %bitcast.25), custom_call_target="tpu_custom_call" | custom-call | flops 3758096384 | bytes 8000000 | tf_op jit(solution)/shard_map/inverse/pallas_call | solution.py:89
  16.8 3.4 %collective-permute-done.3.upper_ref = bf16[2,256,768]{2,1,0:T(8,128)(2,1)S(1)} collective-permute-done((bf16[2,256,768]{2,1,0:T(8,128)(2,1)}, bf16[2,256,768]{2,1,0:T(8,128)(2,1)S(1)}, u32[]{:S(2)}, u32[]{:S(2)}) %collective-permute-start.3) | collective-permute-done | bytes 786464 | tf_op jit(solution)/shard_map/ppermute | solution.py:243
  20.2 0.0 copy-done.1
  20.2 1.6 %scale_upper.1.refs_4_.refs_5_ = bf16[2,4,128,768]{3,2,1,0:T(8,128)(2,1)S(1)} custom-call(s32[4]{0:T(128)S(1)} %compare_select_fusion.2.pos_ref, s32[2,24]{1,0:T(2,128)S(1)} %bitcast.18, bf16[2,512,256]{2,1,0:T(8,128)(2,1)S(1)} %get-tuple-element.16.xh_ref, bf16[2,512,256]{2,1,0:T(8,128)(2,1)S(1)} %get-tuple-element.17.xl_ref, ...), custom_call_target="tpu_custom_call" | custom-call | flops 805306368 | bytes 6291456 | tf_op jit(solution)/shard_map/scale_upper/pallas_call | solution.py:125
  21.7 0.0 collective-permute-done.refs_1_
  21.8 0.5 collective-permute-done.1.refs_2_
  22.3 2.1 %collective-permute-done.2.refs_3_ = bf16[2,4,2,96,128]{4,3,2,1,0:T(8,128)(2,1)S(1)} collective-permute-done((bf16[2,4,2,96,128]{4,3,2,1,0:T(8,128)(2,1)S(1)}, bf16[2,4,2,96,128]{4,3,2,1,0:T(8,128)(2,1)S(1)}, u32[]{:S(2)}, u32[]{:S(2)}) %collective-permute-start.2) | collective-permute-done | bytes 393248 | tf_op jit(solution)/shard_map/ppermute | solution.py:238
  24.4 0.0 copy-done
  24.4 1.4 %shard_map.65 = f32[4,96,768]{2,1,0:T(8,128)S(1)} custom-call(s32[4]{0:T(128)S(1)} %compare_select_fusion.2.pos_ref, s32[2,24]{1,0:T(2,128)S(1)} %bitcast.19, bf16[4,2,2,96,768]{4,3,2,1,0:T(8,128)(2,1)S(1)} %bitcast.14, bf16[2,4,2,96,128]{4,3,2,1,0:T(8,128)(2,1)S(1)} %get-tuple-element.28.refs_0_, ...), custom_call_target="tpu_custom_call" | custom-call | flops 603979776 | bytes 4000000 | tf_op jit(solution)/shard_map/pallas_call | solution.py:161
  25.8 1.6 %collective-permute-start.4 = (f32[4,96,768]{2,1,0:T(8,128)S(1)}, f32[4,96,768]{2,1,0:T(8,128)S(1)}, u32[]{:S(2)}, u32[]{:S(2)}) collective-permute-start(f32[4,96,768]{2,1,0:T(8,128)S(1)} %shard_map.65), channel_id=1, source_target_pairs={{0,8},{8,0},{16,24},{24,16},{32,40},{40,32},{48,56},{56,48},{64,72... | collective-permute-start | bytes 3538952 | tf_op jit(solution)/shard_map/ppermute | solution.py:241
  27.5 2.3 %collective-permute-start.10 = (bf16[2,4,2,96,128]{4,3,2,1,0:T(8,128)(2,1)S(1)}, bf16[2,4,2,96,128]{4,3,2,1,0:T(8,128)(2,1)S(1)}, u32[]{:S(2)}, u32[]{:S(2)}) collective-permute-start(bf16[2,4,2,96,128]{4,3,2,1,0:T(8,128)(2,1)S(1)} %get-tuple-element.27.refs_0_), channel_id=1, source_target_pairs={{0,2},{2,4},{4,6},{6,0},{1,3},{3,5},{5,7},{7,1},{8,10},{10,12},{12... | collective-permute-start | bytes 1179656 | tf_op jit(solution)/shard_map/ppermute | solution.py:238
  29.8 0.0 collective-permute-start.8
  29.8 1.2 %collective-permute-start.9 = (bf16[2,4,2,96,128]{4,3,2,1,0:T(8,128)(2,1)S(1)}, bf16[2,4,2,96,128]{4,3,2,1,0:T(8,128)(2,1)S(1)}, u32[]{:S(2)}, u32[]{:S(2)}) collective-permute-start(bf16[2,4,2,96,128]{4,3,2,1,0:T(8,128)(2,1)S(1)} %get-tuple-element.27.refs_0_), channel_id=1, source_target_pairs={{0,4},{2,6},{4,0},{6,2},{1,5},{3,7},{5,1},{7,3},{8,12},{10,14},{12... | collective-permute-start | bytes 1179656 | tf_op jit(solution)/shard_map/ppermute | solution.py:238
  31.0 1.4 %shard_map.64.kept_ref = f32[4,96,768]{2,1,0:T(8,128)S(1)} custom-call(s32[4]{0:T(128)S(1)} %compare_select_fusion.2.pos_ref, s32[2,24]{1,0:T(2,128)S(1)} %bitcast.20, bf16[4,2,2,96,768]{4,3,2,1,0:T(8,128)(2,1)S(1)} %bitcast.15, bf16[2,4,2,96,128]{4,3,2,1,0:T(8,128)(2,1)S(1)} %get-tuple-element.28.refs_0_, ...), custom_call_target="tpu_custom_call" | custom-call | flops 603979776 | bytes 4000000 | tf_op jit(solution)/shard_map/pallas_call | solution.py:161
  32.5 0.0 collective-permute-done.4.got_ref
  32.5 0.7 round_sums.2
  33.2 13.3 %collective-permute-done.10.refs_3_ = bf16[2,4,2,96,128]{4,3,2,1,0:T(8,128)(2,1)S(1)} collective-permute-done((bf16[2,4,2,96,128]{4,3,2,1,0:T(8,128)(2,1)S(1)}, bf16[2,4,2,96,128]{4,3,2,1,0:T(8,128)(2,1)S(1)}, u32[]{:S(2)}, u32[]{:S(2)}) %collective-permute-start.10) | collective-permute-done | bytes 393248 | tf_op jit(solution)/shard_map/ppermute | solution.py:238
  46.5 3.3 %collective-permute-done.8.refs_1_ = bf16[2,4,2,96,128]{4,3,2,1,0:T(8,128)(2,1)S(1)} collective-permute-done((bf16[2,4,2,96,128]{4,3,2,1,0:T(8,128)(2,1)S(1)}, bf16[2,4,2,96,128]{4,3,2,1,0:T(8,128)(2,1)S(1)}, u32[]{:S(2)}, u32[]{:S(2)}) %collective-permute-start.8) | collective-permute-done | bytes 393248 | tf_op jit(solution)/shard_map/ppermute | solution.py:238
  49.8 0.0 collective-permute-done.9.refs_2_
  49.8 1.4 %shard_map.67 = f32[4,96,768]{2,1,0:T(8,128)S(1)} custom-call(s32[4]{0:T(128)S(1)} %compare_select_fusion.2.pos_ref, s32[2,24]{1,0:T(2,128)S(1)} %bitcast.21, bf16[4,2,2,96,768]{4,3,2,1,0:T(8,128)(2,1)S(1)} %bitcast.16, bf16[2,4,2,96,128]{4,3,2,1,0:T(8,128)(2,1)S(1)} %get-tuple-element.27.refs_0_, ...), custom_call_target="tpu_custom_call" | custom-call | flops 603979776 | bytes 4000000 | tf_op jit(solution)/shard_map/pallas_call | solution.py:161
  51.2 1.3 %collective-permute-start.11 = (f32[4,96,768]{2,1,0:T(8,128)S(1)}, f32[4,96,768]{2,1,0:T(8,128)S(1)}, u32[]{:S(2)}, u32[]{:S(2)}) collective-permute-start(f32[4,96,768]{2,1,0:T(8,128)S(1)} %shard_map.67), channel_id=1, source_target_pairs={{0,8},{8,0},{16,24},{24,16},{32,40},{40,32},{48,56},{56,48},{64,72... | collective-permute-start | bytes 3538952 | tf_op jit(solution)/shard_map/ppermute | solution.py:241
  52.5 0.0 collective-permute-start.5
  52.5 1.6 %collective-permute-start.7 = (bf16[96,768]{1,0:T(8,128)(2,1)S(1)}, bf16[96,768]{1,0:T(8,128)(2,1)S(1)}, u32[]{:S(2)}, u32[]{:S(2)}) collective-permute-start(bf16[96,768]{1,0:T(8,128)(2,1)S(1)} %get-tuple-element.22.refs_5_), channel_id=1, source_target_pairs={{0,16},{8,24},{16,0},{24,8},{32,48},{40,56},{48,32},{56,40},{64,80... | collective-permute-start | bytes 442376 | tf_op jit(solution)/shard_map/ppermute | solution.py:241
  54.2 1.2 %collective-permute-start.6 = (bf16[96,768]{1,0:T(8,128)(2,1)S(1)}, bf16[96,768]{1,0:T(8,128)(2,1)S(1)}, u32[]{:S(2)}, u32[]{:S(2)}) collective-permute-start(bf16[96,768]{1,0:T(8,128)(2,1)S(1)} %get-tuple-element.21), channel_id=1, source_target_pairs={{0,48},{8,56},{16,32},{24,40},{32,16},{40,24},{48,0},{56,8},{64,11... | collective-permute-start | bytes 442376 | tf_op jit(solution)/shard_map/ppermute | solution.py:241
  55.3 1.4 %shard_map.66.kept_ref = f32[4,96,768]{2,1,0:T(8,128)S(1)} custom-call(s32[4]{0:T(128)S(1)} %compare_select_fusion.2.pos_ref, s32[2,24]{1,0:T(2,128)S(1)} %bitcast.22, bf16[4,2,2,96,768]{4,3,2,1,0:T(8,128)(2,1)S(1)} %bitcast.17, bf16[2,4,2,96,128]{4,3,2,1,0:T(8,128)(2,1)S(1)} %get-tuple-element.27.refs_0_, ...), custom_call_target="tpu_custom_call" | custom-call | flops 603979776 | bytes 4000000 | tf_op jit(solution)/shard_map/pallas_call | solution.py:161
  56.8 0.0 collective-permute-done.11.got_ref
  56.8 0.7 round_sums.3
  57.5 1.3 %collective-permute-start.12 = (bf16[96,768]{1,0:T(8,128)(2,1)S(1)}, bf16[96,768]{1,0:T(8,128)(2,1)S(1)}, u32[]{:S(2)}, u32[]{:S(2)}) collective-permute-start(bf16[96,768]{1,0:T(8,128)(2,1)S(1)} %get-tuple-element.24), channel_id=1, source_target_pairs={{0,32},{8,40},{16,48},{24,56},{32,0},{40,8},{48,16},{56,24},{64,96... | collective-permute-start | bytes 442376 | tf_op jit(solution)/shard_map/ppermute | solution.py:241
  58.8 2.4 %collective-permute-start.13 = (bf16[96,768]{1,0:T(8,128)(2,1)S(1)}, bf16[96,768]{1,0:T(8,128)(2,1)S(1)}, u32[]{:S(2)}, u32[]{:S(2)}) collective-permute-start(bf16[96,768]{1,0:T(8,128)(2,1)S(1)} %get-tuple-element.25), channel_id=1, source_target_pairs={{0,48},{8,56},{16,32},{24,40},{32,16},{40,24},{48,0},{56,8},{64,11... | collective-permute-start | bytes 442376 | tf_op jit(solution)/shard_map/ppermute | solution.py:241
  61.1 0.0 collective-permute-done.5.refs_1_
  61.1 2.9 %collective-permute-start.14 = (bf16[96,768]{1,0:T(8,128)(2,1)S(1)}, bf16[96,768]{1,0:T(8,128)(2,1)S(1)}, u32[]{:S(2)}, u32[]{:S(2)}) collective-permute-start(bf16[96,768]{1,0:T(8,128)(2,1)S(1)} %get-tuple-element.26), channel_id=1, source_target_pairs={{0,16},{8,24},{16,0},{24,8},{32,48},{40,56},{48,32},{56,40},{64,80... | collective-permute-start | bytes 442376 | tf_op jit(solution)/shard_map/ppermute | solution.py:241
  64.0 11.0 %collective-permute-done.6.refs_2_ = bf16[96,768]{1,0:T(8,128)(2,1)S(1)} collective-permute-done((bf16[96,768]{1,0:T(8,128)(2,1)S(1)}, bf16[96,768]{1,0:T(8,128)(2,1)S(1)}, u32[]{:S(2)}, u32[]{:S(2)}) %collective-permute-start.6) | collective-permute-done | bytes 147488 | tf_op jit(solution)/shard_map/ppermute | solution.py:241
  75.0 0.0 collective-permute-done.7.refs_3_
  75.0 0.0 collective-permute-done.12.refs_5_
  75.0 6.3 %collective-permute-done.13.refs_6_ = bf16[96,768]{1,0:T(8,128)(2,1)S(1)} collective-permute-done((bf16[96,768]{1,0:T(8,128)(2,1)S(1)}, bf16[96,768]{1,0:T(8,128)(2,1)S(1)}, u32[]{:S(2)}, u32[]{:S(2)}) %collective-permute-start.13) | collective-permute-done | bytes 147488 | tf_op jit(solution)/shard_map/ppermute | solution.py:241
  81.3 0.0 collective-permute-done.14.refs_7_
  81.4 1.2 %final_sums.1 = f32[1,192,768]{2,1,0:T(8,128)} custom-call(f32[96,768]{1,0:T(8,128)S(1)} %get-tuple-element.19.refs_0_, bf16[96,768]{1,0:T(8,128)(2,1)S(1)} %collective-permute-done.5.refs_1_, bf16[96,768]{1,0:T(8,128)(2,1)S(1)} %collective-permute-done.6.refs_2_, bf16[96,768]{1,0:T(8,128)(2,1)S(1)} %collective-permute-done.7.refs_3_, ...), custom_call_target="tpu_custom_call" | custom-call | flops 589824 | bytes 1769472 | tf_op jit(solution)/shard_map/final_sums/pallas_call | solution.py:208
  (3 shorter events, 0.0 us)
Async XLA Ops:
  0.0 7.4 %copy-start.3 = (bf16[1,2,256,768]{3,2,1,0:T(8,128)(2,1)S(1)}, bf16[1,2,256,768]{3,2,1,0:T(8,128)(2,1)}, u32[]{:S(2)}) copy-start(bf16[1,2,256,768]{3,2,1,0:T(8,128)(2,1)} %param.8) | copy-start | bytes 2359300
  0.0 7.4 %copy-start.4 = (s32[1,2]{1,0:T(1,128)S(1)}, s32[1,2]{1,0:T(1,128)}, u32[]{:S(2)}) copy-start(s32[1,2]{1,0:T(1,128)} %param.11) | copy-start | bytes 28
  0.0 20.2 %collective-permute-start.3 = (bf16[2,256,768]{2,1,0:T(8,128)(2,1)}, bf16[2,256,768]{2,1,0:T(8,128)(2,1)S(1)}, u32[]{:S(2)}, u32[]{:S(2)}) collective-permute-start(bf16[2,256,768]{2,1,0:T(8,128)(2,1)} %bitcast.24), channel_id=1, source_target_pairs={{0,1},{1,0},{2,3},{3,2},{4,5},{5,4},{6,7},{7,6},{8,9},{9,8},{10,11... | collective-permute-start | bytes 2359304 | tf_op jit(solution)/shard_map/ppermute | solution.py:243
  4.1 17.7 %collective-permute-start = (bf16[2,4,2,96,128]{4,3,2,1,0:T(8,128)(2,1)S(1)}, bf16[2,4,2,96,128]{4,3,2,1,0:T(8,128)(2,1)S(1)}, u32[]{:S(2)}, u32[]{:S(2)}) collective-permute-start(bf16[2,4,2,96,128]{4,3,2,1,0:T(8,128)(2,1)S(1)} %get-tuple-element.28.refs_0_), channel_id=1, source_target_pairs={{0,6},{2,0},{4,2},{6,4},{1,7},{3,1},{5,3},{7,5},{8,14},{10,8},{12,... | collective-permute-start | bytes 1179656 | tf_op jit(solution)/shard_map/ppermute | solution.py:238
  4.7 17.6 %collective-permute-start.1 = (bf16[2,4,2,96,128]{4,3,2,1,0:T(8,128)(2,1)S(1)}, bf16[2,4,2,96,128]{4,3,2,1,0:T(8,128)(2,1)S(1)}, u32[]{:S(2)}, u32[]{:S(2)}) collective-permute-start(bf16[2,4,2,96,128]{4,3,2,1,0:T(8,128)(2,1)S(1)} %get-tuple-element.28.refs_0_), channel_id=1, source_target_pairs={{0,4},{2,6},{4,0},{6,2},{1,5},{3,7},{5,1},{7,3},{8,12},{10,14},{12... | collective-permute-start | bytes 1179656 | tf_op jit(solution)/shard_map/ppermute | solution.py:238
  5.6 18.9 %collective-permute-start.2 = (bf16[2,4,2,96,128]{4,3,2,1,0:T(8,128)(2,1)S(1)}, bf16[2,4,2,96,128]{4,3,2,1,0:T(8,128)(2,1)S(1)}, u32[]{:S(2)}, u32[]{:S(2)}) collective-permute-start(bf16[2,4,2,96,128]{4,3,2,1,0:T(8,128)(2,1)S(1)} %get-tuple-element.28.refs_0_), channel_id=1, source_target_pairs={{0,2},{2,4},{4,6},{6,0},{1,3},{3,5},{5,7},{7,1},{8,10},{10,12},{12... | collective-permute-start | bytes 1179656 | tf_op jit(solution)/shard_map/ppermute | solution.py:238
  7.4 1.6 %copy-start.2 = (f32[1,2,512,512]{3,2,1,0:T(8,128)S(1)}, f32[1,2,512,512]{3,2,1,0:T(8,128)}, u32[]{:S(2)}) copy-start(f32[1,2,512,512]{3,2,1,0:T(8,128)} %param.9) | copy-start | bytes 6291460
  9.0 11.2 %copy-start.1 = (s32[1,2,24]{2,1,0:T(2,128)S(1)}, s32[1,2,24]{2,1,0:T(2,128)}, u32[]{:S(2)}) copy-start(s32[1,2,24]{2,1,0:T(2,128)} %param.10) | copy-start | bytes 580
  20.2 4.2 %copy-start = (bf16[1,1536,768]{2,1,0:T(8,128)(2,1)S(1)}, bf16[1,1536,768]{2,1,0:T(8,128)(2,1)}, u32[]{:S(2)}) copy-start(bf16[1,1536,768]{2,1,0:T(8,128)(2,1)} %param.6) | copy-start | bytes 7077892
  25.8 6.6 %collective-permute-start.4 = (f32[4,96,768]{2,1,0:T(8,128)S(1)}, f32[4,96,768]{2,1,0:T(8,128)S(1)}, u32[]{:S(2)}, u32[]{:S(2)}) collective-permute-start(f32[4,96,768]{2,1,0:T(8,128)S(1)} %shard_map.65), channel_id=1, source_target_pairs={{0,8},{8,0},{16,24},{24,16},{32,40},{40,32},{48,56},{56,48},{64,72... | collective-permute-start | bytes 3538952 | tf_op jit(solution)/shard_map/ppermute | solution.py:241
  27.5 19.0 %collective-permute-start.10 = (bf16[2,4,2,96,128]{4,3,2,1,0:T(8,128)(2,1)S(1)}, bf16[2,4,2,96,128]{4,3,2,1,0:T(8,128)(2,1)S(1)}, u32[]{:S(2)}, u32[]{:S(2)}) collective-permute-start(bf16[2,4,2,96,128]{4,3,2,1,0:T(8,128)(2,1)S(1)} %get-tuple-element.27.refs_0_), channel_id=1, source_target_pairs={{0,2},{2,4},{4,6},{6,0},{1,3},{3,5},{5,7},{7,1},{8,10},{10,12},{12... | collective-permute-start | bytes 1179656 | tf_op jit(solution)/shard_map/ppermute | solution.py:238
  29.8 19.9 %collective-permute-start.8 = (bf16[2,4,2,96,128]{4,3,2,1,0:T(8,128)(2,1)S(1)}, bf16[2,4,2,96,128]{4,3,2,1,0:T(8,128)(2,1)S(1)}, u32[]{:S(2)}, u32[]{:S(2)}) collective-permute-start(bf16[2,4,2,96,128]{4,3,2,1,0:T(8,128)(2,1)S(1)} %get-tuple-element.27.refs_0_), channel_id=1, source_target_pairs={{0,6},{2,0},{4,2},{6,4},{1,7},{3,1},{5,3},{7,5},{8,14},{10,8},{12,... | collective-permute-start | bytes 1179656 | tf_op jit(solution)/shard_map/ppermute | solution.py:238
  29.8 19.9 %collective-permute-start.9 = (bf16[2,4,2,96,128]{4,3,2,1,0:T(8,128)(2,1)S(1)}, bf16[2,4,2,96,128]{4,3,2,1,0:T(8,128)(2,1)S(1)}, u32[]{:S(2)}, u32[]{:S(2)}) collective-permute-start(bf16[2,4,2,96,128]{4,3,2,1,0:T(8,128)(2,1)S(1)} %get-tuple-element.27.refs_0_), channel_id=1, source_target_pairs={{0,4},{2,6},{4,0},{6,2},{1,5},{3,7},{5,1},{7,3},{8,12},{10,14},{12... | collective-permute-start | bytes 1179656 | tf_op jit(solution)/shard_map/ppermute | solution.py:238
  51.2 5.6 %collective-permute-start.11 = (f32[4,96,768]{2,1,0:T(8,128)S(1)}, f32[4,96,768]{2,1,0:T(8,128)S(1)}, u32[]{:S(2)}, u32[]{:S(2)}) collective-permute-start(f32[4,96,768]{2,1,0:T(8,128)S(1)} %shard_map.67), channel_id=1, source_target_pairs={{0,8},{8,0},{16,24},{24,16},{32,40},{40,32},{48,56},{56,48},{64,72... | collective-permute-start | bytes 3538952 | tf_op jit(solution)/shard_map/ppermute | solution.py:241
  52.5 8.6 %collective-permute-start.5 = (bf16[96,768]{1,0:T(8,128)(2,1)S(1)}, bf16[96,768]{1,0:T(8,128)(2,1)S(1)}, u32[]{:S(2)}, u32[]{:S(2)}) collective-permute-start(bf16[96,768]{1,0:T(8,128)(2,1)S(1)} %get-tuple-element.20), channel_id=1, source_target_pairs={{0,32},{8,40},{16,48},{24,56},{32,0},{40,8},{48,16},{56,24},{64,96... | collective-permute-start | bytes 442376 | tf_op jit(solution)/shard_map/ppermute | solution.py:241
  52.5 22.5 %collective-permute-start.7 = (bf16[96,768]{1,0:T(8,128)(2,1)S(1)}, bf16[96,768]{1,0:T(8,128)(2,1)S(1)}, u32[]{:S(2)}, u32[]{:S(2)}) collective-permute-start(bf16[96,768]{1,0:T(8,128)(2,1)S(1)} %get-tuple-element.22.refs_5_), channel_id=1, source_target_pairs={{0,16},{8,24},{16,0},{24,8},{32,48},{40,56},{48,32},{56,40},{64,80... | collective-permute-start | bytes 442376 | tf_op jit(solution)/shard_map/ppermute | solution.py:241
  54.2 20.9 %collective-permute-start.6 = (bf16[96,768]{1,0:T(8,128)(2,1)S(1)}, bf16[96,768]{1,0:T(8,128)(2,1)S(1)}, u32[]{:S(2)}, u32[]{:S(2)}) collective-permute-start(bf16[96,768]{1,0:T(8,128)(2,1)S(1)} %get-tuple-element.21), channel_id=1, source_target_pairs={{0,48},{8,56},{16,32},{24,40},{32,16},{40,24},{48,0},{56,8},{64,11... | collective-permute-start | bytes 442376 | tf_op jit(solution)/shard_map/ppermute | solution.py:241
  57.5 17.5 %collective-permute-start.12 = (bf16[96,768]{1,0:T(8,128)(2,1)S(1)}, bf16[96,768]{1,0:T(8,128)(2,1)S(1)}, u32[]{:S(2)}, u32[]{:S(2)}) collective-permute-start(bf16[96,768]{1,0:T(8,128)(2,1)S(1)} %get-tuple-element.24), channel_id=1, source_target_pairs={{0,32},{8,40},{16,48},{24,56},{32,0},{40,8},{48,16},{56,24},{64,96... | collective-permute-start | bytes 442376 | tf_op jit(solution)/shard_map/ppermute | solution.py:241
  58.8 22.6 %collective-permute-start.13 = (bf16[96,768]{1,0:T(8,128)(2,1)S(1)}, bf16[96,768]{1,0:T(8,128)(2,1)S(1)}, u32[]{:S(2)}, u32[]{:S(2)}) collective-permute-start(bf16[96,768]{1,0:T(8,128)(2,1)S(1)} %get-tuple-element.25), channel_id=1, source_target_pairs={{0,48},{8,56},{16,32},{24,40},{32,16},{40,24},{48,0},{56,8},{64,11... | collective-permute-start | bytes 442376 | tf_op jit(solution)/shard_map/ppermute | solution.py:241
  61.1 20.2 %collective-permute-start.14 = (bf16[96,768]{1,0:T(8,128)(2,1)S(1)}, bf16[96,768]{1,0:T(8,128)(2,1)S(1)}, u32[]{:S(2)}, u32[]{:S(2)}) collective-permute-start(bf16[96,768]{1,0:T(8,128)(2,1)S(1)} %get-tuple-element.26), channel_id=1, source_target_pairs={{0,16},{8,24},{16,0},{24,8},{32,48},{40,56},{48,32},{56,40},{64,80... | collective-permute-start | bytes 442376 | tf_op jit(solution)/shard_map/ppermute | solution.py:241

commit v3 on v2

v3 whole, which is shorter than its diff:
```python
import jax
import jax.numpy as jnp
from jax import lax
from jax.experimental import pallas as pl
from jax.experimental.pallas import tpu as pltpu
from jax.sharding import PartitionSpec as P


BLOCK = 128
SUB = 32
KNEE = 32.0
STEEP = 1024.0
F32 = jnp.float32
BF16 = jnp.bfloat16
VMEM = pl.BlockSpec(memory_space=pltpu.VMEM)
SMEM = pl.BlockSpec(memory_space=pltpu.SMEM)
ANY = pl.BlockSpec(memory_space=pl.ANY)


def split(x):
    high = x.astype(BF16)
    return high, (x - high.astype(F32)).astype(BF16)


def dot(a, b):
    return jnp.dot(a, b, preferred_element_type=F32)


def dot3(a, b):
    return dot(a[0], b[0]) + (dot(a[0], b[1]) + dot(a[1], b[0]))


def code(v):
    return (v * jnp.clip(jnp.abs(v) * (1.0 / KNEE), 1.0 / STEEP, 1.0)).astype(BF16)


def decode(y):
    y = y.astype(F32)
    return y * jnp.clip(lax.rsqrt(jnp.abs(y) * (1.0 / KNEE)), 1.0, STEEP)


def grant(mebibytes):
    return pltpu.CompilerParams(vmem_limit_bytes=mebibytes * 1024 * 1024)


def cost(flops, moved):
    return pl.CostEstimate(flops=flops, bytes_accessed=moved, transcendentals=0)


def square_masks(order, width):
    rows = lax.broadcasted_iota(jnp.int32, (order, order), 0)
    cols = lax.broadcasted_iota(jnp.int32, (order, order), 1)
    return rows == cols, (rows < width) & (cols < width)


def place_kernel(in_ref, out_ref):
    for k in range(in_ref.shape[0]):
        out_ref[k] = in_ref[k]


def place_call(pos):
    return pl.pallas_call(
        place_kernel,
        in_specs=[SMEM],
        out_specs=SMEM,
        out_shape=jax.ShapeDtypeStruct(pos.shape, pos.dtype),
        cost_estimate=cost(10**10, 10**7),
        name="place",
        compiler_params=grant(1),
    )(pos)


def inverse_call(s, widths, pos, systems, upper):
    order = systems.shape[1]
    half, cols = upper.shape[1:]

    def inverse_kernel(width_ref, pos_ref, system_ref, upper_ref, xh_ref, xl_ref, part_ref):
        swap = pos_ref[2] == 1
        on_diag, inside = square_masks(order, width_ref[s])
        identity = jnp.where(on_diag, 1.0, 0.0)
        system = jnp.where(inside, system_ref[s], identity)
        picked = jnp.where(on_diag, system, 0.0)
        down = 1.0 / jnp.sum(picked, axis=1, keepdims=True)
        across = 1.0 / jnp.sum(picked, axis=0, keepdims=True)
        start = jnp.where(on_diag, down, 0.0)
        inverse = (2.0 * start - down * (system * across)).astype(BF16)
        high, low = split(system)
        residual = identity - (dot(high, inverse) + dot(low, inverse))
        inverse = inverse.astype(F32) + dot(inverse, residual.astype(BF16))
        both = split(inverse)
        residual = identity - dot3((high, low), both)
        inverse = inverse + dot3(both, split(residual))
        inverse = jnp.where(inside, inverse, 0.0)
        mine = jnp.where(swap, inverse[:, half:], inverse[:, :half])
        other = jnp.where(swap, inverse[:, :half], inverse[:, half:])
        high, low = split(mine)
        part_ref[...] = dot(high, upper_ref[s]) + dot(low, upper_ref[s])
        high, low = split(other)
        xh_ref[...] = high
        xl_ref[...] = low

    return pl.pallas_call(
        inverse_kernel,
        in_specs=[SMEM, SMEM, VMEM, VMEM],
        out_specs=[VMEM] * 3,
        out_shape=[
            jax.ShapeDtypeStruct((order, half), BF16),
            jax.ShapeDtypeStruct((order, half), BF16),
            jax.ShapeDtypeStruct((order, cols), F32),
        ],
        cost_estimate=cost(20 * order**3, 4000000),
        compiler_params=grant(16),
    )(widths, pos, systems, upper)


def scale_call(pos, fill, inverses, upper):
    members, half, cols = upper.shape
    order = inverses[0][0].shape[0]

    def scale_kernel(pos_ref, fill_ref, *refs):
        *inverse_refs, upper_ref, out_ref = refs
        pieces = order // BLOCK
        blocks = cols // BLOCK
        col = pos_ref[1]
        for s in range(members):
            xh_ref, xl_ref, part_ref = inverse_refs[3 * s : 3 * s + 3]
            upper = upper_ref[s]
            scaled = part_ref[...] + (dot(xh_ref[...], upper) + dot(xl_ref[...], upper))
            for j in range(blocks):
                used = fill_ref[s, col * blocks + j] != 0
                lanes = slice(j * BLOCK, (j + 1) * BLOCK)
                tile = scaled[:, lanes]
                tile = jnp.where(used, tile, jnp.zeros_like(tile)).astype(BF16)
                for k in range(pieces):
                    spot = lax.rem(k - col + pieces, pieces)
                    out_ref[s, spot, :, lanes] = tile[k * BLOCK : (k + 1) * BLOCK]

    flat = [x for inverse in inverses for x in inverse]
    return pl.pallas_call(
        scale_kernel,
        in_specs=[SMEM, SMEM] + [VMEM] * (len(flat) + 1),
        out_specs=VMEM,
        out_shape=jax.ShapeDtypeStruct((members, order // BLOCK, BLOCK, cols), BF16),
        cost_estimate=cost(4 * members * order * half * cols, 8 * members * order * cols),
        name="scale_upper",
        compiler_params=grant(16),
    )(pos, fill, *flat, upper)


def update_call(flip, chunk, pos, fill, front, lowers, scaled, after):
    spots, _, _, rows, cols = front.shape
    members = scaled.shape[0]
    order = scaled.shape[1] * scaled.shape[2]

    def update_kernel(pos_ref, fill_ref, front_ref, *refs):
        own_ref, next_ref, far_refs, last_ref = refs[0], refs[1], refs[2:4], refs[4]
        scaled_ref, _, out_ref, wide = refs[5:]
        side = 1 - pos_ref[0] if flip else pos_ref[0]
        strip = 2 * rows
        base = pos_ref[2] * (spots * 2 * strip) + side * strip + chunk * rows
        for s in range(members):
            for d in range(spots):
                for j in range(rows // SUB):
                    spot = lax.div(base + d * 2 * strip + j * SUB, BLOCK)
                    used = fill_ref[s, spot] != 0
                    spans = (d, side, slice(j * SUB, (j + 1) * SUB))
                    tiles = (own_ref[s, *spans], next_ref[s, *spans], far_refs[s][*spans], last_ref[s, *spans])
                    for k, tile in enumerate(tiles):
                        begin = s * order + k * BLOCK
                        top = d * rows + j * SUB
                        wide[top : top + SUB, begin : begin + BLOCK] = jnp.where(used, tile, jnp.zeros_like(tile))
        flat = scaled_ref[...].reshape(members * order, cols)
        update = dot(wide[...], flat).reshape(spots, rows, cols)
        for d in range(spots):
            out_ref[d] = front_ref[d, side, chunk].astype(F32) - update[d]

    return pl.pallas_call(
        update_kernel,
        in_specs=[SMEM, SMEM] + [VMEM] * 7 + [ANY],
        out_specs=VMEM,
        scratch_shapes=[pltpu.VMEM((spots * rows, members * order), BF16)],
        out_shape=jax.ShapeDtypeStruct((spots, rows, cols), F32),
        cost_estimate=cost(2 * spots * rows * members * order * cols, 4000000),
        compiler_params=grant(12),
    )(pos, fill, front, *lowers, scaled, after)


def pair_kernel(pos_ref, kept_ref, got_ref, own_ref, out_ref):
    parity = pos_ref[3] & 1
    for j in range(own_ref.shape[0]):
        spot = 2 * j + 1 - parity
        out_ref[j] = code(kept_ref[spot] + got_ref[spot])
    for j in range(own_ref.shape[0]):
        spot = 2 * j + parity
        own_ref[j] = kept_ref[spot] + got_ref[spot]


def pair_call(pos, kept, got):
    spots, rows, cols = kept.shape
    half = (spots // 2, rows, cols)
    return pl.pallas_call(
        pair_kernel,
        in_specs=[SMEM, VMEM, VMEM],
        out_specs=[VMEM] * 2,
        out_shape=[jax.ShapeDtypeStruct(half, F32), jax.ShapeDtypeStruct(half, BF16)],
        cost_estimate=cost(spots * rows * cols, 10 * spots * rows * cols),
        compiler_params=grant(8),
    )(pos, kept, got)


def quarter_kernel(pos_ref, own_ref, got_ref, part_ref, out_ref):
    place = pos_ref[3] >> 1
    out_ref[...] = code(own_ref[1 - place] + decode(got_ref[1 - place]))
    part_ref[...] = own_ref[place] + decode(got_ref[place])


def quarter_call(pos, own, got):
    _, rows, cols = own.shape
    return pl.pallas_call(
        quarter_kernel,
        in_specs=[SMEM, VMEM, VMEM],
        out_specs=[VMEM] * 2,
        out_shape=[jax.ShapeDtypeStruct((rows, cols), F32), jax.ShapeDtypeStruct((rows, cols), BF16)],
        cost_estimate=cost(8 * rows * cols, 16 * rows * cols),
        compiler_params=grant(8),
    )(pos, own, got)


def final_kernel(*refs):
    *in_refs, out_ref = refs
    rows = in_refs[0].shape[0]
    for chunk in range(len(in_refs) // 2):
        part_ref, got_ref = in_refs[2 * chunk : 2 * chunk + 2]
        out_ref[0, chunk * rows : (chunk + 1) * rows] = part_ref[...] + decode(got_ref[...])


def final_call(parts):
    rows, cols = parts[0].shape
    return pl.pallas_call(
        final_kernel,
        in_specs=[VMEM] * len(parts),
        out_specs=VMEM,
        out_shape=jax.ShapeDtypeStruct((1, len(parts) // 2 * rows, cols), F32),
        cost_estimate=cost(len(parts) * rows * cols, 3 * len(parts) * rows * cols),
        name="final_sums",
        compiler_params=grant(8),
    )(*parts)


def on_device(front_copies, lower_panels, upper_panels, diag_blocks, block_fill, widths):
    layers, col_devices = lax.axis_size("layer"), lax.axis_size("col")
    layer = lax.axis_index("layer")
    row_index, col_index = lax.axis_index("row"), lax.axis_index("col")
    which = jnp.arange(4, dtype=jnp.int32)
    pos = jnp.where(
        which == 0,
        layer & 1,
        jnp.where(which == 1, col_index, jnp.where(which == 2, row_index, layer >> 1 & 3)),
    ).astype(jnp.int32)
    pos = place_call(pos)
    upper, fill, width_vec = upper_panels[0], block_fill[0], widths[0]
    row_count, cols = front_copies.shape[1:]
    members = upper.shape[0]
    spots = 4
    rows = row_count // (spots * 4)
    front = front_copies.reshape(spots, 2, 2, rows, cols)
    lower = lower_panels.reshape(members, spots, 2, 2, rows, BLOCK)

    def shift(block, step):
        return lax.ppermute(block, "col", [(i, (i + step) % col_devices) for i in range(col_devices)])

    def across(block, flip):
        return lax.ppermute(block, "layer", [(i, i ^ flip) for i in range(layers)])

    other_upper = lax.ppermute(upper, "row", [(0, 1), (1, 0)])
    near = []
    for chunk in range(2):
        own = lower[:, :, :, chunk]
        near.append((own, shift(own, -1), shift(own, 1)))
    inverses = [inverse_call(s, width_vec, pos, diag_blocks[0], upper) for s in range(members)]
    scaled = scale_call(pos, fill, inverses, other_upper)
    parts = []
    after = scaled
    for chunk in range(2):
        own, following, last = near[chunk]
        far = (shift(last[0], 1), shift(following[1], -1))
        lowers = (own, following, *far, last)
        sent = update_call(True, chunk, pos, fill, front, lowers, scaled, after)
        got = across(sent, 1)
        kept = update_call(False, chunk, pos, fill, front, lowers, scaled, after)
        pair, after = pair_call(pos, kept, got)
        got = across(after, 2)
        part, quarter = quarter_call(pos, pair, got)
        parts += [part, across(quarter, 4)]
    return final_call(parts)


def solution(mesh):
    placed = (
        P("layer", "row", "col"),
        P("layer", None, "row", "col"),
        P("layer", None, "row", "col"),
        P("layer", None, None, None),
        P("layer", None, None),
        P("layer", None),
    )

    return jax.shard_map(on_device, mesh=mesh, in_specs=placed, out_specs=P("layer", "row", "col"), check_vma=False)
```

time: 82.7 us -> 81.3 us (0.983)
  the two profiles are of different devices: /device:TPU:71 before, /device:TPU:1 now
where the time goes in v3:
time: 81.3 us; the launch traced here: 81.1 us
  waiting for transfers between devices  31.7 us (39%)
  starting transfers between devices  26.2 us (32%)
  Pallas kernels  21.2 us (26%)
  local copies, waits for them, and re-layouts  1.83 us (2%)
    ppermute x6, waiting for transfers between devices, across(): return lax.ppermute(block, 'layer', [(i, i ^ flip) for i in range(layers)])  18.7 us
    ppermute x8, starting transfers between devices, shift(): lax.ppermute(block, 'col', [(i, (i + step) % col_devices) for i in range(...  11.9 us
    ppermute x6, starting transfers between devices, across(): return lax.ppermute(block, 'layer', [(i, i ^ flip) for i in range(layers)])  11.2 us
    ppermute x8, waiting for transfers between devices, shift(): lax.ppermute(block, 'col', [(i, (i + step) % col_devices) for i in range(...  10.9 us
    pallas_call x2, Pallas kernels, inverse_call(): pl.pallas_call(inverse_kernel, in_specs=[SMEM, SMEM, VMEM, VMEM], out_spe...  8.96 us
    pallas_call x4, Pallas kernels, update_call(): pl.pallas_call(update_kernel, in_specs=[SMEM, SMEM] + [VMEM] * 7 + [ANY],...  5.7 us
    ppermute x1, starting transfers between devices, on_device(): other_upper = lax.ppermute(upper, 'row', [(0, 1), (1, 0)])  3.02 us
    ppermute x1, waiting for transfers between devices, on_device(): other_upper = lax.ppermute(upper, 'row', [(0, 1), (1, 0)])  2.01 us
  transfers between devices with their start and end apart: 15, of which 6 were waited for; matrix products, arithmetic and copies ran while one was open for 0% of the time, Pallas kernels for 21%

profile of v3, /device:TPU:1, one launch (start us, length us, event | category | flops | bytes accessed | tf_op | source)
XLA Modules:
  0.0 81.1 jit_solution(8551520167293370894)
XLA Ops:
  0.0 1.2 %slice_bitcast_fusion = (bf16[2,4,2,96,128]{4,3,2,1,0:T(8,128)(2,1)S(1)}, bf16[2,4,2,96,128]{4,3,2,1,0:T(8,128)(2,1)S(1)}) fusion(bf16[2,4,2,2,96,128]{5,4,3,2,1,0:T(8,128)(2,1)} %bitcast.38), kind=kLoop, calls=%fused_computation | loop fusion | bytes 1572864 | tf_op jit(solution)/shard_map/squeeze | solution.py:278
  1.3 2.1 %collective-permute-start.1 = (bf16[2,4,2,96,128]{4,3,2,1,0:T(8,128)(2,1)S(1)}, bf16[2,4,2,96,128]{4,3,2,1,0:T(8,128)(2,1)S(1)}, u32[]{:S(2)}, u32[]{:S(2)}) collective-permute-start(bf16[2,4,2,96,128]{4,3,2,1,0:T(8,128)(2,1)S(1)} %get-tuple-element.34.refs_0_), channel_id=1, source_target_pairs={{0,2},{2,4},{4,6},{6,0},{1,3},{3,5},{5,7},{7,1},{8,10},{10,12},{12... | collective-permute-start | bytes 1179656 | tf_op jit(solution)/shard_map/ppermute | solution.py:270
  3.4 1.4 %collective-permute-start = (bf16[2,4,2,96,128]{4,3,2,1,0:T(8,128)(2,1)S(1)}, bf16[2,4,2,96,128]{4,3,2,1,0:T(8,128)(2,1)S(1)}, u32[]{:S(2)}, u32[]{:S(2)}) collective-permute-start(bf16[2,4,2,96,128]{4,3,2,1,0:T(8,128)(2,1)S(1)} %get-tuple-element.34.refs_0_), channel_id=1, source_target_pairs={{0,6},{2,0},{4,2},{6,4},{1,7},{3,1},{5,3},{7,5},{8,14},{10,8},{12,... | collective-permute-start | bytes 1179656 | tf_op jit(solution)/shard_map/ppermute | solution.py:270
  4.7 0.0 copy-done.3
  4.7 3.0 %collective-permute-start.4 = (bf16[2,256,768]{2,1,0:T(8,128)(2,1)S(1)}, bf16[2,256,768]{2,1,0:T(8,128)(2,1)S(1)}, u32[]{:S(2)}, u32[]{:S(2)}) collective-permute-start(bf16[2,256,768]{2,1,0:T(8,128)(2,1)S(1)} %bitcast.33), channel_id=1, source_target_pairs={{0,1},{1,0},{2,3},{3,2},{4,5},{5,4},{6,7},{7,6},{8,9},{9,8},{10,11... | collective-permute-start | bytes 2359304 | tf_op jit(solution)/shard_map/ppermute | solution.py:275
  7.8 1.1 %place.1.pos_ref = s32[4]{0:T(128)S(1)} custom-call(s32[4]{0:T(128)S(1)} %compare_select_fusion.2.in_ref), custom_call_target="tpu_custom_call" | custom-call | flops 10000000000 | bytes 10000000 | tf_op jit(solution)/shard_map/place/pallas_call | solution.py:62
  8.9 0.4 copy-done.2
  9.3 4.5 %shard_map.64 = (bf16[512,256]{1,0:T(8,128)(2,1)S(1)}, bf16[512,256]{1,0:T(8,128)(2,1)S(1)}, f32[512,768]{1,0:T(8,128)S(1)}) custom-call(s32[2]{0:T(128)S(1)} %bitcast.36, s32[4]{0:T(128)S(1)} %place.1.pos_ref, f32[2,512,512]{2,1,0:T(8,128)S(1)} %bitcast.31, bf16[2,256,768]{2,1,0:T(8,128)(2,1)S(1)} %bitcast.34), custom_call_target="tpu_custom_call" | custom-call | flops 2684354560 | bytes 4000000 | tf_op jit(solution)/shard_map/pallas_call | solution.py:102
  13.8 0.0 collective-permute-done.1.refs_4_
  13.9 0.1 collective-permute-start.2
  14.0 0.0 collective-permute-done.refs_1_
  14.0 0.0 copy-start.1
  14.0 2.9 %collective-permute-start.3 = (bf16[4,2,96,128]{3,2,1,0:T(8,128)(2,1)S(1)}, bf16[4,2,96,128]{3,2,1,0:T(8,128)(2,1)S(1)}, u32[]{:S(2)}, u32[]{:S(2)}) collective-permute-start(bf16[4,2,96,128]{3,2,1,0:T(8,128)(2,1)S(1)} %slice_bitcast_fusion.4), channel_id=1, source_target_pairs={{0,6},{2,0},{4,2},{6,4},{1,7},{3,1},{5,3},{7,5},{8,14},{10,8},{12,... | collective-permute-start | bytes 589832 | tf_op jit(solution)/shard_map/ppermute | solution.py:270
  16.9 4.5 %shard_map.65 = (bf16[512,256]{1,0:T(8,128)(2,1)S(1)}, bf16[512,256]{1,0:T(8,128)(2,1)S(1)}, f32[512,768]{1,0:T(8,128)S(1)}) custom-call(s32[2]{0:T(128)S(1)} %bitcast.37, s32[4]{0:T(128)S(1)} %place.1.pos_ref, f32[2,512,512]{2,1,0:T(8,128)S(1)} %bitcast.32, bf16[2,256,768]{2,1,0:T(8,128)(2,1)S(1)} %bitcast.35), custom_call_target="tpu_custom_call" | custom-call | flops 2684354560 | bytes 4000000 | tf_op jit(solution)/shard_map/pallas_call | solution.py:102
  21.4 2.0 %collective-permute-done.4.refs_6_ = bf16[2,256,768]{2,1,0:T(8,128)(2,1)S(1)} collective-permute-done((bf16[2,256,768]{2,1,0:T(8,128)(2,1)S(1)}, bf16[2,256,768]{2,1,0:T(8,128)(2,1)S(1)}, u32[]{:S(2)}, u32[]{:S(2)}) %collective-permute-start.4) | collective-permute-done | bytes 786464 | tf_op jit(solution)/shard_map/ppermute | solution.py:275
  23.4 1.6 %scale_upper.1.refs_5_.refs_6_ = bf16[2,4,128,768]{3,2,1,0:T(8,128)(2,1)S(1)} custom-call(s32[4]{0:T(128)S(1)} %place.1.pos_ref, s32[2,24]{1,0:T(2,128)S(1)} %bitcast.26, bf16[512,256]{1,0:T(8,128)(2,1)S(1)} %get-tuple-element.19.refs_0_, bf16[512,256]{1,0:T(8,128)(2,1)S(1)} %get-tuple-element.20.refs_1_, f32[512,768]{1,0:T(8,128)S(1)} %get-tuple-element.21.refs_2_, ...), custom_call_target="tpu_custom_call" | custom-call | flops 805306368 | bytes 6291456 | tf_op jit(solution)/shard_map/scale_upper/pallas_call | solution.py:139
  25.0 0.0 collective-permute-done.2.refs_2_
  25.0 0.0 collective-permute-done.3.refs_3_
  25.0 0.1 copy-done
  25.1 1.4 %shard_map.67 = f32[4,96,768]{2,1,0:T(8,128)S(1)} custom-call(s32[4]{0:T(128)S(1)} %place.1.pos_ref, s32[2,24]{1,0:T(2,128)S(1)} %bitcast.27, bf16[4,2,2,96,768]{4,3,2,1,0:T(8,128)(2,1)S(1)} %bitcast.22, bf16[2,4,2,96,128]{4,3,2,1,0:T(8,128)(2,1)S(1)} %get-tuple-element.34.refs_0_, bf16[2,4,2,96,128]{4,3,2,1,0:T(8,128)(2,1)S(1)} %collective-permute-done.refs_1_, ...), custom_call_target="tpu_custom_call" | custom-call | flops 603979776 | bytes 4000000 | tf_op jit(solution)/shard_map/pallas_call | solution.py:177
  26.5 2.9 %collective-permute-start.5 = (f32[4,96,768]{2,1,0:T(8,128)S(1)}, f32[4,96,768]{2,1,0:T(8,128)S(1)}, u32[]{:S(2)}, u32[]{:S(2)}) collective-permute-start(f32[4,96,768]{2,1,0:T(8,128)S(1)} %shard_map.67), channel_id=1, source_target_pairs={{0,8},{8,0},{16,24},{24,16},{32,40},{40,32},{48,56},{56,48},{64,72... | collective-permute-start | bytes 3538952 | tf_op jit(solution)/shard_map/ppermute | solution.py:273
  29.4 0.1 collective-permute-start.9
  29.5 2.6 %collective-permute-start.8 = (bf16[2,4,2,96,128]{4,3,2,1,0:T(8,128)(2,1)S(1)}, bf16[2,4,2,96,128]{4,3,2,1,0:T(8,128)(2,1)S(1)}, u32[]{:S(2)}, u32[]{:S(2)}) collective-permute-start(bf16[2,4,2,96,128]{4,3,2,1,0:T(8,128)(2,1)S(1)} %get-tuple-element.33.refs_0_), channel_id=1, source_target_pairs={{0,6},{2,0},{4,2},{6,4},{1,7},{3,1},{5,3},{7,5},{8,14},{10,8},{12,... | collective-permute-start | bytes 1179656 | tf_op jit(solution)/shard_map/ppermute | solution.py:270
  32.1 9.1 %collective-permute-done.9.refs_4_ = bf16[2,4,2,96,128]{4,3,2,1,0:T(8,128)(2,1)S(1)} collective-permute-done((bf16[2,4,2,96,128]{4,3,2,1,0:T(8,128)(2,1)S(1)}, bf16[2,4,2,96,128]{4,3,2,1,0:T(8,128)(2,1)S(1)}, u32[]{:S(2)}, u32[]{:S(2)}) %collective-permute-start.9) | collective-permute-done | bytes 393248 | tf_op jit(solution)/shard_map/ppermute | solution.py:270
  41.2 0.1 collective-permute-start.10
  41.3 0.0 collective-permute-done.8.refs_1_
  41.4 2.7 %collective-permute-start.11 = (bf16[4,2,96,128]{3,2,1,0:T(8,128)(2,1)S(1)}, bf16[4,2,96,128]{3,2,1,0:T(8,128)(2,1)S(1)}, u32[]{:S(2)}, u32[]{:S(2)}) collective-permute-start(bf16[4,2,96,128]{3,2,1,0:T(8,128)(2,1)S(1)} %slice_bitcast_fusion.2), channel_id=1, source_target_pairs={{0,6},{2,0},{4,2},{6,4},{1,7},{3,1},{5,3},{7,5},{8,14},{10,8},{12,... | collective-permute-start | bytes 589832 | tf_op jit(solution)/shard_map/ppermute | solution.py:270
  44.1 1.4 %shard_map.66.kept_ref = f32[4,96,768]{2,1,0:T(8,128)S(1)} custom-call(s32[4]{0:T(128)S(1)} %place.1.pos_ref, s32[2,24]{1,0:T(2,128)S(1)} %bitcast.28, bf16[4,2,2,96,768]{4,3,2,1,0:T(8,128)(2,1)S(1)} %bitcast.23, bf16[2,4,2,96,128]{4,3,2,1,0:T(8,128)(2,1)S(1)} %get-tuple-element.34.refs_0_, bf16[2,4,2,96,128]{4,3,2,1,0:T(8,128)(2,1)S(1)} %collective-permute-done.refs_1_, ...), custom_call_target="tpu_custom_call" | custom-call | flops 603979776 | bytes 4000000 | tf_op jit(solution)/shard_map/pallas_call | solution.py:177
  45.5 0.0 collective-permute-done.5.got_ref
  45.5 0.7 shard_map.68
  46.2 1.8 %collective-permute-done.10.refs_2_ = bf16[4,2,96,128]{3,2,1,0:T(8,128)(2,1)S(1)} collective-permute-done((bf16[4,2,96,128]{3,2,1,0:T(8,128)(2,1)S(1)}, bf16[4,2,96,128]{3,2,1,0:T(8,128)(2,1)S(1)}, u32[]{:S(2)}, u32[]{:S(2)}) %collective-permute-start.10) | collective-permute-done | bytes 196640 | tf_op jit(solution)/shard_map/ppermute | solution.py:270
  48.0 0.0 collective-permute-done.11.refs_3_
  48.0 1.4 %shard_map.71 = f32[4,96,768]{2,1,0:T(8,128)S(1)} custom-call(s32[4]{0:T(128)S(1)} %place.1.pos_ref, s32[2,24]{1,0:T(2,128)S(1)} %bitcast.29, bf16[4,2,2,96,768]{4,3,2,1,0:T(8,128)(2,1)S(1)} %bitcast.24, bf16[2,4,2,96,128]{4,3,2,1,0:T(8,128)(2,1)S(1)} %get-tuple-element.33.refs_0_, bf16[2,4,2,96,128]{4,3,2,1,0:T(8,128)(2,1)S(1)} %collective-permute-done.8.refs_1_, ...), custom_call_target="tpu_custom_call" | custom-call | flops 603979776 | bytes 4000000 | tf_op jit(solution)/shard_map/pallas_call | solution.py:177
  49.5 1.9 %collective-permute-start.12 = (f32[4,96,768]{2,1,0:T(8,128)S(1)}, f32[4,96,768]{2,1,0:T(8,128)S(1)}, u32[]{:S(2)}, u32[]{:S(2)}) collective-permute-start(f32[4,96,768]{2,1,0:T(8,128)S(1)} %shard_map.71), channel_id=1, source_target_pairs={{0,8},{8,0},{16,24},{24,16},{32,40},{40,32},{48,56},{56,48},{64,72... | collective-permute-start | bytes 3538952 | tf_op jit(solution)/shard_map/ppermute | solution.py:273
  51.4 1.7 %collective-permute-start.6 = (bf16[2,96,768]{2,1,0:T(8,128)(2,1)S(1)}, bf16[2,96,768]{2,1,0:T(8,128)(2,1)S(1)}, u32[]{:S(2)}, u32[]{:S(2)}) collective-permute-start(bf16[2,96,768]{2,1,0:T(8,128)(2,1)S(1)} %get-tuple-element.26.refs_6_), channel_id=1, source_target_pairs={{0,16},{8,24},{16,0},{24,8},{32,48},{40,56},{48,32},{56,40},{64,80... | collective-permute-start | bytes 884744 | tf_op jit(solution)/shard_map/ppermute | solution.py:273
  53.1 1.4 %shard_map.70.kept_ref = f32[4,96,768]{2,1,0:T(8,128)S(1)} custom-call(s32[4]{0:T(128)S(1)} %place.1.pos_ref, s32[2,24]{1,0:T(2,128)S(1)} %bitcast.30, bf16[4,2,2,96,768]{4,3,2,1,0:T(8,128)(2,1)S(1)} %bitcast.25, bf16[2,4,2,96,128]{4,3,2,1,0:T(8,128)(2,1)S(1)} %get-tuple-element.33.refs_0_, bf16[2,4,2,96,128]{4,3,2,1,0:T(8,128)(2,1)S(1)} %collective-permute-done.8.refs_1_, ...), custom_call_target="tpu_custom_call" | custom-call | flops 603979776 | bytes 4000000 | tf_op jit(solution)/shard_map/pallas_call | solution.py:177
  54.5 0.0 collective-permute-done.12.got_ref
  54.5 0.7 shard_map.72
  55.2 1.1 %collective-permute-start.13 = (bf16[2,96,768]{2,1,0:T(8,128)(2,1)S(1)}, bf16[2,96,768]{2,1,0:T(8,128)(2,1)S(1)}, u32[]{:S(2)}, u32[]{:S(2)}) collective-permute-start(bf16[2,96,768]{2,1,0:T(8,128)(2,1)S(1)} %get-tuple-element.30), channel_id=1, source_target_pairs={{0,16},{8,24},{16,0},{24,8},{32,48},{40,56},{48,32},{56,40},{64,80... | collective-permute-start | bytes 884744 | tf_op jit(solution)/shard_map/ppermute | solution.py:273
  56.3 3.7 %collective-permute-done.6.got_ref = bf16[2,96,768]{2,1,0:T(8,128)(2,1)S(1)} collective-permute-done((bf16[2,96,768]{2,1,0:T(8,128)(2,1)S(1)}, bf16[2,96,768]{2,1,0:T(8,128)(2,1)S(1)}, u32[]{:S(2)}, u32[]{:S(2)}) %collective-permute-start.6) | collective-permute-done | bytes 294944 | tf_op jit(solution)/shard_map/ppermute | solution.py:273
  60.1 0.7 shard_map.69
  60.8 3.0 %collective-permute-start.7 = (bf16[96,768]{1,0:T(8,128)(2,1)S(1)}, bf16[96,768]{1,0:T(8,128)(2,1)S(1)}, u32[]{:S(2)}, u32[]{:S(2)}) collective-permute-start(bf16[96,768]{1,0:T(8,128)(2,1)S(1)} %get-tuple-element.28), channel_id=1, source_target_pairs={{0,32},{8,40},{16,48},{24,56},{32,0},{40,8},{48,16},{56,24},{64,96... | collective-permute-start | bytes 442376 | tf_op jit(solution)/shard_map/ppermute | solution.py:273
  63.8 5.7 %collective-permute-done.13.got_ref = bf16[2,96,768]{2,1,0:T(8,128)(2,1)S(1)} collective-permute-done((bf16[2,96,768]{2,1,0:T(8,128)(2,1)S(1)}, bf16[2,96,768]{2,1,0:T(8,128)(2,1)S(1)}, u32[]{:S(2)}, u32[]{:S(2)}) %collective-permute-start.13) | collective-permute-done | bytes 294944 | tf_op jit(solution)/shard_map/ppermute | solution.py:273
  69.6 0.7 shard_map.73
  70.3 0.6 collective-permute-start.14
  70.9 0.0 collective-permute-done.7.refs_1_
  70.9 9.3 %collective-permute-done.14.refs_3_ = bf16[96,768]{1,0:T(8,128)(2,1)S(1)} collective-permute-done((bf16[96,768]{1,0:T(8,128)(2,1)S(1)}, bf16[96,768]{1,0:T(8,128)(2,1)S(1)}, u32[]{:S(2)}, u32[]{:S(2)}) %collective-permute-start.14) | collective-permute-done | bytes 147488 | tf_op jit(solution)/shard_map/ppermute | solution.py:273
  80.2 1.0 %final_sums.1 = f32[1,192,768]{2,1,0:T(8,128)} custom-call(f32[96,768]{1,0:T(8,128)S(1)} %get-tuple-element.27.refs_0_, bf16[96,768]{1,0:T(8,128)(2,1)S(1)} %collective-permute-done.7.refs_1_, f32[96,768]{1,0:T(8,128)S(1)} %get-tuple-element.31.refs_2_, bf16[96,768]{1,0:T(8,128)(2,1)S(1)} %collective-permute-done.14.refs_3_), custom_call_target="tpu_custom_call" | custom-call | flops 294912 | bytes 884736 | tf_op jit(solution)/shard_map/final_sums/pallas_call | solution.py:239
  (11 shorter events, 0.1 us)
Async XLA Ops:
  0.0 4.7 %copy-start.3 = (bf16[1,2,256,768]{3,2,1,0:T(8,128)(2,1)S(1)}, bf16[1,2,256,768]{3,2,1,0:T(8,128)(2,1)}, u32[]{:S(2)}) copy-start(bf16[1,2,256,768]{3,2,1,0:T(8,128)(2,1)} %param.8) | copy-start | bytes 2359300
  1.3 12.6 %collective-permute-start.1 = (bf16[2,4,2,96,128]{4,3,2,1,0:T(8,128)(2,1)S(1)}, bf16[2,4,2,96,128]{4,3,2,1,0:T(8,128)(2,1)S(1)}, u32[]{:S(2)}, u32[]{:S(2)}) collective-permute-start(bf16[2,4,2,96,128]{4,3,2,1,0:T(8,128)(2,1)S(1)} %get-tuple-element.34.refs_0_), channel_id=1, source_target_pairs={{0,2},{2,4},{4,6},{6,0},{1,3},{3,5},{5,7},{7,1},{8,10},{10,12},{12... | collective-permute-start | bytes 1179656 | tf_op jit(solution)/shard_map/ppermute | solution.py:270
  3.4 10.6 %collective-permute-start = (bf16[2,4,2,96,128]{4,3,2,1,0:T(8,128)(2,1)S(1)}, bf16[2,4,2,96,128]{4,3,2,1,0:T(8,128)(2,1)S(1)}, u32[]{:S(2)}, u32[]{:S(2)}) collective-permute-start(bf16[2,4,2,96,128]{4,3,2,1,0:T(8,128)(2,1)S(1)} %get-tuple-element.34.refs_0_), channel_id=1, source_target_pairs={{0,6},{2,0},{4,2},{6,4},{1,7},{3,1},{5,3},{7,5},{8,14},{10,8},{12,... | collective-permute-start | bytes 1179656 | tf_op jit(solution)/shard_map/ppermute | solution.py:270
  4.7 18.7 %collective-permute-start.4 = (bf16[2,256,768]{2,1,0:T(8,128)(2,1)S(1)}, bf16[2,256,768]{2,1,0:T(8,128)(2,1)S(1)}, u32[]{:S(2)}, u32[]{:S(2)}) collective-permute-start(bf16[2,256,768]{2,1,0:T(8,128)(2,1)S(1)} %bitcast.33), channel_id=1, source_target_pairs={{0,1},{1,0},{2,3},{3,2},{4,5},{5,4},{6,7},{7,6},{8,9},{9,8},{10,11... | collective-permute-start | bytes 2359304 | tf_op jit(solution)/shard_map/ppermute | solution.py:275
  7.7 1.6 %copy-start.2 = (f32[1,2,512,512]{3,2,1,0:T(8,128)S(1)}, f32[1,2,512,512]{3,2,1,0:T(8,128)}, u32[]{:S(2)}) copy-start(f32[1,2,512,512]{3,2,1,0:T(8,128)} %param.9) | copy-start | bytes 6291460
  7.7 1.6 %copy-start.4 = (s32[1,2]{1,0:T(1,128)S(1)}, s32[1,2]{1,0:T(1,128)}, u32[]{:S(2)}) copy-start(s32[1,2]{1,0:T(1,128)} %param.11) | copy-start | bytes 28
  13.9 11.1 %collective-permute-start.2 = (bf16[4,2,96,128]{3,2,1,0:T(8,128)(2,1)S(1)}, bf16[4,2,96,128]{3,2,1,0:T(8,128)(2,1)S(1)}, u32[]{:S(2)}, u32[]{:S(2)}) collective-permute-start(bf16[4,2,96,128]{3,2,1,0:T(8,128)(2,1)S(1)} %slice_bitcast_fusion.5), channel_id=1, source_target_pairs={{0,2},{2,4},{4,6},{6,0},{1,3},{3,5},{5,7},{7,1},{8,10},{10,12},{12... | collective-permute-start | bytes 589832 | tf_op jit(solution)/shard_map/ppermute | solution.py:270
  14.0 9.4 %copy-start.1 = (s32[1,2,24]{2,1,0:T(2,128)S(1)}, s32[1,2,24]{2,1,0:T(2,128)}, u32[]{:S(2)}) copy-start(s32[1,2,24]{2,1,0:T(2,128)} %param.10) | copy-start | bytes 580
  14.0 11.0 %collective-permute-start.3 = (bf16[4,2,96,128]{3,2,1,0:T(8,128)(2,1)S(1)}, bf16[4,2,96,128]{3,2,1,0:T(8,128)(2,1)S(1)}, u32[]{:S(2)}, u32[]{:S(2)}) collective-permute-start(bf16[4,2,96,128]{3,2,1,0:T(8,128)(2,1)S(1)} %slice_bitcast_fusion.4), channel_id=1, source_target_pairs={{0,6},{2,0},{4,2},{6,4},{1,7},{3,1},{5,3},{7,5},{8,14},{10,8},{12,... | collective-permute-start | bytes 589832 | tf_op jit(solution)/shard_map/ppermute | solution.py:270
  23.4 1.7 %copy-start = (bf16[1,1536,768]{2,1,0:T(8,128)(2,1)S(1)}, bf16[1,1536,768]{2,1,0:T(8,128)(2,1)}, u32[]{:S(2)}) copy-start(bf16[1,1536,768]{2,1,0:T(8,128)(2,1)} %param.6) | copy-start | bytes 7077892
  26.5 19.0 %collective-permute-start.5 = (f32[4,96,768]{2,1,0:T(8,128)S(1)}, f32[4,96,768]{2,1,0:T(8,128)S(1)}, u32[]{:S(2)}, u32[]{:S(2)}) collective-permute-start(f32[4,96,768]{2,1,0:T(8,128)S(1)} %shard_map.67), channel_id=1, source_target_pairs={{0,8},{8,0},{16,24},{24,16},{32,40},{40,32},{48,56},{56,48},{64,72... | collective-permute-start | bytes 3538952 | tf_op jit(solution)/shard_map/ppermute | solution.py:273
  29.4 11.8 %collective-permute-start.9 = (bf16[2,4,2,96,128]{4,3,2,1,0:T(8,128)(2,1)S(1)}, bf16[2,4,2,96,128]{4,3,2,1,0:T(8,128)(2,1)S(1)}, u32[]{:S(2)}, u32[]{:S(2)}) collective-permute-start(bf16[2,4,2,96,128]{4,3,2,1,0:T(8,128)(2,1)S(1)} %get-tuple-element.33.refs_0_), channel_id=1, source_target_pairs={{0,2},{2,4},{4,6},{6,0},{1,3},{3,5},{5,7},{7,1},{8,10},{10,12},{12... | collective-permute-start | bytes 1179656 | tf_op jit(solution)/shard_map/ppermute | solution.py:270
  29.5 11.8 %collective-permute-start.8 = (bf16[2,4,2,96,128]{4,3,2,1,0:T(8,128)(2,1)S(1)}, bf16[2,4,2,96,128]{4,3,2,1,0:T(8,128)(2,1)S(1)}, u32[]{:S(2)}, u32[]{:S(2)}) collective-permute-start(bf16[2,4,2,96,128]{4,3,2,1,0:T(8,128)(2,1)S(1)} %get-tuple-element.33.refs_0_), channel_id=1, source_target_pairs={{0,6},{2,0},{4,2},{6,4},{1,7},{3,1},{5,3},{7,5},{8,14},{10,8},{12,... | collective-permute-start | bytes 1179656 | tf_op jit(solution)/shard_map/ppermute | solution.py:270
  41.2 6.8 %collective-permute-start.10 = (bf16[4,2,96,128]{3,2,1,0:T(8,128)(2,1)S(1)}, bf16[4,2,96,128]{3,2,1,0:T(8,128)(2,1)S(1)}, u32[]{:S(2)}, u32[]{:S(2)}) collective-permute-start(bf16[4,2,96,128]{3,2,1,0:T(8,128)(2,1)S(1)} %slice_bitcast_fusion.3), channel_id=1, source_target_pairs={{0,2},{2,4},{4,6},{6,0},{1,3},{3,5},{5,7},{7,1},{8,10},{10,12},{12... | collective-permute-start | bytes 589832 | tf_op jit(solution)/shard_map/ppermute | solution.py:270
  41.4 6.7 %collective-permute-start.11 = (bf16[4,2,96,128]{3,2,1,0:T(8,128)(2,1)S(1)}, bf16[4,2,96,128]{3,2,1,0:T(8,128)(2,1)S(1)}, u32[]{:S(2)}, u32[]{:S(2)}) collective-permute-start(bf16[4,2,96,128]{3,2,1,0:T(8,128)(2,1)S(1)} %slice_bitcast_fusion.2), channel_id=1, source_target_pairs={{0,6},{2,0},{4,2},{6,4},{1,7},{3,1},{5,3},{7,5},{8,14},{10,8},{12,... | collective-permute-start | bytes 589832 | tf_op jit(solution)/shard_map/ppermute | solution.py:270
  49.5 5.0 %collective-permute-start.12 = (f32[4,96,768]{2,1,0:T(8,128)S(1)}, f32[4,96,768]{2,1,0:T(8,128)S(1)}, u32[]{:S(2)}, u32[]{:S(2)}) collective-permute-start(f32[4,96,768]{2,1,0:T(8,128)S(1)} %shard_map.71), channel_id=1, source_target_pairs={{0,8},{8,0},{16,24},{24,16},{32,40},{40,32},{48,56},{56,48},{64,72... | collective-permute-start | bytes 3538952 | tf_op jit(solution)/shard_map/ppermute | solution.py:273
  51.4 8.7 %collective-permute-start.6 = (bf16[2,96,768]{2,1,0:T(8,128)(2,1)S(1)}, bf16[2,96,768]{2,1,0:T(8,128)(2,1)S(1)}, u32[]{:S(2)}, u32[]{:S(2)}) collective-permute-start(bf16[2,96,768]{2,1,0:T(8,128)(2,1)S(1)} %get-tuple-element.26.refs_6_), channel_id=1, source_target_pairs={{0,16},{8,24},{16,0},{24,8},{32,48},{40,56},{48,32},{56,40},{64,80... | collective-permute-start | bytes 884744 | tf_op jit(solution)/shard_map/ppermute | solution.py:273
  55.2 14.3 %collective-permute-start.13 = (bf16[2,96,768]{2,1,0:T(8,128)(2,1)S(1)}, bf16[2,96,768]{2,1,0:T(8,128)(2,1)S(1)}, u32[]{:S(2)}, u32[]{:S(2)}) collective-permute-start(bf16[2,96,768]{2,1,0:T(8,128)(2,1)S(1)} %get-tuple-element.30), channel_id=1, source_target_pairs={{0,16},{8,24},{16,0},{24,8},{32,48},{40,56},{48,32},{56,40},{64,80... | collective-permute-start | bytes 884744 | tf_op jit(solution)/shard_map/ppermute | solution.py:273
  60.8 10.1 %collective-permute-start.7 = (bf16[96,768]{1,0:T(8,128)(2,1)S(1)}, bf16[96,768]{1,0:T(8,128)(2,1)S(1)}, u32[]{:S(2)}, u32[]{:S(2)}) collective-permute-start(bf16[96,768]{1,0:T(8,128)(2,1)S(1)} %get-tuple-element.28), channel_id=1, source_target_pairs={{0,32},{8,40},{16,48},{24,56},{32,0},{40,8},{48,16},{56,24},{64,96... | collective-permute-start | bytes 442376 | tf_op jit(solution)/shard_map/ppermute | solution.py:273
  70.3 9.9 %collective-permute-start.14 = (bf16[96,768]{1,0:T(8,128)(2,1)S(1)}, bf16[96,768]{1,0:T(8,128)(2,1)S(1)}, u32[]{:S(2)}, u32[]{:S(2)}) collective-permute-start(bf16[96,768]{1,0:T(8,128)(2,1)S(1)} %get-tuple-element.32), channel_id=1, source_target_pairs={{0,32},{8,40},{16,48},{24,56},{32,0},{40,8},{48,16},{56,24},{64,96... | collective-permute-start | bytes 442376 | tf_op jit(solution)/shard_map/ppermute | solution.py:273

commit v4 on v2

--- a/solution.py
+++ b/solution.py
@@ -51,6 +51,23 @@
     rows = lax.broadcasted_iota(jnp.int32, (order, order), 0)
     cols = lax.broadcasted_iota(jnp.int32, (order, order), 1)
     return rows == cols, (rows < width) & (cols < width)
+
+
+def place_kernel(in_ref, out_ref):
+    for k in range(in_ref.shape[0]):
+        out_ref[k] = in_ref[k]
+
+
+def place_call(pos):
+    return pl.pallas_call(
+        place_kernel,
+        in_specs=[SMEM],
+        out_specs=SMEM,
+        out_shape=jax.ShapeDtypeStruct(pos.shape, pos.dtype),
+        cost_estimate=cost(10**10, 10**7),
+        name="place",
+        compiler_params=grant(1),
+    )(pos)
 
 
 def inverse_kernel(width_ref, pos_ref, system_ref, upper_ref, xh_ref, xl_ref, part_ref):
@@ -139,7 +156,9 @@
     order = scaled.shape[1] * scaled.shape[2]
 
     def update_kernel(pos_ref, fill_ref, front_ref, *refs):
-        *piece_refs, scaled_ref, after_ref, out_ref, wide = refs
+        own_ref, next_ref, last_ref, *far_refs, scaled_ref, _, out_ref, wide = refs
+        if len(far_refs) == 1:
+            far_refs = [far_refs[0].at[s] for s in range(members)]
         side = 1 - pos_ref[0] if flip else pos_ref[0]
         strip = 2 * rows
         base = pos_ref[2] * (spots * 2 * strip) + side * strip + chunk * rows
@@ -148,22 +167,24 @@
                 for j in range(rows // SUB):
                     spot = lax.div(base + d * 2 * strip + j * SUB, BLOCK)
                     used = fill_ref[s, spot] != 0
-                    for k, ref in enumerate(piece_refs):
-                        tile = ref[s, d, side, j * SUB : (j + 1) * SUB, :]
+                    spans = (d, side, slice(j * SUB, (j + 1) * SUB))
+                    tiles = (own_ref[s, *spans], next_ref[s, *spans], far_refs[s][*spans], last_ref[s, *spans])
+                    for k, tile in enumerate(tiles):
                         begin = s * order + k * BLOCK
                         top = d * rows + j * SUB
                         wide[top : top + SUB, begin : begin + BLOCK] = jnp.where(used, tile, jnp.zeros_like(tile))
         flat = scaled_ref[...].reshape(members * order, cols)
         update = dot(wide[...], flat).reshape(spots, rows, cols)
         for d in range(spots):
-            out_ref[d] = front_ref[d, side, chunk].astype(F32) - update[d]
+            copy = front_ref[d, side, chunk].astype(F32) - update[d]
+            out_ref[d] = code(copy) if flip else copy
 
     return pl.pallas_call(
         update_kernel,
-        in_specs=[SMEM, SMEM] + [VMEM] * 6 + [ANY],
+        in_specs=[SMEM, SMEM] + [VMEM] * (len(lowers) + 2) + [ANY],
         out_specs=VMEM,
         scratch_shapes=[pltpu.VMEM((spots * rows, members * order), BF16)],
-        out_shape=jax.ShapeDtypeStruct((spots, rows, cols), F32),
+        out_shape=jax.ShapeDtypeStruct((spots, rows, cols), BF16 if flip else F32),
         cost_estimate=cost(2 * spots * rows * members * order * cols, 4000000),
         compiler_params=grant(12),
     )(pos, fill, front, *lowers, scaled, after)
@@ -173,8 +194,8 @@
     place = pos_ref[3]
     for k, out_ref in enumerate(out_refs):
         spot = lax.bitwise_xor(place, k + 1)
-        out_ref[...] = code(kept_ref[spot] + got_ref[spot])
-    own_ref[...] = kept_ref[place] + got_ref[place]
+        out_ref[...] = code(kept_ref[spot] + decode(got_ref[spot]))
+    own_ref[...] = kept_ref[place] + decode(got_ref[place])
 
 
 def round_call(pos, kept, got):
@@ -186,7 +207,6 @@
         out_shape=[jax.ShapeDtypeStruct((rows, cols), F32)]
         + [jax.ShapeDtypeStruct((rows, cols), BF16)] * (spots - 1),
         cost_estimate=cost(spots * rows * cols, 10 * spots * rows * cols),
-        name="round_sums",
         compiler_params=grant(8),
     )(pos, kept, got)
 
@@ -226,6 +246,7 @@
         layer & 1,
         jnp.where(which == 1, col_index, jnp.where(which == 2, row_index, layer >> 1 & 3)),
     ).astype(jnp.int32)
+    pos = place_call(pos)
     upper, fill, width_vec = upper_panels[0], block_fill[0], widths[0]
     row_count, cols = front_copies.shape[1:]
     members = upper.shape[0]
@@ -244,10 +265,12 @@
     lowers = []
     for chunk in range(2):
         own = lower[:, :, :, chunk]
-        last = shift(own, 1)
-        following = shift(own, -1)
-        far = shift(own, 2)
-        lowers.append((own, following, far, last))
+        following, last = shift(own, -1), shift(own, 1)
+        if chunk == 0:
+            far = (shift(own, 2),)
+        else:
+            far = (shift(last[0], 1), shift(following[1], -1))
+        lowers.append((own, following, last, *far))
     xh, xl, part = inverse_call(width_vec, pos, diag_blocks[0], upper)
     scaled = scale_call(pos, fill, xh, xl, part, other_upper)
     finals = []

time: 82.7 us -> 80.4 us (0.972)
  the two profiles are of different devices: /device:TPU:71 before, /device:TPU:79 now
where the time goes in v4:
time: 80.4 us; the launch traced here: 80.2 us
  waiting for transfers between devices  36.8 us (46%)
  starting transfers between devices  22.5 us (28%)
  Pallas kernels  19.5 us (24%)
  local copies, waits for them, and re-layouts  1.27 us (2%)
    ppermute x8, waiting for transfers between devices, across(): return lax.ppermute(block, 'layer', [(i, i ^ flip) for i in range(layers)])  17.3 us
    ppermute x1, waiting for transfers between devices, on_device(): other_upper = lax.ppermute(upper, 'row', [(0, 1), (1, 0)])  14.5 us
    ppermute x8, starting transfers between devices, across(): return lax.ppermute(block, 'layer', [(i, i ^ flip) for i in range(layers)])  13 us
    pallas_call x1, Pallas kernels, inverse_call(): pl.pallas_call(inverse_kernel, in_specs=[SMEM, SMEM, VMEM, VMEM], out_spe...  7.83 us
    ppermute x7, starting transfers between devices, shift(): lax.ppermute(block, 'col', [(i, (i + step) % col_devices) for i in range(...  7.51 us
    pallas_call x4, Pallas kernels, update_call(): pl.pallas_call(update_kernel, in_specs=[SMEM, SMEM] + [VMEM] * (len(lower...  5.83 us
    ppermute x7, waiting for transfers between devices, shift(): lax.ppermute(block, 'col', [(i, (i + step) % col_devices) for i in range(...  4.96 us
    ppermute x1, starting transfers between devices, on_device(): other_upper = lax.ppermute(upper, 'row', [(0, 1), (1, 0)])  2.01 us
  transfers between devices with their start and end apart: 16, of which 5 were waited for; matrix products, arithmetic and copies ran while one was open for 0% of the time, Pallas kernels for 21%

profile of v4, /device:TPU:79, one launch (start us, length us, event | category | flops | bytes accessed | tf_op | source)
XLA Modules:
  0.0 80.2 jit_solution(6430372511027607123)
XLA Ops:
  0.0 1.2 %slice_bitcast_fusion = (bf16[2,4,2,96,128]{4,3,2,1,0:T(8,128)(2,1)S(1)}, bf16[2,4,2,96,128]{4,3,2,1,0:T(8,128)(2,1)S(1)}) fusion(bf16[2,4,2,2,96,128]{5,4,3,2,1,0:T(8,128)(2,1)} %bitcast.31), kind=kLoop, calls=%fused_computation | loop fusion | bytes 1572864 | tf_op jit(solution)/shard_map/squeeze | solution.py:267
  1.2 0.6 collective-permute-start
  1.8 2.1 %collective-permute-start.1 = (bf16[2,4,2,96,128]{4,3,2,1,0:T(8,128)(2,1)S(1)}, bf16[2,4,2,96,128]{4,3,2,1,0:T(8,128)(2,1)S(1)}, u32[]{:S(2)}, u32[]{:S(2)}) collective-permute-start(bf16[2,4,2,96,128]{4,3,2,1,0:T(8,128)(2,1)S(1)} %get-tuple-element.28.refs_0_), channel_id=1, source_target_pairs={{0,2},{2,4},{4,6},{6,0},{1,3},{3,5},{5,7},{7,1},{8,10},{10,12},{12... | collective-permute-start | bytes 1179656 | tf_op jit(solution)/shard_map/ppermute | solution.py:259
  3.9 0.0 collective-permute-start.2
  3.9 2.0 %collective-permute-start.3 = (bf16[2,256,768]{2,1,0:T(8,128)(2,1)}, bf16[2,256,768]{2,1,0:T(8,128)(2,1)S(1)}, u32[]{:S(2)}, u32[]{:S(2)}) collective-permute-start(bf16[2,256,768]{2,1,0:T(8,128)(2,1)} %bitcast.28), channel_id=1, source_target_pairs={{0,1},{1,0},{2,3},{3,2},{4,5},{5,4},{6,7},{7,6},{8,9},{9,8},{10,11... | collective-permute-start | bytes 2359304 | tf_op jit(solution)/shard_map/ppermute | solution.py:264
  6.0 1.7 %collective-permute-start.9 = (bf16[2,4,2,96,128]{4,3,2,1,0:T(8,128)(2,1)S(1)}, bf16[2,4,2,96,128]{4,3,2,1,0:T(8,128)(2,1)S(1)}, u32[]{:S(2)}, u32[]{:S(2)}) collective-permute-start(bf16[2,4,2,96,128]{4,3,2,1,0:T(8,128)(2,1)S(1)} %get-tuple-element.27.refs_0_), channel_id=1, source_target_pairs={{0,2},{2,4},{4,6},{6,0},{1,3},{3,5},{5,7},{7,1},{8,10},{10,12},{12... | collective-permute-start | bytes 1179656 | tf_op jit(solution)/shard_map/ppermute | solution.py:259
  7.7 0.0 copy-start.4
  7.7 1.1 %place.1.pos_ref = s32[4]{0:T(128)S(1)} custom-call(s32[4]{0:T(128)S(1)} %compare_select_fusion.2.in_ref), custom_call_target="tpu_custom_call" | custom-call | flops 10000000000 | bytes 10000000 | tf_op jit(solution)/shard_map/place/pallas_call | solution.py:62
  8.8 14.5 %collective-permute-done.3.upper_ref = bf16[2,256,768]{2,1,0:T(8,128)(2,1)S(1)} collective-permute-done((bf16[2,256,768]{2,1,0:T(8,128)(2,1)}, bf16[2,256,768]{2,1,0:T(8,128)(2,1)S(1)}, u32[]{:S(2)}, u32[]{:S(2)}) %collective-permute-start.3) | collective-permute-done | bytes 786464 | tf_op jit(solution)/shard_map/ppermute | solution.py:264
  23.3 0.8 collective-permute-start.8
  24.1 0.0 copy-done.2
  24.1 0.0 copy-done.3
  24.1 7.8 %inverse.1 = (bf16[2,512,256]{2,1,0:T(8,128)(2,1)S(1)}, bf16[2,512,256]{2,1,0:T(8,128)(2,1)S(1)}, f32[2,512,768]{2,1,0:T(8,128)S(1)}) custom-call(s32[2]{0:T(128)S(1)} %bitcast.30, s32[4]{0:T(128)S(1)} %place.1.pos_ref, f32[2,512,512]{2,1,0:T(8,128)S(1)} %bitcast.27, bf16[2,256,768]{2,1,0:T(8,128)(2,1)S(1)} %bitcast.29), custom_call_target="tpu_custom_call" | custom-call | flops 3758096384 | bytes 8000000 | tf_op jit(solution)/shard_map/inverse/pallas_call | solution.py:106
  31.9 0.0 copy-start
  32.0 1.6 %scale_upper.1.refs_4_.refs_5_ = bf16[2,4,128,768]{3,2,1,0:T(8,128)(2,1)S(1)} custom-call(s32[4]{0:T(128)S(1)} %place.1.pos_ref, s32[2,24]{1,0:T(2,128)S(1)} %bitcast.22, bf16[2,512,256]{2,1,0:T(8,128)(2,1)S(1)} %get-tuple-element.16.xh_ref, bf16[2,512,256]{2,1,0:T(8,128)(2,1)S(1)} %get-tuple-element.17.xl_ref, ...), custom_call_target="tpu_custom_call" | custom-call | flops 805306368 | bytes 6291456 | tf_op jit(solution)/shard_map/scale_upper/pallas_call | solution.py:142
  33.5 0.0 collective-permute-done.refs_1_
  33.5 0.0 collective-permute-done.1.refs_2_
  33.6 0.0 collective-permute-done.2.refs_3_
  33.6 0.1 copy-done
  33.6 1.5 %shard_map.65 = bf16[4,96,768]{2,1,0:T(8,128)(2,1)S(1)} custom-call(s32[4]{0:T(128)S(1)} %place.1.pos_ref, s32[2,24]{1,0:T(2,128)S(1)} %bitcast.23, bf16[4,2,2,96,768]{4,3,2,1,0:T(8,128)(2,1)S(1)} %bitcast.18, bf16[2,4,2,96,128]{4,3,2,1,0:T(8,128)(2,1)S(1)} %get-tuple-element.28.refs_0_, bf16[2,4,2,96,128]{4,3,2,1,0:T(8,128)(2,1)S(1)} %collective-permute-done.refs_1_, ...), custom_call_target="tpu_custom_call" | custom-call | flops 603979776 | bytes 4000000 | tf_op jit(solution)/shard_map/pallas_call | solution.py:182
  35.1 2.6 %collective-permute-start.4 = (bf16[4,96,768]{2,1,0:T(8,128)(2,1)S(1)}, bf16[4,96,768]{2,1,0:T(8,128)(2,1)S(1)}, u32[]{:S(2)}, u32[]{:S(2)}) collective-permute-start(bf16[4,96,768]{2,1,0:T(8,128)(2,1)S(1)} %shard_map.65), channel_id=1, source_target_pairs={{0,8},{8,0},{16,24},{24,16},{32,40},{40,32},{48,56},{56,48},{64,72... | collective-permute-start | bytes 1769480 | tf_op jit(solution)/shard_map/ppermute | solution.py:262
  37.8 0.0 collective-permute-done.9.refs_2_
  37.8 2.2 %collective-permute-start.10 = (bf16[4,2,96,128]{3,2,1,0:T(8,128)(2,1)S(1)}, bf16[4,2,96,128]{3,2,1,0:T(8,128)(2,1)S(1)}, u32[]{:S(2)}, u32[]{:S(2)}) collective-permute-start(bf16[4,2,96,128]{3,2,1,0:T(8,128)(2,1)S(1)} %slice_bitcast_fusion.3), channel_id=1, source_target_pairs={{0,2},{2,4},{4,6},{6,0},{1,3},{3,5},{5,7},{7,1},{8,10},{10,12},{12... | collective-permute-start | bytes 589832 | tf_op jit(solution)/shard_map/ppermute | solution.py:259
  40.0 0.0 collective-permute-done.8.refs_1_
  40.0 0.1 collective-permute-start.11
  40.1 1.4 %shard_map.64.kept_ref = f32[4,96,768]{2,1,0:T(8,128)S(1)} custom-call(s32[4]{0:T(128)S(1)} %place.1.pos_ref, s32[2,24]{1,0:T(2,128)S(1)} %bitcast.24, bf16[4,2,2,96,768]{4,3,2,1,0:T(8,128)(2,1)S(1)} %bitcast.19, bf16[2,4,2,96,128]{4,3,2,1,0:T(8,128)(2,1)S(1)} %get-tuple-element.28.refs_0_, bf16[2,4,2,96,128]{4,3,2,1,0:T(8,128)(2,1)S(1)} %collective-permute-done.refs_1_, ...), custom_call_target="tpu_custom_call" | custom-call | flops 603979776 | bytes 4000000 | tf_op jit(solution)/shard_map/pallas_call | solution.py:182
  41.5 0.0 collective-permute-done.4.got_ref
  41.5 1.0 %shard_map.66 = (f32[96,768]{1,0:T(8,128)S(1)}, bf16[96,768]{1,0:T(8,128)(2,1)S(1)}, bf16[96,768]{1,0:T(8,128)(2,1)S(1)}, bf16[96,768]{1,0:T(8,128)(2,1)S(1)}) custom-call(s32[4]{0:T(128)S(1)} %place.1.pos_ref, f32[4,96,768]{2,1,0:T(8,128)S(1)} %shard_map.64.kept_ref, bf16[4,96,768]{2,1,0:T(8,128)(2,1)S(1)} %collective-permute-done.4.got_ref), custom_call_target="tpu_custom_call" | custom-call | flops 294912 | bytes 2949120 | tf_op jit(solution)/shard_map/pallas_call | solution.py:203
  42.5 2.7 %collective-permute-done.10.refs_3_ = bf16[4,2,96,128]{3,2,1,0:T(8,128)(2,1)S(1)} collective-permute-done((bf16[4,2,96,128]{3,2,1,0:T(8,128)(2,1)S(1)}, bf16[4,2,96,128]{3,2,1,0:T(8,128)(2,1)S(1)}, u32[]{:S(2)}, u32[]{:S(2)}) %collective-permute-start.10) | collective-permute-done | bytes 196640 | tf_op jit(solution)/shard_map/ppermute | solution.py:259
  45.2 2.2 %collective-permute-done.11.refs_4_ = bf16[4,2,96,128]{3,2,1,0:T(8,128)(2,1)S(1)} collective-permute-done((bf16[4,2,96,128]{3,2,1,0:T(8,128)(2,1)S(1)}, bf16[4,2,96,128]{3,2,1,0:T(8,128)(2,1)S(1)}, u32[]{:S(2)}, u32[]{:S(2)}) %collective-permute-start.11) | collective-permute-done | bytes 196640 | tf_op jit(solution)/shard_map/ppermute | solution.py:259
  47.4 1.5 %shard_map.68 = bf16[4,96,768]{2,1,0:T(8,128)(2,1)S(1)} custom-call(s32[4]{0:T(128)S(1)} %place.1.pos_ref, s32[2,24]{1,0:T(2,128)S(1)} %bitcast.25, bf16[4,2,2,96,768]{4,3,2,1,0:T(8,128)(2,1)S(1)} %bitcast.20, bf16[2,4,2,96,128]{4,3,2,1,0:T(8,128)(2,1)S(1)} %get-tuple-element.27.refs_0_, bf16[2,4,2,96,128]{4,3,2,1,0:T(8,128)(2,1)S(1)} %collective-permute-done.8.refs_1_, ...), custom_call_target="tpu_custom_call" | custom-call | flops 603979776 | bytes 4000000 | tf_op jit(solution)/shard_map/pallas_call | solution.py:182
  48.9 1.3 %collective-permute-start.12 = (bf16[4,96,768]{2,1,0:T(8,128)(2,1)S(1)}, bf16[4,96,768]{2,1,0:T(8,128)(2,1)S(1)}, u32[]{:S(2)}, u32[]{:S(2)}) collective-permute-start(bf16[4,96,768]{2,1,0:T(8,128)(2,1)S(1)} %shard_map.68), channel_id=1, source_target_pairs={{0,8},{8,0},{16,24},{24,16},{32,40},{40,32},{48,56},{56,48},{64,72... | collective-permute-start | bytes 1769480 | tf_op jit(solution)/shard_map/ppermute | solution.py:262
  50.2 0.0 collective-permute-start.5
  50.2 1.6 %collective-permute-start.7 = (bf16[96,768]{1,0:T(8,128)(2,1)S(1)}, bf16[96,768]{1,0:T(8,128)(2,1)S(1)}, u32[]{:S(2)}, u32[]{:S(2)}) collective-permute-start(bf16[96,768]{1,0:T(8,128)(2,1)S(1)} %get-tuple-element.22.refs_6_), channel_id=1, source_target_pairs={{0,16},{8,24},{16,0},{24,8},{32,48},{40,56},{48,32},{56,40},{64,80... | collective-permute-start | bytes 442376 | tf_op jit(solution)/shard_map/ppermute | solution.py:262
  51.8 1.2 %collective-permute-start.6 = (bf16[96,768]{1,0:T(8,128)(2,1)S(1)}, bf16[96,768]{1,0:T(8,128)(2,1)S(1)}, u32[]{:S(2)}, u32[]{:S(2)}) collective-permute-start(bf16[96,768]{1,0:T(8,128)(2,1)S(1)} %get-tuple-element.21), channel_id=1, source_target_pairs={{0,48},{8,56},{16,32},{24,40},{32,16},{40,24},{48,0},{56,8},{64,11... | collective-permute-start | bytes 442376 | tf_op jit(solution)/shard_map/ppermute | solution.py:262
  53.0 1.4 %shard_map.67.kept_ref = f32[4,96,768]{2,1,0:T(8,128)S(1)} custom-call(s32[4]{0:T(128)S(1)} %place.1.pos_ref, s32[2,24]{1,0:T(2,128)S(1)} %bitcast.26, bf16[4,2,2,96,768]{4,3,2,1,0:T(8,128)(2,1)S(1)} %bitcast.21, bf16[2,4,2,96,128]{4,3,2,1,0:T(8,128)(2,1)S(1)} %get-tuple-element.27.refs_0_, bf16[2,4,2,96,128]{4,3,2,1,0:T(8,128)(2,1)S(1)} %collective-permute-done.8.refs_1_, ...), custom_call_target="tpu_custom_call" | custom-call | flops 603979776 | bytes 4000000 | tf_op jit(solution)/shard_map/pallas_call | solution.py:182
  54.4 0.0 collective-permute-done.12.got_ref
  54.4 1.0 %shard_map.69 = (f32[96,768]{1,0:T(8,128)S(1)}, bf16[96,768]{1,0:T(8,128)(2,1)S(1)}, bf16[96,768]{1,0:T(8,128)(2,1)S(1)}, bf16[96,768]{1,0:T(8,128)(2,1)S(1)}) custom-call(s32[4]{0:T(128)S(1)} %place.1.pos_ref, f32[4,96,768]{2,1,0:T(8,128)S(1)} %shard_map.67.kept_ref, bf16[4,96,768]{2,1,0:T(8,128)(2,1)S(1)} %collective-permute-done.12.got_ref), custom_call_target="tpu_custom_call" | custom-call | flops 294912 | bytes 2949120 | tf_op jit(solution)/shard_map/pallas_call | solution.py:203
  55.4 1.3 %collective-permute-start.13 = (bf16[96,768]{1,0:T(8,128)(2,1)S(1)}, bf16[96,768]{1,0:T(8,128)(2,1)S(1)}, u32[]{:S(2)}, u32[]{:S(2)}) collective-permute-start(bf16[96,768]{1,0:T(8,128)(2,1)S(1)} %get-tuple-element.24), channel_id=1, source_target_pairs={{0,32},{8,40},{16,48},{24,56},{32,0},{40,8},{48,16},{56,24},{64,96... | collective-permute-start | bytes 442376 | tf_op jit(solution)/shard_map/ppermute | solution.py:262
  56.7 2.4 %collective-permute-start.14 = (bf16[96,768]{1,0:T(8,128)(2,1)S(1)}, bf16[96,768]{1,0:T(8,128)(2,1)S(1)}, u32[]{:S(2)}, u32[]{:S(2)}) collective-permute-start(bf16[96,768]{1,0:T(8,128)(2,1)S(1)} %get-tuple-element.25), channel_id=1, source_target_pairs={{0,48},{8,56},{16,32},{24,40},{32,16},{40,24},{48,0},{56,8},{64,11... | collective-permute-start | bytes 442376 | tf_op jit(solution)/shard_map/ppermute | solution.py:262
  59.0 0.0 collective-permute-done.5.refs_1_
  59.0 2.7 %collective-permute-start.15 = (bf16[96,768]{1,0:T(8,128)(2,1)S(1)}, bf16[96,768]{1,0:T(8,128)(2,1)S(1)}, u32[]{:S(2)}, u32[]{:S(2)}) collective-permute-start(bf16[96,768]{1,0:T(8,128)(2,1)S(1)} %get-tuple-element.26), channel_id=1, source_target_pairs={{0,16},{8,24},{16,0},{24,8},{32,48},{40,56},{48,32},{56,40},{64,80... | collective-permute-start | bytes 442376 | tf_op jit(solution)/shard_map/ppermute | solution.py:262
  61.7 11.0 %collective-permute-done.6.refs_2_ = bf16[96,768]{1,0:T(8,128)(2,1)S(1)} collective-permute-done((bf16[96,768]{1,0:T(8,128)(2,1)S(1)}, bf16[96,768]{1,0:T(8,128)(2,1)S(1)}, u32[]{:S(2)}, u32[]{:S(2)}) %collective-permute-start.6) | collective-permute-done | bytes 147488 | tf_op jit(solution)/shard_map/ppermute | solution.py:262
  72.7 0.0 collective-permute-done.7.refs_3_
  72.7 0.0 collective-permute-done.13.refs_5_
  72.7 6.3 %collective-permute-done.14.refs_6_ = bf16[96,768]{1,0:T(8,128)(2,1)S(1)} collective-permute-done((bf16[96,768]{1,0:T(8,128)(2,1)S(1)}, bf16[96,768]{1,0:T(8,128)(2,1)S(1)}, u32[]{:S(2)}, u32[]{:S(2)}) %collective-permute-start.14) | collective-permute-done | bytes 147488 | tf_op jit(solution)/shard_map/ppermute | solution.py:262
  79.0 0.0 collective-permute-done.15.refs_7_
  79.0 1.2 %final_sums.1 = f32[1,192,768]{2,1,0:T(8,128)} custom-call(f32[96,768]{1,0:T(8,128)S(1)} %get-tuple-element.19.refs_0_, bf16[96,768]{1,0:T(8,128)(2,1)S(1)} %collective-permute-done.5.refs_1_, bf16[96,768]{1,0:T(8,128)(2,1)S(1)} %collective-permute-done.6.refs_2_, bf16[96,768]{1,0:T(8,128)(2,1)S(1)} %collective-permute-done.7.refs_3_, ...), custom_call_target="tpu_custom_call" | custom-call | flops 589824 | bytes 1769472 | tf_op jit(solution)/shard_map/final_sums/pallas_call | solution.py:228
  (8 shorter events, 0.0 us)
Async XLA Ops:
  1.2 32.4 %collective-permute-start = (bf16[2,4,2,96,128]{4,3,2,1,0:T(8,128)(2,1)S(1)}, bf16[2,4,2,96,128]{4,3,2,1,0:T(8,128)(2,1)S(1)}, u32[]{:S(2)}, u32[]{:S(2)}) collective-permute-start(bf16[2,4,2,96,128]{4,3,2,1,0:T(8,128)(2,1)S(1)} %get-tuple-element.28.refs_0_), channel_id=1, source_target_pairs={{0,6},{2,0},{4,2},{6,4},{1,7},{3,1},{5,3},{7,5},{8,14},{10,8},{12,... | collective-permute-start | bytes 1179656 | tf_op jit(solution)/shard_map/ppermute | solution.py:259
  1.8 31.7 %collective-permute-start.1 = (bf16[2,4,2,96,128]{4,3,2,1,0:T(8,128)(2,1)S(1)}, bf16[2,4,2,96,128]{4,3,2,1,0:T(8,128)(2,1)S(1)}, u32[]{:S(2)}, u32[]{:S(2)}) collective-permute-start(bf16[2,4,2,96,128]{4,3,2,1,0:T(8,128)(2,1)S(1)} %get-tuple-element.28.refs_0_), channel_id=1, source_target_pairs={{0,2},{2,4},{4,6},{6,0},{1,3},{3,5},{5,7},{7,1},{8,10},{10,12},{12... | collective-permute-start | bytes 1179656 | tf_op jit(solution)/shard_map/ppermute | solution.py:259
  3.9 29.6 %collective-permute-start.2 = (bf16[2,4,2,96,128]{4,3,2,1,0:T(8,128)(2,1)S(1)}, bf16[2,4,2,96,128]{4,3,2,1,0:T(8,128)(2,1)S(1)}, u32[]{:S(2)}, u32[]{:S(2)}) collective-permute-start(bf16[2,4,2,96,128]{4,3,2,1,0:T(8,128)(2,1)S(1)} %get-tuple-element.28.refs_0_), channel_id=1, source_target_pairs={{0,4},{2,6},{4,0},{6,2},{1,5},{3,7},{5,1},{7,3},{8,12},{10,14},{12... | collective-permute-start | bytes 1179656 | tf_op jit(solution)/shard_map/ppermute | solution.py:259
  3.9 19.4 %collective-permute-start.3 = (bf16[2,256,768]{2,1,0:T(8,128)(2,1)}, bf16[2,256,768]{2,1,0:T(8,128)(2,1)S(1)}, u32[]{:S(2)}, u32[]{:S(2)}) collective-permute-start(bf16[2,256,768]{2,1,0:T(8,128)(2,1)} %bitcast.28), channel_id=1, source_target_pairs={{0,1},{1,0},{2,3},{3,2},{4,5},{5,4},{6,7},{7,6},{8,9},{9,8},{10,11... | collective-permute-start | bytes 2359304 | tf_op jit(solution)/shard_map/ppermute | solution.py:264
  6.0 31.8 %collective-permute-start.9 = (bf16[2,4,2,96,128]{4,3,2,1,0:T(8,128)(2,1)S(1)}, bf16[2,4,2,96,128]{4,3,2,1,0:T(8,128)(2,1)S(1)}, u32[]{:S(2)}, u32[]{:S(2)}) collective-permute-start(bf16[2,4,2,96,128]{4,3,2,1,0:T(8,128)(2,1)S(1)} %get-tuple-element.27.refs_0_), channel_id=1, source_target_pairs={{0,2},{2,4},{4,6},{6,0},{1,3},{3,5},{5,7},{7,1},{8,10},{10,12},{12... | collective-permute-start | bytes 1179656 | tf_op jit(solution)/shard_map/ppermute | solution.py:259
  7.7 16.4 %copy-start.2 = (f32[1,2,512,512]{3,2,1,0:T(8,128)S(1)}, f32[1,2,512,512]{3,2,1,0:T(8,128)}, u32[]{:S(2)}) copy-start(f32[1,2,512,512]{3,2,1,0:T(8,128)} %param.9) | copy-start | bytes 6291460
  7.7 16.4 %copy-start.3 = (bf16[1,2,256,768]{3,2,1,0:T(8,128)(2,1)S(1)}, bf16[1,2,256,768]{3,2,1,0:T(8,128)(2,1)}, u32[]{:S(2)}) copy-start(bf16[1,2,256,768]{3,2,1,0:T(8,128)(2,1)} %param.8) | copy-start | bytes 2359300
  7.7 16.4 %copy-start.4 = (s32[1,2]{1,0:T(1,128)S(1)}, s32[1,2]{1,0:T(1,128)}, u32[]{:S(2)}) copy-start(s32[1,2]{1,0:T(1,128)} %param.11) | copy-start | bytes 28
  23.3 16.6 %collective-permute-start.8 = (bf16[2,4,2,96,128]{4,3,2,1,0:T(8,128)(2,1)S(1)}, bf16[2,4,2,96,128]{4,3,2,1,0:T(8,128)(2,1)S(1)}, u32[]{:S(2)}, u32[]{:S(2)}) collective-permute-start(bf16[2,4,2,96,128]{4,3,2,1,0:T(8,128)(2,1)S(1)} %get-tuple-element.27.refs_0_), channel_id=1, source_target_pairs={{0,6},{2,0},{4,2},{6,4},{1,7},{3,1},{5,3},{7,5},{8,14},{10,8},{12,... | collective-permute-start | bytes 1179656 | tf_op jit(solution)/shard_map/ppermute | solution.py:259
  24.1 7.8 %copy-start.1 = (s32[1,2,24]{2,1,0:T(2,128)S(1)}, s32[1,2,24]{2,1,0:T(2,128)}, u32[]{:S(2)}) copy-start(s32[1,2,24]{2,1,0:T(2,128)} %param.10) | copy-start | bytes 580
  31.9 1.7 %copy-start = (bf16[1,1536,768]{2,1,0:T(8,128)(2,1)S(1)}, bf16[1,1536,768]{2,1,0:T(8,128)(2,1)}, u32[]{:S(2)}) copy-start(bf16[1,1536,768]{2,1,0:T(8,128)(2,1)} %param.6) | copy-start | bytes 7077892
  35.1 6.4 %collective-permute-start.4 = (bf16[4,96,768]{2,1,0:T(8,128)(2,1)S(1)}, bf16[4,96,768]{2,1,0:T(8,128)(2,1)S(1)}, u32[]{:S(2)}, u32[]{:S(2)}) collective-permute-start(bf16[4,96,768]{2,1,0:T(8,128)(2,1)S(1)} %shard_map.65), channel_id=1, source_target_pairs={{0,8},{8,0},{16,24},{24,16},{32,40},{40,32},{48,56},{56,48},{64,72... | collective-permute-start | bytes 1769480 | tf_op jit(solution)/shard_map/ppermute | solution.py:262
  37.8 7.4 %collective-permute-start.10 = (bf16[4,2,96,128]{3,2,1,0:T(8,128)(2,1)S(1)}, bf16[4,2,96,128]{3,2,1,0:T(8,128)(2,1)S(1)}, u32[]{:S(2)}, u32[]{:S(2)}) collective-permute-start(bf16[4,2,96,128]{3,2,1,0:T(8,128)(2,1)S(1)} %slice_bitcast_fusion.3), channel_id=1, source_target_pairs={{0,2},{2,4},{4,6},{6,0},{1,3},{3,5},{5,7},{7,1},{8,10},{10,12},{12... | collective-permute-start | bytes 589832 | tf_op jit(solution)/shard_map/ppermute | solution.py:259
  40.0 7.4 %collective-permute-start.11 = (bf16[4,2,96,128]{3,2,1,0:T(8,128)(2,1)S(1)}, bf16[4,2,96,128]{3,2,1,0:T(8,128)(2,1)S(1)}, u32[]{:S(2)}, u32[]{:S(2)}) collective-permute-start(bf16[4,2,96,128]{3,2,1,0:T(8,128)(2,1)S(1)} %slice_bitcast_fusion.2), channel_id=1, source_target_pairs={{0,6},{2,0},{4,2},{6,4},{1,7},{3,1},{5,3},{7,5},{8,14},{10,8},{12,... | collective-permute-start | bytes 589832 | tf_op jit(solution)/shard_map/ppermute | solution.py:259
  48.9 5.5 %collective-permute-start.12 = (bf16[4,96,768]{2,1,0:T(8,128)(2,1)S(1)}, bf16[4,96,768]{2,1,0:T(8,128)(2,1)S(1)}, u32[]{:S(2)}, u32[]{:S(2)}) collective-permute-start(bf16[4,96,768]{2,1,0:T(8,128)(2,1)S(1)} %shard_map.68), channel_id=1, source_target_pairs={{0,8},{8,0},{16,24},{24,16},{32,40},{40,32},{48,56},{56,48},{64,72... | collective-permute-start | bytes 1769480 | tf_op jit(solution)/shard_map/ppermute | solution.py:262
  50.2 8.9 %collective-permute-start.5 = (bf16[96,768]{1,0:T(8,128)(2,1)S(1)}, bf16[96,768]{1,0:T(8,128)(2,1)S(1)}, u32[]{:S(2)}, u32[]{:S(2)}) collective-permute-start(bf16[96,768]{1,0:T(8,128)(2,1)S(1)} %get-tuple-element.20), channel_id=1, source_target_pairs={{0,32},{8,40},{16,48},{24,56},{32,0},{40,8},{48,16},{56,24},{64,96... | collective-permute-start | bytes 442376 | tf_op jit(solution)/shard_map/ppermute | solution.py:262
  50.2 22.5 %collective-permute-start.7 = (bf16[96,768]{1,0:T(8,128)(2,1)S(1)}, bf16[96,768]{1,0:T(8,128)(2,1)S(1)}, u32[]{:S(2)}, u32[]{:S(2)}) collective-permute-start(bf16[96,768]{1,0:T(8,128)(2,1)S(1)} %get-tuple-element.22.refs_6_), channel_id=1, source_target_pairs={{0,16},{8,24},{16,0},{24,8},{32,48},{40,56},{48,32},{56,40},{64,80... | collective-permute-start | bytes 442376 | tf_op jit(solution)/shard_map/ppermute | solution.py:262
  51.8 20.9 %collective-permute-start.6 = (bf16[96,768]{1,0:T(8,128)(2,1)S(1)}, bf16[96,768]{1,0:T(8,128)(2,1)S(1)}, u32[]{:S(2)}, u32[]{:S(2)}) collective-permute-start(bf16[96,768]{1,0:T(8,128)(2,1)S(1)} %get-tuple-element.21), channel_id=1, source_target_pairs={{0,48},{8,56},{16,32},{24,40},{32,16},{40,24},{48,0},{56,8},{64,11... | collective-permute-start | bytes 442376 | tf_op jit(solution)/shard_map/ppermute | solution.py:262
  55.4 17.3 %collective-permute-start.13 = (bf16[96,768]{1,0:T(8,128)(2,1)S(1)}, bf16[96,768]{1,0:T(8,128)(2,1)S(1)}, u32[]{:S(2)}, u32[]{:S(2)}) collective-permute-start(bf16[96,768]{1,0:T(8,128)(2,1)S(1)} %get-tuple-element.24), channel_id=1, source_target_pairs={{0,32},{8,40},{16,48},{24,56},{32,0},{40,8},{48,16},{56,24},{64,96... | collective-permute-start | bytes 442376 | tf_op jit(solution)/shard_map/ppermute | solution.py:262
  56.7 22.3 %collective-permute-start.14 = (bf16[96,768]{1,0:T(8,128)(2,1)S(1)}, bf16[96,768]{1,0:T(8,128)(2,1)S(1)}, u32[]{:S(2)}, u32[]{:S(2)}) collective-permute-start(bf16[96,768]{1,0:T(8,128)(2,1)S(1)} %get-tuple-element.25), channel_id=1, source_target_pairs={{0,48},{8,56},{16,32},{24,40},{32,16},{40,24},{48,0},{56,8},{64,11... | collective-permute-start | bytes 442376 | tf_op jit(solution)/shard_map/ppermute | solution.py:262
  59.0 20.0 %collective-permute-start.15 = (bf16[96,768]{1,0:T(8,128)(2,1)S(1)}, bf16[96,768]{1,0:T(8,128)(2,1)S(1)}, u32[]{:S(2)}, u32[]{:S(2)}) collective-permute-start(bf16[96,768]{1,0:T(8,128)(2,1)S(1)} %get-tuple-element.26), channel_id=1, source_target_pairs={{0,16},{8,24},{16,0},{24,8},{32,48},{40,56},{48,32},{56,40},{64,80... | collective-permute-start | bytes 442376 | tf_op jit(solution)/shard_map/ppermute | solution.py:262

commit v5 on v4

--- a/solution.py
+++ b/solution.py
@@ -53,19 +53,19 @@
     return rows == cols, (rows < width) & (cols < width)
 
 
-def place_kernel(in_ref, out_ref):
+def mark_kernel(in_ref, out_ref):
     for k in range(in_ref.shape[0]):
         out_ref[k] = in_ref[k]
 
 
-def place_call(pos):
-    return pl.pallas_call(
-        place_kernel,
+def mark_call(pos):
+    return pl.pallas_call(
+        mark_kernel,
         in_specs=[SMEM],
         out_specs=SMEM,
         out_shape=jax.ShapeDtypeStruct(pos.shape, pos.dtype),
         cost_estimate=cost(10**10, 10**7),
-        name="place",
+        name="mark",
         compiler_params=grant(1),
     )(pos)
 
@@ -118,6 +118,26 @@
     )(widths, pos, systems, upper)
 
 
+def pick_kernel(last_ref, following_ref, *out_refs):
+    for chunk in range(2):
+        out_refs[2 * chunk][...] = last_ref[0, :, :, chunk]
+        out_refs[2 * chunk + 1][...] = following_ref[1, :, :, chunk]
+
+
+def pick_call(last, following):
+    _, spots, sides, _, rows, depth = last.shape
+    shape = jax.ShapeDtypeStruct((spots, sides, rows, depth), BF16)
+    return pl.pallas_call(
+        pick_kernel,
+        in_specs=[VMEM] * 2,
+        out_specs=[VMEM] * 4,
+        out_shape=[shape] * 4,
+        cost_estimate=cost(1000, 4000000),
+        name="pick",
+        compiler_params=grant(4),
+    )(last, following)
+
+
 def scale_kernel(pos_ref, fill_ref, xh_ref, xl_ref, part_ref, upper_ref, out_ref):
     members, order, cols = part_ref.shape
     pieces = order // BLOCK
@@ -157,8 +177,6 @@
 
     def update_kernel(pos_ref, fill_ref, front_ref, *refs):
         own_ref, next_ref, last_ref, *far_refs, scaled_ref, _, out_ref, wide = refs
-        if len(far_refs) == 1:
-            far_refs = [far_refs[0].at[s] for s in range(members)]
         side = 1 - pos_ref[0] if flip else pos_ref[0]
         strip = 2 * rows
         base = pos_ref[2] * (spots * 2 * strip) + side * strip + chunk * rows
@@ -167,8 +185,9 @@
                 for j in range(rows // SUB):
                     spot = lax.div(base + d * 2 * strip + j * SUB, BLOCK)
                     used = fill_ref[s, spot] != 0
-                    spans = (d, side, slice(j * SUB, (j + 1) * SUB))
-                    tiles = (own_ref[s, *spans], next_ref[s, *spans], far_refs[s][*spans], last_ref[s, *spans])
+                    span = slice(j * SUB, (j + 1) * SUB)
+                    whole = (s, d, side, chunk, span)
+                    tiles = (own_ref[whole], next_ref[whole], far_refs[s][d, side, span], last_ref[whole])
                     for k, tile in enumerate(tiles):
                         begin = s * order + k * BLOCK
                         top = d * rows + j * SUB
@@ -246,7 +265,7 @@
         layer & 1,
         jnp.where(which == 1, col_index, jnp.where(which == 2, row_index, layer >> 1 & 3)),
     ).astype(jnp.int32)
-    pos = place_call(pos)
+    pos = mark_call(pos)
     upper, fill, width_vec = upper_panels[0], block_fill[0], widths[0]
     row_count, cols = front_copies.shape[1:]
     members = upper.shape[0]
@@ -262,15 +281,15 @@
         return lax.ppermute(block, "layer", [(i, i ^ flip) for i in range(layers)])
 
     other_upper = lax.ppermute(upper, "row", [(0, 1), (1, 0)])
+    flat = lower_panels[0]
+    following = shift(flat, -1).reshape(lower.shape)
+    last = shift(flat, 1).reshape(lower.shape)
+    picked = pick_call(last, following)
     lowers = []
     for chunk in range(2):
-        own = lower[:, :, :, chunk]
-        following, last = shift(own, -1), shift(own, 1)
-        if chunk == 0:
-            far = (shift(own, 2),)
-        else:
-            far = (shift(last[0], 1), shift(following[1], -1))
-        lowers.append((own, following, last, *far))
+        right = shift(picked[2 * chunk], 1)
+        left = shift(picked[2 * chunk + 1], -1)
+        lowers.append((lower, following, last, right, left))
     xh, xl, part = inverse_call(width_vec, pos, diag_blocks[0], upper)
     scaled = scale_call(pos, fill, xh, xl, part, other_upper)
     finals = []

time: 80.4 us -> 78.8 us (0.980)
  the two profiles are of different devices: /device:TPU:79 before, /device:TPU:73 now
where the time goes in v5:
time: 78.8 us; the launch traced here: 78.7 us
  waiting for transfers between devices  37.2 us (47%)
  starting transfers between devices  21.6 us (27%)
  Pallas kernels  19.6 us (25%)
    ppermute x6, waiting for transfers between devices, shift(): lax.ppermute(block, 'col', [(i, (i + step) % col_devices) for i in range(...  19.8 us
    ppermute x8, waiting for transfers between devices, across(): return lax.ppermute(block, 'layer', [(i, i ^ flip) for i in range(layers)])  17.3 us
    ppermute x8, starting transfers between devices, across(): return lax.ppermute(block, 'layer', [(i, i ^ flip) for i in range(layers)])  12.9 us
    pallas_call x1, Pallas kernels, inverse_call(): pl.pallas_call(inverse_kernel, in_specs=[SMEM, SMEM, VMEM, VMEM], out_spe...  7.83 us
    ppermute x6, starting transfers between devices, shift(): lax.ppermute(block, 'col', [(i, (i + step) % col_devices) for i in range(...  6.69 us
    pallas_call x4, Pallas kernels, update_call(): pl.pallas_call(update_kernel, in_specs=[SMEM, SMEM] + [VMEM] * (len(lower...  5.85 us
    ppermute x1, starting transfers between devices, on_device(): other_upper = lax.ppermute(upper, 'row', [(0, 1), (1, 0)])  2.02 us
    pallas_call x2, Pallas kernels, round_call(): pl.pallas_call(round_kernel, in_specs=[SMEM, VMEM, VMEM], out_specs=[VMEM...  1.91 us
  transfers between devices with their start and end apart: 15, of which 6 were waited for; matrix products, arithmetic and copies ran while one was open for 0% of the time, Pallas kernels for 19%

profile of v5, /device:TPU:73, one launch (start us, length us, event | category | flops | bytes accessed | tf_op | source)
XLA Modules:
  0.0 78.7 jit_solution(17915062259578751906)
XLA Ops:
  0.0 2.5 %collective-permute-start = (bf16[2,1536,128]{2,1,0:T(8,128)(2,1)}, bf16[2,1536,128]{2,1,0:T(8,128)(2,1)S(1)}, u32[]{:S(2)}, u32[]{:S(2)}) collective-permute-start(bf16[2,1536,128]{2,1,0:T(8,128)(2,1)} %bitcast.23), channel_id=1, source_target_pairs={{0,6},{2,0},{4,2},{6,4},{1,7},{3,1},{5,3},{7,5},{8,14},{10,8},{12,... | collective-permute-start | bytes 2359304 | tf_op jit(solution)/shard_map/ppermute | solution.py:278
  2.5 0.0 collective-permute-start.1
  2.5 2.0 %collective-permute-start.4 = (bf16[2,256,768]{2,1,0:T(8,128)(2,1)}, bf16[2,256,768]{2,1,0:T(8,128)(2,1)S(1)}, u32[]{:S(2)}, u32[]{:S(2)}) collective-permute-start(bf16[2,256,768]{2,1,0:T(8,128)(2,1)} %bitcast.35), channel_id=1, source_target_pairs={{0,1},{1,0},{2,3},{3,2},{4,5},{5,4},{6,7},{7,6},{8,9},{9,8},{10,11... | collective-permute-start | bytes 2359304 | tf_op jit(solution)/shard_map/ppermute | solution.py:283
  4.5 0.0 copy-start.5
  4.5 1.1 %mark.1.pos_ref = s32[4]{0:T(128)S(1)} custom-call(s32[4]{0:T(128)S(1)} %compare_select_fusion.2.in_ref), custom_call_target="tpu_custom_call" | custom-call | flops 10000000000 | bytes 10000000 | tf_op jit(solution)/shard_map/mark/pallas_call | solution.py:62
  5.7 13.4 %collective-permute-done = bf16[2,1536,128]{2,1,0:T(8,128)(2,1)S(1)} collective-permute-done((bf16[2,1536,128]{2,1,0:T(8,128)(2,1)}, bf16[2,1536,128]{2,1,0:T(8,128)(2,1)S(1)}, u32[]{:S(2)}, u32[]{:S(2)}) %collective-permute-start) | collective-permute-done | bytes 786464 | tf_op jit(solution)/shard_map/ppermute | solution.py:278
  19.0 3.0 %collective-permute-done.1 = bf16[2,1536,128]{2,1,0:T(8,128)(2,1)S(1)} collective-permute-done((bf16[2,1536,128]{2,1,0:T(8,128)(2,1)}, bf16[2,1536,128]{2,1,0:T(8,128)(2,1)S(1)}, u32[]{:S(2)}, u32[]{:S(2)}) %collective-permute-start.1) | collective-permute-done | bytes 786464 | tf_op jit(solution)/shard_map/ppermute | solution.py:278
  22.0 0.1 pick.1
  22.1 0.1 collective-permute-start.2
  22.2 2.7 %collective-permute-start.3 = (bf16[4,2,96,128]{3,2,1,0:T(8,128)(2,1)S(1)}, bf16[4,2,96,128]{3,2,1,0:T(8,128)(2,1)S(1)}, u32[]{:S(2)}, u32[]{:S(2)}) collective-permute-start(bf16[4,2,96,128]{3,2,1,0:T(8,128)(2,1)S(1)} %get-tuple-element.21), channel_id=1, source_target_pairs={{0,6},{2,0},{4,2},{6,4},{1,7},{3,1},{5,3},{7,5},{8,14},{10,8},{12,... | collective-permute-start | bytes 589832 | tf_op jit(solution)/shard_map/ppermute | solution.py:278
  24.9 0.0 copy-done.3
  24.9 0.0 copy-done.4
  24.9 7.8 %inverse.1 = (bf16[2,512,256]{2,1,0:T(8,128)(2,1)S(1)}, bf16[2,512,256]{2,1,0:T(8,128)(2,1)S(1)}, f32[2,512,768]{2,1,0:T(8,128)S(1)}) custom-call(s32[2]{0:T(128)S(1)} %bitcast.37, s32[4]{0:T(128)S(1)} %mark.1.pos_ref, f32[2,512,512]{2,1,0:T(8,128)S(1)} %bitcast.34, bf16[2,256,768]{2,1,0:T(8,128)(2,1)S(1)} %bitcast.36), custom_call_target="tpu_custom_call" | custom-call | flops 3758096384 | bytes 8000000 | tf_op jit(solution)/shard_map/inverse/pallas_call | solution.py:106
  32.7 0.0 collective-permute-done.4.upper_ref
  32.7 0.0 copy-start
  32.7 0.0 copy-start.1
  32.8 1.6 %scale_upper.1.refs_5_.refs_6_ = bf16[2,4,128,768]{3,2,1,0:T(8,128)(2,1)S(1)} custom-call(s32[4]{0:T(128)S(1)} %mark.1.pos_ref, s32[2,24]{1,0:T(2,128)S(1)} %bitcast.29, bf16[2,512,256]{2,1,0:T(8,128)(2,1)S(1)} %get-tuple-element.22.xh_ref, bf16[2,512,256]{2,1,0:T(8,128)(2,1)S(1)} %get-tuple-element.23.xl_ref, ...), custom_call_target="tpu_custom_call" | custom-call | flops 805306368 | bytes 6291456 | tf_op jit(solution)/shard_map/scale_upper/pallas_call | solution.py:162
  34.3 0.0 collective-permute-done.2.refs_3_
  34.3 0.0 collective-permute-done.3.refs_4_
  34.3 0.0 copy-done
  34.4 0.2 copy-done.1
  34.6 1.5 %shard_map.65 = bf16[4,96,768]{2,1,0:T(8,128)(2,1)S(1)} custom-call(s32[4]{0:T(128)S(1)} %mark.1.pos_ref, s32[2,24]{1,0:T(2,128)S(1)} %bitcast.30, bf16[4,2,2,96,768]{4,3,2,1,0:T(8,128)(2,1)S(1)} %bitcast.9, bf16[2,4,2,2,96,128]{5,4,3,2,1,0:T(8,128)(2,1)S(1)} %bitcast.25, bf16[2,4,2,2,96,128]{5,4,3,2,1,0:T(8,128)(2,1)S(1)} %bitcast.14, ...), custom_call_target="tpu_custom_call" | custom-call | flops 603979776 | bytes 4000000 | tf_op jit(solution)/shard_map/pallas_call | solution.py:201
  36.1 2.4 %collective-permute-start.5 = (bf16[4,96,768]{2,1,0:T(8,128)(2,1)S(1)}, bf16[4,96,768]{2,1,0:T(8,128)(2,1)S(1)}, u32[]{:S(2)}, u32[]{:S(2)}) collective-permute-start(bf16[4,96,768]{2,1,0:T(8,128)(2,1)S(1)} %shard_map.65), channel_id=1, source_target_pairs={{0,8},{8,0},{16,24},{24,16},{32,40},{40,32},{48,56},{56,48},{64,72... | collective-permute-start | bytes 1769480 | tf_op jit(solution)/shard_map/ppermute | solution.py:281
  38.5 0.0 collective-permute-start.10
  38.5 1.5 %collective-permute-start.9 = (bf16[4,2,96,128]{3,2,1,0:T(8,128)(2,1)S(1)}, bf16[4,2,96,128]{3,2,1,0:T(8,128)(2,1)S(1)}, u32[]{:S(2)}, u32[]{:S(2)}) collective-permute-start(bf16[4,2,96,128]{3,2,1,0:T(8,128)(2,1)S(1)} %get-tuple-element.29), channel_id=1, source_target_pairs={{0,2},{2,4},{4,6},{6,0},{1,3},{3,5},{5,7},{7,1},{8,10},{10,12},{12... | collective-permute-start | bytes 589832 | tf_op jit(solution)/shard_map/ppermute | solution.py:278
  40.0 1.4 %shard_map.64.kept_ref = f32[4,96,768]{2,1,0:T(8,128)S(1)} custom-call(s32[4]{0:T(128)S(1)} %mark.1.pos_ref, s32[2,24]{1,0:T(2,128)S(1)} %bitcast.31, bf16[4,2,2,96,768]{4,3,2,1,0:T(8,128)(2,1)S(1)} %bitcast.10, bf16[2,4,2,2,96,128]{5,4,3,2,1,0:T(8,128)(2,1)S(1)} %bitcast.26, bf16[2,4,2,2,96,128]{5,4,3,2,1,0:T(8,128)(2,1)S(1)} %bitcast.15, ...), custom_call_target="tpu_custom_call" | custom-call | flops 603979776 | bytes 4000000 | tf_op jit(solution)/shard_map/pallas_call | solution.py:201
  41.4 0.0 collective-permute-done.5.got_ref
  41.4 1.0 %shard_map.66 = (f32[96,768]{1,0:T(8,128)S(1)}, bf16[96,768]{1,0:T(8,128)(2,1)S(1)}, bf16[96,768]{1,0:T(8,128)(2,1)S(1)}, bf16[96,768]{1,0:T(8,128)(2,1)S(1)}) custom-call(s32[4]{0:T(128)S(1)} %mark.1.pos_ref, f32[4,96,768]{2,1,0:T(8,128)S(1)} %shard_map.64.kept_ref, bf16[4,96,768]{2,1,0:T(8,128)(2,1)S(1)} %collective-permute-done.5.got_ref), custom_call_target="tpu_custom_call" | custom-call | flops 294912 | bytes 2949120 | tf_op jit(solution)/shard_map/pallas_call | solution.py:222
  42.4 2.3 %collective-permute-done.10.refs_4_ = bf16[4,2,96,128]{3,2,1,0:T(8,128)(2,1)S(1)} collective-permute-done((bf16[4,2,96,128]{3,2,1,0:T(8,128)(2,1)S(1)}, bf16[4,2,96,128]{3,2,1,0:T(8,128)(2,1)S(1)}, u32[]{:S(2)}, u32[]{:S(2)}) %collective-permute-start.10) | collective-permute-done | bytes 196640 | tf_op jit(solution)/shard_map/ppermute | solution.py:278
  44.7 1.1 %collective-permute-done.9.refs_3_ = bf16[4,2,96,128]{3,2,1,0:T(8,128)(2,1)S(1)} collective-permute-done((bf16[4,2,96,128]{3,2,1,0:T(8,128)(2,1)S(1)}, bf16[4,2,96,128]{3,2,1,0:T(8,128)(2,1)S(1)}, u32[]{:S(2)}, u32[]{:S(2)}) %collective-permute-start.9) | collective-permute-done | bytes 196640 | tf_op jit(solution)/shard_map/ppermute | solution.py:278
  45.8 1.5 %shard_map.68 = bf16[4,96,768]{2,1,0:T(8,128)(2,1)S(1)} custom-call(s32[4]{0:T(128)S(1)} %mark.1.pos_ref, s32[2,24]{1,0:T(2,128)S(1)} %bitcast.32, bf16[4,2,2,96,768]{4,3,2,1,0:T(8,128)(2,1)S(1)} %bitcast.11, bf16[2,4,2,2,96,128]{5,4,3,2,1,0:T(8,128)(2,1)S(1)} %bitcast.27, bf16[2,4,2,2,96,128]{5,4,3,2,1,0:T(8,128)(2,1)S(1)} %bitcast.16, ...), custom_call_target="tpu_custom_call" | custom-call | flops 603979776 | bytes 4000000 | tf_op jit(solution)/shard_map/pallas_call | solution.py:201
  47.4 1.3 %collective-permute-start.11 = (bf16[4,96,768]{2,1,0:T(8,128)(2,1)S(1)}, bf16[4,96,768]{2,1,0:T(8,128)(2,1)S(1)}, u32[]{:S(2)}, u32[]{:S(2)}) collective-permute-start(bf16[4,96,768]{2,1,0:T(8,128)(2,1)S(1)} %shard_map.68), channel_id=1, source_target_pairs={{0,8},{8,0},{16,24},{24,16},{32,40},{40,32},{48,56},{56,48},{64,72... | collective-permute-start | bytes 1769480 | tf_op jit(solution)/shard_map/ppermute | solution.py:281
  48.7 0.0 collective-permute-start.6
  48.7 1.6 %collective-permute-start.8 = (bf16[96,768]{1,0:T(8,128)(2,1)S(1)}, bf16[96,768]{1,0:T(8,128)(2,1)S(1)}, u32[]{:S(2)}, u32[]{:S(2)}) collective-permute-start(bf16[96,768]{1,0:T(8,128)(2,1)S(1)} %get-tuple-element.28.refs_6_), channel_id=1, source_target_pairs={{0,16},{8,24},{16,0},{24,8},{32,48},{40,56},{48,32},{56,40},{64,80... | collective-permute-start | bytes 442376 | tf_op jit(solution)/shard_map/ppermute | solution.py:281
  50.3 1.2 %collective-permute-start.7 = (bf16[96,768]{1,0:T(8,128)(2,1)S(1)}, bf16[96,768]{1,0:T(8,128)(2,1)S(1)}, u32[]{:S(2)}, u32[]{:S(2)}) collective-permute-start(bf16[96,768]{1,0:T(8,128)(2,1)S(1)} %get-tuple-element.27), channel_id=1, source_target_pairs={{0,48},{8,56},{16,32},{24,40},{32,16},{40,24},{48,0},{56,8},{64,11... | collective-permute-start | bytes 442376 | tf_op jit(solution)/shard_map/ppermute | solution.py:281
  51.5 1.4 %shard_map.67.kept_ref = f32[4,96,768]{2,1,0:T(8,128)S(1)} custom-call(s32[4]{0:T(128)S(1)} %mark.1.pos_ref, s32[2,24]{1,0:T(2,128)S(1)} %bitcast.33, bf16[4,2,2,96,768]{4,3,2,1,0:T(8,128)(2,1)S(1)} %bitcast.12, bf16[2,4,2,2,96,128]{5,4,3,2,1,0:T(8,128)(2,1)S(1)} %bitcast.28, bf16[2,4,2,2,96,128]{5,4,3,2,1,0:T(8,128)(2,1)S(1)} %bitcast.17, ...), custom_call_target="tpu_custom_call" | custom-call | flops 603979776 | bytes 4000000 | tf_op jit(solution)/shard_map/pallas_call | solution.py:201
  52.9 0.0 collective-permute-done.11.got_ref
  52.9 1.0 %shard_map.69 = (f32[96,768]{1,0:T(8,128)S(1)}, bf16[96,768]{1,0:T(8,128)(2,1)S(1)}, bf16[96,768]{1,0:T(8,128)(2,1)S(1)}, bf16[96,768]{1,0:T(8,128)(2,1)S(1)}) custom-call(s32[4]{0:T(128)S(1)} %mark.1.pos_ref, f32[4,96,768]{2,1,0:T(8,128)S(1)} %shard_map.67.kept_ref, bf16[4,96,768]{2,1,0:T(8,128)(2,1)S(1)} %collective-permute-done.11.got_ref), custom_call_target="tpu_custom_call" | custom-call | flops 294912 | bytes 2949120 | tf_op jit(solution)/shard_map/pallas_call | solution.py:222
  53.9 1.3 %collective-permute-start.12 = (bf16[96,768]{1,0:T(8,128)(2,1)S(1)}, bf16[96,768]{1,0:T(8,128)(2,1)S(1)}, u32[]{:S(2)}, u32[]{:S(2)}) collective-permute-start(bf16[96,768]{1,0:T(8,128)(2,1)S(1)} %get-tuple-element.32), channel_id=1, source_target_pairs={{0,32},{8,40},{16,48},{24,56},{32,0},{40,8},{48,16},{56,24},{64,96... | collective-permute-start | bytes 442376 | tf_op jit(solution)/shard_map/ppermute | solution.py:281
  55.2 2.4 %collective-permute-start.13 = (bf16[96,768]{1,0:T(8,128)(2,1)S(1)}, bf16[96,768]{1,0:T(8,128)(2,1)S(1)}, u32[]{:S(2)}, u32[]{:S(2)}) collective-permute-start(bf16[96,768]{1,0:T(8,128)(2,1)S(1)} %get-tuple-element.33), channel_id=1, source_target_pairs={{0,48},{8,56},{16,32},{24,40},{32,16},{40,24},{48,0},{56,8},{64,11... | collective-permute-start | bytes 442376 | tf_op jit(solution)/shard_map/ppermute | solution.py:281
  57.5 0.0 collective-permute-done.6.refs_1_
  57.5 2.7 %collective-permute-start.14 = (bf16[96,768]{1,0:T(8,128)(2,1)S(1)}, bf16[96,768]{1,0:T(8,128)(2,1)S(1)}, u32[]{:S(2)}, u32[]{:S(2)}) collective-permute-start(bf16[96,768]{1,0:T(8,128)(2,1)S(1)} %get-tuple-element.34), channel_id=1, source_target_pairs={{0,16},{8,24},{16,0},{24,8},{32,48},{40,56},{48,32},{56,40},{64,80... | collective-permute-start | bytes 442376 | tf_op jit(solution)/shard_map/ppermute | solution.py:281
  60.2 11.0 %collective-permute-done.7.refs_2_ = bf16[96,768]{1,0:T(8,128)(2,1)S(1)} collective-permute-done((bf16[96,768]{1,0:T(8,128)(2,1)S(1)}, bf16[96,768]{1,0:T(8,128)(2,1)S(1)}, u32[]{:S(2)}, u32[]{:S(2)}) %collective-permute-start.7) | collective-permute-done | bytes 147488 | tf_op jit(solution)/shard_map/ppermute | solution.py:281
  71.2 0.0 collective-permute-done.8.refs_3_
  71.2 0.0 collective-permute-done.12.refs_5_
  71.2 6.3 %collective-permute-done.13.refs_6_ = bf16[96,768]{1,0:T(8,128)(2,1)S(1)} collective-permute-done((bf16[96,768]{1,0:T(8,128)(2,1)S(1)}, bf16[96,768]{1,0:T(8,128)(2,1)S(1)}, u32[]{:S(2)}, u32[]{:S(2)}) %collective-permute-start.13) | collective-permute-done | bytes 147488 | tf_op jit(solution)/shard_map/ppermute | solution.py:281
  77.5 0.0 collective-permute-done.14.refs_7_
  77.5 1.2 %final_sums.1 = f32[1,192,768]{2,1,0:T(8,128)} custom-call(f32[96,768]{1,0:T(8,128)S(1)} %get-tuple-element.25.refs_0_, bf16[96,768]{1,0:T(8,128)(2,1)S(1)} %collective-permute-done.6.refs_1_, bf16[96,768]{1,0:T(8,128)(2,1)S(1)} %collective-permute-done.7.refs_2_, bf16[96,768]{1,0:T(8,128)(2,1)S(1)} %collective-permute-done.8.refs_3_, ...), custom_call_target="tpu_custom_call" | custom-call | flops 589824 | bytes 1769472 | tf_op jit(solution)/shard_map/final_sums/pallas_call | solution.py:247
  (6 shorter events, 0.0 us)
Async XLA Ops:
  0.0 19.0 %collective-permute-start = (bf16[2,1536,128]{2,1,0:T(8,128)(2,1)}, bf16[2,1536,128]{2,1,0:T(8,128)(2,1)S(1)}, u32[]{:S(2)}, u32[]{:S(2)}) collective-permute-start(bf16[2,1536,128]{2,1,0:T(8,128)(2,1)} %bitcast.23), channel_id=1, source_target_pairs={{0,6},{2,0},{4,2},{6,4},{1,7},{3,1},{5,3},{7,5},{8,14},{10,8},{12,... | collective-permute-start | bytes 2359304 | tf_op jit(solution)/shard_map/ppermute | solution.py:278
  2.5 19.6 %collective-permute-start.1 = (bf16[2,1536,128]{2,1,0:T(8,128)(2,1)}, bf16[2,1536,128]{2,1,0:T(8,128)(2,1)S(1)}, u32[]{:S(2)}, u32[]{:S(2)}) collective-permute-start(bf16[2,1536,128]{2,1,0:T(8,128)(2,1)} %bitcast.24), channel_id=1, source_target_pairs={{0,2},{2,4},{4,6},{6,0},{1,3},{3,5},{5,7},{7,1},{8,10},{10,12},{12... | collective-permute-start | bytes 2359304 | tf_op jit(solution)/shard_map/ppermute | solution.py:278
  2.5 30.2 %collective-permute-start.4 = (bf16[2,256,768]{2,1,0:T(8,128)(2,1)}, bf16[2,256,768]{2,1,0:T(8,128)(2,1)S(1)}, u32[]{:S(2)}, u32[]{:S(2)}) collective-permute-start(bf16[2,256,768]{2,1,0:T(8,128)(2,1)} %bitcast.35), channel_id=1, source_target_pairs={{0,1},{1,0},{2,3},{3,2},{4,5},{5,4},{6,7},{7,6},{8,9},{9,8},{10,11... | collective-permute-start | bytes 2359304 | tf_op jit(solution)/shard_map/ppermute | solution.py:283
  4.5 20.4 %copy-start.3 = (f32[1,2,512,512]{3,2,1,0:T(8,128)S(1)}, f32[1,2,512,512]{3,2,1,0:T(8,128)}, u32[]{:S(2)}) copy-start(f32[1,2,512,512]{3,2,1,0:T(8,128)} %param.9) | copy-start | bytes 6291460
  4.5 20.4 %copy-start.4 = (bf16[1,2,256,768]{3,2,1,0:T(8,128)(2,1)S(1)}, bf16[1,2,256,768]{3,2,1,0:T(8,128)(2,1)}, u32[]{:S(2)}) copy-start(bf16[1,2,256,768]{3,2,1,0:T(8,128)(2,1)} %param.8) | copy-start | bytes 2359300
  4.5 20.4 %copy-start.5 = (s32[1,2]{1,0:T(1,128)S(1)}, s32[1,2]{1,0:T(1,128)}, u32[]{:S(2)}) copy-start(s32[1,2]{1,0:T(1,128)} %param.11) | copy-start | bytes 28
  22.1 12.2 %collective-permute-start.2 = (bf16[4,2,96,128]{3,2,1,0:T(8,128)(2,1)S(1)}, bf16[4,2,96,128]{3,2,1,0:T(8,128)(2,1)S(1)}, u32[]{:S(2)}, u32[]{:S(2)}) collective-permute-start(bf16[4,2,96,128]{3,2,1,0:T(8,128)(2,1)S(1)} %get-tuple-element.20), channel_id=1, source_target_pairs={{0,2},{2,4},{4,6},{6,0},{1,3},{3,5},{5,7},{7,1},{8,10},{10,12},{12... | collective-permute-start | bytes 589832 | tf_op jit(solution)/shard_map/ppermute | solution.py:278
  22.2 12.1 %collective-permute-start.3 = (bf16[4,2,96,128]{3,2,1,0:T(8,128)(2,1)S(1)}, bf16[4,2,96,128]{3,2,1,0:T(8,128)(2,1)S(1)}, u32[]{:S(2)}, u32[]{:S(2)}) collective-permute-start(bf16[4,2,96,128]{3,2,1,0:T(8,128)(2,1)S(1)} %get-tuple-element.21), channel_id=1, source_target_pairs={{0,6},{2,0},{4,2},{6,4},{1,7},{3,1},{5,3},{7,5},{8,14},{10,8},{12,... | collective-permute-start | bytes 589832 | tf_op jit(solution)/shard_map/ppermute | solution.py:278
  24.9 7.9 %copy-start.2 = (s32[1,2,24]{2,1,0:T(2,128)S(1)}, s32[1,2,24]{2,1,0:T(2,128)}, u32[]{:S(2)}) copy-start(s32[1,2,24]{2,1,0:T(2,128)} %param.10) | copy-start | bytes 580
  32.7 1.7 %copy-start = (bf16[1,1536,768]{2,1,0:T(8,128)(2,1)S(1)}, bf16[1,1536,768]{2,1,0:T(8,128)(2,1)}, u32[]{:S(2)}) copy-start(bf16[1,1536,768]{2,1,0:T(8,128)(2,1)} %param.6) | copy-start | bytes 7077892
  32.7 1.8 %copy-start.1 = (bf16[1,2,1536,128]{3,2,1,0:T(8,128)(2,1)S(1)}, bf16[1,2,1536,128]{3,2,1,0:T(8,128)(2,1)}, u32[]{:S(2)}) copy-start(bf16[1,2,1536,128]{3,2,1,0:T(8,128)(2,1)} %param.7) | copy-start | bytes 2359300
  36.1 5.3 %collective-permute-start.5 = (bf16[4,96,768]{2,1,0:T(8,128)(2,1)S(1)}, bf16[4,96,768]{2,1,0:T(8,128)(2,1)S(1)}, u32[]{:S(2)}, u32[]{:S(2)}) collective-permute-start(bf16[4,96,768]{2,1,0:T(8,128)(2,1)S(1)} %shard_map.65), channel_id=1, source_target_pairs={{0,8},{8,0},{16,24},{24,16},{32,40},{40,32},{48,56},{56,48},{64,72... | collective-permute-start | bytes 1769480 | tf_op jit(solution)/shard_map/ppermute | solution.py:281
  38.5 6.2 %collective-permute-start.10 = (bf16[4,2,96,128]{3,2,1,0:T(8,128)(2,1)S(1)}, bf16[4,2,96,128]{3,2,1,0:T(8,128)(2,1)S(1)}, u32[]{:S(2)}, u32[]{:S(2)}) collective-permute-start(bf16[4,2,96,128]{3,2,1,0:T(8,128)(2,1)S(1)} %get-tuple-element.30), channel_id=1, source_target_pairs={{0,6},{2,0},{4,2},{6,4},{1,7},{3,1},{5,3},{7,5},{8,14},{10,8},{12,... | collective-permute-start | bytes 589832 | tf_op jit(solution)/shard_map/ppermute | solution.py:278
  38.5 7.3 %collective-permute-start.9 = (bf16[4,2,96,128]{3,2,1,0:T(8,128)(2,1)S(1)}, bf16[4,2,96,128]{3,2,1,0:T(8,128)(2,1)S(1)}, u32[]{:S(2)}, u32[]{:S(2)}) collective-permute-start(bf16[4,2,96,128]{3,2,1,0:T(8,128)(2,1)S(1)} %get-tuple-element.29), channel_id=1, source_target_pairs={{0,2},{2,4},{4,6},{6,0},{1,3},{3,5},{5,7},{7,1},{8,10},{10,12},{12... | collective-permute-start | bytes 589832 | tf_op jit(solution)/shard_map/ppermute | solution.py:278
  47.4 5.6 %collective-permute-start.11 = (bf16[4,96,768]{2,1,0:T(8,128)(2,1)S(1)}, bf16[4,96,768]{2,1,0:T(8,128)(2,1)S(1)}, u32[]{:S(2)}, u32[]{:S(2)}) collective-permute-start(bf16[4,96,768]{2,1,0:T(8,128)(2,1)S(1)} %shard_map.68), channel_id=1, source_target_pairs={{0,8},{8,0},{16,24},{24,16},{32,40},{40,32},{48,56},{56,48},{64,72... | collective-permute-start | bytes 1769480 | tf_op jit(solution)/shard_map/ppermute | solution.py:281
  48.7 8.9 %collective-permute-start.6 = (bf16[96,768]{1,0:T(8,128)(2,1)S(1)}, bf16[96,768]{1,0:T(8,128)(2,1)S(1)}, u32[]{:S(2)}, u32[]{:S(2)}) collective-permute-start(bf16[96,768]{1,0:T(8,128)(2,1)S(1)} %get-tuple-element.26), channel_id=1, source_target_pairs={{0,32},{8,40},{16,48},{24,56},{32,0},{40,8},{48,16},{56,24},{64,96... | collective-permute-start | bytes 442376 | tf_op jit(solution)/shard_map/ppermute | solution.py:281
  48.7 22.5 %collective-permute-start.8 = (bf16[96,768]{1,0:T(8,128)(2,1)S(1)}, bf16[96,768]{1,0:T(8,128)(2,1)S(1)}, u32[]{:S(2)}, u32[]{:S(2)}) collective-permute-start(bf16[96,768]{1,0:T(8,128)(2,1)S(1)} %get-tuple-element.28.refs_6_), channel_id=1, source_target_pairs={{0,16},{8,24},{16,0},{24,8},{32,48},{40,56},{48,32},{56,40},{64,80... | collective-permute-start | bytes 442376 | tf_op jit(solution)/shard_map/ppermute | solution.py:281
  50.3 20.9 %collective-permute-start.7 = (bf16[96,768]{1,0:T(8,128)(2,1)S(1)}, bf16[96,768]{1,0:T(8,128)(2,1)S(1)}, u32[]{:S(2)}, u32[]{:S(2)}) collective-permute-start(bf16[96,768]{1,0:T(8,128)(2,1)S(1)} %get-tuple-element.27), channel_id=1, source_target_pairs={{0,48},{8,56},{16,32},{24,40},{32,16},{40,24},{48,0},{56,8},{64,11... | collective-permute-start | bytes 442376 | tf_op jit(solution)/shard_map/ppermute | solution.py:281
  53.9 17.3 %collective-permute-start.12 = (bf16[96,768]{1,0:T(8,128)(2,1)S(1)}, bf16[96,768]{1,0:T(8,128)(2,1)S(1)}, u32[]{:S(2)}, u32[]{:S(2)}) collective-permute-start(bf16[96,768]{1,0:T(8,128)(2,1)S(1)} %get-tuple-element.32), channel_id=1, source_target_pairs={{0,32},{8,40},{16,48},{24,56},{32,0},{40,8},{48,16},{56,24},{64,96... | collective-permute-start | bytes 442376 | tf_op jit(solution)/shard_map/ppermute | solution.py:281
  55.2 22.3 %collective-permute-start.13 = (bf16[96,768]{1,0:T(8,128)(2,1)S(1)}, bf16[96,768]{1,0:T(8,128)(2,1)S(1)}, u32[]{:S(2)}, u32[]{:S(2)}) collective-permute-start(bf16[96,768]{1,0:T(8,128)(2,1)S(1)} %get-tuple-element.33), channel_id=1, source_target_pairs={{0,48},{8,56},{16,32},{24,40},{32,16},{40,24},{48,0},{56,8},{64,11... | collective-permute-start | bytes 442376 | tf_op jit(solution)/shard_map/ppermute | solution.py:281
  57.5 20.0 %collective-permute-start.14 = (bf16[96,768]{1,0:T(8,128)(2,1)S(1)}, bf16[96,768]{1,0:T(8,128)(2,1)S(1)}, u32[]{:S(2)}, u32[]{:S(2)}) collective-permute-start(bf16[96,768]{1,0:T(8,128)(2,1)S(1)} %get-tuple-element.34), channel_id=1, source_target_pairs={{0,16},{8,24},{16,0},{24,8},{32,48},{40,56},{48,32},{56,40},{64,80... | collective-permute-start | bytes 442376 | tf_op jit(solution)/shard_map/ppermute | solution.py:281

commit v6 on v4

--- a/solution.py
+++ b/solution.py
@@ -157,8 +157,6 @@
 
     def update_kernel(pos_ref, fill_ref, front_ref, *refs):
         own_ref, next_ref, last_ref, *far_refs, scaled_ref, _, out_ref, wide = refs
-        if len(far_refs) == 1:
-            far_refs = [far_refs[0].at[s] for s in range(members)]
         side = 1 - pos_ref[0] if flip else pos_ref[0]
         strip = 2 * rows
         base = pos_ref[2] * (spots * 2 * strip) + side * strip + chunk * rows
@@ -266,11 +264,8 @@
     for chunk in range(2):
         own = lower[:, :, :, chunk]
         following, last = shift(own, -1), shift(own, 1)
-        if chunk == 0:
-            far = (shift(own, 2),)
-        else:
-            far = (shift(last[0], 1), shift(following[1], -1))
-        lowers.append((own, following, last, *far))
+        right, left = shift(last[0], 1), shift(following[1], -1)
+        lowers.append((own, following, last, right, left))
     xh, xl, part = inverse_call(width_vec, pos, diag_blocks[0], upper)
     scaled = scale_call(pos, fill, xh, xl, part, other_upper)
     finals = []

time: 80.4 us -> 72.2 us (0.90)
  the two profiles are of different devices: /device:TPU:79 before, /device:TPU:87 now
where the time goes in v6:
time: 72.2 us; the launch traced here: 72.1 us
  waiting for transfers between devices  30.4 us (42%)
  starting transfers between devices  20.8 us (29%)
  Pallas kernels  19.5 us (27%)
  local copies, waits for them, and re-layouts  1.24 us (2%)
    ppermute x8, waiting for transfers between devices, across(): return lax.ppermute(block, 'layer', [(i, i ^ flip) for i in range(layers)])  17.1 us
    ppermute x8, starting transfers between devices, across(): return lax.ppermute(block, 'layer', [(i, i ^ flip) for i in range(layers)])  13.1 us
    ppermute x8, waiting for transfers between devices, shift(): lax.ppermute(block, 'col', [(i, (i + step) % col_devices) for i in range(...  11 us
    pallas_call x1, Pallas kernels, inverse_call(): pl.pallas_call(inverse_kernel, in_specs=[SMEM, SMEM, VMEM, VMEM], out_spe...  7.83 us
    ppermute x8, starting transfers between devices, shift(): lax.ppermute(block, 'col', [(i, (i + step) % col_devices) for i in range(...  7.59 us
    pallas_call x4, Pallas kernels, update_call(): pl.pallas_call(update_kernel, in_specs=[SMEM, SMEM] + [VMEM] * (len(lower...  5.85 us
    ppermute x1, waiting for transfers between devices, on_device(): other_upper = lax.ppermute(upper, 'row', [(0, 1), (1, 0)])  2.26 us
    pallas_call x2, Pallas kernels, round_call(): pl.pallas_call(round_kernel, in_specs=[SMEM, VMEM, VMEM], out_specs=[VMEM...  1.9 us
  transfers between devices with their start and end apart: 17, of which 7 were waited for; matrix products, arithmetic and copies ran while one was open for 0% of the time, Pallas kernels for 23%

profile of v6, /device:TPU:87, one launch (start us, length us, event | category | flops | bytes accessed | tf_op | source)
XLA Modules:
  0.0 72.1 jit_solution(12893148274346566957)
XLA Ops:
  0.0 1.2 %slice_bitcast_fusion = (bf16[2,4,2,96,128]{4,3,2,1,0:T(8,128)(2,1)S(1)}, bf16[2,4,2,96,128]{4,3,2,1,0:T(8,128)(2,1)S(1)}) fusion(bf16[2,4,2,2,96,128]{5,4,3,2,1,0:T(8,128)(2,1)} %bitcast.35), kind=kLoop, calls=%fused_computation | loop fusion | bytes 1572864 | tf_op jit(solution)/shard_map/squeeze | solution.py:265
  1.2 0.3 collective-permute-start.1
  1.5 1.3 %collective-permute-start = (bf16[2,4,2,96,128]{4,3,2,1,0:T(8,128)(2,1)S(1)}, bf16[2,4,2,96,128]{4,3,2,1,0:T(8,128)(2,1)S(1)}, u32[]{:S(2)}, u32[]{:S(2)}) collective-permute-start(bf16[2,4,2,96,128]{4,3,2,1,0:T(8,128)(2,1)S(1)} %get-tuple-element.28.refs_0_), channel_id=1, source_target_pairs={{0,6},{2,0},{4,2},{6,4},{1,7},{3,1},{5,3},{7,5},{8,14},{10,8},{12,... | collective-permute-start | bytes 1179656 | tf_op jit(solution)/shard_map/ppermute | solution.py:257
  2.7 1.4 %collective-permute-start.10 = (bf16[2,4,2,96,128]{4,3,2,1,0:T(8,128)(2,1)S(1)}, bf16[2,4,2,96,128]{4,3,2,1,0:T(8,128)(2,1)S(1)}, u32[]{:S(2)}, u32[]{:S(2)}) collective-permute-start(bf16[2,4,2,96,128]{4,3,2,1,0:T(8,128)(2,1)S(1)} %get-tuple-element.27.refs_0_), channel_id=1, source_target_pairs={{0,2},{2,4},{4,6},{6,0},{1,3},{3,5},{5,7},{7,1},{8,10},{10,12},{12... | collective-permute-start | bytes 1179656 | tf_op jit(solution)/shard_map/ppermute | solution.py:257
  4.1 0.1 collective-permute-start.9
  4.2 0.1 collective-permute-start.4
  4.3 0.0 copy-start.4
  4.3 1.1 %place.1.pos_ref = s32[4]{0:T(128)S(1)} custom-call(s32[4]{0:T(128)S(1)} %compare_select_fusion.2.in_ref), custom_call_target="tpu_custom_call" | custom-call | flops 10000000000 | bytes 10000000 | tf_op jit(solution)/shard_map/place/pallas_call | solution.py:62
  5.4 5.8 %collective-permute-done.1.refs_2_ = bf16[2,4,2,96,128]{4,3,2,1,0:T(8,128)(2,1)S(1)} collective-permute-done((bf16[2,4,2,96,128]{4,3,2,1,0:T(8,128)(2,1)S(1)}, bf16[2,4,2,96,128]{4,3,2,1,0:T(8,128)(2,1)S(1)}, u32[]{:S(2)}, u32[]{:S(2)}) %collective-permute-start.1) | collective-permute-done | bytes 393248 | tf_op jit(solution)/shard_map/ppermute | solution.py:257
  11.3 1.5 %collective-permute-start.2 = (bf16[4,2,96,128]{3,2,1,0:T(8,128)(2,1)S(1)}, bf16[4,2,96,128]{3,2,1,0:T(8,128)(2,1)S(1)}, u32[]{:S(2)}, u32[]{:S(2)}) collective-permute-start(bf16[4,2,96,128]{3,2,1,0:T(8,128)(2,1)S(1)} %slice_bitcast_fusion.5), channel_id=1, source_target_pairs={{0,2},{2,4},{4,6},{6,0},{1,3},{3,5},{5,7},{7,1},{8,10},{10,12},{12... | collective-permute-start | bytes 589832 | tf_op jit(solution)/shard_map/ppermute | solution.py:257
  12.8 0.0 collective-permute-done.refs_1_
  12.8 0.3 collective-permute-start.3
  13.1 0.0 copy-done.3
  13.1 7.8 %inverse.1 = (bf16[2,512,256]{2,1,0:T(8,128)(2,1)S(1)}, bf16[2,512,256]{2,1,0:T(8,128)(2,1)S(1)}, f32[2,512,768]{2,1,0:T(8,128)S(1)}) custom-call(s32[2]{0:T(128)S(1)} %bitcast.34, s32[4]{0:T(128)S(1)} %place.1.pos_ref, f32[2,512,512]{2,1,0:T(8,128)S(1)} %bitcast.31, bf16[2,256,768]{2,1,0:T(8,128)(2,1)S(1)} %bitcast.33), custom_call_target="tpu_custom_call" | custom-call | flops 3758096384 | bytes 8000000 | tf_op jit(solution)/shard_map/inverse/pallas_call | solution.py:106
  20.9 2.3 %collective-permute-done.4.upper_ref = bf16[2,256,768]{2,1,0:T(8,128)(2,1)S(1)} collective-permute-done((bf16[2,256,768]{2,1,0:T(8,128)(2,1)}, bf16[2,256,768]{2,1,0:T(8,128)(2,1)S(1)}, u32[]{:S(2)}, u32[]{:S(2)}) %collective-permute-start.4) | collective-permute-done | bytes 786464 | tf_op jit(solution)/shard_map/ppermute | solution.py:262
  23.2 0.0 copy-done.1
  23.2 1.6 %scale_upper.1.refs_5_.refs_6_ = bf16[2,4,128,768]{3,2,1,0:T(8,128)(2,1)S(1)} custom-call(s32[4]{0:T(128)S(1)} %place.1.pos_ref, s32[2,24]{1,0:T(2,128)S(1)} %bitcast.26, bf16[2,512,256]{2,1,0:T(8,128)(2,1)S(1)} %get-tuple-element.16.xh_ref, bf16[2,512,256]{2,1,0:T(8,128)(2,1)S(1)} %get-tuple-element.17.xl_ref, ...), custom_call_target="tpu_custom_call" | custom-call | flops 805306368 | bytes 6291456 | tf_op jit(solution)/shard_map/scale_upper/pallas_call | solution.py:142
  24.8 0.0 collective-permute-done.2.refs_3_
  24.8 0.2 collective-permute-done.3.refs_4_
  25.0 1.5 %shard_map.65 = bf16[4,96,768]{2,1,0:T(8,128)(2,1)S(1)} custom-call(s32[4]{0:T(128)S(1)} %place.1.pos_ref, s32[2,24]{1,0:T(2,128)S(1)} %bitcast.27, bf16[4,2,2,96,768]{4,3,2,1,0:T(8,128)(2,1)S(1)} %bitcast.22, bf16[2,4,2,96,128]{4,3,2,1,0:T(8,128)(2,1)S(1)} %get-tuple-element.28.refs_0_, bf16[2,4,2,96,128]{4,3,2,1,0:T(8,128)(2,1)S(1)} %collective-permute-done.refs_1_, ...), custom_call_target="tpu_custom_call" | custom-call | flops 603979776 | bytes 4000000 | tf_op jit(solution)/shard_map/pallas_call | solution.py:180
  26.5 2.6 %collective-permute-start.5 = (bf16[4,96,768]{2,1,0:T(8,128)(2,1)S(1)}, bf16[4,96,768]{2,1,0:T(8,128)(2,1)S(1)}, u32[]{:S(2)}, u32[]{:S(2)}) collective-permute-start(bf16[4,96,768]{2,1,0:T(8,128)(2,1)S(1)} %shard_map.65), channel_id=1, source_target_pairs={{0,8},{8,0},{16,24},{24,16},{32,40},{40,32},{48,56},{56,48},{64,72... | collective-permute-start | bytes 1769480 | tf_op jit(solution)/shard_map/ppermute | solution.py:260
  29.1 0.0 collective-permute-done.10.refs_2_
  29.1 2.7 %collective-permute-start.11 = (bf16[4,2,96,128]{3,2,1,0:T(8,128)(2,1)S(1)}, bf16[4,2,96,128]{3,2,1,0:T(8,128)(2,1)S(1)}, u32[]{:S(2)}, u32[]{:S(2)}) collective-permute-start(bf16[4,2,96,128]{3,2,1,0:T(8,128)(2,1)S(1)} %slice_bitcast_fusion.3), channel_id=1, source_target_pairs={{0,2},{2,4},{4,6},{6,0},{1,3},{3,5},{5,7},{7,1},{8,10},{10,12},{12... | collective-permute-start | bytes 589832 | tf_op jit(solution)/shard_map/ppermute | solution.py:257
  31.8 0.0 collective-permute-done.9.refs_1_
  31.9 0.1 collective-permute-start.12
  32.0 1.4 %shard_map.64.kept_ref = f32[4,96,768]{2,1,0:T(8,128)S(1)} custom-call(s32[4]{0:T(128)S(1)} %place.1.pos_ref, s32[2,24]{1,0:T(2,128)S(1)} %bitcast.28, bf16[4,2,2,96,768]{4,3,2,1,0:T(8,128)(2,1)S(1)} %bitcast.23, bf16[2,4,2,96,128]{4,3,2,1,0:T(8,128)(2,1)S(1)} %get-tuple-element.28.refs_0_, bf16[2,4,2,96,128]{4,3,2,1,0:T(8,128)(2,1)S(1)} %collective-permute-done.refs_1_, ...), custom_call_target="tpu_custom_call" | custom-call | flops 603979776 | bytes 4000000 | tf_op jit(solution)/shard_map/pallas_call | solution.py:180
  33.4 0.0 collective-permute-done.5.got_ref
  33.4 1.0 %shard_map.66 = (f32[96,768]{1,0:T(8,128)S(1)}, bf16[96,768]{1,0:T(8,128)(2,1)S(1)}, bf16[96,768]{1,0:T(8,128)(2,1)S(1)}, bf16[96,768]{1,0:T(8,128)(2,1)S(1)}) custom-call(s32[4]{0:T(128)S(1)} %place.1.pos_ref, f32[4,96,768]{2,1,0:T(8,128)S(1)} %shard_map.64.kept_ref, bf16[4,96,768]{2,1,0:T(8,128)(2,1)S(1)} %collective-permute-done.5.got_ref), custom_call_target="tpu_custom_call" | custom-call | flops 294912 | bytes 2949120 | tf_op jit(solution)/shard_map/pallas_call | solution.py:201
  34.4 1.7 %collective-permute-done.11.refs_3_ = bf16[4,2,96,128]{3,2,1,0:T(8,128)(2,1)S(1)} collective-permute-done((bf16[4,2,96,128]{3,2,1,0:T(8,128)(2,1)S(1)}, bf16[4,2,96,128]{3,2,1,0:T(8,128)(2,1)S(1)}, u32[]{:S(2)}, u32[]{:S(2)}) %collective-permute-start.11) | collective-permute-done | bytes 196640 | tf_op jit(solution)/shard_map/ppermute | solution.py:257
  36.1 3.2 %collective-permute-done.12.refs_4_ = bf16[4,2,96,128]{3,2,1,0:T(8,128)(2,1)S(1)} collective-permute-done((bf16[4,2,96,128]{3,2,1,0:T(8,128)(2,1)S(1)}, bf16[4,2,96,128]{3,2,1,0:T(8,128)(2,1)S(1)}, u32[]{:S(2)}, u32[]{:S(2)}) %collective-permute-start.12) | collective-permute-done | bytes 196640 | tf_op jit(solution)/shard_map/ppermute | solution.py:257
  39.3 1.5 %shard_map.68 = bf16[4,96,768]{2,1,0:T(8,128)(2,1)S(1)} custom-call(s32[4]{0:T(128)S(1)} %place.1.pos_ref, s32[2,24]{1,0:T(2,128)S(1)} %bitcast.29, bf16[4,2,2,96,768]{4,3,2,1,0:T(8,128)(2,1)S(1)} %bitcast.24, bf16[2,4,2,96,128]{4,3,2,1,0:T(8,128)(2,1)S(1)} %get-tuple-element.27.refs_0_, bf16[2,4,2,96,128]{4,3,2,1,0:T(8,128)(2,1)S(1)} %collective-permute-done.9.refs_1_, ...), custom_call_target="tpu_custom_call" | custom-call | flops 603979776 | bytes 4000000 | tf_op jit(solution)/shard_map/pallas_call | solution.py:180
  40.8 1.3 %collective-permute-start.13 = (bf16[4,96,768]{2,1,0:T(8,128)(2,1)S(1)}, bf16[4,96,768]{2,1,0:T(8,128)(2,1)S(1)}, u32[]{:S(2)}, u32[]{:S(2)}) collective-permute-start(bf16[4,96,768]{2,1,0:T(8,128)(2,1)S(1)} %shard_map.68), channel_id=1, source_target_pairs={{0,8},{8,0},{16,24},{24,16},{32,40},{40,32},{48,56},{56,48},{64,72... | collective-permute-start | bytes 1769480 | tf_op jit(solution)/shard_map/ppermute | solution.py:260
  42.1 0.0 collective-permute-start.6
  42.1 1.6 %collective-permute-start.8 = (bf16[96,768]{1,0:T(8,128)(2,1)S(1)}, bf16[96,768]{1,0:T(8,128)(2,1)S(1)}, u32[]{:S(2)}, u32[]{:S(2)}) collective-permute-start(bf16[96,768]{1,0:T(8,128)(2,1)S(1)} %get-tuple-element.22.refs_6_), channel_id=1, source_target_pairs={{0,16},{8,24},{16,0},{24,8},{32,48},{40,56},{48,32},{56,40},{64,80... | collective-permute-start | bytes 442376 | tf_op jit(solution)/shard_map/ppermute | solution.py:260
  43.7 1.2 %collective-permute-start.7 = (bf16[96,768]{1,0:T(8,128)(2,1)S(1)}, bf16[96,768]{1,0:T(8,128)(2,1)S(1)}, u32[]{:S(2)}, u32[]{:S(2)}) collective-permute-start(bf16[96,768]{1,0:T(8,128)(2,1)S(1)} %get-tuple-element.21), channel_id=1, source_target_pairs={{0,48},{8,56},{16,32},{24,40},{32,16},{40,24},{48,0},{56,8},{64,11... | collective-permute-start | bytes 442376 | tf_op jit(solution)/shard_map/ppermute | solution.py:260
  44.9 1.4 %shard_map.67.kept_ref = f32[4,96,768]{2,1,0:T(8,128)S(1)} custom-call(s32[4]{0:T(128)S(1)} %place.1.pos_ref, s32[2,24]{1,0:T(2,128)S(1)} %bitcast.30, bf16[4,2,2,96,768]{4,3,2,1,0:T(8,128)(2,1)S(1)} %bitcast.25, bf16[2,4,2,96,128]{4,3,2,1,0:T(8,128)(2,1)S(1)} %get-tuple-element.27.refs_0_, bf16[2,4,2,96,128]{4,3,2,1,0:T(8,128)(2,1)S(1)} %collective-permute-done.9.refs_1_, ...), custom_call_target="tpu_custom_call" | custom-call | flops 603979776 | bytes 4000000 | tf_op jit(solution)/shard_map/pallas_call | solution.py:180
  46.3 0.0 collective-permute-done.13.got_ref
  46.3 1.0 %shard_map.69 = (f32[96,768]{1,0:T(8,128)S(1)}, bf16[96,768]{1,0:T(8,128)(2,1)S(1)}, bf16[96,768]{1,0:T(8,128)(2,1)S(1)}, bf16[96,768]{1,0:T(8,128)(2,1)S(1)}) custom-call(s32[4]{0:T(128)S(1)} %place.1.pos_ref, f32[4,96,768]{2,1,0:T(8,128)S(1)} %shard_map.67.kept_ref, bf16[4,96,768]{2,1,0:T(8,128)(2,1)S(1)} %collective-permute-done.13.got_ref), custom_call_target="tpu_custom_call" | custom-call | flops 294912 | bytes 2949120 | tf_op jit(solution)/shard_map/pallas_call | solution.py:201
  47.3 1.3 %collective-permute-start.14 = (bf16[96,768]{1,0:T(8,128)(2,1)S(1)}, bf16[96,768]{1,0:T(8,128)(2,1)S(1)}, u32[]{:S(2)}, u32[]{:S(2)}) collective-permute-start(bf16[96,768]{1,0:T(8,128)(2,1)S(1)} %get-tuple-element.24), channel_id=1, source_target_pairs={{0,32},{8,40},{16,48},{24,56},{32,0},{40,8},{48,16},{56,24},{64,96... | collective-permute-start | bytes 442376 | tf_op jit(solution)/shard_map/ppermute | solution.py:260
  48.6 2.4 %collective-permute-start.15 = (bf16[96,768]{1,0:T(8,128)(2,1)S(1)}, bf16[96,768]{1,0:T(8,128)(2,1)S(1)}, u32[]{:S(2)}, u32[]{:S(2)}) collective-permute-start(bf16[96,768]{1,0:T(8,128)(2,1)S(1)} %get-tuple-element.25), channel_id=1, source_target_pairs={{0,48},{8,56},{16,32},{24,40},{32,16},{40,24},{48,0},{56,8},{64,11... | collective-permute-start | bytes 442376 | tf_op jit(solution)/shard_map/ppermute | solution.py:260
  50.9 0.0 collective-permute-done.6.refs_1_
  50.9 2.8 %collective-permute-start.16 = (bf16[96,768]{1,0:T(8,128)(2,1)S(1)}, bf16[96,768]{1,0:T(8,128)(2,1)S(1)}, u32[]{:S(2)}, u32[]{:S(2)}) collective-permute-start(bf16[96,768]{1,0:T(8,128)(2,1)S(1)} %get-tuple-element.26), channel_id=1, source_target_pairs={{0,16},{8,24},{16,0},{24,8},{32,48},{40,56},{48,32},{56,40},{64,80... | collective-permute-start | bytes 442376 | tf_op jit(solution)/shard_map/ppermute | solution.py:260
  53.8 10.8 %collective-permute-done.7.refs_2_ = bf16[96,768]{1,0:T(8,128)(2,1)S(1)} collective-permute-done((bf16[96,768]{1,0:T(8,128)(2,1)S(1)}, bf16[96,768]{1,0:T(8,128)(2,1)S(1)}, u32[]{:S(2)}, u32[]{:S(2)}) %collective-permute-start.7) | collective-permute-done | bytes 147488 | tf_op jit(solution)/shard_map/ppermute | solution.py:260
  64.6 0.0 collective-permute-done.8.refs_3_
  64.6 0.0 collective-permute-done.14.refs_5_
  64.6 6.3 %collective-permute-done.15.refs_6_ = bf16[96,768]{1,0:T(8,128)(2,1)S(1)} collective-permute-done((bf16[96,768]{1,0:T(8,128)(2,1)S(1)}, bf16[96,768]{1,0:T(8,128)(2,1)S(1)}, u32[]{:S(2)}, u32[]{:S(2)}) %collective-permute-start.15) | collective-permute-done | bytes 147488 | tf_op jit(solution)/shard_map/ppermute | solution.py:260
  70.9 0.0 collective-permute-done.16.refs_7_
  70.9 1.2 %final_sums.1 = f32[1,192,768]{2,1,0:T(8,128)} custom-call(f32[96,768]{1,0:T(8,128)S(1)} %get-tuple-element.19.refs_0_, bf16[96,768]{1,0:T(8,128)(2,1)S(1)} %collective-permute-done.6.refs_1_, bf16[96,768]{1,0:T(8,128)(2,1)S(1)} %collective-permute-done.7.refs_2_, bf16[96,768]{1,0:T(8,128)(2,1)S(1)} %collective-permute-done.8.refs_3_, ...), custom_call_target="tpu_custom_call" | custom-call | flops 589824 | bytes 1769472 | tf_op jit(solution)/shard_map/final_sums/pallas_call | solution.py:226
  (12 shorter events, 0.1 us)
Async XLA Ops:
  1.2 10.1 %collective-permute-start.1 = (bf16[2,4,2,96,128]{4,3,2,1,0:T(8,128)(2,1)S(1)}, bf16[2,4,2,96,128]{4,3,2,1,0:T(8,128)(2,1)S(1)}, u32[]{:S(2)}, u32[]{:S(2)}) collective-permute-start(bf16[2,4,2,96,128]{4,3,2,1,0:T(8,128)(2,1)S(1)} %get-tuple-element.28.refs_0_), channel_id=1, source_target_pairs={{0,2},{2,4},{4,6},{6,0},{1,3},{3,5},{5,7},{7,1},{8,10},{10,12},{12... | collective-permute-start | bytes 1179656 | tf_op jit(solution)/shard_map/ppermute | solution.py:257
  1.5 11.3 %collective-permute-start = (bf16[2,4,2,96,128]{4,3,2,1,0:T(8,128)(2,1)S(1)}, bf16[2,4,2,96,128]{4,3,2,1,0:T(8,128)(2,1)S(1)}, u32[]{:S(2)}, u32[]{:S(2)}) collective-permute-start(bf16[2,4,2,96,128]{4,3,2,1,0:T(8,128)(2,1)S(1)} %get-tuple-element.28.refs_0_), channel_id=1, source_target_pairs={{0,6},{2,0},{4,2},{6,4},{1,7},{3,1},{5,3},{7,5},{8,14},{10,8},{12,... | collective-permute-start | bytes 1179656 | tf_op jit(solution)/shard_map/ppermute | solution.py:257
  2.7 26.4 %collective-permute-start.10 = (bf16[2,4,2,96,128]{4,3,2,1,0:T(8,128)(2,1)S(1)}, bf16[2,4,2,96,128]{4,3,2,1,0:T(8,128)(2,1)S(1)}, u32[]{:S(2)}, u32[]{:S(2)}) collective-permute-start(bf16[2,4,2,96,128]{4,3,2,1,0:T(8,128)(2,1)S(1)} %get-tuple-element.27.refs_0_), channel_id=1, source_target_pairs={{0,2},{2,4},{4,6},{6,0},{1,3},{3,5},{5,7},{7,1},{8,10},{10,12},{12... | collective-permute-start | bytes 1179656 | tf_op jit(solution)/shard_map/ppermute | solution.py:257
  4.1 27.7 %collective-permute-start.9 = (bf16[2,4,2,96,128]{4,3,2,1,0:T(8,128)(2,1)S(1)}, bf16[2,4,2,96,128]{4,3,2,1,0:T(8,128)(2,1)S(1)}, u32[]{:S(2)}, u32[]{:S(2)}) collective-permute-start(bf16[2,4,2,96,128]{4,3,2,1,0:T(8,128)(2,1)S(1)} %get-tuple-element.27.refs_0_), channel_id=1, source_target_pairs={{0,6},{2,0},{4,2},{6,4},{1,7},{3,1},{5,3},{7,5},{8,14},{10,8},{12,... | collective-permute-start | bytes 1179656 | tf_op jit(solution)/shard_map/ppermute | solution.py:257
  4.2 19.0 %collective-permute-start.4 = (bf16[2,256,768]{2,1,0:T(8,128)(2,1)}, bf16[2,256,768]{2,1,0:T(8,128)(2,1)S(1)}, u32[]{:S(2)}, u32[]{:S(2)}) collective-permute-start(bf16[2,256,768]{2,1,0:T(8,128)(2,1)} %bitcast.32), channel_id=1, source_target_pairs={{0,1},{1,0},{2,3},{3,2},{4,5},{5,4},{6,7},{7,6},{8,9},{9,8},{10,11... | collective-permute-start | bytes 2359304 | tf_op jit(solution)/shard_map/ppermute | solution.py:262
  4.2 8.8 %copy-start.2 = (f32[1,2,512,512]{3,2,1,0:T(8,128)S(1)}, f32[1,2,512,512]{3,2,1,0:T(8,128)}, u32[]{:S(2)}) copy-start(f32[1,2,512,512]{3,2,1,0:T(8,128)} %param.9) | copy-start | bytes 6291460
  4.3 8.8 %copy-start.3 = (bf16[1,2,256,768]{3,2,1,0:T(8,128)(2,1)S(1)}, bf16[1,2,256,768]{3,2,1,0:T(8,128)(2,1)}, u32[]{:S(2)}) copy-start(bf16[1,2,256,768]{3,2,1,0:T(8,128)(2,1)} %param.8) | copy-start | bytes 2359300
  4.3 8.8 %copy-start.4 = (s32[1,2]{1,0:T(1,128)S(1)}, s32[1,2]{1,0:T(1,128)}, u32[]{:S(2)}) copy-start(s32[1,2]{1,0:T(1,128)} %param.11) | copy-start | bytes 28
  11.3 13.5 %collective-permute-start.2 = (bf16[4,2,96,128]{3,2,1,0:T(8,128)(2,1)S(1)}, bf16[4,2,96,128]{3,2,1,0:T(8,128)(2,1)S(1)}, u32[]{:S(2)}, u32[]{:S(2)}) collective-permute-start(bf16[4,2,96,128]{3,2,1,0:T(8,128)(2,1)S(1)} %slice_bitcast_fusion.5), channel_id=1, source_target_pairs={{0,2},{2,4},{4,6},{6,0},{1,3},{3,5},{5,7},{7,1},{8,10},{10,12},{12... | collective-permute-start | bytes 589832 | tf_op jit(solution)/shard_map/ppermute | solution.py:257
  12.8 12.2 %collective-permute-start.3 = (bf16[4,2,96,128]{3,2,1,0:T(8,128)(2,1)S(1)}, bf16[4,2,96,128]{3,2,1,0:T(8,128)(2,1)S(1)}, u32[]{:S(2)}, u32[]{:S(2)}) collective-permute-start(bf16[4,2,96,128]{3,2,1,0:T(8,128)(2,1)S(1)} %slice_bitcast_fusion.4), channel_id=1, source_target_pairs={{0,6},{2,0},{4,2},{6,4},{1,7},{3,1},{5,3},{7,5},{8,14},{10,8},{12,... | collective-permute-start | bytes 589832 | tf_op jit(solution)/shard_map/ppermute | solution.py:257
  13.1 10.1 %copy-start.1 = (s32[1,2,24]{2,1,0:T(2,128)S(1)}, s32[1,2,24]{2,1,0:T(2,128)}, u32[]{:S(2)}) copy-start(s32[1,2,24]{2,1,0:T(2,128)} %param.10) | copy-start | bytes 580
  23.2 1.8 %copy-start = (bf16[1,1536,768]{2,1,0:T(8,128)(2,1)S(1)}, bf16[1,1536,768]{2,1,0:T(8,128)(2,1)}, u32[]{:S(2)}) copy-start(bf16[1,1536,768]{2,1,0:T(8,128)(2,1)} %param.6) | copy-start | bytes 7077892
  26.5 6.9 %collective-permute-start.5 = (bf16[4,96,768]{2,1,0:T(8,128)(2,1)S(1)}, bf16[4,96,768]{2,1,0:T(8,128)(2,1)S(1)}, u32[]{:S(2)}, u32[]{:S(2)}) collective-permute-start(bf16[4,96,768]{2,1,0:T(8,128)(2,1)S(1)} %shard_map.65), channel_id=1, source_target_pairs={{0,8},{8,0},{16,24},{24,16},{32,40},{40,32},{48,56},{56,48},{64,72... | collective-permute-start | bytes 1769480 | tf_op jit(solution)/shard_map/ppermute | solution.py:260
  29.1 6.9 %collective-permute-start.11 = (bf16[4,2,96,128]{3,2,1,0:T(8,128)(2,1)S(1)}, bf16[4,2,96,128]{3,2,1,0:T(8,128)(2,1)S(1)}, u32[]{:S(2)}, u32[]{:S(2)}) collective-permute-start(bf16[4,2,96,128]{3,2,1,0:T(8,128)(2,1)S(1)} %slice_bitcast_fusion.3), channel_id=1, source_target_pairs={{0,2},{2,4},{4,6},{6,0},{1,3},{3,5},{5,7},{7,1},{8,10},{10,12},{12... | collective-permute-start | bytes 589832 | tf_op jit(solution)/shard_map/ppermute | solution.py:257
  31.9 7.4 %collective-permute-start.12 = (bf16[4,2,96,128]{3,2,1,0:T(8,128)(2,1)S(1)}, bf16[4,2,96,128]{3,2,1,0:T(8,128)(2,1)S(1)}, u32[]{:S(2)}, u32[]{:S(2)}) collective-permute-start(bf16[4,2,96,128]{3,2,1,0:T(8,128)(2,1)S(1)} %slice_bitcast_fusion.2), channel_id=1, source_target_pairs={{0,6},{2,0},{4,2},{6,4},{1,7},{3,1},{5,3},{7,5},{8,14},{10,8},{12,... | collective-permute-start | bytes 589832 | tf_op jit(solution)/shard_map/ppermute | solution.py:257
  40.8 5.5 %collective-permute-start.13 = (bf16[4,96,768]{2,1,0:T(8,128)(2,1)S(1)}, bf16[4,96,768]{2,1,0:T(8,128)(2,1)S(1)}, u32[]{:S(2)}, u32[]{:S(2)}) collective-permute-start(bf16[4,96,768]{2,1,0:T(8,128)(2,1)S(1)} %shard_map.68), channel_id=1, source_target_pairs={{0,8},{8,0},{16,24},{24,16},{32,40},{40,32},{48,56},{56,48},{64,72... | collective-permute-start | bytes 1769480 | tf_op jit(solution)/shard_map/ppermute | solution.py:260
  42.1 8.9 %collective-permute-start.6 = (bf16[96,768]{1,0:T(8,128)(2,1)S(1)}, bf16[96,768]{1,0:T(8,128)(2,1)S(1)}, u32[]{:S(2)}, u32[]{:S(2)}) collective-permute-start(bf16[96,768]{1,0:T(8,128)(2,1)S(1)} %get-tuple-element.20), channel_id=1, source_target_pairs={{0,32},{8,40},{16,48},{24,56},{32,0},{40,8},{48,16},{56,24},{64,96... | collective-permute-start | bytes 442376 | tf_op jit(solution)/shard_map/ppermute | solution.py:260
  42.1 22.5 %collective-permute-start.8 = (bf16[96,768]{1,0:T(8,128)(2,1)S(1)}, bf16[96,768]{1,0:T(8,128)(2,1)S(1)}, u32[]{:S(2)}, u32[]{:S(2)}) collective-permute-start(bf16[96,768]{1,0:T(8,128)(2,1)S(1)} %get-tuple-element.22.refs_6_), channel_id=1, source_target_pairs={{0,16},{8,24},{16,0},{24,8},{32,48},{40,56},{48,32},{56,40},{64,80... | collective-permute-start | bytes 442376 | tf_op jit(solution)/shard_map/ppermute | solution.py:260
  43.7 20.9 %collective-permute-start.7 = (bf16[96,768]{1,0:T(8,128)(2,1)S(1)}, bf16[96,768]{1,0:T(8,128)(2,1)S(1)}, u32[]{:S(2)}, u32[]{:S(2)}) collective-permute-start(bf16[96,768]{1,0:T(8,128)(2,1)S(1)} %get-tuple-element.21), channel_id=1, source_target_pairs={{0,48},{8,56},{16,32},{24,40},{32,16},{40,24},{48,0},{56,8},{64,11... | collective-permute-start | bytes 442376 | tf_op jit(solution)/shard_map/ppermute | solution.py:260
  47.3 17.3 %collective-permute-start.14 = (bf16[96,768]{1,0:T(8,128)(2,1)S(1)}, bf16[96,768]{1,0:T(8,128)(2,1)S(1)}, u32[]{:S(2)}, u32[]{:S(2)}) collective-permute-start(bf16[96,768]{1,0:T(8,128)(2,1)S(1)} %get-tuple-element.24), channel_id=1, source_target_pairs={{0,32},{8,40},{16,48},{24,56},{32,0},{40,8},{48,16},{56,24},{64,96... | collective-permute-start | bytes 442376 | tf_op jit(solution)/shard_map/ppermute | solution.py:260
  48.6 22.3 %collective-permute-start.15 = (bf16[96,768]{1,0:T(8,128)(2,1)S(1)}, bf16[96,768]{1,0:T(8,128)(2,1)S(1)}, u32[]{:S(2)}, u32[]{:S(2)}) collective-permute-start(bf16[96,768]{1,0:T(8,128)(2,1)S(1)} %get-tuple-element.25), channel_id=1, source_target_pairs={{0,48},{8,56},{16,32},{24,40},{32,16},{40,24},{48,0},{56,8},{64,11... | collective-permute-start | bytes 442376 | tf_op jit(solution)/shard_map/ppermute | solution.py:260
  50.9 20.0 %collective-permute-start.16 = (bf16[96,768]{1,0:T(8,128)(2,1)S(1)}, bf16[96,768]{1,0:T(8,128)(2,1)S(1)}, u32[]{:S(2)}, u32[]{:S(2)}) collective-permute-start(bf16[96,768]{1,0:T(8,128)(2,1)S(1)} %get-tuple-element.26), channel_id=1, source_target_pairs={{0,16},{8,24},{16,0},{24,8},{32,48},{40,56},{48,32},{56,40},{64,80... | collective-permute-start | bytes 442376 | tf_op jit(solution)/shard_map/ppermute | solution.py:260

commit v7 on v6

--- a/solution.py
+++ b/solution.py
@@ -209,29 +209,48 @@
     )(pos, kept, got)
 
 
-def final_kernel(*refs):
-    out_ref = refs[-1]
-    per = (len(refs) - 1) // 2
-    rows = refs[0].shape[0]
-    for chunk in range(2):
-        group = refs[chunk * per : (chunk + 1) * per]
-        total = group[0][...]
-        for ref in group[1:]:
-            total = total + decode(ref[...])
-        out_ref[0, chunk * rows : (chunk + 1) * rows] = total
-
-
-def final_call(parts):
+def chunk_kernel(own_ref, *refs):
+    *got_refs, out_ref = refs
+    total = own_ref[...]
+    for ref in got_refs:
+        total = total + decode(ref[...])
+    out_ref[...] = total
+
+
+def chunk_call(parts):
     rows, cols = parts[0].shape
     return pl.pallas_call(
+        chunk_kernel,
+        in_specs=[VMEM] * len(parts),
+        out_specs=VMEM,
+        out_shape=jax.ShapeDtypeStruct((rows, cols), F32),
+        cost_estimate=cost(len(parts) * rows * cols, 3 * len(parts) * rows * cols),
+        name="chunk_sums",
+        compiler_params=grant(8),
+    )(*parts)
+
+
+def final_kernel(early_ref, own_ref, *refs):
+    *got_refs, out_ref = refs
+    rows = own_ref.shape[0]
+    out_ref[0, :rows] = early_ref[...]
+    total = own_ref[...]
+    for ref in got_refs:
+        total = total + decode(ref[...])
+    out_ref[0, rows:] = total
+
+
+def final_call(early, parts):
+    rows, cols = parts[0].shape
+    return pl.pallas_call(
         final_kernel,
-        in_specs=[VMEM] * len(parts),
+        in_specs=[VMEM] * (len(parts) + 1),
         out_specs=VMEM,
         out_shape=jax.ShapeDtypeStruct((1, 2 * rows, cols), F32),
         cost_estimate=cost(len(parts) * rows * cols, 3 * len(parts) * rows * cols),
         name="final_sums",
         compiler_params=grant(8),
-    )(*parts)
+    )(early, *parts)
 
 
 def on_device(front_copies, lower_panels, upper_panels, diag_blocks, block_fill, widths):
@@ -277,7 +296,8 @@
         own, one, two, three = round_call(pos, kept, got)
         after = one
         finals += [own, across(two, 4), across(three, 6), across(one, 2)]
-    return final_call(finals)
+    half = len(finals) // 2
+    return final_call(chunk_call(finals[:half]), finals[half:])
 
 
 def solution(mesh):

time: 72.2 us -> 72 us (level)
  transfers between devices with their start and end apart: 17 -> 17, of which waited for: 7 -> 7; matrix products, arithmetic and copies ran while one was open for 0% -> 0% of each run, Pallas kernels for 23% -> 24%
where the time goes in v7:
time: 72 us; the launch traced here: 71.9 us
  waiting for transfers between devices  30.2 us (42%)
  starting transfers between devices  20.8 us (29%)
  Pallas kernels  19.5 us (27%)
  local copies, waits for them, and re-layouts  1.24 us (2%)
    ppermute x8, waiting for transfers between devices, across(): return lax.ppermute(block, 'layer', [(i, i ^ flip) for i in range(layers)])  16.9 us
    ppermute x8, starting transfers between devices, across(): return lax.ppermute(block, 'layer', [(i, i ^ flip) for i in range(layers)])  13.1 us
    ppermute x8, waiting for transfers between devices, shift(): lax.ppermute(block, 'col', [(i, (i + step) % col_devices) for i in range(...  11 us
    pallas_call x1, Pallas kernels, inverse_call(): pl.pallas_call(inverse_kernel, in_specs=[SMEM, SMEM, VMEM, VMEM], out_spe...  7.83 us
    ppermute x8, starting transfers between devices, shift(): lax.ppermute(block, 'col', [(i, (i + step) % col_devices) for i in range(...  7.59 us
    pallas_call x4, Pallas kernels, update_call(): pl.pallas_call(update_kernel, in_specs=[SMEM, SMEM] + [VMEM] * (len(lower...  5.85 us
    ppermute x1, waiting for transfers between devices, on_device(): other_upper = lax.ppermute(upper, 'row', [(0, 1), (1, 0)])  2.26 us
    pallas_call x2, Pallas kernels, round_call(): pl.pallas_call(round_kernel, in_specs=[SMEM, VMEM, VMEM], out_specs=[VMEM...  1.9 us
  transfers between devices with their start and end apart: 17, of which 7 were waited for; matrix products, arithmetic and copies ran while one was open for 0% of the time, Pallas kernels for 24%

profile of v7, /device:TPU:87, one launch (start us, length us, event | category | flops | bytes accessed | tf_op | source)
XLA Modules:
  0.0 71.9 jit_solution(12420622388512025619)
XLA Ops:
  0.0 1.2 %slice_bitcast_fusion = (bf16[2,4,2,96,128]{4,3,2,1,0:T(8,128)(2,1)S(1)}, bf16[2,4,2,96,128]{4,3,2,1,0:T(8,128)(2,1)S(1)}) fusion(bf16[2,4,2,2,96,128]{5,4,3,2,1,0:T(8,128)(2,1)} %bitcast.35), kind=kLoop, calls=%fused_computation | loop fusion | bytes 1572864 | tf_op jit(solution)/shard_map/squeeze | solution.py:284
  1.2 0.3 collective-permute-start.1
  1.5 1.3 %collective-permute-start = (bf16[2,4,2,96,128]{4,3,2,1,0:T(8,128)(2,1)S(1)}, bf16[2,4,2,96,128]{4,3,2,1,0:T(8,128)(2,1)S(1)}, u32[]{:S(2)}, u32[]{:S(2)}) collective-permute-start(bf16[2,4,2,96,128]{4,3,2,1,0:T(8,128)(2,1)S(1)} %get-tuple-element.28.refs_0_), channel_id=1, source_target_pairs={{0,6},{2,0},{4,2},{6,4},{1,7},{3,1},{5,3},{7,5},{8,14},{10,8},{12,... | collective-permute-start | bytes 1179656 | tf_op jit(solution)/shard_map/ppermute | solution.py:276
  2.7 1.4 %collective-permute-start.10 = (bf16[2,4,2,96,128]{4,3,2,1,0:T(8,128)(2,1)S(1)}, bf16[2,4,2,96,128]{4,3,2,1,0:T(8,128)(2,1)S(1)}, u32[]{:S(2)}, u32[]{:S(2)}) collective-permute-start(bf16[2,4,2,96,128]{4,3,2,1,0:T(8,128)(2,1)S(1)} %get-tuple-element.27.refs_0_), channel_id=1, source_target_pairs={{0,2},{2,4},{4,6},{6,0},{1,3},{3,5},{5,7},{7,1},{8,10},{10,12},{12... | collective-permute-start | bytes 1179656 | tf_op jit(solution)/shard_map/ppermute | solution.py:276
  4.1 0.1 collective-permute-start.9
  4.2 0.1 collective-permute-start.4
  4.3 0.0 copy-start.4
  4.3 1.1 %place.1.pos_ref = s32[4]{0:T(128)S(1)} custom-call(s32[4]{0:T(128)S(1)} %compare_select_fusion.2.in_ref), custom_call_target="tpu_custom_call" | custom-call | flops 10000000000 | bytes 10000000 | tf_op jit(solution)/shard_map/place/pallas_call | solution.py:62
  5.4 5.8 %collective-permute-done.1.refs_2_ = bf16[2,4,2,96,128]{4,3,2,1,0:T(8,128)(2,1)S(1)} collective-permute-done((bf16[2,4,2,96,128]{4,3,2,1,0:T(8,128)(2,1)S(1)}, bf16[2,4,2,96,128]{4,3,2,1,0:T(8,128)(2,1)S(1)}, u32[]{:S(2)}, u32[]{:S(2)}) %collective-permute-start.1) | collective-permute-done | bytes 393248 | tf_op jit(solution)/shard_map/ppermute | solution.py:276
  11.3 1.5 %collective-permute-start.2 = (bf16[4,2,96,128]{3,2,1,0:T(8,128)(2,1)S(1)}, bf16[4,2,96,128]{3,2,1,0:T(8,128)(2,1)S(1)}, u32[]{:S(2)}, u32[]{:S(2)}) collective-permute-start(bf16[4,2,96,128]{3,2,1,0:T(8,128)(2,1)S(1)} %slice_bitcast_fusion.5), channel_id=1, source_target_pairs={{0,2},{2,4},{4,6},{6,0},{1,3},{3,5},{5,7},{7,1},{8,10},{10,12},{12... | collective-permute-start | bytes 589832 | tf_op jit(solution)/shard_map/ppermute | solution.py:276
  12.8 0.0 collective-permute-done.refs_1_
  12.8 0.3 collective-permute-start.3
  13.1 0.0 copy-done.3
  13.1 7.8 %inverse.1 = (bf16[2,512,256]{2,1,0:T(8,128)(2,1)S(1)}, bf16[2,512,256]{2,1,0:T(8,128)(2,1)S(1)}, f32[2,512,768]{2,1,0:T(8,128)S(1)}) custom-call(s32[2]{0:T(128)S(1)} %bitcast.34, s32[4]{0:T(128)S(1)} %place.1.pos_ref, f32[2,512,512]{2,1,0:T(8,128)S(1)} %bitcast.31, bf16[2,256,768]{2,1,0:T(8,128)(2,1)S(1)} %bitcast.33), custom_call_target="tpu_custom_call" | custom-call | flops 3758096384 | bytes 8000000 | tf_op jit(solution)/shard_map/inverse/pallas_call | solution.py:106
  20.9 2.3 %collective-permute-done.4.upper_ref = bf16[2,256,768]{2,1,0:T(8,128)(2,1)S(1)} collective-permute-done((bf16[2,256,768]{2,1,0:T(8,128)(2,1)}, bf16[2,256,768]{2,1,0:T(8,128)(2,1)S(1)}, u32[]{:S(2)}, u32[]{:S(2)}) %collective-permute-start.4) | collective-permute-done | bytes 786464 | tf_op jit(solution)/shard_map/ppermute | solution.py:281
  23.2 1.6 %scale_upper.1.refs_5_.refs_6_ = bf16[2,4,128,768]{3,2,1,0:T(8,128)(2,1)S(1)} custom-call(s32[4]{0:T(128)S(1)} %place.1.pos_ref, s32[2,24]{1,0:T(2,128)S(1)} %bitcast.26, bf16[2,512,256]{2,1,0:T(8,128)(2,1)S(1)} %get-tuple-element.16.xh_ref, bf16[2,512,256]{2,1,0:T(8,128)(2,1)S(1)} %get-tuple-element.17.xl_ref, ...), custom_call_target="tpu_custom_call" | custom-call | flops 805306368 | bytes 6291456 | tf_op jit(solution)/shard_map/scale_upper/pallas_call | solution.py:142
  24.8 0.0 collective-permute-done.2.refs_3_
  24.8 0.2 collective-permute-done.3.refs_4_
  25.0 1.5 %shard_map.65 = bf16[4,96,768]{2,1,0:T(8,128)(2,1)S(1)} custom-call(s32[4]{0:T(128)S(1)} %place.1.pos_ref, s32[2,24]{1,0:T(2,128)S(1)} %bitcast.27, bf16[4,2,2,96,768]{4,3,2,1,0:T(8,128)(2,1)S(1)} %bitcast.22, bf16[2,4,2,96,128]{4,3,2,1,0:T(8,128)(2,1)S(1)} %get-tuple-element.28.refs_0_, bf16[2,4,2,96,128]{4,3,2,1,0:T(8,128)(2,1)S(1)} %collective-permute-done.refs_1_, ...), custom_call_target="tpu_custom_call" | custom-call | flops 603979776 | bytes 4000000 | tf_op jit(solution)/shard_map/pallas_call | solution.py:180
  26.5 2.6 %collective-permute-start.5 = (bf16[4,96,768]{2,1,0:T(8,128)(2,1)S(1)}, bf16[4,96,768]{2,1,0:T(8,128)(2,1)S(1)}, u32[]{:S(2)}, u32[]{:S(2)}) collective-permute-start(bf16[4,96,768]{2,1,0:T(8,128)(2,1)S(1)} %shard_map.65), channel_id=1, source_target_pairs={{0,8},{8,0},{16,24},{24,16},{32,40},{40,32},{48,56},{56,48},{64,72... | collective-permute-start | bytes 1769480 | tf_op jit(solution)/shard_map/ppermute | solution.py:279
  29.1 0.0 collective-permute-done.10.refs_2_
  29.1 2.7 %collective-permute-start.11 = (bf16[4,2,96,128]{3,2,1,0:T(8,128)(2,1)S(1)}, bf16[4,2,96,128]{3,2,1,0:T(8,128)(2,1)S(1)}, u32[]{:S(2)}, u32[]{:S(2)}) collective-permute-start(bf16[4,2,96,128]{3,2,1,0:T(8,128)(2,1)S(1)} %slice_bitcast_fusion.3), channel_id=1, source_target_pairs={{0,2},{2,4},{4,6},{6,0},{1,3},{3,5},{5,7},{7,1},{8,10},{10,12},{12... | collective-permute-start | bytes 589832 | tf_op jit(solution)/shard_map/ppermute | solution.py:276
  31.8 0.0 collective-permute-done.9.refs_1_
  31.9 0.1 collective-permute-start.12
  32.0 1.4 %shard_map.64.kept_ref = f32[4,96,768]{2,1,0:T(8,128)S(1)} custom-call(s32[4]{0:T(128)S(1)} %place.1.pos_ref, s32[2,24]{1,0:T(2,128)S(1)} %bitcast.28, bf16[4,2,2,96,768]{4,3,2,1,0:T(8,128)(2,1)S(1)} %bitcast.23, bf16[2,4,2,96,128]{4,3,2,1,0:T(8,128)(2,1)S(1)} %get-tuple-element.28.refs_0_, bf16[2,4,2,96,128]{4,3,2,1,0:T(8,128)(2,1)S(1)} %collective-permute-done.refs_1_, ...), custom_call_target="tpu_custom_call" | custom-call | flops 603979776 | bytes 4000000 | tf_op jit(solution)/shard_map/pallas_call | solution.py:180
  33.4 0.0 collective-permute-done.5.got_ref
  33.4 1.0 %shard_map.66 = (f32[96,768]{1,0:T(8,128)S(1)}, bf16[96,768]{1,0:T(8,128)(2,1)S(1)}, bf16[96,768]{1,0:T(8,128)(2,1)S(1)}, bf16[96,768]{1,0:T(8,128)(2,1)S(1)}) custom-call(s32[4]{0:T(128)S(1)} %place.1.pos_ref, f32[4,96,768]{2,1,0:T(8,128)S(1)} %shard_map.64.kept_ref, bf16[4,96,768]{2,1,0:T(8,128)(2,1)S(1)} %collective-permute-done.5.got_ref), custom_call_target="tpu_custom_call" | custom-call | flops 294912 | bytes 2949120 | tf_op jit(solution)/shard_map/pallas_call | solution.py:201
  34.4 1.7 %collective-permute-done.11.refs_3_ = bf16[4,2,96,128]{3,2,1,0:T(8,128)(2,1)S(1)} collective-permute-done((bf16[4,2,96,128]{3,2,1,0:T(8,128)(2,1)S(1)}, bf16[4,2,96,128]{3,2,1,0:T(8,128)(2,1)S(1)}, u32[]{:S(2)}, u32[]{:S(2)}) %collective-permute-start.11) | collective-permute-done | bytes 196640 | tf_op jit(solution)/shard_map/ppermute | solution.py:276
  36.1 3.2 %collective-permute-done.12.refs_4_ = bf16[4,2,96,128]{3,2,1,0:T(8,128)(2,1)S(1)} collective-permute-done((bf16[4,2,96,128]{3,2,1,0:T(8,128)(2,1)S(1)}, bf16[4,2,96,128]{3,2,1,0:T(8,128)(2,1)S(1)}, u32[]{:S(2)}, u32[]{:S(2)}) %collective-permute-start.12) | collective-permute-done | bytes 196640 | tf_op jit(solution)/shard_map/ppermute | solution.py:276
  39.3 1.5 %shard_map.68 = bf16[4,96,768]{2,1,0:T(8,128)(2,1)S(1)} custom-call(s32[4]{0:T(128)S(1)} %place.1.pos_ref, s32[2,24]{1,0:T(2,128)S(1)} %bitcast.29, bf16[4,2,2,96,768]{4,3,2,1,0:T(8,128)(2,1)S(1)} %bitcast.24, bf16[2,4,2,96,128]{4,3,2,1,0:T(8,128)(2,1)S(1)} %get-tuple-element.27.refs_0_, bf16[2,4,2,96,128]{4,3,2,1,0:T(8,128)(2,1)S(1)} %collective-permute-done.9.refs_1_, ...), custom_call_target="tpu_custom_call" | custom-call | flops 603979776 | bytes 4000000 | tf_op jit(solution)/shard_map/pallas_call | solution.py:180
  40.8 1.3 %collective-permute-start.13 = (bf16[4,96,768]{2,1,0:T(8,128)(2,1)S(1)}, bf16[4,96,768]{2,1,0:T(8,128)(2,1)S(1)}, u32[]{:S(2)}, u32[]{:S(2)}) collective-permute-start(bf16[4,96,768]{2,1,0:T(8,128)(2,1)S(1)} %shard_map.68), channel_id=1, source_target_pairs={{0,8},{8,0},{16,24},{24,16},{32,40},{40,32},{48,56},{56,48},{64,72... | collective-permute-start | bytes 1769480 | tf_op jit(solution)/shard_map/ppermute | solution.py:279
  42.1 0.0 collective-permute-start.6
  42.1 1.6 %collective-permute-start.8 = (bf16[96,768]{1,0:T(8,128)(2,1)S(1)}, bf16[96,768]{1,0:T(8,128)(2,1)S(1)}, u32[]{:S(2)}, u32[]{:S(2)}) collective-permute-start(bf16[96,768]{1,0:T(8,128)(2,1)S(1)} %get-tuple-element.22.refs_6_), channel_id=1, source_target_pairs={{0,16},{8,24},{16,0},{24,8},{32,48},{40,56},{48,32},{56,40},{64,80... | collective-permute-start | bytes 442376 | tf_op jit(solution)/shard_map/ppermute | solution.py:279
  43.7 1.2 %collective-permute-start.7 = (bf16[96,768]{1,0:T(8,128)(2,1)S(1)}, bf16[96,768]{1,0:T(8,128)(2,1)S(1)}, u32[]{:S(2)}, u32[]{:S(2)}) collective-permute-start(bf16[96,768]{1,0:T(8,128)(2,1)S(1)} %get-tuple-element.21), channel_id=1, source_target_pairs={{0,48},{8,56},{16,32},{24,40},{32,16},{40,24},{48,0},{56,8},{64,11... | collective-permute-start | bytes 442376 | tf_op jit(solution)/shard_map/ppermute | solution.py:279
  44.9 1.4 %shard_map.67.kept_ref = f32[4,96,768]{2,1,0:T(8,128)S(1)} custom-call(s32[4]{0:T(128)S(1)} %place.1.pos_ref, s32[2,24]{1,0:T(2,128)S(1)} %bitcast.30, bf16[4,2,2,96,768]{4,3,2,1,0:T(8,128)(2,1)S(1)} %bitcast.25, bf16[2,4,2,96,128]{4,3,2,1,0:T(8,128)(2,1)S(1)} %get-tuple-element.27.refs_0_, bf16[2,4,2,96,128]{4,3,2,1,0:T(8,128)(2,1)S(1)} %collective-permute-done.9.refs_1_, ...), custom_call_target="tpu_custom_call" | custom-call | flops 603979776 | bytes 4000000 | tf_op jit(solution)/shard_map/pallas_call | solution.py:180
  46.3 0.0 collective-permute-done.13.got_ref
  46.3 1.0 %shard_map.69 = (f32[96,768]{1,0:T(8,128)S(1)}, bf16[96,768]{1,0:T(8,128)(2,1)S(1)}, bf16[96,768]{1,0:T(8,128)(2,1)S(1)}, bf16[96,768]{1,0:T(8,128)(2,1)S(1)}) custom-call(s32[4]{0:T(128)S(1)} %place.1.pos_ref, f32[4,96,768]{2,1,0:T(8,128)S(1)} %shard_map.67.kept_ref, bf16[4,96,768]{2,1,0:T(8,128)(2,1)S(1)} %collective-permute-done.13.got_ref), custom_call_target="tpu_custom_call" | custom-call | flops 294912 | bytes 2949120 | tf_op jit(solution)/shard_map/pallas_call | solution.py:201
  47.3 1.3 %collective-permute-start.14 = (bf16[96,768]{1,0:T(8,128)(2,1)S(1)}, bf16[96,768]{1,0:T(8,128)(2,1)S(1)}, u32[]{:S(2)}, u32[]{:S(2)}) collective-permute-start(bf16[96,768]{1,0:T(8,128)(2,1)S(1)} %get-tuple-element.24), channel_id=1, source_target_pairs={{0,32},{8,40},{16,48},{24,56},{32,0},{40,8},{48,16},{56,24},{64,96... | collective-permute-start | bytes 442376 | tf_op jit(solution)/shard_map/ppermute | solution.py:279
  48.6 2.4 %collective-permute-start.15 = (bf16[96,768]{1,0:T(8,128)(2,1)S(1)}, bf16[96,768]{1,0:T(8,128)(2,1)S(1)}, u32[]{:S(2)}, u32[]{:S(2)}) collective-permute-start(bf16[96,768]{1,0:T(8,128)(2,1)S(1)} %get-tuple-element.25), channel_id=1, source_target_pairs={{0,48},{8,56},{16,32},{24,40},{32,16},{40,24},{48,0},{56,8},{64,11... | collective-permute-start | bytes 442376 | tf_op jit(solution)/shard_map/ppermute | solution.py:279
  50.9 0.0 collective-permute-done.6.refs_0_
  50.9 2.8 %collective-permute-start.16 = (bf16[96,768]{1,0:T(8,128)(2,1)S(1)}, bf16[96,768]{1,0:T(8,128)(2,1)S(1)}, u32[]{:S(2)}, u32[]{:S(2)}) collective-permute-start(bf16[96,768]{1,0:T(8,128)(2,1)S(1)} %get-tuple-element.26), channel_id=1, source_target_pairs={{0,16},{8,24},{16,0},{24,8},{32,48},{40,56},{48,32},{56,40},{64,80... | collective-permute-start | bytes 442376 | tf_op jit(solution)/shard_map/ppermute | solution.py:279
  53.8 10.8 %collective-permute-done.7.refs_1_ = bf16[96,768]{1,0:T(8,128)(2,1)S(1)} collective-permute-done((bf16[96,768]{1,0:T(8,128)(2,1)S(1)}, bf16[96,768]{1,0:T(8,128)(2,1)S(1)}, u32[]{:S(2)}, u32[]{:S(2)}) %collective-permute-start.7) | collective-permute-done | bytes 147488 | tf_op jit(solution)/shard_map/ppermute | solution.py:279
  64.6 0.0 collective-permute-done.8.refs_2_
  64.6 0.2 chunk_sums.1.early_ref
  64.8 0.0 collective-permute-done.14.refs_0_
  64.8 6.1 %collective-permute-done.15.refs_1_ = bf16[96,768]{1,0:T(8,128)(2,1)S(1)} collective-permute-done((bf16[96,768]{1,0:T(8,128)(2,1)S(1)}, bf16[96,768]{1,0:T(8,128)(2,1)S(1)}, u32[]{:S(2)}, u32[]{:S(2)}) %collective-permute-start.15) | collective-permute-done | bytes 147488 | tf_op jit(solution)/shard_map/ppermute | solution.py:279
  70.9 0.0 collective-permute-done.16.refs_2_
  70.9 1.0 %final_sums.1 = f32[1,192,768]{2,1,0:T(8,128)} custom-call(f32[96,768]{1,0:T(8,128)S(1)} %chunk_sums.1.early_ref, f32[96,768]{1,0:T(8,128)S(1)} %get-tuple-element.23.own_ref, bf16[96,768]{1,0:T(8,128)(2,1)S(1)} %collective-permute-done.14.refs_0_, bf16[96,768]{1,0:T(8,128)(2,1)S(1)} %collective-permute-done.15.refs_1_, ...), custom_call_target="tpu_custom_call" | custom-call | flops 294912 | bytes 884736 | tf_op jit(solution)/shard_map/final_sums/pallas_call | solution.py:245
  (13 shorter events, 0.1 us)
Async XLA Ops:
  1.2 10.1 %collective-permute-start.1 = (bf16[2,4,2,96,128]{4,3,2,1,0:T(8,128)(2,1)S(1)}, bf16[2,4,2,96,128]{4,3,2,1,0:T(8,128)(2,1)S(1)}, u32[]{:S(2)}, u32[]{:S(2)}) collective-permute-start(bf16[2,4,2,96,128]{4,3,2,1,0:T(8,128)(2,1)S(1)} %get-tuple-element.28.refs_0_), channel_id=1, source_target_pairs={{0,2},{2,4},{4,6},{6,0},{1,3},{3,5},{5,7},{7,1},{8,10},{10,12},{12... | collective-permute-start | bytes 1179656 | tf_op jit(solution)/shard_map/ppermute | solution.py:276
  1.5 11.3 %collective-permute-start = (bf16[2,4,2,96,128]{4,3,2,1,0:T(8,128)(2,1)S(1)}, bf16[2,4,2,96,128]{4,3,2,1,0:T(8,128)(2,1)S(1)}, u32[]{:S(2)}, u32[]{:S(2)}) collective-permute-start(bf16[2,4,2,96,128]{4,3,2,1,0:T(8,128)(2,1)S(1)} %get-tuple-element.28.refs_0_), channel_id=1, source_target_pairs={{0,6},{2,0},{4,2},{6,4},{1,7},{3,1},{5,3},{7,5},{8,14},{10,8},{12,... | collective-permute-start | bytes 1179656 | tf_op jit(solution)/shard_map/ppermute | solution.py:276
  2.7 26.4 %collective-permute-start.10 = (bf16[2,4,2,96,128]{4,3,2,1,0:T(8,128)(2,1)S(1)}, bf16[2,4,2,96,128]{4,3,2,1,0:T(8,128)(2,1)S(1)}, u32[]{:S(2)}, u32[]{:S(2)}) collective-permute-start(bf16[2,4,2,96,128]{4,3,2,1,0:T(8,128)(2,1)S(1)} %get-tuple-element.27.refs_0_), channel_id=1, source_target_pairs={{0,2},{2,4},{4,6},{6,0},{1,3},{3,5},{5,7},{7,1},{8,10},{10,12},{12... | collective-permute-start | bytes 1179656 | tf_op jit(solution)/shard_map/ppermute | solution.py:276
  4.1 27.7 %collective-permute-start.9 = (bf16[2,4,2,96,128]{4,3,2,1,0:T(8,128)(2,1)S(1)}, bf16[2,4,2,96,128]{4,3,2,1,0:T(8,128)(2,1)S(1)}, u32[]{:S(2)}, u32[]{:S(2)}) collective-permute-start(bf16[2,4,2,96,128]{4,3,2,1,0:T(8,128)(2,1)S(1)} %get-tuple-element.27.refs_0_), channel_id=1, source_target_pairs={{0,6},{2,0},{4,2},{6,4},{1,7},{3,1},{5,3},{7,5},{8,14},{10,8},{12,... | collective-permute-start | bytes 1179656 | tf_op jit(solution)/shard_map/ppermute | solution.py:276
  4.2 19.0 %collective-permute-start.4 = (bf16[2,256,768]{2,1,0:T(8,128)(2,1)}, bf16[2,256,768]{2,1,0:T(8,128)(2,1)S(1)}, u32[]{:S(2)}, u32[]{:S(2)}) collective-permute-start(bf16[2,256,768]{2,1,0:T(8,128)(2,1)} %bitcast.32), channel_id=1, source_target_pairs={{0,1},{1,0},{2,3},{3,2},{4,5},{5,4},{6,7},{7,6},{8,9},{9,8},{10,11... | collective-permute-start | bytes 2359304 | tf_op jit(solution)/shard_map/ppermute | solution.py:281
  4.2 8.8 %copy-start.2 = (f32[1,2,512,512]{3,2,1,0:T(8,128)S(1)}, f32[1,2,512,512]{3,2,1,0:T(8,128)}, u32[]{:S(2)}) copy-start(f32[1,2,512,512]{3,2,1,0:T(8,128)} %param.9) | copy-start | bytes 6291460
  4.3 8.8 %copy-start.3 = (bf16[1,2,256,768]{3,2,1,0:T(8,128)(2,1)S(1)}, bf16[1,2,256,768]{3,2,1,0:T(8,128)(2,1)}, u32[]{:S(2)}) copy-start(bf16[1,2,256,768]{3,2,1,0:T(8,128)(2,1)} %param.8) | copy-start | bytes 2359300
  4.3 8.8 %copy-start.4 = (s32[1,2]{1,0:T(1,128)S(1)}, s32[1,2]{1,0:T(1,128)}, u32[]{:S(2)}) copy-start(s32[1,2]{1,0:T(1,128)} %param.11) | copy-start | bytes 28
  11.3 13.5 %collective-permute-start.2 = (bf16[4,2,96,128]{3,2,1,0:T(8,128)(2,1)S(1)}, bf16[4,2,96,128]{3,2,1,0:T(8,128)(2,1)S(1)}, u32[]{:S(2)}, u32[]{:S(2)}) collective-permute-start(bf16[4,2,96,128]{3,2,1,0:T(8,128)(2,1)S(1)} %slice_bitcast_fusion.5), channel_id=1, source_target_pairs={{0,2},{2,4},{4,6},{6,0},{1,3},{3,5},{5,7},{7,1},{8,10},{10,12},{12... | collective-permute-start | bytes 589832 | tf_op jit(solution)/shard_map/ppermute | solution.py:276
  12.8 12.2 %collective-permute-start.3 = (bf16[4,2,96,128]{3,2,1,0:T(8,128)(2,1)S(1)}, bf16[4,2,96,128]{3,2,1,0:T(8,128)(2,1)S(1)}, u32[]{:S(2)}, u32[]{:S(2)}) collective-permute-start(bf16[4,2,96,128]{3,2,1,0:T(8,128)(2,1)S(1)} %slice_bitcast_fusion.4), channel_id=1, source_target_pairs={{0,6},{2,0},{4,2},{6,4},{1,7},{3,1},{5,3},{7,5},{8,14},{10,8},{12,... | collective-permute-start | bytes 589832 | tf_op jit(solution)/shard_map/ppermute | solution.py:276
  13.1 10.1 %copy-start.1 = (s32[1,2,24]{2,1,0:T(2,128)S(1)}, s32[1,2,24]{2,1,0:T(2,128)}, u32[]{:S(2)}) copy-start(s32[1,2,24]{2,1,0:T(2,128)} %param.10) | copy-start | bytes 580
  23.2 1.8 %copy-start = (bf16[1,1536,768]{2,1,0:T(8,128)(2,1)S(1)}, bf16[1,1536,768]{2,1,0:T(8,128)(2,1)}, u32[]{:S(2)}) copy-start(bf16[1,1536,768]{2,1,0:T(8,128)(2,1)} %param.6) | copy-start | bytes 7077892
  26.5 6.9 %collective-permute-start.5 = (bf16[4,96,768]{2,1,0:T(8,128)(2,1)S(1)}, bf16[4,96,768]{2,1,0:T(8,128)(2,1)S(1)}, u32[]{:S(2)}, u32[]{:S(2)}) collective-permute-start(bf16[4,96,768]{2,1,0:T(8,128)(2,1)S(1)} %shard_map.65), channel_id=1, source_target_pairs={{0,8},{8,0},{16,24},{24,16},{32,40},{40,32},{48,56},{56,48},{64,72... | collective-permute-start | bytes 1769480 | tf_op jit(solution)/shard_map/ppermute | solution.py:279
  29.1 6.9 %collective-permute-start.11 = (bf16[4,2,96,128]{3,2,1,0:T(8,128)(2,1)S(1)}, bf16[4,2,96,128]{3,2,1,0:T(8,128)(2,1)S(1)}, u32[]{:S(2)}, u32[]{:S(2)}) collective-permute-start(bf16[4,2,96,128]{3,2,1,0:T(8,128)(2,1)S(1)} %slice_bitcast_fusion.3), channel_id=1, source_target_pairs={{0,2},{2,4},{4,6},{6,0},{1,3},{3,5},{5,7},{7,1},{8,10},{10,12},{12... | collective-permute-start | bytes 589832 | tf_op jit(solution)/shard_map/ppermute | solution.py:276
  31.9 7.4 %collective-permute-start.12 = (bf16[4,2,96,128]{3,2,1,0:T(8,128)(2,1)S(1)}, bf16[4,2,96,128]{3,2,1,0:T(8,128)(2,1)S(1)}, u32[]{:S(2)}, u32[]{:S(2)}) collective-permute-start(bf16[4,2,96,128]{3,2,1,0:T(8,128)(2,1)S(1)} %slice_bitcast_fusion.2), channel_id=1, source_target_pairs={{0,6},{2,0},{4,2},{6,4},{1,7},{3,1},{5,3},{7,5},{8,14},{10,8},{12,... | collective-permute-start | bytes 589832 | tf_op jit(solution)/shard_map/ppermute | solution.py:276
  40.8 5.5 %collective-permute-start.13 = (bf16[4,96,768]{2,1,0:T(8,128)(2,1)S(1)}, bf16[4,96,768]{2,1,0:T(8,128)(2,1)S(1)}, u32[]{:S(2)}, u32[]{:S(2)}) collective-permute-start(bf16[4,96,768]{2,1,0:T(8,128)(2,1)S(1)} %shard_map.68), channel_id=1, source_target_pairs={{0,8},{8,0},{16,24},{24,16},{32,40},{40,32},{48,56},{56,48},{64,72... | collective-permute-start | bytes 1769480 | tf_op jit(solution)/shard_map/ppermute | solution.py:279
  42.1 8.9 %collective-permute-start.6 = (bf16[96,768]{1,0:T(8,128)(2,1)S(1)}, bf16[96,768]{1,0:T(8,128)(2,1)S(1)}, u32[]{:S(2)}, u32[]{:S(2)}) collective-permute-start(bf16[96,768]{1,0:T(8,128)(2,1)S(1)} %get-tuple-element.20), channel_id=1, source_target_pairs={{0,32},{8,40},{16,48},{24,56},{32,0},{40,8},{48,16},{56,24},{64,96... | collective-permute-start | bytes 442376 | tf_op jit(solution)/shard_map/ppermute | solution.py:279
  42.1 22.5 %collective-permute-start.8 = (bf16[96,768]{1,0:T(8,128)(2,1)S(1)}, bf16[96,768]{1,0:T(8,128)(2,1)S(1)}, u32[]{:S(2)}, u32[]{:S(2)}) collective-permute-start(bf16[96,768]{1,0:T(8,128)(2,1)S(1)} %get-tuple-element.22.refs_6_), channel_id=1, source_target_pairs={{0,16},{8,24},{16,0},{24,8},{32,48},{40,56},{48,32},{56,40},{64,80... | collective-permute-start | bytes 442376 | tf_op jit(solution)/shard_map/ppermute | solution.py:279
  43.7 20.9 %collective-permute-start.7 = (bf16[96,768]{1,0:T(8,128)(2,1)S(1)}, bf16[96,768]{1,0:T(8,128)(2,1)S(1)}, u32[]{:S(2)}, u32[]{:S(2)}) collective-permute-start(bf16[96,768]{1,0:T(8,128)(2,1)S(1)} %get-tuple-element.21), channel_id=1, source_target_pairs={{0,48},{8,56},{16,32},{24,40},{32,16},{40,24},{48,0},{56,8},{64,11... | collective-permute-start | bytes 442376 | tf_op jit(solution)/shard_map/ppermute | solution.py:279
  47.3 17.5 %collective-permute-start.14 = (bf16[96,768]{1,0:T(8,128)(2,1)S(1)}, bf16[96,768]{1,0:T(8,128)(2,1)S(1)}, u32[]{:S(2)}, u32[]{:S(2)}) collective-permute-start(bf16[96,768]{1,0:T(8,128)(2,1)S(1)} %get-tuple-element.24), channel_id=1, source_target_pairs={{0,32},{8,40},{16,48},{24,56},{32,0},{40,8},{48,16},{56,24},{64,96... | collective-permute-start | bytes 442376 | tf_op jit(solution)/shard_map/ppermute | solution.py:279
  48.6 22.3 %collective-permute-start.15 = (bf16[96,768]{1,0:T(8,128)(2,1)S(1)}, bf16[96,768]{1,0:T(8,128)(2,1)S(1)}, u32[]{:S(2)}, u32[]{:S(2)}) collective-permute-start(bf16[96,768]{1,0:T(8,128)(2,1)S(1)} %get-tuple-element.25), channel_id=1, source_target_pairs={{0,48},{8,56},{16,32},{24,40},{32,16},{40,24},{48,0},{56,8},{64,11... | collective-permute-start | bytes 442376 | tf_op jit(solution)/shard_map/ppermute | solution.py:279
  50.9 20.0 %collective-permute-start.16 = (bf16[96,768]{1,0:T(8,128)(2,1)S(1)}, bf16[96,768]{1,0:T(8,128)(2,1)S(1)}, u32[]{:S(2)}, u32[]{:S(2)}) collective-permute-start(bf16[96,768]{1,0:T(8,128)(2,1)S(1)} %get-tuple-element.26), channel_id=1, source_target_pairs={{0,16},{8,24},{16,0},{24,8},{32,48},{40,56},{48,32},{56,40},{64,80... | collective-permute-start | bytes 442376 | tf_op jit(solution)/shard_map/ppermute | solution.py:279

commit v8 on v7

--- a/solution.py
+++ b/solution.py
@@ -188,12 +188,96 @@
     )(pos, fill, front, *lowers, scaled, after)
 
 
-def round_kernel(pos_ref, kept_ref, got_ref, own_ref, *out_refs):
+def fill_wide(wide, fill_ref, base, strip, tiles_of, spots, rows, members):
+    for s in range(members):
+        for d in range(spots):
+            for j in range(rows // SUB):
+                spot = lax.div(base + d * 2 * strip + j * SUB, BLOCK)
+                used = fill_ref[s, spot] != 0
+                top = d * rows + j * SUB
+                for begin, tile in tiles_of(s, d, slice(j * SUB, (j + 1) * SUB)):
+                    wide[top : top + SUB, begin : begin + BLOCK] = jnp.where(used, tile, jnp.zeros_like(tile))
+
+
+def joined(scaled_ref, piece):
+    members = scaled_ref.shape[0]
+    return jnp.concatenate([scaled_ref[s, piece] for s in range(members)], axis=0)
+
+
+def near_call(chunk, pos, fill, front, own, following, last, scaled, after):
+    spots, sides, _, rows, cols = front.shape
+    members, pieces = scaled.shape[:2]
+    double = 2 * BLOCK
+
+    def near_kernel(pos_ref, fill_ref, front_ref, own_ref, next_ref, last_ref, scaled_ref, _, out_ref, wide):
+        strip = 2 * rows
+        ends = joined(scaled_ref, pieces - 1)
+        for side in range(sides):
+            base = pos_ref[2] * (spots * 2 * strip) + side * strip + chunk * rows
+
+            def tiles_of(s, d, span):
+                where = (s, d, side, span)
+                return (
+                    (s * double, own_ref[where]),
+                    (s * double + BLOCK, next_ref[where]),
+                    (members * double + s * BLOCK, last_ref[where]),
+                )
+
+            fill_wide(wide, fill_ref, base, strip, tiles_of, spots, rows, members)
+            total = dot(wide[:, members * double :], ends)
+            for s in range(members):
+                pair = scaled_ref[s, :2].reshape(double, cols)
+                total = total + dot(wide[:, s * double : (s + 1) * double], pair)
+            total = total.reshape(spots, rows, cols)
+            for d in range(spots):
+                out_ref[side, d] = front_ref[d, side, chunk].astype(F32) - total[d]
+
+    return pl.pallas_call(
+        near_kernel,
+        in_specs=[SMEM, SMEM] + [VMEM] * 5 + [ANY],
+        out_specs=VMEM,
+        scratch_shapes=[pltpu.VMEM((spots * rows, members * 3 * BLOCK), BF16)],
+        out_shape=jax.ShapeDtypeStruct((sides, spots, rows, cols), F32),
+        cost_estimate=cost(4 * spots * rows * members * 3 * BLOCK * cols, 8000000),
+        compiler_params=grant(14),
+    )(pos, fill, front, own, following, last, scaled, after)
+
+
+def far_call(flip, chunk, pos, fill, near, right, left, scaled):
+    _, spots, rows, cols = near.shape
+    members = scaled.shape[0]
+
+    def far_kernel(pos_ref, fill_ref, near_ref, right_ref, left_ref, scaled_ref, out_ref, wide):
+        side = 1 - pos_ref[0] if flip else pos_ref[0]
+        strip = 2 * rows
+        base = pos_ref[2] * (spots * 2 * strip) + side * strip + chunk * rows
+        far_refs = (right_ref, left_ref)
+
+        def tiles_of(s, d, span):
+            return ((s * BLOCK, far_refs[s][d, side, span]),)
+
+        fill_wide(wide, fill_ref, base, strip, tiles_of, spots, rows, members)
+        total = dot(wide[...], joined(scaled_ref, 2)).reshape(spots, rows, cols)
+        for d in range(spots):
+            copy = near_ref[side, d] - total[d]
+            out_ref[d] = code(copy) if flip else copy
+
+    return pl.pallas_call(
+        far_kernel,
+        in_specs=[SMEM, SMEM] + [VMEM] * 4,
+        out_specs=VMEM,
+        scratch_shapes=[pltpu.VMEM((spots * rows, members * BLOCK), BF16)],
+        out_shape=jax.ShapeDtypeStruct((spots, rows, cols), BF16 if flip else F32),
+        cost_estimate=cost(2 * spots * rows * members * BLOCK * cols, 4000000),
+        compiler_params=grant(12),
+    )(pos, fill, near, right, left, scaled)
+
+
+def round_kernel(pos_ref, kept_ref, got_ref, *out_refs):
     place = pos_ref[3]
     for k, out_ref in enumerate(out_refs):
         spot = lax.bitwise_xor(place, k + 1)
         out_ref[...] = code(kept_ref[spot] + decode(got_ref[spot]))
-    own_ref[...] = kept_ref[place] + decode(got_ref[place])
 
 
 def round_call(pos, kept, got):
@@ -201,33 +285,32 @@
     return pl.pallas_call(
         round_kernel,
         in_specs=[SMEM, VMEM, VMEM],
-        out_specs=[VMEM] * spots,
-        out_shape=[jax.ShapeDtypeStruct((rows, cols), F32)]
-        + [jax.ShapeDtypeStruct((rows, cols), BF16)] * (spots - 1),
+        out_specs=[VMEM] * (spots - 1),
+        out_shape=[jax.ShapeDtypeStruct((rows, cols), BF16)] * (spots - 1),
         cost_estimate=cost(spots * rows * cols, 10 * spots * rows * cols),
         compiler_params=grant(8),
     )(pos, kept, got)
 
 
-def chunk_kernel(own_ref, *refs):
+def chunk_kernel(pos_ref, kept_ref, core_ref, *refs):
     *got_refs, out_ref = refs
-    total = own_ref[...]
+    place = pos_ref[3]
+    total = kept_ref[place] + decode(core_ref[place])
     for ref in got_refs:
         total = total + decode(ref[...])
     out_ref[...] = total
 
 
-def chunk_call(parts):
-    rows, cols = parts[0].shape
+def chunk_call(pos, kept, core, parts):
+    _, rows, cols = kept.shape
     return pl.pallas_call(
         chunk_kernel,
-        in_specs=[VMEM] * len(parts),
+        in_specs=[SMEM] + [VMEM] * (len(parts) + 2),
         out_specs=VMEM,
         out_shape=jax.ShapeDtypeStruct((rows, cols), F32),
         cost_estimate=cost(len(parts) * rows * cols, 3 * len(parts) * rows * cols),
-        name="chunk_sums",
         compiler_params=grant(8),
-    )(*parts)
+    )(pos, kept, core, *parts)
 
 
 def final_kernel(early_ref, own_ref, *refs):
@@ -287,17 +370,28 @@
         lowers.append((own, following, last, right, left))
     xh, xl, part = inverse_call(width_vec, pos, diag_blocks[0], upper)
     scaled = scale_call(pos, fill, xh, xl, part, other_upper)
-    finals = []
+    sums = []
     after = scaled
     for chunk in range(2):
-        sent = update_call(True, chunk, pos, fill, front, lowers[chunk], scaled, after)
-        got = across(sent, 1)
-        kept = update_call(False, chunk, pos, fill, front, lowers[chunk], scaled, after)
-        own, one, two, three = round_call(pos, kept, got)
+        if chunk == 0:
+            sent = update_call(True, chunk, pos, fill, front, lowers[chunk], scaled, after)
+        else:
+            *near, right, left = lowers[chunk]
+            near = near_call(chunk, pos, fill, front, *near, scaled, after)
+            sent = far_call(True, chunk, pos, fill, near, right, left, scaled)
+        core = across(sent, 1)
+        if chunk == 0:
+            kept = update_call(False, chunk, pos, fill, front, lowers[chunk], scaled, after)
+        else:
+            kept = far_call(False, chunk, pos, fill, near, right, left, scaled)
+        one, two, three = round_call(pos, kept, core)
         after = one
-        finals += [own, across(two, 4), across(three, 6), across(one, 2)]
-    half = len(finals) // 2
-    return final_call(chunk_call(finals[:half]), finals[half:])
+        parts = [across(two, 4), across(three, 6), across(one, 2)]
+        if chunk == 0:
+            sums.append(chunk_call(pos, kept, core, parts))
+        else:
+            sums += [chunk_call(pos, kept, core, []), *parts]
+    return final_call(sums[0], sums[1:])
 
 
 def solution(mesh):

time: 72 us -> 71.7 us (level)
  the two profiles are of different devices: /device:TPU:87 before, /device:TPU:71 now
where the time goes in v8:
time: 71.7 us; the launch traced here: 71.6 us
  waiting for transfers between devices  24.6 us (34%)
  starting transfers between devices  24.3 us (34%)
  Pallas kernels  21.3 us (30%)
  local copies, waits for them, and re-layouts  1.24 us (2%)
    ppermute x8, waiting for transfers between devices, across(): return lax.ppermute(block, 'layer', [(i, i ^ flip) for i in range(layers)])  15.9 us
    ppermute x8, starting transfers between devices, across(): return lax.ppermute(block, 'layer', [(i, i ^ flip) for i in range(layers)])  13.7 us
    pallas_call x1, Pallas kernels, inverse_call(): pl.pallas_call(inverse_kernel, in_specs=[SMEM, SMEM, VMEM, VMEM], out_spe...  7.83 us
    ppermute x8, starting transfers between devices, shift(): lax.ppermute(block, 'col', [(i, (i + step) % col_devices) for i in range(...  7.59 us
    ppermute x8, waiting for transfers between devices, shift(): lax.ppermute(block, 'col', [(i, (i + step) % col_devices) for i in range(...  6.44 us
    pallas_call x2, Pallas kernels, update_call(): pl.pallas_call(update_kernel, in_specs=[SMEM, SMEM] + [VMEM] * (len(lower...  2.93 us
    ppermute x1, starting transfers between devices, on_device(): other_upper = lax.ppermute(upper, 'row', [(0, 1), (1, 0)])  2.91 us
    ppermute x1, waiting for transfers between devices, on_device(): other_upper = lax.ppermute(upper, 'row', [(0, 1), (1, 0)])  2.26 us
  transfers between devices with their start and end apart: 17, of which 6 were waited for; matrix products, arithmetic and copies ran while one was open for 0% of the time, Pallas kernels for 27%

profile of v8, /device:TPU:71, one launch (start us, length us, event | category | flops | bytes accessed | tf_op | source)
XLA Modules:
  0.0 71.6 jit_solution(16377385598493536105)
XLA Ops:
  0.0 1.2 %slice_bitcast_fusion = (bf16[2,4,2,96,128]{4,3,2,1,0:T(8,128)(2,1)S(1)}, bf16[2,4,2,96,128]{4,3,2,1,0:T(8,128)(2,1)S(1)}) fusion(bf16[2,4,2,2,96,128]{5,4,3,2,1,0:T(8,128)(2,1)} %bitcast.35), kind=kLoop, calls=%fused_computation | loop fusion | bytes 1572864 | tf_op jit(solution)/shard_map/squeeze | solution.py:367
  1.2 0.3 collective-permute-start.1
  1.5 1.3 %collective-permute-start = (bf16[2,4,2,96,128]{4,3,2,1,0:T(8,128)(2,1)S(1)}, bf16[2,4,2,96,128]{4,3,2,1,0:T(8,128)(2,1)S(1)}, u32[]{:S(2)}, u32[]{:S(2)}) collective-permute-start(bf16[2,4,2,96,128]{4,3,2,1,0:T(8,128)(2,1)S(1)} %get-tuple-element.24.refs_0_), channel_id=1, source_target_pairs={{0,6},{2,0},{4,2},{6,4},{1,7},{3,1},{5,3},{7,5},{8,14},{10,8},{12,... | collective-permute-start | bytes 1179656 | tf_op jit(solution)/shard_map/ppermute | solution.py:359
  2.7 1.4 %collective-permute-start.10 = (bf16[2,4,2,96,128]{4,3,2,1,0:T(8,128)(2,1)S(1)}, bf16[2,4,2,96,128]{4,3,2,1,0:T(8,128)(2,1)S(1)}, u32[]{:S(2)}, u32[]{:S(2)}) collective-permute-start(bf16[2,4,2,96,128]{4,3,2,1,0:T(8,128)(2,1)S(1)} %get-tuple-element.23.own_ref), channel_id=1, source_target_pairs={{0,2},{2,4},{4,6},{6,0},{1,3},{3,5},{5,7},{7,1},{8,10},{10,12},{12... | collective-permute-start | bytes 1179656 | tf_op jit(solution)/shard_map/ppermute | solution.py:359
  4.1 0.1 collective-permute-start.9
  4.2 2.9 %collective-permute-start.4 = (bf16[2,256,768]{2,1,0:T(8,128)(2,1)}, bf16[2,256,768]{2,1,0:T(8,128)(2,1)S(1)}, u32[]{:S(2)}, u32[]{:S(2)}) collective-permute-start(bf16[2,256,768]{2,1,0:T(8,128)(2,1)} %bitcast.32), channel_id=1, source_target_pairs={{0,1},{1,0},{2,3},{3,2},{4,5},{5,4},{6,7},{7,6},{8,9},{9,8},{10,11... | collective-permute-start | bytes 2359304 | tf_op jit(solution)/shard_map/ppermute | solution.py:364
  7.1 0.0 copy-start.4
  7.1 1.1 %place.1.pos_ref = s32[4]{0:T(128)S(1)} custom-call(s32[4]{0:T(128)S(1)} %compare_select_fusion.2.in_ref), custom_call_target="tpu_custom_call" | custom-call | flops 10000000000 | bytes 10000000 | tf_op jit(solution)/shard_map/place/pallas_call | solution.py:62
  8.3 3.0 %collective-permute-done.1.refs_2_ = bf16[2,4,2,96,128]{4,3,2,1,0:T(8,128)(2,1)S(1)} collective-permute-done((bf16[2,4,2,96,128]{4,3,2,1,0:T(8,128)(2,1)S(1)}, bf16[2,4,2,96,128]{4,3,2,1,0:T(8,128)(2,1)S(1)}, u32[]{:S(2)}, u32[]{:S(2)}) %collective-permute-start.1) | collective-permute-done | bytes 393248 | tf_op jit(solution)/shard_map/ppermute | solution.py:359
  11.3 1.5 %collective-permute-start.2 = (bf16[4,2,96,128]{3,2,1,0:T(8,128)(2,1)S(1)}, bf16[4,2,96,128]{3,2,1,0:T(8,128)(2,1)S(1)}, u32[]{:S(2)}, u32[]{:S(2)}) collective-permute-start(bf16[4,2,96,128]{3,2,1,0:T(8,128)(2,1)S(1)} %slice_bitcast_fusion.5), channel_id=1, source_target_pairs={{0,2},{2,4},{4,6},{6,0},{1,3},{3,5},{5,7},{7,1},{8,10},{10,12},{12... | collective-permute-start | bytes 589832 | tf_op jit(solution)/shard_map/ppermute | solution.py:359
  12.8 0.0 collective-permute-done.refs_1_
  12.8 0.3 collective-permute-start.3
  13.1 7.8 %inverse.1 = (bf16[2,512,256]{2,1,0:T(8,128)(2,1)S(1)}, bf16[2,512,256]{2,1,0:T(8,128)(2,1)S(1)}, f32[2,512,768]{2,1,0:T(8,128)S(1)}) custom-call(s32[2]{0:T(128)S(1)} %bitcast.34, s32[4]{0:T(128)S(1)} %place.1.pos_ref, f32[2,512,512]{2,1,0:T(8,128)S(1)} %bitcast.31, bf16[2,256,768]{2,1,0:T(8,128)(2,1)S(1)} %bitcast.33), custom_call_target="tpu_custom_call" | custom-call | flops 3758096384 | bytes 8000000 | tf_op jit(solution)/shard_map/inverse/pallas_call | solution.py:106
  20.9 2.3 %collective-permute-done.4.upper_ref = bf16[2,256,768]{2,1,0:T(8,128)(2,1)S(1)} collective-permute-done((bf16[2,256,768]{2,1,0:T(8,128)(2,1)}, bf16[2,256,768]{2,1,0:T(8,128)(2,1)S(1)}, u32[]{:S(2)}, u32[]{:S(2)}) %collective-permute-start.4) | collective-permute-done | bytes 786464 | tf_op jit(solution)/shard_map/ppermute | solution.py:364
  23.2 1.6 %scale_upper.1.refs_5_.refs_6_.scaled_ref = bf16[2,4,128,768]{3,2,1,0:T(8,128)(2,1)S(1)} custom-call(s32[4]{0:T(128)S(1)} %place.1.pos_ref, s32[2,24]{1,0:T(2,128)S(1)} %bitcast.25, bf16[2,512,256]{2,1,0:T(8,128)(2,1)S(1)} %get-tuple-element.14.xh_ref, bf16[2,512,256]{2,1,0:T(8,128)(2,1)S(1)} %get-tuple-element.15.xl_ref, ...), custom_call_target="tpu_custom_call" | custom-call | flops 805306368 | bytes 6291456 | tf_op jit(solution)/shard_map/scale_upper/pallas_call | solution.py:142
  24.8 0.0 collective-permute-done.2.refs_3_
  24.8 0.2 collective-permute-done.3.refs_4_
  25.0 1.5 %shard_map.65 = bf16[4,96,768]{2,1,0:T(8,128)(2,1)S(1)} custom-call(s32[4]{0:T(128)S(1)} %place.1.pos_ref, s32[2,24]{1,0:T(2,128)S(1)} %bitcast.26, bf16[4,2,2,96,768]{4,3,2,1,0:T(8,128)(2,1)S(1)} %bitcast.22, bf16[2,4,2,96,128]{4,3,2,1,0:T(8,128)(2,1)S(1)} %get-tuple-element.24.refs_0_, bf16[2,4,2,96,128]{4,3,2,1,0:T(8,128)(2,1)S(1)} %collective-permute-done.refs_1_, ...), custom_call_target="tpu_custom_call" | custom-call | flops 603979776 | bytes 4000000 | tf_op jit(solution)/shard_map/pallas_call | solution.py:180
  26.5 2.6 %collective-permute-start.5 = (bf16[4,96,768]{2,1,0:T(8,128)(2,1)S(1)}, bf16[4,96,768]{2,1,0:T(8,128)(2,1)S(1)}, u32[]{:S(2)}, u32[]{:S(2)}) collective-permute-start(bf16[4,96,768]{2,1,0:T(8,128)(2,1)S(1)} %shard_map.65), channel_id=1, source_target_pairs={{0,8},{8,0},{16,24},{24,16},{32,40},{40,32},{48,56},{56,48},{64,72... | collective-permute-start | bytes 1769480 | tf_op jit(solution)/shard_map/ppermute | solution.py:362
  29.1 0.0 collective-permute-done.10.last_ref
  29.1 2.7 %collective-permute-start.11 = (bf16[4,2,96,128]{3,2,1,0:T(8,128)(2,1)S(1)}, bf16[4,2,96,128]{3,2,1,0:T(8,128)(2,1)S(1)}, u32[]{:S(2)}, u32[]{:S(2)}) collective-permute-start(bf16[4,2,96,128]{3,2,1,0:T(8,128)(2,1)S(1)} %slice_bitcast_fusion.3), channel_id=1, source_target_pairs={{0,2},{2,4},{4,6},{6,0},{1,3},{3,5},{5,7},{7,1},{8,10},{10,12},{12... | collective-permute-start | bytes 589832 | tf_op jit(solution)/shard_map/ppermute | solution.py:359
  31.8 0.0 collective-permute-done.9.next_ref
  31.9 0.1 collective-permute-start.12
  32.0 1.4 %shard_map.64.kept_ref = f32[4,96,768]{2,1,0:T(8,128)S(1)} custom-call(s32[4]{0:T(128)S(1)} %place.1.pos_ref, s32[2,24]{1,0:T(2,128)S(1)} %bitcast.27, bf16[4,2,2,96,768]{4,3,2,1,0:T(8,128)(2,1)S(1)} %bitcast.23, bf16[2,4,2,96,128]{4,3,2,1,0:T(8,128)(2,1)S(1)} %get-tuple-element.24.refs_0_, bf16[2,4,2,96,128]{4,3,2,1,0:T(8,128)(2,1)S(1)} %collective-permute-done.refs_1_, ...), custom_call_target="tpu_custom_call" | custom-call | flops 603979776 | bytes 4000000 | tf_op jit(solution)/shard_map/pallas_call | solution.py:180
  33.4 0.0 collective-permute-done.5.got_ref.core_ref
  33.4 0.9 %shard_map.66 = (bf16[96,768]{1,0:T(8,128)(2,1)S(1)}, bf16[96,768]{1,0:T(8,128)(2,1)S(1)}, bf16[96,768]{1,0:T(8,128)(2,1)S(1)}) custom-call(s32[4]{0:T(128)S(1)} %place.1.pos_ref, f32[4,96,768]{2,1,0:T(8,128)S(1)} %shard_map.64.kept_ref, bf16[4,96,768]{2,1,0:T(8,128)(2,1)S(1)} %collective-permute-done.5.got_ref.core_ref), custom_call_target="tpu_custom_call" | custom-call | flops 294912 | bytes 2949120 | tf_op jit(solution)/shard_map/pallas_call | solution.py:285
  34.3 1.8 %shard_map.68.near_ref = f32[2,4,96,768]{3,2,1,0:T(8,128)S(1)} custom-call(s32[4]{0:T(128)S(1)} %place.1.pos_ref, s32[2,24]{1,0:T(2,128)S(1)} %bitcast.28, bf16[4,2,2,96,768]{4,3,2,1,0:T(8,128)(2,1)S(1)} %bitcast.24, bf16[2,4,2,96,128]{4,3,2,1,0:T(8,128)(2,1)S(1)} %get-tuple-element.23.own_ref, ...), custom_call_target="tpu_custom_call" | custom-call | flops 905969664 | bytes 8000000 | tf_op jit(solution)/shard_map/pallas_call | solution.py:235
  36.1 0.0 collective-permute-done.11.right_ref
  36.1 3.2 %collective-permute-done.12.left_ref = bf16[4,2,96,128]{3,2,1,0:T(8,128)(2,1)S(1)} collective-permute-done((bf16[4,2,96,128]{3,2,1,0:T(8,128)(2,1)S(1)}, bf16[4,2,96,128]{3,2,1,0:T(8,128)(2,1)S(1)}, u32[]{:S(2)}, u32[]{:S(2)}) %collective-permute-start.12) | collective-permute-done | bytes 196640 | tf_op jit(solution)/shard_map/ppermute | solution.py:359
  39.3 0.9 %shard_map.70 = bf16[4,96,768]{2,1,0:T(8,128)(2,1)S(1)} custom-call(s32[4]{0:T(128)S(1)} %place.1.pos_ref, s32[2,24]{1,0:T(2,128)S(1)} %bitcast.29, f32[2,4,96,768]{3,2,1,0:T(8,128)S(1)} %shard_map.68.near_ref, bf16[4,2,96,128]{3,2,1,0:T(8,128)(2,1)S(1)} %collective-permute-done.11.right_ref, bf16[4,2,96,128]{3,2,1,0:T(8,128)(2,1)S(1)} %collective-permute-done.12.left_ref, ...), custom_call_target="tpu_custom_call" | custom-call | flops 150994944 | bytes 4000000 | tf_op jit(solution)/shard_map/pallas_call | solution.py:265
  40.3 1.5 %collective-permute-start.13 = (bf16[4,96,768]{2,1,0:T(8,128)(2,1)S(1)}, bf16[4,96,768]{2,1,0:T(8,128)(2,1)S(1)}, u32[]{:S(2)}, u32[]{:S(2)}) collective-permute-start(bf16[4,96,768]{2,1,0:T(8,128)(2,1)S(1)} %shard_map.70), channel_id=1, source_target_pairs={{0,8},{8,0},{16,24},{24,16},{32,40},{40,32},{48,56},{56,48},{64,72... | collective-permute-start | bytes 1769480 | tf_op jit(solution)/shard_map/ppermute | solution.py:362
  41.7 0.0 collective-permute-start.6
  41.7 1.6 %collective-permute-start.8 = (bf16[96,768]{1,0:T(8,128)(2,1)S(1)}, bf16[96,768]{1,0:T(8,128)(2,1)S(1)}, u32[]{:S(2)}, u32[]{:S(2)}) collective-permute-start(bf16[96,768]{1,0:T(8,128)(2,1)S(1)} %get-tuple-element.19._), channel_id=1, source_target_pairs={{0,16},{8,24},{16,0},{24,8},{32,48},{40,56},{48,32},{56,40},{64,80... | collective-permute-start | bytes 442376 | tf_op jit(solution)/shard_map/ppermute | solution.py:362
  43.4 1.2 %collective-permute-start.7 = (bf16[96,768]{1,0:T(8,128)(2,1)S(1)}, bf16[96,768]{1,0:T(8,128)(2,1)S(1)}, u32[]{:S(2)}, u32[]{:S(2)}) collective-permute-start(bf16[96,768]{1,0:T(8,128)(2,1)S(1)} %get-tuple-element.18), channel_id=1, source_target_pairs={{0,48},{8,56},{16,32},{24,40},{32,16},{40,24},{48,0},{56,8},{64,11... | collective-permute-start | bytes 442376 | tf_op jit(solution)/shard_map/ppermute | solution.py:362
  44.5 0.9 %shard_map.69.kept_ref = f32[4,96,768]{2,1,0:T(8,128)S(1)} custom-call(s32[4]{0:T(128)S(1)} %place.1.pos_ref, s32[2,24]{1,0:T(2,128)S(1)} %bitcast.30, f32[2,4,96,768]{3,2,1,0:T(8,128)S(1)} %shard_map.68.near_ref, bf16[4,2,96,128]{3,2,1,0:T(8,128)(2,1)S(1)} %collective-permute-done.11.right_ref, ...), custom_call_target="tpu_custom_call" | custom-call | flops 150994944 | bytes 4000000 | tf_op jit(solution)/shard_map/pallas_call | solution.py:265
  45.5 0.0 collective-permute-done.13.core_ref.got_ref
  45.5 0.9 %shard_map.72 = (bf16[96,768]{1,0:T(8,128)(2,1)S(1)}, bf16[96,768]{1,0:T(8,128)(2,1)S(1)}, bf16[96,768]{1,0:T(8,128)(2,1)S(1)}) custom-call(s32[4]{0:T(128)S(1)} %place.1.pos_ref, f32[4,96,768]{2,1,0:T(8,128)S(1)} %shard_map.69.kept_ref, bf16[4,96,768]{2,1,0:T(8,128)(2,1)S(1)} %collective-permute-done.13.core_ref.got_ref), custom_call_target="tpu_custom_call" | custom-call | flops 294912 | bytes 2949120 | tf_op jit(solution)/shard_map/pallas_call | solution.py:285
  46.4 1.3 %collective-permute-start.14 = (bf16[96,768]{1,0:T(8,128)(2,1)S(1)}, bf16[96,768]{1,0:T(8,128)(2,1)S(1)}, u32[]{:S(2)}, u32[]{:S(2)}) collective-permute-start(bf16[96,768]{1,0:T(8,128)(2,1)S(1)} %get-tuple-element.20), channel_id=1, source_target_pairs={{0,32},{8,40},{16,48},{24,56},{32,0},{40,8},{48,16},{56,24},{64,96... | collective-permute-start | bytes 442376 | tf_op jit(solution)/shard_map/ppermute | solution.py:362
  47.6 2.4 %collective-permute-start.15 = (bf16[96,768]{1,0:T(8,128)(2,1)S(1)}, bf16[96,768]{1,0:T(8,128)(2,1)S(1)}, u32[]{:S(2)}, u32[]{:S(2)}) collective-permute-start(bf16[96,768]{1,0:T(8,128)(2,1)S(1)} %get-tuple-element.21), channel_id=1, source_target_pairs={{0,48},{8,56},{16,32},{24,40},{32,16},{40,24},{48,0},{56,8},{64,11... | collective-permute-start | bytes 442376 | tf_op jit(solution)/shard_map/ppermute | solution.py:362
  50.0 0.0 collective-permute-done.6.refs_0_
  50.0 3.2 %collective-permute-start.16 = (bf16[96,768]{1,0:T(8,128)(2,1)S(1)}, bf16[96,768]{1,0:T(8,128)(2,1)S(1)}, u32[]{:S(2)}, u32[]{:S(2)}) collective-permute-start(bf16[96,768]{1,0:T(8,128)(2,1)S(1)} %get-tuple-element.22), channel_id=1, source_target_pairs={{0,16},{8,24},{16,0},{24,8},{32,48},{40,56},{48,32},{56,40},{64,80... | collective-permute-start | bytes 442376 | tf_op jit(solution)/shard_map/ppermute | solution.py:362
  53.2 11.0 %collective-permute-done.7.refs_1_ = bf16[96,768]{1,0:T(8,128)(2,1)S(1)} collective-permute-done((bf16[96,768]{1,0:T(8,128)(2,1)S(1)}, bf16[96,768]{1,0:T(8,128)(2,1)S(1)}, u32[]{:S(2)}, u32[]{:S(2)}) %collective-permute-start.7) | collective-permute-done | bytes 147488 | tf_op jit(solution)/shard_map/ppermute | solution.py:362
  64.2 0.0 collective-permute-done.8.refs_2_
  64.2 0.8 %shard_map.67.early_ref = f32[96,768]{1,0:T(8,128)S(1)} custom-call(s32[4]{0:T(128)S(1)} %place.1.pos_ref, f32[4,96,768]{2,1,0:T(8,128)S(1)} %shard_map.64.kept_ref, bf16[4,96,768]{2,1,0:T(8,128)(2,1)S(1)} %collective-permute-done.5.got_ref.core_ref, bf16[96,768]{1,0:T(8,128)(2,1)S(1)} %collective-permute-done.6.refs_0_, ...), custom_call_target="tpu_custom_call" | custom-call | flops 221184 | bytes 663552 | tf_op jit(solution)/shard_map/pallas_call | solution.py:306
  65.1 0.6 shard_map.71.own_ref
  65.7 0.0 collective-permute-done.14.refs_0_
  65.7 4.9 %collective-permute-done.15.refs_1_ = bf16[96,768]{1,0:T(8,128)(2,1)S(1)} collective-permute-done((bf16[96,768]{1,0:T(8,128)(2,1)S(1)}, bf16[96,768]{1,0:T(8,128)(2,1)S(1)}, u32[]{:S(2)}, u32[]{:S(2)}) %collective-permute-start.15) | collective-permute-done | bytes 147488 | tf_op jit(solution)/shard_map/ppermute | solution.py:362
  70.6 1.0 %final_sums.1 = f32[1,192,768]{2,1,0:T(8,128)} custom-call(f32[96,768]{1,0:T(8,128)S(1)} %shard_map.67.early_ref, f32[96,768]{1,0:T(8,128)S(1)} %shard_map.71.own_ref, bf16[96,768]{1,0:T(8,128)(2,1)S(1)} %collective-permute-done.14.refs_0_, bf16[96,768]{1,0:T(8,128)(2,1)S(1)} %collective-permute-done.15.refs_1_, ...), custom_call_target="tpu_custom_call" | custom-call | flops 294912 | bytes 884736 | tf_op jit(solution)/shard_map/final_sums/pallas_call | solution.py:328
  (15 shorter events, 0.1 us)
Async XLA Ops:
  1.2 10.1 %collective-permute-start.1 = (bf16[2,4,2,96,128]{4,3,2,1,0:T(8,128)(2,1)S(1)}, bf16[2,4,2,96,128]{4,3,2,1,0:T(8,128)(2,1)S(1)}, u32[]{:S(2)}, u32[]{:S(2)}) collective-permute-start(bf16[2,4,2,96,128]{4,3,2,1,0:T(8,128)(2,1)S(1)} %get-tuple-element.24.refs_0_), channel_id=1, source_target_pairs={{0,2},{2,4},{4,6},{6,0},{1,3},{3,5},{5,7},{7,1},{8,10},{10,12},{12... | collective-permute-start | bytes 1179656 | tf_op jit(solution)/shard_map/ppermute | solution.py:359
  1.5 11.3 %collective-permute-start = (bf16[2,4,2,96,128]{4,3,2,1,0:T(8,128)(2,1)S(1)}, bf16[2,4,2,96,128]{4,3,2,1,0:T(8,128)(2,1)S(1)}, u32[]{:S(2)}, u32[]{:S(2)}) collective-permute-start(bf16[2,4,2,96,128]{4,3,2,1,0:T(8,128)(2,1)S(1)} %get-tuple-element.24.refs_0_), channel_id=1, source_target_pairs={{0,6},{2,0},{4,2},{6,4},{1,7},{3,1},{5,3},{7,5},{8,14},{10,8},{12,... | collective-permute-start | bytes 1179656 | tf_op jit(solution)/shard_map/ppermute | solution.py:359
  2.7 26.4 %collective-permute-start.10 = (bf16[2,4,2,96,128]{4,3,2,1,0:T(8,128)(2,1)S(1)}, bf16[2,4,2,96,128]{4,3,2,1,0:T(8,128)(2,1)S(1)}, u32[]{:S(2)}, u32[]{:S(2)}) collective-permute-start(bf16[2,4,2,96,128]{4,3,2,1,0:T(8,128)(2,1)S(1)} %get-tuple-element.23.own_ref), channel_id=1, source_target_pairs={{0,2},{2,4},{4,6},{6,0},{1,3},{3,5},{5,7},{7,1},{8,10},{10,12},{12... | collective-permute-start | bytes 1179656 | tf_op jit(solution)/shard_map/ppermute | solution.py:359
  4.1 27.7 %collective-permute-start.9 = (bf16[2,4,2,96,128]{4,3,2,1,0:T(8,128)(2,1)S(1)}, bf16[2,4,2,96,128]{4,3,2,1,0:T(8,128)(2,1)S(1)}, u32[]{:S(2)}, u32[]{:S(2)}) collective-permute-start(bf16[2,4,2,96,128]{4,3,2,1,0:T(8,128)(2,1)S(1)} %get-tuple-element.23.own_ref), channel_id=1, source_target_pairs={{0,6},{2,0},{4,2},{6,4},{1,7},{3,1},{5,3},{7,5},{8,14},{10,8},{12,... | collective-permute-start | bytes 1179656 | tf_op jit(solution)/shard_map/ppermute | solution.py:359
  4.2 19.0 %collective-permute-start.4 = (bf16[2,256,768]{2,1,0:T(8,128)(2,1)}, bf16[2,256,768]{2,1,0:T(8,128)(2,1)S(1)}, u32[]{:S(2)}, u32[]{:S(2)}) collective-permute-start(bf16[2,256,768]{2,1,0:T(8,128)(2,1)} %bitcast.32), channel_id=1, source_target_pairs={{0,1},{1,0},{2,3},{3,2},{4,5},{5,4},{6,7},{7,6},{8,9},{9,8},{10,11... | collective-permute-start | bytes 2359304 | tf_op jit(solution)/shard_map/ppermute | solution.py:364
  7.1 6.0 %copy-start.2 = (f32[1,2,512,512]{3,2,1,0:T(8,128)S(1)}, f32[1,2,512,512]{3,2,1,0:T(8,128)}, u32[]{:S(2)}) copy-start(f32[1,2,512,512]{3,2,1,0:T(8,128)} %param.9) | copy-start | bytes 6291460
  7.1 6.0 %copy-start.3 = (bf16[1,2,256,768]{3,2,1,0:T(8,128)(2,1)S(1)}, bf16[1,2,256,768]{3,2,1,0:T(8,128)(2,1)}, u32[]{:S(2)}) copy-start(bf16[1,2,256,768]{3,2,1,0:T(8,128)(2,1)} %param.8) | copy-start | bytes 2359300
  7.1 6.0 %copy-start.4 = (s32[1,2]{1,0:T(1,128)S(1)}, s32[1,2]{1,0:T(1,128)}, u32[]{:S(2)}) copy-start(s32[1,2]{1,0:T(1,128)} %param.11) | copy-start | bytes 28
  11.3 13.5 %collective-permute-start.2 = (bf16[4,2,96,128]{3,2,1,0:T(8,128)(2,1)S(1)}, bf16[4,2,96,128]{3,2,1,0:T(8,128)(2,1)S(1)}, u32[]{:S(2)}, u32[]{:S(2)}) collective-permute-start(bf16[4,2,96,128]{3,2,1,0:T(8,128)(2,1)S(1)} %slice_bitcast_fusion.5), channel_id=1, source_target_pairs={{0,2},{2,4},{4,6},{6,0},{1,3},{3,5},{5,7},{7,1},{8,10},{10,12},{12... | collective-permute-start | bytes 589832 | tf_op jit(solution)/shard_map/ppermute | solution.py:359
  12.8 12.2 %collective-permute-start.3 = (bf16[4,2,96,128]{3,2,1,0:T(8,128)(2,1)S(1)}, bf16[4,2,96,128]{3,2,1,0:T(8,128)(2,1)S(1)}, u32[]{:S(2)}, u32[]{:S(2)}) collective-permute-start(bf16[4,2,96,128]{3,2,1,0:T(8,128)(2,1)S(1)} %slice_bitcast_fusion.4), channel_id=1, source_target_pairs={{0,6},{2,0},{4,2},{6,4},{1,7},{3,1},{5,3},{7,5},{8,14},{10,8},{12,... | collective-permute-start | bytes 589832 | tf_op jit(solution)/shard_map/ppermute | solution.py:359
  13.1 10.1 %copy-start.1 = (s32[1,2,24]{2,1,0:T(2,128)S(1)}, s32[1,2,24]{2,1,0:T(2,128)}, u32[]{:S(2)}) copy-start(s32[1,2,24]{2,1,0:T(2,128)} %param.10) | copy-start | bytes 580
  23.2 1.8 %copy-start = (bf16[1,1536,768]{2,1,0:T(8,128)(2,1)S(1)}, bf16[1,1536,768]{2,1,0:T(8,128)(2,1)}, u32[]{:S(2)}) copy-start(bf16[1,1536,768]{2,1,0:T(8,128)(2,1)} %param.6) | copy-start | bytes 7077892
  26.5 6.9 %collective-permute-start.5 = (bf16[4,96,768]{2,1,0:T(8,128)(2,1)S(1)}, bf16[4,96,768]{2,1,0:T(8,128)(2,1)S(1)}, u32[]{:S(2)}, u32[]{:S(2)}) collective-permute-start(bf16[4,96,768]{2,1,0:T(8,128)(2,1)S(1)} %shard_map.65), channel_id=1, source_target_pairs={{0,8},{8,0},{16,24},{24,16},{32,40},{40,32},{48,56},{56,48},{64,72... | collective-permute-start | bytes 1769480 | tf_op jit(solution)/shard_map/ppermute | solution.py:362
  29.1 6.9 %collective-permute-start.11 = (bf16[4,2,96,128]{3,2,1,0:T(8,128)(2,1)S(1)}, bf16[4,2,96,128]{3,2,1,0:T(8,128)(2,1)S(1)}, u32[]{:S(2)}, u32[]{:S(2)}) collective-permute-start(bf16[4,2,96,128]{3,2,1,0:T(8,128)(2,1)S(1)} %slice_bitcast_fusion.3), channel_id=1, source_target_pairs={{0,2},{2,4},{4,6},{6,0},{1,3},{3,5},{5,7},{7,1},{8,10},{10,12},{12... | collective-permute-start | bytes 589832 | tf_op jit(solution)/shard_map/ppermute | solution.py:359
  31.9 7.4 %collective-permute-start.12 = (bf16[4,2,96,128]{3,2,1,0:T(8,128)(2,1)S(1)}, bf16[4,2,96,128]{3,2,1,0:T(8,128)(2,1)S(1)}, u32[]{:S(2)}, u32[]{:S(2)}) collective-permute-start(bf16[4,2,96,128]{3,2,1,0:T(8,128)(2,1)S(1)} %slice_bitcast_fusion.2), channel_id=1, source_target_pairs={{0,6},{2,0},{4,2},{6,4},{1,7},{3,1},{5,3},{7,5},{8,14},{10,8},{12,... | collective-permute-start | bytes 589832 | tf_op jit(solution)/shard_map/ppermute | solution.py:359
  40.3 5.2 %collective-permute-start.13 = (bf16[4,96,768]{2,1,0:T(8,128)(2,1)S(1)}, bf16[4,96,768]{2,1,0:T(8,128)(2,1)S(1)}, u32[]{:S(2)}, u32[]{:S(2)}) collective-permute-start(bf16[4,96,768]{2,1,0:T(8,128)(2,1)S(1)} %shard_map.70), channel_id=1, source_target_pairs={{0,8},{8,0},{16,24},{24,16},{32,40},{40,32},{48,56},{56,48},{64,72... | collective-permute-start | bytes 1769480 | tf_op jit(solution)/shard_map/ppermute | solution.py:362
  41.7 8.3 %collective-permute-start.6 = (bf16[96,768]{1,0:T(8,128)(2,1)S(1)}, bf16[96,768]{1,0:T(8,128)(2,1)S(1)}, u32[]{:S(2)}, u32[]{:S(2)}) collective-permute-start(bf16[96,768]{1,0:T(8,128)(2,1)S(1)} %get-tuple-element.17), channel_id=1, source_target_pairs={{0,32},{8,40},{16,48},{24,56},{32,0},{40,8},{48,16},{56,24},{64,96... | collective-permute-start | bytes 442376 | tf_op jit(solution)/shard_map/ppermute | solution.py:362
  41.7 22.5 %collective-permute-start.8 = (bf16[96,768]{1,0:T(8,128)(2,1)S(1)}, bf16[96,768]{1,0:T(8,128)(2,1)S(1)}, u32[]{:S(2)}, u32[]{:S(2)}) collective-permute-start(bf16[96,768]{1,0:T(8,128)(2,1)S(1)} %get-tuple-element.19._), channel_id=1, source_target_pairs={{0,16},{8,24},{16,0},{24,8},{32,48},{40,56},{48,32},{56,40},{64,80... | collective-permute-start | bytes 442376 | tf_op jit(solution)/shard_map/ppermute | solution.py:362
  43.4 20.9 %collective-permute-start.7 = (bf16[96,768]{1,0:T(8,128)(2,1)S(1)}, bf16[96,768]{1,0:T(8,128)(2,1)S(1)}, u32[]{:S(2)}, u32[]{:S(2)}) collective-permute-start(bf16[96,768]{1,0:T(8,128)(2,1)S(1)} %get-tuple-element.18), channel_id=1, source_target_pairs={{0,48},{8,56},{16,32},{24,40},{32,16},{40,24},{48,0},{56,8},{64,11... | collective-permute-start | bytes 442376 | tf_op jit(solution)/shard_map/ppermute | solution.py:362
  46.4 19.3 %collective-permute-start.14 = (bf16[96,768]{1,0:T(8,128)(2,1)S(1)}, bf16[96,768]{1,0:T(8,128)(2,1)S(1)}, u32[]{:S(2)}, u32[]{:S(2)}) collective-permute-start(bf16[96,768]{1,0:T(8,128)(2,1)S(1)} %get-tuple-element.20), channel_id=1, source_target_pairs={{0,32},{8,40},{16,48},{24,56},{32,0},{40,8},{48,16},{56,24},{64,96... | collective-permute-start | bytes 442376 | tf_op jit(solution)/shard_map/ppermute | solution.py:362
  47.6 22.9 %collective-permute-start.15 = (bf16[96,768]{1,0:T(8,128)(2,1)S(1)}, bf16[96,768]{1,0:T(8,128)(2,1)S(1)}, u32[]{:S(2)}, u32[]{:S(2)}) collective-permute-start(bf16[96,768]{1,0:T(8,128)(2,1)S(1)} %get-tuple-element.21), channel_id=1, source_target_pairs={{0,48},{8,56},{16,32},{24,40},{32,16},{40,24},{48,0},{56,8},{64,11... | collective-permute-start | bytes 442376 | tf_op jit(solution)/shard_map/ppermute | solution.py:362
  50.0 20.6 %collective-permute-start.16 = (bf16[96,768]{1,0:T(8,128)(2,1)S(1)}, bf16[96,768]{1,0:T(8,128)(2,1)S(1)}, u32[]{:S(2)}, u32[]{:S(2)}) collective-permute-start(bf16[96,768]{1,0:T(8,128)(2,1)S(1)} %get-tuple-element.22), channel_id=1, source_target_pairs={{0,16},{8,24},{16,0},{24,8},{32,48},{40,56},{48,32},{56,40},{64,80... | collective-permute-start | bytes 442376 | tf_op jit(solution)/shard_map/ppermute | solution.py:362

commit v9 on v8

--- a/solution.py
+++ b/solution.py
@@ -37,6 +37,15 @@
 def decode(y):
     y = y.astype(F32)
     return y * jnp.clip(lax.rsqrt(jnp.abs(y) * (1.0 / KNEE)), 1.0, STEEP)
+
+
+def here():
+    layer = lax.axis_index("layer")
+    return layer & 1, lax.axis_index("col"), lax.axis_index("row"), layer >> 1 & 3
+
+
+def masked(tile, mask):
+    return (tile.reshape(-1, *mask.shape) * mask[None]).reshape(tile.shape)
 
 
 def grant(mebibytes):
@@ -118,59 +127,58 @@
     )(widths, pos, systems, upper)
 
 
-def scale_kernel(pos_ref, fill_ref, xh_ref, xl_ref, part_ref, upper_ref, out_ref):
+def scale_kernel(mask_ref, xh_ref, xl_ref, part_ref, upper_ref, out_ref):
     members, order, cols = part_ref.shape
     pieces = order // BLOCK
     blocks = cols // BLOCK
-    col = pos_ref[1]
+    _, col, _, _ = here()
     for s in range(members):
         upper = upper_ref[s]
         scaled = part_ref[s] + (dot(xh_ref[s], upper) + dot(xl_ref[s], upper))
         for j in range(blocks):
-            used = fill_ref[s, col * blocks + j] != 0
             lanes = slice(j * BLOCK, (j + 1) * BLOCK)
-            tile = scaled[:, lanes]
-            tile = jnp.where(used, tile, jnp.zeros_like(tile)).astype(BF16)
+            tile = masked(scaled[:, lanes].astype(BF16), mask_ref[s, col * blocks + j])
             for k in range(pieces):
                 spot = lax.rem(k - col + pieces, pieces)
                 out_ref[s, spot, :, lanes] = tile[k * BLOCK : (k + 1) * BLOCK]
 
 
-def scale_call(pos, fill, xh, xl, part, upper):
+def scale_call(masks, xh, xl, part, upper):
     members, order, half = xh.shape
     cols = upper.shape[2]
     return pl.pallas_call(
         scale_kernel,
-        in_specs=[SMEM, SMEM] + [VMEM] * 4,
+        in_specs=[VMEM] * 5,
         out_specs=VMEM,
         out_shape=jax.ShapeDtypeStruct((members, order // BLOCK, BLOCK, cols), BF16),
         cost_estimate=cost(4 * members * order * half * cols, 8 * members * order * cols),
         name="scale_upper",
         compiler_params=grant(16),
-    )(pos, fill, xh, xl, part, upper)
-
-
-def update_call(flip, chunk, pos, fill, front, lowers, scaled, after):
+    )(masks, xh, xl, part, upper)
+
+
+def update_call(flip, chunk, masks, front, lowers, scaled, after):
     spots, _, _, rows, cols = front.shape
     members = scaled.shape[0]
     order = scaled.shape[1] * scaled.shape[2]
 
-    def update_kernel(pos_ref, fill_ref, front_ref, *refs):
+    def update_kernel(mask_ref, front_ref, *refs):
         own_ref, next_ref, last_ref, *far_refs, scaled_ref, _, out_ref, wide = refs
-        side = 1 - pos_ref[0] if flip else pos_ref[0]
+        core, _, row, _ = here()
+        side = 1 - core if flip else core
         strip = 2 * rows
-        base = pos_ref[2] * (spots * 2 * strip) + side * strip + chunk * rows
+        base = row * (spots * 2 * strip) + side * strip + chunk * rows
         for s in range(members):
             for d in range(spots):
                 for j in range(rows // SUB):
                     spot = lax.div(base + d * 2 * strip + j * SUB, BLOCK)
-                    used = fill_ref[s, spot] != 0
+                    mask = mask_ref[s, spot]
                     spans = (d, side, slice(j * SUB, (j + 1) * SUB))
                     tiles = (own_ref[s, *spans], next_ref[s, *spans], far_refs[s][*spans], last_ref[s, *spans])
                     for k, tile in enumerate(tiles):
                         begin = s * order + k * BLOCK
                         top = d * rows + j * SUB
-                        wide[top : top + SUB, begin : begin + BLOCK] = jnp.where(used, tile, jnp.zeros_like(tile))
+                        wide[top : top + SUB, begin : begin + BLOCK] = masked(tile, mask)
         flat = scaled_ref[...].reshape(members * order, cols)
         update = dot(wide[...], flat).reshape(spots, rows, cols)
         for d in range(spots):
@@ -179,24 +187,24 @@
 
     return pl.pallas_call(
         update_kernel,
-        in_specs=[SMEM, SMEM] + [VMEM] * (len(lowers) + 2) + [ANY],
+        in_specs=[VMEM] * (len(lowers) + 3) + [ANY],
         out_specs=VMEM,
         scratch_shapes=[pltpu.VMEM((spots * rows, members * order), BF16)],
         out_shape=jax.ShapeDtypeStruct((spots, rows, cols), BF16 if flip else F32),
         cost_estimate=cost(2 * spots * rows * members * order * cols, 4000000),
         compiler_params=grant(12),
-    )(pos, fill, front, *lowers, scaled, after)
-
-
-def fill_wide(wide, fill_ref, base, strip, tiles_of, spots, rows, members):
+    )(masks, front, *lowers, scaled, after)
+
+
+def fill_wide(wide, mask_ref, base, strip, tiles_of, spots, rows, members):
     for s in range(members):
         for d in range(spots):
             for j in range(rows // SUB):
                 spot = lax.div(base + d * 2 * strip + j * SUB, BLOCK)
-                used = fill_ref[s, spot] != 0
+                mask = mask_ref[s, spot]
                 top = d * rows + j * SUB
                 for begin, tile in tiles_of(s, d, slice(j * SUB, (j + 1) * SUB)):
-                    wide[top : top + SUB, begin : begin + BLOCK] = jnp.where(used, tile, jnp.zeros_like(tile))
+                    wide[top : top + SUB, begin : begin + BLOCK] = masked(tile, mask)
 
 
 def joined(scaled_ref, piece):
@@ -204,16 +212,17 @@
     return jnp.concatenate([scaled_ref[s, piece] for s in range(members)], axis=0)
 
 
-def near_call(chunk, pos, fill, front, own, following, last, scaled, after):
+def near_call(chunk, masks, front, own, following, last, scaled, after):
     spots, sides, _, rows, cols = front.shape
     members, pieces = scaled.shape[:2]
     double = 2 * BLOCK
 
-    def near_kernel(pos_ref, fill_ref, front_ref, own_ref, next_ref, last_ref, scaled_ref, _, out_ref, wide):
+    def near_kernel(mask_ref, front_ref, own_ref, next_ref, last_ref, scaled_ref, _, out_ref, wide):
         strip = 2 * rows
         ends = joined(scaled_ref, pieces - 1)
+        row = here()[2]
         for side in range(sides):
-            base = pos_ref[2] * (spots * 2 * strip) + side * strip + chunk * rows
+            base = row * (spots * 2 * strip) + side * strip + chunk * rows
 
             def tiles_of(s, d, span):
                 where = (s, d, side, span)
@@ -223,7 +232,7 @@
                     (members * double + s * BLOCK, last_ref[where]),
                 )
 
-            fill_wide(wide, fill_ref, base, strip, tiles_of, spots, rows, members)
+            fill_wide(wide, mask_ref, base, strip, tiles_of, spots, rows, members)
             total = dot(wide[:, members * double :], ends)
             for s in range(members):
                 pair = scaled_ref[s, :2].reshape(double, cols)
@@ -234,29 +243,30 @@
 
     return pl.pallas_call(
         near_kernel,
-        in_specs=[SMEM, SMEM] + [VMEM] * 5 + [ANY],
+        in_specs=[VMEM] * 6 + [ANY],
         out_specs=VMEM,
         scratch_shapes=[pltpu.VMEM((spots * rows, members * 3 * BLOCK), BF16)],
         out_shape=jax.ShapeDtypeStruct((sides, spots, rows, cols), F32),
         cost_estimate=cost(4 * spots * rows * members * 3 * BLOCK * cols, 8000000),
         compiler_params=grant(14),
-    )(pos, fill, front, own, following, last, scaled, after)
-
-
-def far_call(flip, chunk, pos, fill, near, right, left, scaled):
+    )(masks, front, own, following, last, scaled, after)
+
+
+def far_call(flip, chunk, masks, near, right, left, scaled):
     _, spots, rows, cols = near.shape
     members = scaled.shape[0]
 
-    def far_kernel(pos_ref, fill_ref, near_ref, right_ref, left_ref, scaled_ref, out_ref, wide):
-        side = 1 - pos_ref[0] if flip else pos_ref[0]
+    def far_kernel(mask_ref, near_ref, right_ref, left_ref, scaled_ref, out_ref, wide):
+        core, _, row, _ = here()
+        side = 1 - core if flip else core
         strip = 2 * rows
-        base = pos_ref[2] * (spots * 2 * strip) + side * strip + chunk * rows
+        base = row * (spots * 2 * strip) + side * strip + chunk * rows
         far_refs = (right_ref, left_ref)
 
         def tiles_of(s, d, span):
             return ((s * BLOCK, far_refs[s][d, side, span]),)
 
-        fill_wide(wide, fill_ref, base, strip, tiles_of, spots, rows, members)
+        fill_wide(wide, mask_ref, base, strip, tiles_of, spots, rows, members)
         total = dot(wide[...], joined(scaled_ref, 2)).reshape(spots, rows, cols)
         for d in range(spots):
             copy = near_ref[side, d] - total[d]
@@ -264,53 +274,53 @@
 
     return pl.pallas_call(
         far_kernel,
-        in_specs=[SMEM, SMEM] + [VMEM] * 4,
+        in_specs=[VMEM] * 5,
         out_specs=VMEM,
         scratch_shapes=[pltpu.VMEM((spots * rows, members * BLOCK), BF16)],
         out_shape=jax.ShapeDtypeStruct((spots, rows, cols), BF16 if flip else F32),
         cost_estimate=cost(2 * spots * rows * members * BLOCK * cols, 4000000),
         compiler_params=grant(12),
-    )(pos, fill, near, right, left, scaled)
-
-
-def round_kernel(pos_ref, kept_ref, got_ref, *out_refs):
-    place = pos_ref[3]
+    )(masks, near, right, left, scaled)
+
+
+def round_kernel(kept_ref, got_ref, *out_refs):
+    place = here()[3]
     for k, out_ref in enumerate(out_refs):
         spot = lax.bitwise_xor(place, k + 1)
         out_ref[...] = code(kept_ref[spot] + decode(got_ref[spot]))
 
 
-def round_call(pos, kept, got):
+def round_call(kept, got):
     spots, rows, cols = kept.shape
     return pl.pallas_call(
         round_kernel,
-        in_specs=[SMEM, VMEM, VMEM],
+        in_specs=[VMEM, VMEM],
         out_specs=[VMEM] * (spots - 1),
         out_shape=[jax.ShapeDtypeStruct((rows, cols), BF16)] * (spots - 1),
         cost_estimate=cost(spots * rows * cols, 10 * spots * rows * cols),
         compiler_params=grant(8),
-    )(pos, kept, got)
-
-
-def chunk_kernel(pos_ref, kept_ref, core_ref, *refs):
+    )(kept, got)
+
+
+def chunk_kernel(kept_ref, core_ref, *refs):
     *got_refs, out_ref = refs
-    place = pos_ref[3]
+    place = here()[3]
     total = kept_ref[place] + decode(core_ref[place])
     for ref in got_refs:
         total = total + decode(ref[...])
     out_ref[...] = total
 
 
-def chunk_call(pos, kept, core, parts):
+def chunk_call(kept, core, parts):
     _, rows, cols = kept.shape
     return pl.pallas_call(
         chunk_kernel,
-        in_specs=[SMEM] + [VMEM] * (len(parts) + 2),
+        in_specs=[VMEM] * (len(parts) + 2),
         out_specs=VMEM,
         out_shape=jax.ShapeDtypeStruct((rows, cols), F32),
         cost_estimate=cost(len(parts) * rows * cols, 3 * len(parts) * rows * cols),
         compiler_params=grant(8),
-    )(pos, kept, core, *parts)
+    )(kept, core, *parts)
 
 
 def final_kernel(early_ref, own_ref, *refs):
@@ -348,6 +358,7 @@
     ).astype(jnp.int32)
     pos = place_call(pos)
     upper, fill, width_vec = upper_panels[0], block_fill[0], widths[0]
+    masks = jnp.broadcast_to(fill.astype(BF16)[:, :, None, None], (*fill.shape, 16, BLOCK))
     row_count, cols = front_copies.shape[1:]
     members = upper.shape[0]
     spots = 4
@@ -369,28 +380,28 @@
         right, left = shift(last[0], 1), shift(following[1], -1)
         lowers.append((own, following, last, right, left))
     xh, xl, part = inverse_call(width_vec, pos, diag_blocks[0], upper)
-    scaled = scale_call(pos, fill, xh, xl, part, other_upper)
+    scaled = scale_call(masks, xh, xl, part, other_upper)
     sums = []
     after = scaled
     for chunk in range(2):
         if chunk == 0:
-            sent = update_call(True, chunk, pos, fill, front, lowers[chunk], scaled, after)
+            sent = update_call(True, chunk, masks, front, lowers[chunk], scaled, after)
         else:
             *near, right, left = lowers[chunk]
-            near = near_call(chunk, pos, fill, front, *near, scaled, after)
-            sent = far_call(True, chunk, pos, fill, near, right, left, scaled)
+            near = near_call(chunk, masks, front, *near, scaled, after)
+            sent = far_call(True, chunk, masks, near, right, left, scaled)
         core = across(sent, 1)
         if chunk == 0:
-            kept = update_call(False, chunk, pos, fill, front, lowers[chunk], scaled, after)
+            kept = update_call(False, chunk, masks, front, lowers[chunk], scaled, after)
         else:
-            kept = far_call(False, chunk, pos, fill, near, right, left, scaled)
-        one, two, three = round_call(pos, kept, core)
+            kept = far_call(False, chunk, masks, near, right, left, scaled)
+        one, two, three = round_call(kept, core)
         after = one
         parts = [across(two, 4), across(three, 6), across(one, 2)]
         if chunk == 0:
-            sums.append(chunk_call(pos, kept, core, parts))
+            sums.append(chunk_call(kept, core, parts))
         else:
-            sums += [chunk_call(pos, kept, core, []), *parts]
+            sums += [chunk_call(kept, core, []), *parts]
     return final_call(sums[0], sums[1:])
 
 

time: 71.7 us -> 70.6 us (0.985)
  the two profiles are of different devices: /device:TPU:71 before, /device:TPU:79 now
where the time goes in v9:
time: 70.6 us; the launch traced here: 70.4 us
  waiting for transfers between devices  26.6 us (38%)
  starting transfers between devices  25.6 us (36%)
  Pallas kernels  15.8 us (22%)
  local copies, waits for them, and re-layouts  2.26 us (3%)
    ppermute x8, waiting for transfers between devices, across(): return lax.ppermute(block, 'layer', [(i, i ^ flip) for i in range(layers)])  16.9 us
    ppermute x8, starting transfers between devices, across(): return lax.ppermute(block, 'layer', [(i, i ^ flip) for i in range(layers)])  15.2 us
    ppermute x8, starting transfers between devices, shift(): lax.ppermute(block, 'col', [(i, (i + step) % col_devices) for i in range(...  8.34 us
    pallas_call x1, Pallas kernels, inverse_call(): pl.pallas_call(inverse_kernel, in_specs=[SMEM, SMEM, VMEM, VMEM], out_spe...  7.83 us
    ppermute x8, waiting for transfers between devices, shift(): lax.ppermute(block, 'col', [(i, (i + step) % col_devices) for i in range(...  5.27 us
    ppermute x1, waiting for transfers between devices, on_device(): other_upper = lax.ppermute(upper, 'row', [(0, 1), (1, 0)])  4.35 us
    ppermute x1, starting transfers between devices, on_device(): other_upper = lax.ppermute(upper, 'row', [(0, 1), (1, 0)])  2.01 us
    pallas_call x2, Pallas kernels, update_call(): pl.pallas_call(update_kernel, in_specs=[VMEM] * (len(lowers) + 3) + [ANY]...  1.74 us
  transfers between devices with their start and end apart: 17, of which 6 were waited for; matrix products, arithmetic and copies ran while one was open for 0% of the time, Pallas kernels for 20%

profile of v9, /device:TPU:79, one launch (start us, length us, event | category | flops | bytes accessed | tf_op | source)
XLA Modules:
  0.0 70.4 jit_solution(7465162375127731758)
XLA Ops:
  0.0 1.2 %slice_bitcast_fusion = (bf16[2,4,2,96,128]{4,3,2,1,0:T(8,128)(2,1)S(1)}, bf16[2,4,2,96,128]{4,3,2,1,0:T(8,128)(2,1)S(1)}) fusion(bf16[2,4,2,2,96,128]{5,4,3,2,1,0:T(8,128)(2,1)} %bitcast.30), kind=kLoop, calls=%fused_computation | loop fusion | bytes 1572864 | tf_op jit(solution)/shard_map/squeeze | solution.py:378
  1.2 0.3 collective-permute-start.1
  1.5 1.3 %collective-permute-start = (bf16[2,4,2,96,128]{4,3,2,1,0:T(8,128)(2,1)S(1)}, bf16[2,4,2,96,128]{4,3,2,1,0:T(8,128)(2,1)S(1)}, u32[]{:S(2)}, u32[]{:S(2)}) collective-permute-start(bf16[2,4,2,96,128]{4,3,2,1,0:T(8,128)(2,1)S(1)} %get-tuple-element.24.refs_0_), channel_id=1, source_target_pairs={{0,6},{2,0},{4,2},{6,4},{1,7},{3,1},{5,3},{7,5},{8,14},{10,8},{12,... | collective-permute-start | bytes 1179656 | tf_op jit(solution)/shard_map/ppermute | solution.py:370
  2.7 1.4 %collective-permute-start.10 = (bf16[2,4,2,96,128]{4,3,2,1,0:T(8,128)(2,1)S(1)}, bf16[2,4,2,96,128]{4,3,2,1,0:T(8,128)(2,1)S(1)}, u32[]{:S(2)}, u32[]{:S(2)}) collective-permute-start(bf16[2,4,2,96,128]{4,3,2,1,0:T(8,128)(2,1)S(1)} %get-tuple-element.23.own_ref), channel_id=1, source_target_pairs={{0,2},{2,4},{4,6},{6,0},{1,3},{3,5},{5,7},{7,1},{8,10},{10,12},{12... | collective-permute-start | bytes 1179656 | tf_op jit(solution)/shard_map/ppermute | solution.py:370
  4.1 0.1 collective-permute-start.9
  4.2 2.0 %collective-permute-start.4 = (bf16[2,256,768]{2,1,0:T(8,128)(2,1)}, bf16[2,256,768]{2,1,0:T(8,128)(2,1)S(1)}, u32[]{:S(2)}, u32[]{:S(2)}) collective-permute-start(bf16[2,256,768]{2,1,0:T(8,128)(2,1)} %bitcast.27), channel_id=1, source_target_pairs={{0,1},{1,0},{2,3},{3,2},{4,5},{5,4},{6,7},{7,6},{8,9},{9,8},{10,11... | collective-permute-start | bytes 2359304 | tf_op jit(solution)/shard_map/ppermute | solution.py:375
  6.2 0.0 copy-start.3
  6.2 1.1 %place.1.pos_ref = s32[4]{0:T(128)S(1)} custom-call(s32[4]{0:T(128)S(1)} %compare_select_fusion.2.in_ref), custom_call_target="tpu_custom_call" | custom-call | flops 10000000000 | bytes 10000000 | tf_op jit(solution)/shard_map/place/pallas_call | solution.py:71
  7.4 0.4 copy-done.1
  7.8 0.2 copy-done.2
  8.0 7.8 %inverse.1 = (bf16[2,512,256]{2,1,0:T(8,128)(2,1)S(1)}, bf16[2,512,256]{2,1,0:T(8,128)(2,1)S(1)}, f32[2,512,768]{2,1,0:T(8,128)S(1)}) custom-call(s32[2]{0:T(128)S(1)} %bitcast.29, s32[4]{0:T(128)S(1)} %place.1.pos_ref, f32[2,512,512]{2,1,0:T(8,128)S(1)} %bitcast.26, bf16[2,256,768]{2,1,0:T(8,128)(2,1)S(1)} %bitcast.28), custom_call_target="tpu_custom_call" | custom-call | flops 3758096384 | bytes 8000000 | tf_op jit(solution)/shard_map/inverse/pallas_call | solution.py:115
  15.8 0.0 collective-permute-done.1.refs_2_
  15.8 2.7 %collective-permute-start.2 = (bf16[4,2,96,128]{3,2,1,0:T(8,128)(2,1)S(1)}, bf16[4,2,96,128]{3,2,1,0:T(8,128)(2,1)S(1)}, u32[]{:S(2)}, u32[]{:S(2)}) collective-permute-start(bf16[4,2,96,128]{3,2,1,0:T(8,128)(2,1)S(1)} %slice_bitcast_fusion.5), channel_id=1, source_target_pairs={{0,2},{2,4},{4,6},{6,0},{1,3},{3,5},{5,7},{7,1},{8,10},{10,12},{12... | collective-permute-start | bytes 589832 | tf_op jit(solution)/shard_map/ppermute | solution.py:370
  18.5 0.0 collective-permute-done.refs_1_
  18.6 0.3 collective-permute-start.3
  18.9 4.3 %collective-permute-done.4.upper_ref = bf16[2,256,768]{2,1,0:T(8,128)(2,1)S(1)} collective-permute-done((bf16[2,256,768]{2,1,0:T(8,128)(2,1)}, bf16[2,256,768]{2,1,0:T(8,128)(2,1)S(1)}, u32[]{:S(2)}, u32[]{:S(2)}) %collective-permute-start.4) | collective-permute-done | bytes 786464 | tf_op jit(solution)/shard_map/ppermute | solution.py:375
  23.2 0.1 broadcast_in_dim.21.mask_ref
  23.3 0.0 copy-start
  23.3 1.0 %scale_upper.1.refs_5_.refs_6_.scaled_ref = bf16[2,4,128,768]{3,2,1,0:T(8,128)(2,1)S(1)} custom-call(bf16[2,24,16,128]{3,2,1,0:T(8,128)(2,1)S(1)} %broadcast_in_dim.21.mask_ref, bf16[2,512,256]{2,1,0:T(8,128)(2,1)S(1)} %get-tuple-element.14.xh_ref, bf16[2,512,256]{2,1,0:T(8,128)(2,1)S(1)} %get-tuple-element.15.xl_ref, ...), custom_call_target="tpu_custom_call" | custom-call | flops 805306368 | bytes 6291456 | tf_op jit(solution)/shard_map/scale_upper/pallas_call | solution.py:149
  24.3 0.0 collective-permute-done.2.refs_3_
  24.3 0.3 collective-permute-done.3.refs_4_
  24.7 0.3 copy-done
  25.0 0.9 %shard_map.65 = bf16[4,96,768]{2,1,0:T(8,128)(2,1)S(1)} custom-call(bf16[2,24,16,128]{3,2,1,0:T(8,128)(2,1)S(1)} %broadcast_in_dim.21.mask_ref, bf16[4,2,2,96,768]{4,3,2,1,0:T(8,128)(2,1)S(1)} %bitcast.23, bf16[2,4,2,96,128]{4,3,2,1,0:T(8,128)(2,1)S(1)} %get-tuple-element.24.refs_0_, bf16[2,4,2,96,128]{4,3,2,1,0:T(8,128)(2,1)S(1)} %collective-permute-done.refs_1_, ...), custom_call_target="tpu_custom_call" | custom-call | flops 603979776 | bytes 4000000 | tf_op jit(solution)/shard_map/pallas_call | solution.py:188
  25.9 3.2 %collective-permute-start.5 = (bf16[4,96,768]{2,1,0:T(8,128)(2,1)S(1)}, bf16[4,96,768]{2,1,0:T(8,128)(2,1)S(1)}, u32[]{:S(2)}, u32[]{:S(2)}) collective-permute-start(bf16[4,96,768]{2,1,0:T(8,128)(2,1)S(1)} %shard_map.65), channel_id=1, source_target_pairs={{0,8},{8,0},{16,24},{24,16},{32,40},{40,32},{48,56},{56,48},{64,72... | collective-permute-start | bytes 1769480 | tf_op jit(solution)/shard_map/ppermute | solution.py:373
  29.1 2.3 %collective-permute-start.11 = (bf16[4,2,96,128]{3,2,1,0:T(8,128)(2,1)S(1)}, bf16[4,2,96,128]{3,2,1,0:T(8,128)(2,1)S(1)}, u32[]{:S(2)}, u32[]{:S(2)}) collective-permute-start(bf16[4,2,96,128]{3,2,1,0:T(8,128)(2,1)S(1)} %slice_bitcast_fusion.3), channel_id=1, source_target_pairs={{0,2},{2,4},{4,6},{6,0},{1,3},{3,5},{5,7},{7,1},{8,10},{10,12},{12... | collective-permute-start | bytes 589832 | tf_op jit(solution)/shard_map/ppermute | solution.py:370
  31.4 0.1 collective-permute-start.12
  31.5 0.8 %shard_map.64.kept_ref = f32[4,96,768]{2,1,0:T(8,128)S(1)} custom-call(bf16[2,24,16,128]{3,2,1,0:T(8,128)(2,1)S(1)} %broadcast_in_dim.21.mask_ref, bf16[4,2,2,96,768]{4,3,2,1,0:T(8,128)(2,1)S(1)} %bitcast.24, bf16[2,4,2,96,128]{4,3,2,1,0:T(8,128)(2,1)S(1)} %get-tuple-element.24.refs_0_, bf16[2,4,2,96,128]{4,3,2,1,0:T(8,128)(2,1)S(1)} %collective-permute-done.refs_1_, ...), custom_call_target="tpu_custom_call" | custom-call | flops 603979776 | bytes 4000000 | tf_op jit(solution)/shard_map/pallas_call | solution.py:188
  32.3 0.0 collective-permute-done.5.got_ref.core_ref
  32.4 0.4 shard_map.66
  32.7 1.2 %shard_map.68.near_ref = f32[2,4,96,768]{3,2,1,0:T(8,128)S(1)} custom-call(bf16[2,24,16,128]{3,2,1,0:T(8,128)(2,1)S(1)} %broadcast_in_dim.21.mask_ref, bf16[4,2,2,96,768]{4,3,2,1,0:T(8,128)(2,1)S(1)} %bitcast.25, bf16[2,4,2,96,128]{4,3,2,1,0:T(8,128)(2,1)S(1)} %get-tuple-element.23.own_ref, bf16[2,4,2,96,128]{4,3,2,1,0:T(8,128)(2,1)S(1)} %collective-permute-done.9.next_ref, ...), custom_call_target="tpu_custom_call" | custom-call | flops 905969664 | bytes 8000000 | tf_op jit(solution)/shard_map/pallas_call | solution.py:244
  33.9 1.7 %collective-permute-done.11.right_ref = bf16[4,2,96,128]{3,2,1,0:T(8,128)(2,1)S(1)} collective-permute-done((bf16[4,2,96,128]{3,2,1,0:T(8,128)(2,1)S(1)}, bf16[4,2,96,128]{3,2,1,0:T(8,128)(2,1)S(1)}, u32[]{:S(2)}, u32[]{:S(2)}) %collective-permute-start.11) | collective-permute-done | bytes 196640 | tf_op jit(solution)/shard_map/ppermute | solution.py:370
  35.6 3.2 %collective-permute-done.12.left_ref = bf16[4,2,96,128]{3,2,1,0:T(8,128)(2,1)S(1)} collective-permute-done((bf16[4,2,96,128]{3,2,1,0:T(8,128)(2,1)S(1)}, bf16[4,2,96,128]{3,2,1,0:T(8,128)(2,1)S(1)}, u32[]{:S(2)}, u32[]{:S(2)}) %collective-permute-start.12) | collective-permute-done | bytes 196640 | tf_op jit(solution)/shard_map/ppermute | solution.py:370
  38.8 0.4 shard_map.70
  39.3 1.3 %collective-permute-start.13 = (bf16[4,96,768]{2,1,0:T(8,128)(2,1)S(1)}, bf16[4,96,768]{2,1,0:T(8,128)(2,1)S(1)}, u32[]{:S(2)}, u32[]{:S(2)}) collective-permute-start(bf16[4,96,768]{2,1,0:T(8,128)(2,1)S(1)} %shard_map.70), channel_id=1, source_target_pairs={{0,8},{8,0},{16,24},{24,16},{32,40},{40,32},{48,56},{56,48},{64,72... | collective-permute-start | bytes 1769480 | tf_op jit(solution)/shard_map/ppermute | solution.py:373
  40.5 0.0 collective-permute-start.6
  40.5 1.6 %collective-permute-start.8 = (bf16[96,768]{1,0:T(8,128)(2,1)S(1)}, bf16[96,768]{1,0:T(8,128)(2,1)S(1)}, u32[]{:S(2)}, u32[]{:S(2)}) collective-permute-start(bf16[96,768]{1,0:T(8,128)(2,1)S(1)} %get-tuple-element.19._), channel_id=1, source_target_pairs={{0,16},{8,24},{16,0},{24,8},{32,48},{40,56},{48,32},{56,40},{64,80... | collective-permute-start | bytes 442376 | tf_op jit(solution)/shard_map/ppermute | solution.py:373
  42.1 1.2 %collective-permute-start.7 = (bf16[96,768]{1,0:T(8,128)(2,1)S(1)}, bf16[96,768]{1,0:T(8,128)(2,1)S(1)}, u32[]{:S(2)}, u32[]{:S(2)}) collective-permute-start(bf16[96,768]{1,0:T(8,128)(2,1)S(1)} %get-tuple-element.18), channel_id=1, source_target_pairs={{0,48},{8,56},{16,32},{24,40},{32,16},{40,24},{48,0},{56,8},{64,11... | collective-permute-start | bytes 442376 | tf_op jit(solution)/shard_map/ppermute | solution.py:373
  43.3 0.3 shard_map.69.kept_ref
  43.7 0.0 collective-permute-done.13.core_ref.got_ref
  43.7 0.4 shard_map.72
  44.0 1.3 %collective-permute-start.14 = (bf16[96,768]{1,0:T(8,128)(2,1)S(1)}, bf16[96,768]{1,0:T(8,128)(2,1)S(1)}, u32[]{:S(2)}, u32[]{:S(2)}) collective-permute-start(bf16[96,768]{1,0:T(8,128)(2,1)S(1)} %get-tuple-element.20), channel_id=1, source_target_pairs={{0,32},{8,40},{16,48},{24,56},{32,0},{40,8},{48,16},{56,24},{64,96... | collective-permute-start | bytes 442376 | tf_op jit(solution)/shard_map/ppermute | solution.py:373
  45.3 2.4 %collective-permute-start.15 = (bf16[96,768]{1,0:T(8,128)(2,1)S(1)}, bf16[96,768]{1,0:T(8,128)(2,1)S(1)}, u32[]{:S(2)}, u32[]{:S(2)}) collective-permute-start(bf16[96,768]{1,0:T(8,128)(2,1)S(1)} %get-tuple-element.21), channel_id=1, source_target_pairs={{0,48},{8,56},{16,32},{24,40},{32,16},{40,24},{48,0},{56,8},{64,11... | collective-permute-start | bytes 442376 | tf_op jit(solution)/shard_map/ppermute | solution.py:373
  47.7 4.4 %collective-permute-start.16 = (bf16[96,768]{1,0:T(8,128)(2,1)S(1)}, bf16[96,768]{1,0:T(8,128)(2,1)S(1)}, u32[]{:S(2)}, u32[]{:S(2)}) collective-permute-start(bf16[96,768]{1,0:T(8,128)(2,1)S(1)} %get-tuple-element.22), channel_id=1, source_target_pairs={{0,16},{8,24},{16,0},{24,8},{32,48},{40,56},{48,32},{56,40},{64,80... | collective-permute-start | bytes 442376 | tf_op jit(solution)/shard_map/ppermute | solution.py:373
  52.0 11.0 %collective-permute-done.7.refs_1_ = bf16[96,768]{1,0:T(8,128)(2,1)S(1)} collective-permute-done((bf16[96,768]{1,0:T(8,128)(2,1)S(1)}, bf16[96,768]{1,0:T(8,128)(2,1)S(1)}, u32[]{:S(2)}, u32[]{:S(2)}) %collective-permute-start.7) | collective-permute-done | bytes 147488 | tf_op jit(solution)/shard_map/ppermute | solution.py:373
  63.0 0.3 shard_map.67.early_ref
  63.3 0.1 shard_map.71.own_ref
  63.4 5.9 %collective-permute-done.15.refs_1_ = bf16[96,768]{1,0:T(8,128)(2,1)S(1)} collective-permute-done((bf16[96,768]{1,0:T(8,128)(2,1)S(1)}, bf16[96,768]{1,0:T(8,128)(2,1)S(1)}, u32[]{:S(2)}, u32[]{:S(2)}) %collective-permute-start.15) | collective-permute-done | bytes 147488 | tf_op jit(solution)/shard_map/ppermute | solution.py:373
  69.4 1.0 %final_sums.1 = f32[1,192,768]{2,1,0:T(8,128)} custom-call(f32[96,768]{1,0:T(8,128)S(1)} %shard_map.67.early_ref, f32[96,768]{1,0:T(8,128)S(1)} %shard_map.71.own_ref, bf16[96,768]{1,0:T(8,128)(2,1)S(1)} %collective-permute-done.14.refs_0_, bf16[96,768]{1,0:T(8,128)(2,1)S(1)} %collective-permute-done.15.refs_1_, ...), custom_call_target="tpu_custom_call" | custom-call | flops 294912 | bytes 884736 | tf_op jit(solution)/shard_map/final_sums/pallas_call | solution.py:338
  (17 shorter events, 0.1 us)
Async XLA Ops:
  1.2 14.6 %collective-permute-start.1 = (bf16[2,4,2,96,128]{4,3,2,1,0:T(8,128)(2,1)S(1)}, bf16[2,4,2,96,128]{4,3,2,1,0:T(8,128)(2,1)S(1)}, u32[]{:S(2)}, u32[]{:S(2)}) collective-permute-start(bf16[2,4,2,96,128]{4,3,2,1,0:T(8,128)(2,1)S(1)} %get-tuple-element.24.refs_0_), channel_id=1, source_target_pairs={{0,2},{2,4},{4,6},{6,0},{1,3},{3,5},{5,7},{7,1},{8,10},{10,12},{12... | collective-permute-start | bytes 1179656 | tf_op jit(solution)/shard_map/ppermute | solution.py:370
  1.5 17.1 %collective-permute-start = (bf16[2,4,2,96,128]{4,3,2,1,0:T(8,128)(2,1)S(1)}, bf16[2,4,2,96,128]{4,3,2,1,0:T(8,128)(2,1)S(1)}, u32[]{:S(2)}, u32[]{:S(2)}) collective-permute-start(bf16[2,4,2,96,128]{4,3,2,1,0:T(8,128)(2,1)S(1)} %get-tuple-element.24.refs_0_), channel_id=1, source_target_pairs={{0,6},{2,0},{4,2},{6,4},{1,7},{3,1},{5,3},{7,5},{8,14},{10,8},{12,... | collective-permute-start | bytes 1179656 | tf_op jit(solution)/shard_map/ppermute | solution.py:370
  2.7 26.4 %collective-permute-start.10 = (bf16[2,4,2,96,128]{4,3,2,1,0:T(8,128)(2,1)S(1)}, bf16[2,4,2,96,128]{4,3,2,1,0:T(8,128)(2,1)S(1)}, u32[]{:S(2)}, u32[]{:S(2)}) collective-permute-start(bf16[2,4,2,96,128]{4,3,2,1,0:T(8,128)(2,1)S(1)} %get-tuple-element.23.own_ref), channel_id=1, source_target_pairs={{0,2},{2,4},{4,6},{6,0},{1,3},{3,5},{5,7},{7,1},{8,10},{10,12},{12... | collective-permute-start | bytes 1179656 | tf_op jit(solution)/shard_map/ppermute | solution.py:370
  4.1 27.3 %collective-permute-start.9 = (bf16[2,4,2,96,128]{4,3,2,1,0:T(8,128)(2,1)S(1)}, bf16[2,4,2,96,128]{4,3,2,1,0:T(8,128)(2,1)S(1)}, u32[]{:S(2)}, u32[]{:S(2)}) collective-permute-start(bf16[2,4,2,96,128]{4,3,2,1,0:T(8,128)(2,1)S(1)} %get-tuple-element.23.own_ref), channel_id=1, source_target_pairs={{0,6},{2,0},{4,2},{6,4},{1,7},{3,1},{5,3},{7,5},{8,14},{10,8},{12,... | collective-permute-start | bytes 1179656 | tf_op jit(solution)/shard_map/ppermute | solution.py:370
  4.2 19.0 %collective-permute-start.4 = (bf16[2,256,768]{2,1,0:T(8,128)(2,1)}, bf16[2,256,768]{2,1,0:T(8,128)(2,1)S(1)}, u32[]{:S(2)}, u32[]{:S(2)}) collective-permute-start(bf16[2,256,768]{2,1,0:T(8,128)(2,1)} %bitcast.27), channel_id=1, source_target_pairs={{0,1},{1,0},{2,3},{3,2},{4,5},{5,4},{6,7},{7,6},{8,9},{9,8},{10,11... | collective-permute-start | bytes 2359304 | tf_op jit(solution)/shard_map/ppermute | solution.py:375
  6.2 1.6 %copy-start.1 = (f32[1,2,512,512]{3,2,1,0:T(8,128)S(1)}, f32[1,2,512,512]{3,2,1,0:T(8,128)}, u32[]{:S(2)}) copy-start(f32[1,2,512,512]{3,2,1,0:T(8,128)} %param.9) | copy-start | bytes 6291460
  6.2 1.8 %copy-start.2 = (bf16[1,2,256,768]{3,2,1,0:T(8,128)(2,1)S(1)}, bf16[1,2,256,768]{3,2,1,0:T(8,128)(2,1)}, u32[]{:S(2)}) copy-start(bf16[1,2,256,768]{3,2,1,0:T(8,128)(2,1)} %param.8) | copy-start | bytes 2359300
  6.2 1.8 %copy-start.3 = (s32[1,2]{1,0:T(1,128)S(1)}, s32[1,2]{1,0:T(1,128)}, u32[]{:S(2)}) copy-start(s32[1,2]{1,0:T(1,128)} %param.11) | copy-start | bytes 28
  8.0 10.9 %copy-start.4 = (s32[1,2,24]{2,1,0:T(2,128)S(1)}, s32[1,2,24]{2,1,0:T(2,128)}, u32[]{:S(2)}) copy-start(s32[1,2,24]{2,1,0:T(2,128)} %param.10) | copy-start | bytes 580
  15.8 8.5 %collective-permute-start.2 = (bf16[4,2,96,128]{3,2,1,0:T(8,128)(2,1)S(1)}, bf16[4,2,96,128]{3,2,1,0:T(8,128)(2,1)S(1)}, u32[]{:S(2)}, u32[]{:S(2)}) collective-permute-start(bf16[4,2,96,128]{3,2,1,0:T(8,128)(2,1)S(1)} %slice_bitcast_fusion.5), channel_id=1, source_target_pairs={{0,2},{2,4},{4,6},{6,0},{1,3},{3,5},{5,7},{7,1},{8,10},{10,12},{12... | collective-permute-start | bytes 589832 | tf_op jit(solution)/shard_map/ppermute | solution.py:370
  18.6 6.1 %collective-permute-start.3 = (bf16[4,2,96,128]{3,2,1,0:T(8,128)(2,1)S(1)}, bf16[4,2,96,128]{3,2,1,0:T(8,128)(2,1)S(1)}, u32[]{:S(2)}, u32[]{:S(2)}) collective-permute-start(bf16[4,2,96,128]{3,2,1,0:T(8,128)(2,1)S(1)} %slice_bitcast_fusion.4), channel_id=1, source_target_pairs={{0,6},{2,0},{4,2},{6,4},{1,7},{3,1},{5,3},{7,5},{8,14},{10,8},{12,... | collective-permute-start | bytes 589832 | tf_op jit(solution)/shard_map/ppermute | solution.py:370
  23.3 1.7 %copy-start = (bf16[1,1536,768]{2,1,0:T(8,128)(2,1)S(1)}, bf16[1,1536,768]{2,1,0:T(8,128)(2,1)}, u32[]{:S(2)}) copy-start(bf16[1,1536,768]{2,1,0:T(8,128)(2,1)} %param.6) | copy-start | bytes 7077892
  25.9 6.4 %collective-permute-start.5 = (bf16[4,96,768]{2,1,0:T(8,128)(2,1)S(1)}, bf16[4,96,768]{2,1,0:T(8,128)(2,1)S(1)}, u32[]{:S(2)}, u32[]{:S(2)}) collective-permute-start(bf16[4,96,768]{2,1,0:T(8,128)(2,1)S(1)} %shard_map.65), channel_id=1, source_target_pairs={{0,8},{8,0},{16,24},{24,16},{32,40},{40,32},{48,56},{56,48},{64,72... | collective-permute-start | bytes 1769480 | tf_op jit(solution)/shard_map/ppermute | solution.py:373
  29.1 6.5 %collective-permute-start.11 = (bf16[4,2,96,128]{3,2,1,0:T(8,128)(2,1)S(1)}, bf16[4,2,96,128]{3,2,1,0:T(8,128)(2,1)S(1)}, u32[]{:S(2)}, u32[]{:S(2)}) collective-permute-start(bf16[4,2,96,128]{3,2,1,0:T(8,128)(2,1)S(1)} %slice_bitcast_fusion.3), channel_id=1, source_target_pairs={{0,2},{2,4},{4,6},{6,0},{1,3},{3,5},{5,7},{7,1},{8,10},{10,12},{12... | collective-permute-start | bytes 589832 | tf_op jit(solution)/shard_map/ppermute | solution.py:370
  31.4 7.4 %collective-permute-start.12 = (bf16[4,2,96,128]{3,2,1,0:T(8,128)(2,1)S(1)}, bf16[4,2,96,128]{3,2,1,0:T(8,128)(2,1)S(1)}, u32[]{:S(2)}, u32[]{:S(2)}) collective-permute-start(bf16[4,2,96,128]{3,2,1,0:T(8,128)(2,1)S(1)} %slice_bitcast_fusion.2), channel_id=1, source_target_pairs={{0,6},{2,0},{4,2},{6,4},{1,7},{3,1},{5,3},{7,5},{8,14},{10,8},{12,... | collective-permute-start | bytes 589832 | tf_op jit(solution)/shard_map/ppermute | solution.py:370
  39.3 4.4 %collective-permute-start.13 = (bf16[4,96,768]{2,1,0:T(8,128)(2,1)S(1)}, bf16[4,96,768]{2,1,0:T(8,128)(2,1)S(1)}, u32[]{:S(2)}, u32[]{:S(2)}) collective-permute-start(bf16[4,96,768]{2,1,0:T(8,128)(2,1)S(1)} %shard_map.70), channel_id=1, source_target_pairs={{0,8},{8,0},{16,24},{24,16},{32,40},{40,32},{48,56},{56,48},{64,72... | collective-permute-start | bytes 1769480 | tf_op jit(solution)/shard_map/ppermute | solution.py:373
  40.5 7.2 %collective-permute-start.6 = (bf16[96,768]{1,0:T(8,128)(2,1)S(1)}, bf16[96,768]{1,0:T(8,128)(2,1)S(1)}, u32[]{:S(2)}, u32[]{:S(2)}) collective-permute-start(bf16[96,768]{1,0:T(8,128)(2,1)S(1)} %get-tuple-element.17), channel_id=1, source_target_pairs={{0,32},{8,40},{16,48},{24,56},{32,0},{40,8},{48,16},{56,24},{64,96... | collective-permute-start | bytes 442376 | tf_op jit(solution)/shard_map/ppermute | solution.py:373
  40.5 22.5 %collective-permute-start.8 = (bf16[96,768]{1,0:T(8,128)(2,1)S(1)}, bf16[96,768]{1,0:T(8,128)(2,1)S(1)}, u32[]{:S(2)}, u32[]{:S(2)}) collective-permute-start(bf16[96,768]{1,0:T(8,128)(2,1)S(1)} %get-tuple-element.19._), channel_id=1, source_target_pairs={{0,16},{8,24},{16,0},{24,8},{32,48},{40,56},{48,32},{56,40},{64,80... | collective-permute-start | bytes 442376 | tf_op jit(solution)/shard_map/ppermute | solution.py:373
  42.1 20.9 %collective-permute-start.7 = (bf16[96,768]{1,0:T(8,128)(2,1)S(1)}, bf16[96,768]{1,0:T(8,128)(2,1)S(1)}, u32[]{:S(2)}, u32[]{:S(2)}) collective-permute-start(bf16[96,768]{1,0:T(8,128)(2,1)S(1)} %get-tuple-element.18), channel_id=1, source_target_pairs={{0,48},{8,56},{16,32},{24,40},{32,16},{40,24},{48,0},{56,8},{64,11... | collective-permute-start | bytes 442376 | tf_op jit(solution)/shard_map/ppermute | solution.py:373
  44.0 19.4 %collective-permute-start.14 = (bf16[96,768]{1,0:T(8,128)(2,1)S(1)}, bf16[96,768]{1,0:T(8,128)(2,1)S(1)}, u32[]{:S(2)}, u32[]{:S(2)}) collective-permute-start(bf16[96,768]{1,0:T(8,128)(2,1)S(1)} %get-tuple-element.20), channel_id=1, source_target_pairs={{0,32},{8,40},{16,48},{24,56},{32,0},{40,8},{48,16},{56,24},{64,96... | collective-permute-start | bytes 442376 | tf_op jit(solution)/shard_map/ppermute | solution.py:373
  45.3 24.0 %collective-permute-start.15 = (bf16[96,768]{1,0:T(8,128)(2,1)S(1)}, bf16[96,768]{1,0:T(8,128)(2,1)S(1)}, u32[]{:S(2)}, u32[]{:S(2)}) collective-permute-start(bf16[96,768]{1,0:T(8,128)(2,1)S(1)} %get-tuple-element.21), channel_id=1, source_target_pairs={{0,48},{8,56},{16,32},{24,40},{32,16},{40,24},{48,0},{56,8},{64,11... | collective-permute-start | bytes 442376 | tf_op jit(solution)/shard_map/ppermute | solution.py:373
  47.7 21.7 %collective-permute-start.16 = (bf16[96,768]{1,0:T(8,128)(2,1)S(1)}, bf16[96,768]{1,0:T(8,128)(2,1)S(1)}, u32[]{:S(2)}, u32[]{:S(2)}) collective-permute-start(bf16[96,768]{1,0:T(8,128)(2,1)S(1)} %get-tuple-element.22), channel_id=1, source_target_pairs={{0,16},{8,24},{16,0},{24,8},{32,48},{40,56},{48,32},{56,40},{64,80... | collective-permute-start | bytes 442376 | tf_op jit(solution)/shard_map/ppermute | solution.py:373

commit v10 on v9

--- a/solution.py
+++ b/solution.py
@@ -62,27 +62,26 @@
     return rows == cols, (rows < width) & (cols < width)
 
 
-def place_kernel(in_ref, out_ref):
-    for k in range(in_ref.shape[0]):
-        out_ref[k] = in_ref[k]
-
-
-def place_call(pos):
+def place_kernel(out_ref):
+    out_ref[...] = jnp.zeros_like(out_ref)
+
+
+def place_call():
     return pl.pallas_call(
         place_kernel,
-        in_specs=[SMEM],
-        out_specs=SMEM,
-        out_shape=jax.ShapeDtypeStruct(pos.shape, pos.dtype),
+        in_specs=[],
+        out_specs=VMEM,
+        out_shape=jax.ShapeDtypeStruct((8, BLOCK), F32),
         cost_estimate=cost(10**10, 10**7),
         name="place",
         compiler_params=grant(1),
-    )(pos)
-
-
-def inverse_kernel(width_ref, pos_ref, system_ref, upper_ref, xh_ref, xl_ref, part_ref):
+    )()
+
+
+def inverse_kernel(width_ref, system_ref, upper_ref, _, xh_ref, xl_ref, part_ref):
     members, order, _ = system_ref.shape
     half = upper_ref.shape[1]
-    swap = pos_ref[2] == 1
+    swap = lax.axis_index("row") == 1
     for s in range(members):
         on_diag, inside = square_masks(order, width_ref[s])
         identity = jnp.where(on_diag, 1.0, 0.0)
@@ -109,12 +108,12 @@
         xl_ref[s] = low
 
 
-def inverse_call(widths, pos, systems, upper):
+def inverse_call(widths, systems, upper, mark):
     members, order, _ = systems.shape
     half, cols = upper.shape[1:]
     return pl.pallas_call(
         inverse_kernel,
-        in_specs=[SMEM, SMEM, VMEM, VMEM],
+        in_specs=[SMEM, VMEM, VMEM, ANY],
         out_specs=[VMEM] * 3,
         out_shape=[
             jax.ShapeDtypeStruct((members, order, half), BF16),
@@ -124,7 +123,7 @@
         cost_estimate=cost(14 * members * order**3, 8000000),
         name="inverse",
         compiler_params=grant(20),
-    )(widths, pos, systems, upper)
+    )(widths, systems, upper, mark)
 
 
 def scale_kernel(mask_ref, xh_ref, xl_ref, part_ref, upper_ref, out_ref):
@@ -348,15 +347,6 @@
 
 def on_device(front_copies, lower_panels, upper_panels, diag_blocks, block_fill, widths):
     layers, col_devices = lax.axis_size("layer"), lax.axis_size("col")
-    layer = lax.axis_index("layer")
-    row_index, col_index = lax.axis_index("row"), lax.axis_index("col")
-    which = jnp.arange(4, dtype=jnp.int32)
-    pos = jnp.where(
-        which == 0,
-        layer & 1,
-        jnp.where(which == 1, col_index, jnp.where(which == 2, row_index, layer >> 1 & 3)),
-    ).astype(jnp.int32)
-    pos = place_call(pos)
     upper, fill, width_vec = upper_panels[0], block_fill[0], widths[0]
     masks = jnp.broadcast_to(fill.astype(BF16)[:, :, None, None], (*fill.shape, 16, BLOCK))
     row_count, cols = front_copies.shape[1:]
@@ -379,7 +369,7 @@
         following, last = shift(own, -1), shift(own, 1)
         right, left = shift(last[0], 1), shift(following[1], -1)
         lowers.append((own, following, last, right, left))
-    xh, xl, part = inverse_call(width_vec, pos, diag_blocks[0], upper)
+    xh, xl, part = inverse_call(width_vec, diag_blocks[0], upper, place_call())
     scaled = scale_call(masks, xh, xl, part, other_upper)
     sums = []
     after = scaled

time: 70.6 us -> 70.6 us (level)
  waiting for transfers between devices: 26.6 us -> 28.4 us
  Pallas kernels: 15.8 us -> 14.7 us
    ppermute x1, waiting for transfers between devices: 4.35 us -> 6.19 us  [on_device(): other_upper = lax.ppermute(upper, 'row', [(0, 1), (1, 0)])]
    pallas_call x2, Pallas kernels: 8.97 us -> 7.84 us  [the longest x1 7.84 us: inverse_call(): pl.pallas_call(inverse_kernel, in_specs=[SMEM, VMEM, VMEM, ANY], out_spec...]
  transfers between devices with their start and end apart: 17 -> 17, of which waited for: 6 -> 6; matrix products, arithmetic and copies ran while one was open for 0% -> 0% of each run, Pallas kernels for 20% -> 19%
where the time goes in v10:
time: 70.6 us; the launch traced here: 70.4 us
  waiting for transfers between devices  28.4 us (40%)
  starting transfers between devices  25.5 us (36%)
  Pallas kernels  14.7 us (21%)
  local copies, waits for them, and re-layouts  1.61 us (2%)
    ppermute x8, waiting for transfers between devices, across(): return lax.ppermute(block, 'layer', [(i, i ^ flip) for i in range(layers)])  16.9 us
    ppermute x8, starting transfers between devices, across(): return lax.ppermute(block, 'layer', [(i, i ^ flip) for i in range(layers)])  14.7 us
    ppermute x8, starting transfers between devices, shift(): lax.ppermute(block, 'col', [(i, (i + step) % col_devices) for i in range(...  8.65 us
    pallas_call x1, Pallas kernels, inverse_call(): pl.pallas_call(inverse_kernel, in_specs=[SMEM, VMEM, VMEM, ANY], out_spec...  7.84 us
    ppermute x1, waiting for transfers between devices, on_device(): other_upper = lax.ppermute(upper, 'row', [(0, 1), (1, 0)])  6.19 us
    ppermute x8, waiting for transfers between devices, shift(): lax.ppermute(block, 'col', [(i, (i + step) % col_devices) for i in range(...  5.28 us
    ppermute x1, starting transfers between devices, on_device(): other_upper = lax.ppermute(upper, 'row', [(0, 1), (1, 0)])  2.06 us
    pallas_call x2, Pallas kernels, update_call(): pl.pallas_call(update_kernel, in_specs=[VMEM] * (len(lowers) + 3) + [ANY]...  1.74 us
  transfers between devices with their start and end apart: 17, of which 6 were waited for; matrix products, arithmetic and copies ran while one was open for 0% of the time, Pallas kernels for 19%

profile of v10, /device:TPU:79, one launch (start us, length us, event | category | flops | bytes accessed | tf_op | source)
XLA Modules:
  0.0 70.4 jit_solution(16291339955604384528)
XLA Ops:
  0.0 1.2 %slice_bitcast_fusion = (bf16[2,4,2,96,128]{4,3,2,1,0:T(8,128)(2,1)S(1)}, bf16[2,4,2,96,128]{4,3,2,1,0:T(8,128)(2,1)S(1)}) fusion(bf16[2,4,2,2,96,128]{5,4,3,2,1,0:T(8,128)(2,1)} %bitcast.30), kind=kLoop, calls=%fused_computation | loop fusion | bytes 1572864 | tf_op jit(solution)/shard_map/squeeze | solution.py:368
  1.2 0.3 collective-permute-start.1
  1.5 1.3 %collective-permute-start = (bf16[2,4,2,96,128]{4,3,2,1,0:T(8,128)(2,1)S(1)}, bf16[2,4,2,96,128]{4,3,2,1,0:T(8,128)(2,1)S(1)}, u32[]{:S(2)}, u32[]{:S(2)}) collective-permute-start(bf16[2,4,2,96,128]{4,3,2,1,0:T(8,128)(2,1)S(1)} %get-tuple-element.24.refs_0_), channel_id=1, source_target_pairs={{0,6},{2,0},{4,2},{6,4},{1,7},{3,1},{5,3},{7,5},{8,14},{10,8},{12,... | collective-permute-start | bytes 1179656 | tf_op jit(solution)/shard_map/ppermute | solution.py:360
  2.7 1.4 %collective-permute-start.10 = (bf16[2,4,2,96,128]{4,3,2,1,0:T(8,128)(2,1)S(1)}, bf16[2,4,2,96,128]{4,3,2,1,0:T(8,128)(2,1)S(1)}, u32[]{:S(2)}, u32[]{:S(2)}) collective-permute-start(bf16[2,4,2,96,128]{4,3,2,1,0:T(8,128)(2,1)S(1)} %get-tuple-element.23.own_ref), channel_id=1, source_target_pairs={{0,2},{2,4},{4,6},{6,0},{1,3},{3,5},{5,7},{7,1},{8,10},{10,12},{12... | collective-permute-start | bytes 1179656 | tf_op jit(solution)/shard_map/ppermute | solution.py:360
  4.1 0.1 collective-permute-start.9
  4.2 2.1 %collective-permute-start.4 = (bf16[2,256,768]{2,1,0:T(8,128)(2,1)}, bf16[2,256,768]{2,1,0:T(8,128)(2,1)S(1)}, u32[]{:S(2)}, u32[]{:S(2)}) collective-permute-start(bf16[2,256,768]{2,1,0:T(8,128)(2,1)} %bitcast.27), channel_id=1, source_target_pairs={{0,1},{1,0},{2,3},{3,2},{4,5},{5,4},{6,7},{7,6},{8,9},{9,8},{10,11... | collective-permute-start | bytes 2359304 | tf_op jit(solution)/shard_map/ppermute | solution.py:365
  6.3 0.0 copy-start.4
  6.3 7.8 %inverse.1 = (bf16[2,512,256]{2,1,0:T(8,128)(2,1)S(1)}, bf16[2,512,256]{2,1,0:T(8,128)(2,1)S(1)}, f32[2,512,768]{2,1,0:T(8,128)S(1)}) custom-call(s32[2]{0:T(128)S(1)} %bitcast.29, f32[2,512,512]{2,1,0:T(8,128)S(1)} %bitcast.26, bf16[2,256,768]{2,1,0:T(8,128)(2,1)S(1)} %bitcast.28, f32[8,128]{1,0:T(8,128)S(1)} %place.1._), custom_call_target="tpu_custom_call" | custom-call | flops 3758096384 | bytes 8000000 | tf_op jit(solution)/shard_map/inverse/pallas_call | solution.py:114
  14.1 0.0 collective-permute-done.1.refs_2_
  14.2 2.6 %collective-permute-start.2 = (bf16[4,2,96,128]{3,2,1,0:T(8,128)(2,1)S(1)}, bf16[4,2,96,128]{3,2,1,0:T(8,128)(2,1)S(1)}, u32[]{:S(2)}, u32[]{:S(2)}) collective-permute-start(bf16[4,2,96,128]{3,2,1,0:T(8,128)(2,1)S(1)} %slice_bitcast_fusion.5), channel_id=1, source_target_pairs={{0,2},{2,4},{4,6},{6,0},{1,3},{3,5},{5,7},{7,1},{8,10},{10,12},{12... | collective-permute-start | bytes 589832 | tf_op jit(solution)/shard_map/ppermute | solution.py:360
  16.8 0.0 collective-permute-done.refs_1_
  16.8 0.3 collective-permute-start.3
  17.1 6.2 %collective-permute-done.4.upper_ref = bf16[2,256,768]{2,1,0:T(8,128)(2,1)S(1)} collective-permute-done((bf16[2,256,768]{2,1,0:T(8,128)(2,1)}, bf16[2,256,768]{2,1,0:T(8,128)(2,1)S(1)}, u32[]{:S(2)}, u32[]{:S(2)}) %collective-permute-start.4) | collective-permute-done | bytes 786464 | tf_op jit(solution)/shard_map/ppermute | solution.py:365
  23.3 0.1 broadcast_in_dim.2.mask_ref
  23.4 0.0 copy-start
  23.4 1.0 %scale_upper.1.refs_5_.refs_6_.scaled_ref = bf16[2,4,128,768]{3,2,1,0:T(8,128)(2,1)S(1)} custom-call(bf16[2,24,16,128]{3,2,1,0:T(8,128)(2,1)S(1)} %broadcast_in_dim.2.mask_ref, bf16[2,512,256]{2,1,0:T(8,128)(2,1)S(1)} %get-tuple-element.14.xh_ref, bf16[2,512,256]{2,1,0:T(8,128)(2,1)S(1)} %get-tuple-element.15.xl_ref, ...), custom_call_target="tpu_custom_call" | custom-call | flops 805306368 | bytes 6291456 | tf_op jit(solution)/shard_map/scale_upper/pallas_call | solution.py:148
  24.5 0.0 collective-permute-done.2.refs_3_
  24.5 0.4 collective-permute-done.3.refs_4_
  24.8 0.3 copy-done
  25.1 0.9 %shard_map.65 = bf16[4,96,768]{2,1,0:T(8,128)(2,1)S(1)} custom-call(bf16[2,24,16,128]{3,2,1,0:T(8,128)(2,1)S(1)} %broadcast_in_dim.2.mask_ref, bf16[4,2,2,96,768]{4,3,2,1,0:T(8,128)(2,1)S(1)} %bitcast.23, bf16[2,4,2,96,128]{4,3,2,1,0:T(8,128)(2,1)S(1)} %get-tuple-element.24.refs_0_, bf16[2,4,2,96,128]{4,3,2,1,0:T(8,128)(2,1)S(1)} %collective-permute-done.refs_1_, ...), custom_call_target="tpu_custom_call" | custom-call | flops 603979776 | bytes 4000000 | tf_op jit(solution)/shard_map/pallas_call | solution.py:187
  26.0 2.7 %collective-permute-start.5 = (bf16[4,96,768]{2,1,0:T(8,128)(2,1)S(1)}, bf16[4,96,768]{2,1,0:T(8,128)(2,1)S(1)}, u32[]{:S(2)}, u32[]{:S(2)}) collective-permute-start(bf16[4,96,768]{2,1,0:T(8,128)(2,1)S(1)} %shard_map.65), channel_id=1, source_target_pairs={{0,8},{8,0},{16,24},{24,16},{32,40},{40,32},{48,56},{56,48},{64,72... | collective-permute-start | bytes 1769480 | tf_op jit(solution)/shard_map/ppermute | solution.py:363
  28.7 0.0 collective-permute-done.10.last_ref
  28.7 2.6 %collective-permute-start.11 = (bf16[4,2,96,128]{3,2,1,0:T(8,128)(2,1)S(1)}, bf16[4,2,96,128]{3,2,1,0:T(8,128)(2,1)S(1)}, u32[]{:S(2)}, u32[]{:S(2)}) collective-permute-start(bf16[4,2,96,128]{3,2,1,0:T(8,128)(2,1)S(1)} %slice_bitcast_fusion.3), channel_id=1, source_target_pairs={{0,2},{2,4},{4,6},{6,0},{1,3},{3,5},{5,7},{7,1},{8,10},{10,12},{12... | collective-permute-start | bytes 589832 | tf_op jit(solution)/shard_map/ppermute | solution.py:360
  31.4 0.0 collective-permute-done.9.next_ref
  31.4 0.1 collective-permute-start.12
  31.5 0.8 %shard_map.64.kept_ref = f32[4,96,768]{2,1,0:T(8,128)S(1)} custom-call(bf16[2,24,16,128]{3,2,1,0:T(8,128)(2,1)S(1)} %broadcast_in_dim.2.mask_ref, bf16[4,2,2,96,768]{4,3,2,1,0:T(8,128)(2,1)S(1)} %bitcast.24, bf16[2,4,2,96,128]{4,3,2,1,0:T(8,128)(2,1)S(1)} %get-tuple-element.24.refs_0_, bf16[2,4,2,96,128]{4,3,2,1,0:T(8,128)(2,1)S(1)} %collective-permute-done.refs_1_, ...), custom_call_target="tpu_custom_call" | custom-call | flops 603979776 | bytes 4000000 | tf_op jit(solution)/shard_map/pallas_call | solution.py:187
  32.3 0.0 collective-permute-done.5.got_ref.core_ref
  32.4 0.4 shard_map.66
  32.7 1.2 %shard_map.68.near_ref = f32[2,4,96,768]{3,2,1,0:T(8,128)S(1)} custom-call(bf16[2,24,16,128]{3,2,1,0:T(8,128)(2,1)S(1)} %broadcast_in_dim.2.mask_ref, bf16[4,2,2,96,768]{4,3,2,1,0:T(8,128)(2,1)S(1)} %bitcast.25, bf16[2,4,2,96,128]{4,3,2,1,0:T(8,128)(2,1)S(1)} %get-tuple-element.23.own_ref, bf16[2,4,2,96,128]{4,3,2,1,0:T(8,128)(2,1)S(1)} %collective-permute-done.9.next_ref, ...), custom_call_target="tpu_custom_call" | custom-call | flops 905969664 | bytes 8000000 | tf_op jit(solution)/shard_map/pallas_call | solution.py:243
  33.9 1.7 %collective-permute-done.11.right_ref = bf16[4,2,96,128]{3,2,1,0:T(8,128)(2,1)S(1)} collective-permute-done((bf16[4,2,96,128]{3,2,1,0:T(8,128)(2,1)S(1)}, bf16[4,2,96,128]{3,2,1,0:T(8,128)(2,1)S(1)}, u32[]{:S(2)}, u32[]{:S(2)}) %collective-permute-start.11) | collective-permute-done | bytes 196640 | tf_op jit(solution)/shard_map/ppermute | solution.py:360
  35.6 3.2 %collective-permute-done.12.left_ref = bf16[4,2,96,128]{3,2,1,0:T(8,128)(2,1)S(1)} collective-permute-done((bf16[4,2,96,128]{3,2,1,0:T(8,128)(2,1)S(1)}, bf16[4,2,96,128]{3,2,1,0:T(8,128)(2,1)S(1)}, u32[]{:S(2)}, u32[]{:S(2)}) %collective-permute-start.12) | collective-permute-done | bytes 196640 | tf_op jit(solution)/shard_map/ppermute | solution.py:360
  38.8 0.4 shard_map.70
  39.3 1.3 %collective-permute-start.13 = (bf16[4,96,768]{2,1,0:T(8,128)(2,1)S(1)}, bf16[4,96,768]{2,1,0:T(8,128)(2,1)S(1)}, u32[]{:S(2)}, u32[]{:S(2)}) collective-permute-start(bf16[4,96,768]{2,1,0:T(8,128)(2,1)S(1)} %shard_map.70), channel_id=1, source_target_pairs={{0,8},{8,0},{16,24},{24,16},{32,40},{40,32},{48,56},{56,48},{64,72... | collective-permute-start | bytes 1769480 | tf_op jit(solution)/shard_map/ppermute | solution.py:363
  40.5 0.0 collective-permute-start.6
  40.5 1.6 %collective-permute-start.8 = (bf16[96,768]{1,0:T(8,128)(2,1)S(1)}, bf16[96,768]{1,0:T(8,128)(2,1)S(1)}, u32[]{:S(2)}, u32[]{:S(2)}) collective-permute-start(bf16[96,768]{1,0:T(8,128)(2,1)S(1)} %get-tuple-element.19._), channel_id=1, source_target_pairs={{0,16},{8,24},{16,0},{24,8},{32,48},{40,56},{48,32},{56,40},{64,80... | collective-permute-start | bytes 442376 | tf_op jit(solution)/shard_map/ppermute | solution.py:363
  42.1 1.2 %collective-permute-start.7 = (bf16[96,768]{1,0:T(8,128)(2,1)S(1)}, bf16[96,768]{1,0:T(8,128)(2,1)S(1)}, u32[]{:S(2)}, u32[]{:S(2)}) collective-permute-start(bf16[96,768]{1,0:T(8,128)(2,1)S(1)} %get-tuple-element.18), channel_id=1, source_target_pairs={{0,48},{8,56},{16,32},{24,40},{32,16},{40,24},{48,0},{56,8},{64,11... | collective-permute-start | bytes 442376 | tf_op jit(solution)/shard_map/ppermute | solution.py:363
  43.3 0.3 shard_map.69.kept_ref
  43.7 0.0 collective-permute-done.13.core_ref.got_ref
  43.7 0.4 shard_map.72
  44.0 1.3 %collective-permute-start.14 = (bf16[96,768]{1,0:T(8,128)(2,1)S(1)}, bf16[96,768]{1,0:T(8,128)(2,1)S(1)}, u32[]{:S(2)}, u32[]{:S(2)}) collective-permute-start(bf16[96,768]{1,0:T(8,128)(2,1)S(1)} %get-tuple-element.20), channel_id=1, source_target_pairs={{0,32},{8,40},{16,48},{24,56},{32,0},{40,8},{48,16},{56,24},{64,96... | collective-permute-start | bytes 442376 | tf_op jit(solution)/shard_map/ppermute | solution.py:363
  45.3 2.4 %collective-permute-start.15 = (bf16[96,768]{1,0:T(8,128)(2,1)S(1)}, bf16[96,768]{1,0:T(8,128)(2,1)S(1)}, u32[]{:S(2)}, u32[]{:S(2)}) collective-permute-start(bf16[96,768]{1,0:T(8,128)(2,1)S(1)} %get-tuple-element.21), channel_id=1, source_target_pairs={{0,48},{8,56},{16,32},{24,40},{32,16},{40,24},{48,0},{56,8},{64,11... | collective-permute-start | bytes 442376 | tf_op jit(solution)/shard_map/ppermute | solution.py:363
  47.7 0.0 collective-permute-done.6.refs_0_
  47.7 4.3 %collective-permute-start.16 = (bf16[96,768]{1,0:T(8,128)(2,1)S(1)}, bf16[96,768]{1,0:T(8,128)(2,1)S(1)}, u32[]{:S(2)}, u32[]{:S(2)}) collective-permute-start(bf16[96,768]{1,0:T(8,128)(2,1)S(1)} %get-tuple-element.22), channel_id=1, source_target_pairs={{0,16},{8,24},{16,0},{24,8},{32,48},{40,56},{48,32},{56,40},{64,80... | collective-permute-start | bytes 442376 | tf_op jit(solution)/shard_map/ppermute | solution.py:363
  52.0 11.0 %collective-permute-done.7.refs_1_ = bf16[96,768]{1,0:T(8,128)(2,1)S(1)} collective-permute-done((bf16[96,768]{1,0:T(8,128)(2,1)S(1)}, bf16[96,768]{1,0:T(8,128)(2,1)S(1)}, u32[]{:S(2)}, u32[]{:S(2)}) %collective-permute-start.7) | collective-permute-done | bytes 147488 | tf_op jit(solution)/shard_map/ppermute | solution.py:363
  63.0 0.3 shard_map.67.early_ref
  63.3 0.1 shard_map.71.own_ref
  63.4 5.9 %collective-permute-done.15.refs_1_ = bf16[96,768]{1,0:T(8,128)(2,1)S(1)} collective-permute-done((bf16[96,768]{1,0:T(8,128)(2,1)S(1)}, bf16[96,768]{1,0:T(8,128)(2,1)S(1)}, u32[]{:S(2)}, u32[]{:S(2)}) %collective-permute-start.15) | collective-permute-done | bytes 147488 | tf_op jit(solution)/shard_map/ppermute | solution.py:363
  69.3 1.0 %final_sums.1 = f32[1,192,768]{2,1,0:T(8,128)} custom-call(f32[96,768]{1,0:T(8,128)S(1)} %shard_map.67.early_ref, f32[96,768]{1,0:T(8,128)S(1)} %shard_map.71.own_ref, bf16[96,768]{1,0:T(8,128)(2,1)S(1)} %collective-permute-done.14.refs_0_, bf16[96,768]{1,0:T(8,128)(2,1)S(1)} %collective-permute-done.15.refs_1_, ...), custom_call_target="tpu_custom_call" | custom-call | flops 294912 | bytes 884736 | tf_op jit(solution)/shard_map/final_sums/pallas_call | solution.py:337
  (16 shorter events, 0.1 us)
Async XLA Ops:
  1.2 12.9 %collective-permute-start.1 = (bf16[2,4,2,96,128]{4,3,2,1,0:T(8,128)(2,1)S(1)}, bf16[2,4,2,96,128]{4,3,2,1,0:T(8,128)(2,1)S(1)}, u32[]{:S(2)}, u32[]{:S(2)}) collective-permute-start(bf16[2,4,2,96,128]{4,3,2,1,0:T(8,128)(2,1)S(1)} %get-tuple-element.24.refs_0_), channel_id=1, source_target_pairs={{0,2},{2,4},{4,6},{6,0},{1,3},{3,5},{5,7},{7,1},{8,10},{10,12},{12... | collective-permute-start | bytes 1179656 | tf_op jit(solution)/shard_map/ppermute | solution.py:360
  1.5 15.4 %collective-permute-start = (bf16[2,4,2,96,128]{4,3,2,1,0:T(8,128)(2,1)S(1)}, bf16[2,4,2,96,128]{4,3,2,1,0:T(8,128)(2,1)S(1)}, u32[]{:S(2)}, u32[]{:S(2)}) collective-permute-start(bf16[2,4,2,96,128]{4,3,2,1,0:T(8,128)(2,1)S(1)} %get-tuple-element.24.refs_0_), channel_id=1, source_target_pairs={{0,6},{2,0},{4,2},{6,4},{1,7},{3,1},{5,3},{7,5},{8,14},{10,8},{12,... | collective-permute-start | bytes 1179656 | tf_op jit(solution)/shard_map/ppermute | solution.py:360
  2.7 26.0 %collective-permute-start.10 = (bf16[2,4,2,96,128]{4,3,2,1,0:T(8,128)(2,1)S(1)}, bf16[2,4,2,96,128]{4,3,2,1,0:T(8,128)(2,1)S(1)}, u32[]{:S(2)}, u32[]{:S(2)}) collective-permute-start(bf16[2,4,2,96,128]{4,3,2,1,0:T(8,128)(2,1)S(1)} %get-tuple-element.23.own_ref), channel_id=1, source_target_pairs={{0,2},{2,4},{4,6},{6,0},{1,3},{3,5},{5,7},{7,1},{8,10},{10,12},{12... | collective-permute-start | bytes 1179656 | tf_op jit(solution)/shard_map/ppermute | solution.py:360
  4.1 27.3 %collective-permute-start.9 = (bf16[2,4,2,96,128]{4,3,2,1,0:T(8,128)(2,1)S(1)}, bf16[2,4,2,96,128]{4,3,2,1,0:T(8,128)(2,1)S(1)}, u32[]{:S(2)}, u32[]{:S(2)}) collective-permute-start(bf16[2,4,2,96,128]{4,3,2,1,0:T(8,128)(2,1)S(1)} %get-tuple-element.23.own_ref), channel_id=1, source_target_pairs={{0,6},{2,0},{4,2},{6,4},{1,7},{3,1},{5,3},{7,5},{8,14},{10,8},{12,... | collective-permute-start | bytes 1179656 | tf_op jit(solution)/shard_map/ppermute | solution.py:360
  4.2 2.1 %copy-start.1 = (f32[1,2,512,512]{3,2,1,0:T(8,128)S(1)}, f32[1,2,512,512]{3,2,1,0:T(8,128)}, u32[]{:S(2)}) copy-start(f32[1,2,512,512]{3,2,1,0:T(8,128)} %param.9) | copy-start | bytes 6291460
  4.2 2.1 %copy-start.2 = (bf16[1,2,256,768]{3,2,1,0:T(8,128)(2,1)S(1)}, bf16[1,2,256,768]{3,2,1,0:T(8,128)(2,1)}, u32[]{:S(2)}) copy-start(bf16[1,2,256,768]{3,2,1,0:T(8,128)(2,1)} %param.8) | copy-start | bytes 2359300
  4.2 2.1 %copy-start.3 = (s32[1,2]{1,0:T(1,128)S(1)}, s32[1,2]{1,0:T(1,128)}, u32[]{:S(2)}) copy-start(s32[1,2]{1,0:T(1,128)} %param.11) | copy-start | bytes 28
  4.2 19.1 %collective-permute-start.4 = (bf16[2,256,768]{2,1,0:T(8,128)(2,1)}, bf16[2,256,768]{2,1,0:T(8,128)(2,1)S(1)}, u32[]{:S(2)}, u32[]{:S(2)}) collective-permute-start(bf16[2,256,768]{2,1,0:T(8,128)(2,1)} %bitcast.27), channel_id=1, source_target_pairs={{0,1},{1,0},{2,3},{3,2},{4,5},{5,4},{6,7},{7,6},{8,9},{9,8},{10,11... | collective-permute-start | bytes 2359304 | tf_op jit(solution)/shard_map/ppermute | solution.py:365
  6.3 10.8 %copy-start.4 = (s32[1,2,24]{2,1,0:T(2,128)S(1)}, s32[1,2,24]{2,1,0:T(2,128)}, u32[]{:S(2)}) copy-start(s32[1,2,24]{2,1,0:T(2,128)} %param.10) | copy-start | bytes 580
  14.2 10.3 %collective-permute-start.2 = (bf16[4,2,96,128]{3,2,1,0:T(8,128)(2,1)S(1)}, bf16[4,2,96,128]{3,2,1,0:T(8,128)(2,1)S(1)}, u32[]{:S(2)}, u32[]{:S(2)}) collective-permute-start(bf16[4,2,96,128]{3,2,1,0:T(8,128)(2,1)S(1)} %slice_bitcast_fusion.5), channel_id=1, source_target_pairs={{0,2},{2,4},{4,6},{6,0},{1,3},{3,5},{5,7},{7,1},{8,10},{10,12},{12... | collective-permute-start | bytes 589832 | tf_op jit(solution)/shard_map/ppermute | solution.py:360
  16.8 8.0 %collective-permute-start.3 = (bf16[4,2,96,128]{3,2,1,0:T(8,128)(2,1)S(1)}, bf16[4,2,96,128]{3,2,1,0:T(8,128)(2,1)S(1)}, u32[]{:S(2)}, u32[]{:S(2)}) collective-permute-start(bf16[4,2,96,128]{3,2,1,0:T(8,128)(2,1)S(1)} %slice_bitcast_fusion.4), channel_id=1, source_target_pairs={{0,6},{2,0},{4,2},{6,4},{1,7},{3,1},{5,3},{7,5},{8,14},{10,8},{12,... | collective-permute-start | bytes 589832 | tf_op jit(solution)/shard_map/ppermute | solution.py:360
  23.4 1.7 %copy-start = (bf16[1,1536,768]{2,1,0:T(8,128)(2,1)S(1)}, bf16[1,1536,768]{2,1,0:T(8,128)(2,1)}, u32[]{:S(2)}) copy-start(bf16[1,1536,768]{2,1,0:T(8,128)(2,1)} %param.6) | copy-start | bytes 7077892
  26.0 6.3 %collective-permute-start.5 = (bf16[4,96,768]{2,1,0:T(8,128)(2,1)S(1)}, bf16[4,96,768]{2,1,0:T(8,128)(2,1)S(1)}, u32[]{:S(2)}, u32[]{:S(2)}) collective-permute-start(bf16[4,96,768]{2,1,0:T(8,128)(2,1)S(1)} %shard_map.65), channel_id=1, source_target_pairs={{0,8},{8,0},{16,24},{24,16},{32,40},{40,32},{48,56},{56,48},{64,72... | collective-permute-start | bytes 1769480 | tf_op jit(solution)/shard_map/ppermute | solution.py:363
  28.7 6.9 %collective-permute-start.11 = (bf16[4,2,96,128]{3,2,1,0:T(8,128)(2,1)S(1)}, bf16[4,2,96,128]{3,2,1,0:T(8,128)(2,1)S(1)}, u32[]{:S(2)}, u32[]{:S(2)}) collective-permute-start(bf16[4,2,96,128]{3,2,1,0:T(8,128)(2,1)S(1)} %slice_bitcast_fusion.3), channel_id=1, source_target_pairs={{0,2},{2,4},{4,6},{6,0},{1,3},{3,5},{5,7},{7,1},{8,10},{10,12},{12... | collective-permute-start | bytes 589832 | tf_op jit(solution)/shard_map/ppermute | solution.py:360
  31.4 7.4 %collective-permute-start.12 = (bf16[4,2,96,128]{3,2,1,0:T(8,128)(2,1)S(1)}, bf16[4,2,96,128]{3,2,1,0:T(8,128)(2,1)S(1)}, u32[]{:S(2)}, u32[]{:S(2)}) collective-permute-start(bf16[4,2,96,128]{3,2,1,0:T(8,128)(2,1)S(1)} %slice_bitcast_fusion.2), channel_id=1, source_target_pairs={{0,6},{2,0},{4,2},{6,4},{1,7},{3,1},{5,3},{7,5},{8,14},{10,8},{12,... | collective-permute-start | bytes 589832 | tf_op jit(solution)/shard_map/ppermute | solution.py:360
  39.3 4.4 %collective-permute-start.13 = (bf16[4,96,768]{2,1,0:T(8,128)(2,1)S(1)}, bf16[4,96,768]{2,1,0:T(8,128)(2,1)S(1)}, u32[]{:S(2)}, u32[]{:S(2)}) collective-permute-start(bf16[4,96,768]{2,1,0:T(8,128)(2,1)S(1)} %shard_map.70), channel_id=1, source_target_pairs={{0,8},{8,0},{16,24},{24,16},{32,40},{40,32},{48,56},{56,48},{64,72... | collective-permute-start | bytes 1769480 | tf_op jit(solution)/shard_map/ppermute | solution.py:363
  40.5 7.2 %collective-permute-start.6 = (bf16[96,768]{1,0:T(8,128)(2,1)S(1)}, bf16[96,768]{1,0:T(8,128)(2,1)S(1)}, u32[]{:S(2)}, u32[]{:S(2)}) collective-permute-start(bf16[96,768]{1,0:T(8,128)(2,1)S(1)} %get-tuple-element.17), channel_id=1, source_target_pairs={{0,32},{8,40},{16,48},{24,56},{32,0},{40,8},{48,16},{56,24},{64,96... | collective-permute-start | bytes 442376 | tf_op jit(solution)/shard_map/ppermute | solution.py:363
  40.5 22.5 %collective-permute-start.8 = (bf16[96,768]{1,0:T(8,128)(2,1)S(1)}, bf16[96,768]{1,0:T(8,128)(2,1)S(1)}, u32[]{:S(2)}, u32[]{:S(2)}) collective-permute-start(bf16[96,768]{1,0:T(8,128)(2,1)S(1)} %get-tuple-element.19._), channel_id=1, source_target_pairs={{0,16},{8,24},{16,0},{24,8},{32,48},{40,56},{48,32},{56,40},{64,80... | collective-permute-start | bytes 442376 | tf_op jit(solution)/shard_map/ppermute | solution.py:363
  42.1 20.9 %collective-permute-start.7 = (bf16[96,768]{1,0:T(8,128)(2,1)S(1)}, bf16[96,768]{1,0:T(8,128)(2,1)S(1)}, u32[]{:S(2)}, u32[]{:S(2)}) collective-permute-start(bf16[96,768]{1,0:T(8,128)(2,1)S(1)} %get-tuple-element.18), channel_id=1, source_target_pairs={{0,48},{8,56},{16,32},{24,40},{32,16},{40,24},{48,0},{56,8},{64,11... | collective-permute-start | bytes 442376 | tf_op jit(solution)/shard_map/ppermute | solution.py:363
  44.0 19.4 %collective-permute-start.14 = (bf16[96,768]{1,0:T(8,128)(2,1)S(1)}, bf16[96,768]{1,0:T(8,128)(2,1)S(1)}, u32[]{:S(2)}, u32[]{:S(2)}) collective-permute-start(bf16[96,768]{1,0:T(8,128)(2,1)S(1)} %get-tuple-element.20), channel_id=1, source_target_pairs={{0,32},{8,40},{16,48},{24,56},{32,0},{40,8},{48,16},{56,24},{64,96... | collective-permute-start | bytes 442376 | tf_op jit(solution)/shard_map/ppermute | solution.py:363
  45.3 24.0 %collective-permute-start.15 = (bf16[96,768]{1,0:T(8,128)(2,1)S(1)}, bf16[96,768]{1,0:T(8,128)(2,1)S(1)}, u32[]{:S(2)}, u32[]{:S(2)}) collective-permute-start(bf16[96,768]{1,0:T(8,128)(2,1)S(1)} %get-tuple-element.21), channel_id=1, source_target_pairs={{0,48},{8,56},{16,32},{24,40},{32,16},{40,24},{48,0},{56,8},{64,11... | collective-permute-start | bytes 442376 | tf_op jit(solution)/shard_map/ppermute | solution.py:363
  47.7 21.7 %collective-permute-start.16 = (bf16[96,768]{1,0:T(8,128)(2,1)S(1)}, bf16[96,768]{1,0:T(8,128)(2,1)S(1)}, u32[]{:S(2)}, u32[]{:S(2)}) collective-permute-start(bf16[96,768]{1,0:T(8,128)(2,1)S(1)} %get-tuple-element.22), channel_id=1, source_target_pairs={{0,16},{8,24},{16,0},{24,8},{32,48},{40,56},{48,32},{56,40},{64,80... | collective-permute-start | bytes 442376 | tf_op jit(solution)/shard_map/ppermute | solution.py:363

commit v11 on v10

--- a/solution.py
+++ b/solution.py
@@ -78,7 +78,7 @@
     )()
 
 
-def inverse_kernel(width_ref, system_ref, upper_ref, _, xh_ref, xl_ref, part_ref):
+def inverse_kernel(width_ref, system_ref, upper_ref, mark_ref, front_ref, xh_ref, xl_ref, part_ref):
     members, order, _ = system_ref.shape
     half = upper_ref.shape[1]
     swap = lax.axis_index("row") == 1
@@ -108,12 +108,12 @@
         xl_ref[s] = low
 
 
-def inverse_call(widths, systems, upper, mark):
+def inverse_call(widths, systems, upper, mark, front):
     members, order, _ = systems.shape
     half, cols = upper.shape[1:]
     return pl.pallas_call(
         inverse_kernel,
-        in_specs=[SMEM, VMEM, VMEM, ANY],
+        in_specs=[SMEM, VMEM, VMEM, ANY, VMEM],
         out_specs=[VMEM] * 3,
         out_shape=[
             jax.ShapeDtypeStruct((members, order, half), BF16),
@@ -123,7 +123,7 @@
         cost_estimate=cost(14 * members * order**3, 8000000),
         name="inverse",
         compiler_params=grant(20),
-    )(widths, systems, upper, mark)
+    )(widths, systems, upper, mark, front)
 
 
 def scale_kernel(mask_ref, xh_ref, xl_ref, part_ref, upper_ref, out_ref):
@@ -369,7 +369,7 @@
         following, last = shift(own, -1), shift(own, 1)
         right, left = shift(last[0], 1), shift(following[1], -1)
         lowers.append((own, following, last, right, left))
-    xh, xl, part = inverse_call(width_vec, diag_blocks[0], upper, place_call())
+    xh, xl, part = inverse_call(width_vec, diag_blocks[0], upper, place_call(), front)
     scaled = scale_call(masks, xh, xl, part, other_upper)
     sums = []
     after = scaled

time: 70.6 us -> 70 us (level)
  the two profiles are of different devices: /device:TPU:79 before, /device:TPU:87 now
where the time goes in v11:
time: 70 us; the launch traced here: 69.9 us
  waiting for transfers between devices  27.8 us (40%)
  starting transfers between devices  23.5 us (34%)
  Pallas kernels  14.7 us (21%)
  local copies, waits for them, and re-layouts  3.67 us (5%)
    ppermute x8, waiting for transfers between devices, across(): return lax.ppermute(block, 'layer', [(i, i ^ flip) for i in range(layers)])  16.9 us
    ppermute x8, starting transfers between devices, across(): return lax.ppermute(block, 'layer', [(i, i ^ flip) for i in range(layers)])  14.6 us
    ppermute x8, starting transfers between devices, shift(): lax.ppermute(block, 'col', [(i, (i + step) % col_devices) for i in range(...  8.74 us
    pallas_call x1, Pallas kernels, inverse_call(): pl.pallas_call(inverse_kernel, in_specs=[SMEM, VMEM, VMEM, ANY, VMEM], ou...  7.83 us
    ppermute x1, waiting for transfers between devices, on_device(): other_upper = lax.ppermute(upper, 'row', [(0, 1), (1, 0)])  5.76 us
    ppermute x8, waiting for transfers between devices, shift(): lax.ppermute(block, 'col', [(i, (i + step) % col_devices) for i in range(...  5.1 us
    unnamed x10, local copies, waits for them, and re-layouts  2.33 us
    pallas_call x2, Pallas kernels, update_call(): pl.pallas_call(update_kernel, in_specs=[VMEM] * (len(lowers) + 3) + [ANY]...  1.74 us
  transfers between devices with their start and end apart: 17, of which 6 were waited for; matrix products, arithmetic and copies ran while one was open for 0% of the time, Pallas kernels for 19%

profile of v11, /device:TPU:87, one launch (start us, length us, event | category | flops | bytes accessed | tf_op | source)
XLA Modules:
  0.0 69.9 jit_solution(6559934462104773302)
XLA Ops:
  0.0 1.2 %slice_bitcast_fusion = (bf16[2,4,2,96,128]{4,3,2,1,0:T(8,128)(2,1)S(1)}, bf16[2,4,2,96,128]{4,3,2,1,0:T(8,128)(2,1)S(1)}) fusion(bf16[2,4,2,2,96,128]{5,4,3,2,1,0:T(8,128)(2,1)} %bitcast.31), kind=kLoop, calls=%fused_computation | loop fusion | bytes 1572864 | tf_op jit(solution)/shard_map/squeeze | solution.py:368
  1.2 0.3 collective-permute-start.1
  1.5 1.3 %collective-permute-start = (bf16[2,4,2,96,128]{4,3,2,1,0:T(8,128)(2,1)S(1)}, bf16[2,4,2,96,128]{4,3,2,1,0:T(8,128)(2,1)S(1)}, u32[]{:S(2)}, u32[]{:S(2)}) collective-permute-start(bf16[2,4,2,96,128]{4,3,2,1,0:T(8,128)(2,1)S(1)} %get-tuple-element.24.refs_0_), channel_id=1, source_target_pairs={{0,6},{2,0},{4,2},{6,4},{1,7},{3,1},{5,3},{7,5},{8,14},{10,8},{12,... | collective-permute-start | bytes 1179656 | tf_op jit(solution)/shard_map/ppermute | solution.py:360
  2.7 1.4 %collective-permute-start.10 = (bf16[2,4,2,96,128]{4,3,2,1,0:T(8,128)(2,1)S(1)}, bf16[2,4,2,96,128]{4,3,2,1,0:T(8,128)(2,1)S(1)}, u32[]{:S(2)}, u32[]{:S(2)}) collective-permute-start(bf16[2,4,2,96,128]{4,3,2,1,0:T(8,128)(2,1)S(1)} %get-tuple-element.23.own_ref), channel_id=1, source_target_pairs={{0,2},{2,4},{4,6},{6,0},{1,3},{3,5},{5,7},{7,1},{8,10},{10,12},{12... | collective-permute-start | bytes 1179656 | tf_op jit(solution)/shard_map/ppermute | solution.py:360
  4.1 0.1 collective-permute-start.9
  4.2 0.1 collective-permute-start.4
  4.3 1.5 %copy-done = bf16[1,1536,768]{2,1,0:T(8,128)(2,1)S(1)} copy-done((bf16[1,1536,768]{2,1,0:T(8,128)(2,1)S(1)}, bf16[1,1536,768]{2,1,0:T(8,128)(2,1)}, u32[]{:S(2)}) %copy-start) | copy-done | bytes 2359320
  5.9 0.6 copy-done.1
  6.5 0.2 copy-done.2
  6.7 7.8 %inverse.1 = (bf16[2,512,256]{2,1,0:T(8,128)(2,1)S(1)}, bf16[2,512,256]{2,1,0:T(8,128)(2,1)S(1)}, f32[2,512,768]{2,1,0:T(8,128)S(1)}) custom-call(s32[2]{0:T(128)S(1)} %bitcast.30, f32[2,512,512]{2,1,0:T(8,128)S(1)} %bitcast.27, bf16[2,256,768]{2,1,0:T(8,128)(2,1)S(1)} %bitcast.29, f32[8,128]{1,0:T(8,128)S(1)} %place.1.mark_ref, ...), custom_call_target="tpu_custom_call" | custom-call | flops 3758096384 | bytes 8000000 | tf_op jit(solution)/shard_map/inverse/pallas_call | solution.py:114
  14.5 0.0 collective-permute-done.1.refs_2_
  14.5 2.7 %collective-permute-start.2 = (bf16[4,2,96,128]{3,2,1,0:T(8,128)(2,1)S(1)}, bf16[4,2,96,128]{3,2,1,0:T(8,128)(2,1)S(1)}, u32[]{:S(2)}, u32[]{:S(2)}) collective-permute-start(bf16[4,2,96,128]{3,2,1,0:T(8,128)(2,1)S(1)} %slice_bitcast_fusion.5), channel_id=1, source_target_pairs={{0,2},{2,4},{4,6},{6,0},{1,3},{3,5},{5,7},{7,1},{8,10},{10,12},{12... | collective-permute-start | bytes 589832 | tf_op jit(solution)/shard_map/ppermute | solution.py:360
  17.2 0.0 collective-permute-done.refs_1_
  17.2 0.3 collective-permute-start.3
  17.5 5.8 %collective-permute-done.4.upper_ref = bf16[2,256,768]{2,1,0:T(8,128)(2,1)S(1)} collective-permute-done((bf16[2,256,768]{2,1,0:T(8,128)(2,1)}, bf16[2,256,768]{2,1,0:T(8,128)(2,1)S(1)}, u32[]{:S(2)}, u32[]{:S(2)}) %collective-permute-start.4) | collective-permute-done | bytes 786464 | tf_op jit(solution)/shard_map/ppermute | solution.py:365
  23.3 0.1 broadcast_in_dim.2.mask_ref
  23.4 1.0 %scale_upper.1.refs_5_.refs_6_.scaled_ref = bf16[2,4,128,768]{3,2,1,0:T(8,128)(2,1)S(1)} custom-call(bf16[2,24,16,128]{3,2,1,0:T(8,128)(2,1)S(1)} %broadcast_in_dim.2.mask_ref, bf16[2,512,256]{2,1,0:T(8,128)(2,1)S(1)} %get-tuple-element.14.xh_ref, bf16[2,512,256]{2,1,0:T(8,128)(2,1)S(1)} %get-tuple-element.15.xl_ref, ...), custom_call_target="tpu_custom_call" | custom-call | flops 805306368 | bytes 6291456 | tf_op jit(solution)/shard_map/scale_upper/pallas_call | solution.py:148
  24.5 0.0 collective-permute-done.2.refs_3_
  24.5 0.2 collective-permute-done.3.refs_4_
  24.7 0.9 %shard_map.65 = bf16[4,96,768]{2,1,0:T(8,128)(2,1)S(1)} custom-call(bf16[2,24,16,128]{3,2,1,0:T(8,128)(2,1)S(1)} %broadcast_in_dim.2.mask_ref, bf16[4,2,2,96,768]{4,3,2,1,0:T(8,128)(2,1)S(1)} %bitcast.24, bf16[2,4,2,96,128]{4,3,2,1,0:T(8,128)(2,1)S(1)} %get-tuple-element.24.refs_0_, bf16[2,4,2,96,128]{4,3,2,1,0:T(8,128)(2,1)S(1)} %collective-permute-done.refs_1_, ...), custom_call_target="tpu_custom_call" | custom-call | flops 603979776 | bytes 4000000 | tf_op jit(solution)/shard_map/pallas_call | solution.py:187
  25.6 2.6 %collective-permute-start.5 = (bf16[4,96,768]{2,1,0:T(8,128)(2,1)S(1)}, bf16[4,96,768]{2,1,0:T(8,128)(2,1)S(1)}, u32[]{:S(2)}, u32[]{:S(2)}) collective-permute-start(bf16[4,96,768]{2,1,0:T(8,128)(2,1)S(1)} %shard_map.65), channel_id=1, source_target_pairs={{0,8},{8,0},{16,24},{24,16},{32,40},{40,32},{48,56},{56,48},{64,72... | collective-permute-start | bytes 1769480 | tf_op jit(solution)/shard_map/ppermute | solution.py:363
  28.2 0.0 collective-permute-done.10.last_ref
  28.2 2.7 %collective-permute-start.11 = (bf16[4,2,96,128]{3,2,1,0:T(8,128)(2,1)S(1)}, bf16[4,2,96,128]{3,2,1,0:T(8,128)(2,1)S(1)}, u32[]{:S(2)}, u32[]{:S(2)}) collective-permute-start(bf16[4,2,96,128]{3,2,1,0:T(8,128)(2,1)S(1)} %slice_bitcast_fusion.3), channel_id=1, source_target_pairs={{0,2},{2,4},{4,6},{6,0},{1,3},{3,5},{5,7},{7,1},{8,10},{10,12},{12... | collective-permute-start | bytes 589832 | tf_op jit(solution)/shard_map/ppermute | solution.py:360
  30.9 0.0 collective-permute-done.9.next_ref
  30.9 0.1 collective-permute-start.12
  31.0 0.8 %shard_map.64.kept_ref = f32[4,96,768]{2,1,0:T(8,128)S(1)} custom-call(bf16[2,24,16,128]{3,2,1,0:T(8,128)(2,1)S(1)} %broadcast_in_dim.2.mask_ref, bf16[4,2,2,96,768]{4,3,2,1,0:T(8,128)(2,1)S(1)} %bitcast.25, bf16[2,4,2,96,128]{4,3,2,1,0:T(8,128)(2,1)S(1)} %get-tuple-element.24.refs_0_, bf16[2,4,2,96,128]{4,3,2,1,0:T(8,128)(2,1)S(1)} %collective-permute-done.refs_1_, ...), custom_call_target="tpu_custom_call" | custom-call | flops 603979776 | bytes 4000000 | tf_op jit(solution)/shard_map/pallas_call | solution.py:187
  31.9 0.4 shard_map.66
  32.2 1.3 %shard_map.68.near_ref = f32[2,4,96,768]{3,2,1,0:T(8,128)S(1)} custom-call(bf16[2,24,16,128]{3,2,1,0:T(8,128)(2,1)S(1)} %broadcast_in_dim.2.mask_ref, bf16[4,2,2,96,768]{4,3,2,1,0:T(8,128)(2,1)S(1)} %bitcast.26, bf16[2,4,2,96,128]{4,3,2,1,0:T(8,128)(2,1)S(1)} %get-tuple-element.23.own_ref, bf16[2,4,2,96,128]{4,3,2,1,0:T(8,128)(2,1)S(1)} %collective-permute-done.9.next_ref, ...), custom_call_target="tpu_custom_call" | custom-call | flops 905969664 | bytes 8000000 | tf_op jit(solution)/shard_map/pallas_call | solution.py:243
  33.5 1.6 %collective-permute-done.11.right_ref = bf16[4,2,96,128]{3,2,1,0:T(8,128)(2,1)S(1)} collective-permute-done((bf16[4,2,96,128]{3,2,1,0:T(8,128)(2,1)S(1)}, bf16[4,2,96,128]{3,2,1,0:T(8,128)(2,1)S(1)}, u32[]{:S(2)}, u32[]{:S(2)}) %collective-permute-start.11) | collective-permute-done | bytes 196640 | tf_op jit(solution)/shard_map/ppermute | solution.py:360
  35.1 3.2 %collective-permute-done.12.left_ref = bf16[4,2,96,128]{3,2,1,0:T(8,128)(2,1)S(1)} collective-permute-done((bf16[4,2,96,128]{3,2,1,0:T(8,128)(2,1)S(1)}, bf16[4,2,96,128]{3,2,1,0:T(8,128)(2,1)S(1)}, u32[]{:S(2)}, u32[]{:S(2)}) %collective-permute-start.12) | collective-permute-done | bytes 196640 | tf_op jit(solution)/shard_map/ppermute | solution.py:360
  38.3 0.4 shard_map.70
  38.8 1.3 %collective-permute-start.13 = (bf16[4,96,768]{2,1,0:T(8,128)(2,1)S(1)}, bf16[4,96,768]{2,1,0:T(8,128)(2,1)S(1)}, u32[]{:S(2)}, u32[]{:S(2)}) collective-permute-start(bf16[4,96,768]{2,1,0:T(8,128)(2,1)S(1)} %shard_map.70), channel_id=1, source_target_pairs={{0,8},{8,0},{16,24},{24,16},{32,40},{40,32},{48,56},{56,48},{64,72... | collective-permute-start | bytes 1769480 | tf_op jit(solution)/shard_map/ppermute | solution.py:363
  40.0 0.0 collective-permute-start.6
  40.0 1.6 %collective-permute-start.8 = (bf16[96,768]{1,0:T(8,128)(2,1)S(1)}, bf16[96,768]{1,0:T(8,128)(2,1)S(1)}, u32[]{:S(2)}, u32[]{:S(2)}) collective-permute-start(bf16[96,768]{1,0:T(8,128)(2,1)S(1)} %get-tuple-element.19._), channel_id=1, source_target_pairs={{0,16},{8,24},{16,0},{24,8},{32,48},{40,56},{48,32},{56,40},{64,80... | collective-permute-start | bytes 442376 | tf_op jit(solution)/shard_map/ppermute | solution.py:363
  41.6 1.2 %collective-permute-start.7 = (bf16[96,768]{1,0:T(8,128)(2,1)S(1)}, bf16[96,768]{1,0:T(8,128)(2,1)S(1)}, u32[]{:S(2)}, u32[]{:S(2)}) collective-permute-start(bf16[96,768]{1,0:T(8,128)(2,1)S(1)} %get-tuple-element.18), channel_id=1, source_target_pairs={{0,48},{8,56},{16,32},{24,40},{32,16},{40,24},{48,0},{56,8},{64,11... | collective-permute-start | bytes 442376 | tf_op jit(solution)/shard_map/ppermute | solution.py:363
  42.8 0.3 shard_map.69.kept_ref
  43.2 0.4 shard_map.72
  43.5 1.3 %collective-permute-start.14 = (bf16[96,768]{1,0:T(8,128)(2,1)S(1)}, bf16[96,768]{1,0:T(8,128)(2,1)S(1)}, u32[]{:S(2)}, u32[]{:S(2)}) collective-permute-start(bf16[96,768]{1,0:T(8,128)(2,1)S(1)} %get-tuple-element.20), channel_id=1, source_target_pairs={{0,32},{8,40},{16,48},{24,56},{32,0},{40,8},{48,16},{56,24},{64,96... | collective-permute-start | bytes 442376 | tf_op jit(solution)/shard_map/ppermute | solution.py:363
  44.8 2.4 %collective-permute-start.15 = (bf16[96,768]{1,0:T(8,128)(2,1)S(1)}, bf16[96,768]{1,0:T(8,128)(2,1)S(1)}, u32[]{:S(2)}, u32[]{:S(2)}) collective-permute-start(bf16[96,768]{1,0:T(8,128)(2,1)S(1)} %get-tuple-element.21), channel_id=1, source_target_pairs={{0,48},{8,56},{16,32},{24,40},{32,16},{40,24},{48,0},{56,8},{64,11... | collective-permute-start | bytes 442376 | tf_op jit(solution)/shard_map/ppermute | solution.py:363
  47.2 0.0 collective-permute-done.6.refs_0_
  47.2 4.3 %collective-permute-start.16 = (bf16[96,768]{1,0:T(8,128)(2,1)S(1)}, bf16[96,768]{1,0:T(8,128)(2,1)S(1)}, u32[]{:S(2)}, u32[]{:S(2)}) collective-permute-start(bf16[96,768]{1,0:T(8,128)(2,1)S(1)} %get-tuple-element.22), channel_id=1, source_target_pairs={{0,16},{8,24},{16,0},{24,8},{32,48},{40,56},{48,32},{56,40},{64,80... | collective-permute-start | bytes 442376 | tf_op jit(solution)/shard_map/ppermute | solution.py:363
  51.5 11.0 %collective-permute-done.7.refs_1_ = bf16[96,768]{1,0:T(8,128)(2,1)S(1)} collective-permute-done((bf16[96,768]{1,0:T(8,128)(2,1)S(1)}, bf16[96,768]{1,0:T(8,128)(2,1)S(1)}, u32[]{:S(2)}, u32[]{:S(2)}) %collective-permute-start.7) | collective-permute-done | bytes 147488 | tf_op jit(solution)/shard_map/ppermute | solution.py:363
  62.5 0.0 collective-permute-done.8.refs_2_
  62.5 0.3 shard_map.67.early_ref
  62.8 0.1 shard_map.71.own_ref
  62.9 5.9 %collective-permute-done.15.refs_1_ = bf16[96,768]{1,0:T(8,128)(2,1)S(1)} collective-permute-done((bf16[96,768]{1,0:T(8,128)(2,1)S(1)}, bf16[96,768]{1,0:T(8,128)(2,1)S(1)}, u32[]{:S(2)}, u32[]{:S(2)}) %collective-permute-start.15) | collective-permute-done | bytes 147488 | tf_op jit(solution)/shard_map/ppermute | solution.py:363
  68.8 0.0 collective-permute-done.16.refs_2_
  68.8 1.0 %final_sums.1 = f32[1,192,768]{2,1,0:T(8,128)} custom-call(f32[96,768]{1,0:T(8,128)S(1)} %shard_map.67.early_ref, f32[96,768]{1,0:T(8,128)S(1)} %shard_map.71.own_ref, bf16[96,768]{1,0:T(8,128)(2,1)S(1)} %collective-permute-done.14.refs_0_, bf16[96,768]{1,0:T(8,128)(2,1)S(1)} %collective-permute-done.15.refs_1_, ...), custom_call_target="tpu_custom_call" | custom-call | flops 294912 | bytes 884736 | tf_op jit(solution)/shard_map/final_sums/pallas_call | solution.py:337
  (16 shorter events, 0.1 us)
Async XLA Ops:
  1.2 13.3 %collective-permute-start.1 = (bf16[2,4,2,96,128]{4,3,2,1,0:T(8,128)(2,1)S(1)}, bf16[2,4,2,96,128]{4,3,2,1,0:T(8,128)(2,1)S(1)}, u32[]{:S(2)}, u32[]{:S(2)}) collective-permute-start(bf16[2,4,2,96,128]{4,3,2,1,0:T(8,128)(2,1)S(1)} %get-tuple-element.24.refs_0_), channel_id=1, source_target_pairs={{0,2},{2,4},{4,6},{6,0},{1,3},{3,5},{5,7},{7,1},{8,10},{10,12},{12... | collective-permute-start | bytes 1179656 | tf_op jit(solution)/shard_map/ppermute | solution.py:360
  1.5 15.8 %collective-permute-start = (bf16[2,4,2,96,128]{4,3,2,1,0:T(8,128)(2,1)S(1)}, bf16[2,4,2,96,128]{4,3,2,1,0:T(8,128)(2,1)S(1)}, u32[]{:S(2)}, u32[]{:S(2)}) collective-permute-start(bf16[2,4,2,96,128]{4,3,2,1,0:T(8,128)(2,1)S(1)} %get-tuple-element.24.refs_0_), channel_id=1, source_target_pairs={{0,6},{2,0},{4,2},{6,4},{1,7},{3,1},{5,3},{7,5},{8,14},{10,8},{12,... | collective-permute-start | bytes 1179656 | tf_op jit(solution)/shard_map/ppermute | solution.py:360
  2.7 25.4 %collective-permute-start.10 = (bf16[2,4,2,96,128]{4,3,2,1,0:T(8,128)(2,1)S(1)}, bf16[2,4,2,96,128]{4,3,2,1,0:T(8,128)(2,1)S(1)}, u32[]{:S(2)}, u32[]{:S(2)}) collective-permute-start(bf16[2,4,2,96,128]{4,3,2,1,0:T(8,128)(2,1)S(1)} %get-tuple-element.23.own_ref), channel_id=1, source_target_pairs={{0,2},{2,4},{4,6},{6,0},{1,3},{3,5},{5,7},{7,1},{8,10},{10,12},{12... | collective-permute-start | bytes 1179656 | tf_op jit(solution)/shard_map/ppermute | solution.py:360
  4.1 26.8 %collective-permute-start.9 = (bf16[2,4,2,96,128]{4,3,2,1,0:T(8,128)(2,1)S(1)}, bf16[2,4,2,96,128]{4,3,2,1,0:T(8,128)(2,1)S(1)}, u32[]{:S(2)}, u32[]{:S(2)}) collective-permute-start(bf16[2,4,2,96,128]{4,3,2,1,0:T(8,128)(2,1)S(1)} %get-tuple-element.23.own_ref), channel_id=1, source_target_pairs={{0,6},{2,0},{4,2},{6,4},{1,7},{3,1},{5,3},{7,5},{8,14},{10,8},{12,... | collective-permute-start | bytes 1179656 | tf_op jit(solution)/shard_map/ppermute | solution.py:360
  4.2 1.7 %copy-start = (bf16[1,1536,768]{2,1,0:T(8,128)(2,1)S(1)}, bf16[1,1536,768]{2,1,0:T(8,128)(2,1)}, u32[]{:S(2)}) copy-start(bf16[1,1536,768]{2,1,0:T(8,128)(2,1)} %param.6) | copy-start | bytes 7077892
  4.2 2.3 %copy-start.1 = (f32[1,2,512,512]{3,2,1,0:T(8,128)S(1)}, f32[1,2,512,512]{3,2,1,0:T(8,128)}, u32[]{:S(2)}) copy-start(f32[1,2,512,512]{3,2,1,0:T(8,128)} %param.9) | copy-start | bytes 6291460
  4.2 2.5 %copy-start.2 = (bf16[1,2,256,768]{3,2,1,0:T(8,128)(2,1)S(1)}, bf16[1,2,256,768]{3,2,1,0:T(8,128)(2,1)}, u32[]{:S(2)}) copy-start(bf16[1,2,256,768]{3,2,1,0:T(8,128)(2,1)} %param.8) | copy-start | bytes 2359300
  4.2 2.5 %copy-start.3 = (s32[1,2]{1,0:T(1,128)S(1)}, s32[1,2]{1,0:T(1,128)}, u32[]{:S(2)}) copy-start(s32[1,2]{1,0:T(1,128)} %param.11) | copy-start | bytes 28
  4.2 19.1 %collective-permute-start.4 = (bf16[2,256,768]{2,1,0:T(8,128)(2,1)}, bf16[2,256,768]{2,1,0:T(8,128)(2,1)S(1)}, u32[]{:S(2)}, u32[]{:S(2)}) collective-permute-start(bf16[2,256,768]{2,1,0:T(8,128)(2,1)} %bitcast.28), channel_id=1, source_target_pairs={{0,1},{1,0},{2,3},{3,2},{4,5},{5,4},{6,7},{7,6},{8,9},{9,8},{10,11... | collective-permute-start | bytes 2359304 | tf_op jit(solution)/shard_map/ppermute | solution.py:365
  6.7 10.9 %copy-start.4 = (s32[1,2,24]{2,1,0:T(2,128)S(1)}, s32[1,2,24]{2,1,0:T(2,128)}, u32[]{:S(2)}) copy-start(s32[1,2,24]{2,1,0:T(2,128)} %param.10) | copy-start | bytes 580
  14.5 9.9 %collective-permute-start.2 = (bf16[4,2,96,128]{3,2,1,0:T(8,128)(2,1)S(1)}, bf16[4,2,96,128]{3,2,1,0:T(8,128)(2,1)S(1)}, u32[]{:S(2)}, u32[]{:S(2)}) collective-permute-start(bf16[4,2,96,128]{3,2,1,0:T(8,128)(2,1)S(1)} %slice_bitcast_fusion.5), channel_id=1, source_target_pairs={{0,2},{2,4},{4,6},{6,0},{1,3},{3,5},{5,7},{7,1},{8,10},{10,12},{12... | collective-permute-start | bytes 589832 | tf_op jit(solution)/shard_map/ppermute | solution.py:360
  17.2 7.4 %collective-permute-start.3 = (bf16[4,2,96,128]{3,2,1,0:T(8,128)(2,1)S(1)}, bf16[4,2,96,128]{3,2,1,0:T(8,128)(2,1)S(1)}, u32[]{:S(2)}, u32[]{:S(2)}) collective-permute-start(bf16[4,2,96,128]{3,2,1,0:T(8,128)(2,1)S(1)} %slice_bitcast_fusion.4), channel_id=1, source_target_pairs={{0,6},{2,0},{4,2},{6,4},{1,7},{3,1},{5,3},{7,5},{8,14},{10,8},{12,... | collective-permute-start | bytes 589832 | tf_op jit(solution)/shard_map/ppermute | solution.py:360
  25.6 6.3 %collective-permute-start.5 = (bf16[4,96,768]{2,1,0:T(8,128)(2,1)S(1)}, bf16[4,96,768]{2,1,0:T(8,128)(2,1)S(1)}, u32[]{:S(2)}, u32[]{:S(2)}) collective-permute-start(bf16[4,96,768]{2,1,0:T(8,128)(2,1)S(1)} %shard_map.65), channel_id=1, source_target_pairs={{0,8},{8,0},{16,24},{24,16},{32,40},{40,32},{48,56},{56,48},{64,72... | collective-permute-start | bytes 1769480 | tf_op jit(solution)/shard_map/ppermute | solution.py:363
  28.2 6.9 %collective-permute-start.11 = (bf16[4,2,96,128]{3,2,1,0:T(8,128)(2,1)S(1)}, bf16[4,2,96,128]{3,2,1,0:T(8,128)(2,1)S(1)}, u32[]{:S(2)}, u32[]{:S(2)}) collective-permute-start(bf16[4,2,96,128]{3,2,1,0:T(8,128)(2,1)S(1)} %slice_bitcast_fusion.3), channel_id=1, source_target_pairs={{0,2},{2,4},{4,6},{6,0},{1,3},{3,5},{5,7},{7,1},{8,10},{10,12},{12... | collective-permute-start | bytes 589832 | tf_op jit(solution)/shard_map/ppermute | solution.py:360
  30.9 7.4 %collective-permute-start.12 = (bf16[4,2,96,128]{3,2,1,0:T(8,128)(2,1)S(1)}, bf16[4,2,96,128]{3,2,1,0:T(8,128)(2,1)S(1)}, u32[]{:S(2)}, u32[]{:S(2)}) collective-permute-start(bf16[4,2,96,128]{3,2,1,0:T(8,128)(2,1)S(1)} %slice_bitcast_fusion.2), channel_id=1, source_target_pairs={{0,6},{2,0},{4,2},{6,4},{1,7},{3,1},{5,3},{7,5},{8,14},{10,8},{12,... | collective-permute-start | bytes 589832 | tf_op jit(solution)/shard_map/ppermute | solution.py:360
  38.8 4.4 %collective-permute-start.13 = (bf16[4,96,768]{2,1,0:T(8,128)(2,1)S(1)}, bf16[4,96,768]{2,1,0:T(8,128)(2,1)S(1)}, u32[]{:S(2)}, u32[]{:S(2)}) collective-permute-start(bf16[4,96,768]{2,1,0:T(8,128)(2,1)S(1)} %shard_map.70), channel_id=1, source_target_pairs={{0,8},{8,0},{16,24},{24,16},{32,40},{40,32},{48,56},{56,48},{64,72... | collective-permute-start | bytes 1769480 | tf_op jit(solution)/shard_map/ppermute | solution.py:363
  40.0 7.2 %collective-permute-start.6 = (bf16[96,768]{1,0:T(8,128)(2,1)S(1)}, bf16[96,768]{1,0:T(8,128)(2,1)S(1)}, u32[]{:S(2)}, u32[]{:S(2)}) collective-permute-start(bf16[96,768]{1,0:T(8,128)(2,1)S(1)} %get-tuple-element.17), channel_id=1, source_target_pairs={{0,32},{8,40},{16,48},{24,56},{32,0},{40,8},{48,16},{56,24},{64,96... | collective-permute-start | bytes 442376 | tf_op jit(solution)/shard_map/ppermute | solution.py:363
  40.0 22.5 %collective-permute-start.8 = (bf16[96,768]{1,0:T(8,128)(2,1)S(1)}, bf16[96,768]{1,0:T(8,128)(2,1)S(1)}, u32[]{:S(2)}, u32[]{:S(2)}) collective-permute-start(bf16[96,768]{1,0:T(8,128)(2,1)S(1)} %get-tuple-element.19._), channel_id=1, source_target_pairs={{0,16},{8,24},{16,0},{24,8},{32,48},{40,56},{48,32},{56,40},{64,80... | collective-permute-start | bytes 442376 | tf_op jit(solution)/shard_map/ppermute | solution.py:363
  41.6 20.9 %collective-permute-start.7 = (bf16[96,768]{1,0:T(8,128)(2,1)S(1)}, bf16[96,768]{1,0:T(8,128)(2,1)S(1)}, u32[]{:S(2)}, u32[]{:S(2)}) collective-permute-start(bf16[96,768]{1,0:T(8,128)(2,1)S(1)} %get-tuple-element.18), channel_id=1, source_target_pairs={{0,48},{8,56},{16,32},{24,40},{32,16},{40,24},{48,0},{56,8},{64,11... | collective-permute-start | bytes 442376 | tf_op jit(solution)/shard_map/ppermute | solution.py:363
  43.5 19.4 %collective-permute-start.14 = (bf16[96,768]{1,0:T(8,128)(2,1)S(1)}, bf16[96,768]{1,0:T(8,128)(2,1)S(1)}, u32[]{:S(2)}, u32[]{:S(2)}) collective-permute-start(bf16[96,768]{1,0:T(8,128)(2,1)S(1)} %get-tuple-element.20), channel_id=1, source_target_pairs={{0,32},{8,40},{16,48},{24,56},{32,0},{40,8},{48,16},{56,24},{64,96... | collective-permute-start | bytes 442376 | tf_op jit(solution)/shard_map/ppermute | solution.py:363
  44.8 24.0 %collective-permute-start.15 = (bf16[96,768]{1,0:T(8,128)(2,1)S(1)}, bf16[96,768]{1,0:T(8,128)(2,1)S(1)}, u32[]{:S(2)}, u32[]{:S(2)}) collective-permute-start(bf16[96,768]{1,0:T(8,128)(2,1)S(1)} %get-tuple-element.21), channel_id=1, source_target_pairs={{0,48},{8,56},{16,32},{24,40},{32,16},{40,24},{48,0},{56,8},{64,11... | collective-permute-start | bytes 442376 | tf_op jit(solution)/shard_map/ppermute | solution.py:363
  47.2 21.7 %collective-permute-start.16 = (bf16[96,768]{1,0:T(8,128)(2,1)S(1)}, bf16[96,768]{1,0:T(8,128)(2,1)S(1)}, u32[]{:S(2)}, u32[]{:S(2)}) collective-permute-start(bf16[96,768]{1,0:T(8,128)(2,1)S(1)} %get-tuple-element.22), channel_id=1, source_target_pairs={{0,16},{8,24},{16,0},{24,8},{32,48},{40,56},{48,32},{56,40},{64,80... | collective-permute-start | bytes 442376 | tf_op jit(solution)/shard_map/ppermute | solution.py:363
